TPU v7x, 128 devices: a whole 4x4x4 slice. The times are simulated.
128 devices in a mesh: gz: 16 (over x, y_lo, core), gy: 8 (over y_hi, z).
Axes of the slice: x: 4, y: 4 (y_hi: 2, y_lo: 2; y = y_hi * 2 + y_lo), z: 4, core: 2. Of those that a mesh axis runs over, the one named last changes fastest.
Arguments:
- e_field: float32 [3, 512, 128, 256], P(None, 'gz', 'gy'), may hold values from -6 to 6
- h_field: float32 [3, 512, 128, 256], P(None, 'gz', 'gy'), may hold values from -6 to 6
- e_coef: float32 [512, 128, 256], P('gz', 'gy'), may hold values from 0.14 to 0.55
- e_loss: float32 [512, 128, 256], P('gz', 'gy'), may hold values from 0 to 0.1
- port_cell: int32 [4096], P(('gz', 'gy')), may hold values from 0 to 131071
- port_node: int32 [4096], replicated, may hold values from 0 to 16383
- port_gain: float32 [4096], replicated, may hold values from 0.5 to 2
- diag_blocks: float32 [256, 64, 64], P(('gz', 'gy')), may hold values from -0.5 to 4.5, as said below
- inv_blocks: float32 [256, 64, 64], P(('gz', 'gy')), may hold values from -0.012 to 0.247, as said below
- off_blocks: float32 [256, 4, 64, 64], P(('gz', 'gy')), may hold values from -0.1875 to 0.1875
- off_cols: int32 [256, 4], P(('gz', 'gy')), may hold values from 0 to 255
- volts_init: float32 [16384], P(('gz', 'gy')), may hold values from -6 to 6
Outputs:
- e_final: float32 [3, 512, 128, 256], P(None, 'gz', 'gy')
- h_final: float32 [3, 512, 128, 256], P(None, 'gz', 'gy')
- node_volts: float32 [16384], P(('gz', 'gy'))
Inputs may be any that keep to these rules, and one draw needn't show every extreme that they name: `diag_blocks`: 4 times the identity plus independent entries of spread 1/8. `inv_blocks`: 0.235 times the identity plus small independent entries. `port_cell`: ports may share a cell.
All inputs are finite; a program needn't handle non-finite values.
Results may differ from a plain program's by a relative error of at most 0.00019.
Values sent between devices are 32-bit elements; how exact they have to be, the bound alone decides.
No kernel may reach another device: no remote copies, remote signals or barrier semaphores. Data moves between devices by JAX's collectives and lax.ppermute only.
A program may use at most 64 MiB of HBM per device.

v0:
```python
import jax
import jax.numpy as jnp
from jax import lax
from jax.sharding import PartitionSpec as P

STEPS = 5
NEWTON = 2
BS = 64
NB_DEV = 2
PORT_DEV = 32


precise = lax.Precision.HIGHEST
time_step = 0.55
charge_scale = 4.0
diode_weight = 0.5


def shifted(value, axis, steps):
    count = lax.axis_size(axis)
    first, last = (max(0, -steps), min(count, count - steps))
    return lax.ppermute(value, axis, [(source, source + steps) for source in range(first, last)])


def update_magnetic(e_now, h_now):
    upper_z = shifted(e_now[0:2, 0], "gz", -1)
    upper_y = shifted(jnp.stack([e_now[0, :, 0], e_now[2, :, 0]]), "gy", -1)
    above_z = jnp.concatenate([e_now[0:2, 1:], upper_z[:, None]], axis=1)
    inner_y = jnp.stack([e_now[0, :, 1:], e_now[2, :, 1:]])
    above_y = jnp.concatenate([inner_y, upper_y[:, :, None]], axis=2)
    blank = jnp.zeros((2,) + e_now.shape[1:3] + (1,), jnp.float32)
    above_x = jnp.concatenate([e_now[1:3, :, :, 1:], blank], axis=3)
    curl_x = above_y[1] - e_now[2] - (above_z[1] - e_now[1])
    curl_y = above_z[0] - e_now[0] - (above_x[1] - e_now[2])
    curl_z = above_x[0] - e_now[1] - (above_y[0] - e_now[0])
    return h_now - time_step * jnp.stack([curl_x, curl_y, curl_z])


def update_electric(e_now, h_now, e_coef, e_loss):
    lower_z = shifted(h_now[0:2, -1], "gz", 1)
    lower_y = shifted(jnp.stack([h_now[0, :, -1], h_now[2, :, -1]]), "gy", 1)
    below_z = jnp.concatenate([lower_z[:, None], h_now[0:2, :-1]], axis=1)
    inner_y = jnp.stack([h_now[0, :, :-1], h_now[2, :, :-1]])
    below_y = jnp.concatenate([lower_y[:, :, None], inner_y], axis=2)
    blank = jnp.zeros((2,) + h_now.shape[1:3] + (1,), jnp.float32)
    below_x = jnp.concatenate([blank, h_now[1:3, :, :, :-1]], axis=3)
    back_x = h_now[2] - below_y[1] - (h_now[1] - below_z[1])
    back_y = h_now[0] - below_z[0] - (h_now[2] - below_x[1])
    back_z = h_now[1] - below_x[0] - (h_now[0] - below_y[0])
    return (1.0 - e_loss) * e_now + e_coef * jnp.stack([back_x, back_y, back_z])


def whole_terms(
    volts_all, samples_all, port_node, port_gain, off_blocks, off_cols, own_nodes, first_node
):
    blocks_all = volts_all.reshape(-1, BS)
    picked = blocks_all[off_cols]
    offsum = jnp.einsum("jkab,jkb->ja", off_blocks, picked, precision=precise)
    columns = jnp.arange(NB_DEV * BS, dtype=jnp.int32)
    onehot = ((port_node - first_node)[:, None] == columns[None, :]).astype(jnp.float32)
    inject = jnp.dot(port_gain * samples_all, onehot, precision=precise).reshape(NB_DEV, BS)
    near = volts_all[own_nodes]
    return (offsum, inject, near)


def newton_solve(volts, offsum, inject, diag_blocks, inv_blocks):
    vstart = volts.reshape(NB_DEV, BS)
    target = charge_scale * vstart + inject - offsum
    iterate = vstart
    for newton_round in range(NEWTON):
        resid = (
            jnp.einsum("jab,jb->ja", diag_blocks, iterate, precision=precise)
            + diode_weight * jnp.tanh(iterate)
            - target
        )
        iterate = iterate - jnp.einsum("jab,jb->ja", inv_blocks, resid, precision=precise)
    return iterate.reshape(-1)


def body(
    e_field,
    h_field,
    e_coef,
    e_loss,
    port_cell,
    port_node,
    port_gain,
    diag_blocks,
    inv_blocks,
    off_blocks,
    off_cols,
    volts_init,
):
    device = lax.axis_index(("gz", "gy"))
    first_node = device * (NB_DEV * BS)
    own_nodes = lax.dynamic_slice_in_dim(port_node, device * PORT_DEV, PORT_DEV)
    own_gain = lax.dynamic_slice_in_dim(port_gain, device * PORT_DEV, PORT_DEV)
    coef_flat = e_coef.reshape(-1)
    cell_coef = coef_flat[port_cell]
    depth, height, width = e_coef.shape

    def circuit_inputs(volts, samples):
        volts_all, samples_all = (
            lax.all_gather(volts, ("gz", "gy"), axis=0, tiled=True),
            lax.all_gather(samples, ("gz", "gy"), axis=0, tiled=True),
        )
        return whole_terms(
            volts_all,
            samples_all,
            port_node,
            port_gain,
            off_blocks,
            off_cols,
            own_nodes,
            first_node,
        )

    def advance(step_index, state):
        e_now, h_now, volts, samples = state
        offsum, inject, near = circuit_inputs(volts, samples)
        h_new = update_magnetic(e_now, h_now)
        e_new = update_electric(e_now, h_new, e_coef, e_loss)
        current = own_gain * (samples - near)
        new_z = e_new[2].reshape(-1).at[port_cell].add(-cell_coef * current)
        e_new = jnp.stack([e_new[0], e_new[1], new_z.reshape(depth, height, width)])
        volts_new = newton_solve(volts, offsum, inject, diag_blocks, inv_blocks)
        samples_new = e_new[2].reshape(-1)[port_cell]
        return (e_new, h_new, volts_new, samples_new)

    samples_start = e_field[2].reshape(-1)[port_cell]
    e_end, h_end, volts_end, samples_end = lax.fori_loop(
        0, STEPS, advance, (e_field, h_field, volts_init, samples_start)
    )
    return (e_end, h_end, volts_end)


def solution(mesh):
    placed = (
        P(None, "gz", "gy", None),
        P(None, "gz", "gy", None),
        P("gz", "gy", None),
        P("gz", "gy", None),
        P(("gz", "gy")),
        P(),
        P(),
        P(("gz", "gy"), None, None),
        P(("gz", "gy"), None, None),
        P(("gz", "gy"), None, None, None),
        P(("gz", "gy"), None),
        P(("gz", "gy")),
    )
    return jax.shard_map(
        body,
        mesh=mesh,
        in_specs=placed,
        out_specs=(P(None, "gz", "gy", None), P(None, "gz", "gy", None), P(("gz", "gy"))),
        check_vma=False,
    )
```

profile of v0, /device:TPU:1, one launch (start us, length us, event | category | flops | bytes accessed | tf_op | source)
XLA Modules:
  0.0 2141.8 jit_solution(3278946582006856271)
XLA Ops:
  0.6 1.4 copy.82
  4.6 2.1 gather_fusion.3
  6.8 2.1 copy.48
  8.9 1.6 gather_fusion.4
  11.0 2129.1 %while.18 = (s32[]{:T(128)}, f32[3,32,16,256]{3,2,1,0:T(8,128)S(1)}, f32[3,32,16,256]{3,2,1,0:T(8,128)S(1)}, f32[128]{0:T(128)S(1)}, f32[32]{0:T(128)}, /*index=...) while((s32[]{:T(128)}, ...), condition=%wide.region_2.0_spmd, body=%wide.region_0.0_spmd.sunk | while | flops 15647837 | bytes 67082616 | solution.py:131
  14.5 3.3 collective-permute-start
  19.0 1.3 slice.340
  22.6 1.9 broadcast_subtract_fusion.4
  24.5 304.1 %all-gather.2 = f32[128,1,128]{2,1,0:T(1,128)S(1)} all-gather(f32[1,1,128]{2,1,0:T(1,128)S(1)} %bitcast.168), channel_id=1, replica_groups=mesh['gz'=16,'gy'=8] {'gz','gy'}, dimensions={0}, use_global_device_ids=true | all-gather | bytes 66048 | tf_op jit(solution)/shard_map/while/body/eval_jaxpr/all_gather | solution.py:104
  333.5 76.8 %all-reduce.4 = f32[4096]{0:T(1024)S(1)} all-reduce(f32[4096]{0:T(1024)S(1)} %dynamic-update-slice.2), channel_id=1, replica_groups=mesh['gz'=16,'gy'=8] {'gz','gy'}, use_global_device_ids=true, to_apply=%add.2 | all-reduce | flops 4096 | bytes 32768 | tf_op jit(solution)/shard_map/while
  412.1 1.5 gather_fusion.1
  423.5 1.3 pad_maximum_fusion.11
  424.9 1.3 fusion.82
  426.8 1.3 collective-permute-start.3
  428.3 3.5 collective-permute-start.2
  437.8 1.3 gather_fusion.2
  439.2 1.5 pad_maximum_fusion.13
  444.2 1.9 collective-permute-start
  447.3 1.3 slice.340
  450.9 1.9 broadcast_subtract_fusion.4
  452.8 300.7 %all-gather.2 = f32[128,1,128]{2,1,0:T(1,128)S(1)} all-gather(f32[1,1,128]{2,1,0:T(1,128)S(1)} %bitcast.168), channel_id=1, replica_groups=mesh['gz'=16,'gy'=8] {'gz','gy'}, dimensions={0}, use_global_device_ids=true | all-gather | bytes 66048 | tf_op jit(solution)/shard_map/while/body/eval_jaxpr/all_gather | solution.py:104
  758.4 76.8 %all-reduce.4 = f32[4096]{0:T(1024)S(1)} all-reduce(f32[4096]{0:T(1024)S(1)} %dynamic-update-slice.2), channel_id=1, replica_groups=mesh['gz'=16,'gy'=8] {'gz','gy'}, use_global_device_ids=true, to_apply=%add.2 | all-reduce | flops 4096 | bytes 32768 | tf_op jit(solution)/shard_map/while
  837.0 1.5 gather_fusion.1
  848.3 1.3 pad_maximum_fusion.11
  849.7 1.3 fusion.82
  851.7 1.3 collective-permute-start.3
  853.1 3.5 collective-permute-start.2
  862.7 1.3 gather_fusion.2
  864.0 1.5 pad_maximum_fusion.13
  869.1 1.9 collective-permute-start
  872.1 1.3 slice.340
  875.7 1.9 broadcast_subtract_fusion.4
  877.6 300.7 %all-gather.2 = f32[128,1,128]{2,1,0:T(1,128)S(1)} all-gather(f32[1,1,128]{2,1,0:T(1,128)S(1)} %bitcast.168), channel_id=1, replica_groups=mesh['gz'=16,'gy'=8] {'gz','gy'}, dimensions={0}, use_global_device_ids=true | all-gather | bytes 66048 | tf_op jit(solution)/shard_map/while/body/eval_jaxpr/all_gather | solution.py:104
  1183.2 76.8 %all-reduce.4 = f32[4096]{0:T(1024)S(1)} all-reduce(f32[4096]{0:T(1024)S(1)} %dynamic-update-slice.2), channel_id=1, replica_groups=mesh['gz'=16,'gy'=8] {'gz','gy'}, use_global_device_ids=true, to_apply=%add.2 | all-reduce | flops 4096 | bytes 32768 | tf_op jit(solution)/shard_map/while
  1261.8 1.5 gather_fusion.1
  1273.2 1.3 pad_maximum_fusion.11
  1274.6 1.3 fusion.82
  1276.5 1.3 collective-permute-start.3
  1278.0 3.5 collective-permute-start.2
  1287.5 1.3 gather_fusion.2
  1288.9 1.5 pad_maximum_fusion.13
  1293.9 1.9 collective-permute-start
  1297.0 1.3 slice.340
  1300.6 1.9 broadcast_subtract_fusion.4
  1302.5 300.7 %all-gather.2 = f32[128,1,128]{2,1,0:T(1,128)S(1)} all-gather(f32[1,1,128]{2,1,0:T(1,128)S(1)} %bitcast.168), channel_id=1, replica_groups=mesh['gz'=16,'gy'=8] {'gz','gy'}, dimensions={0}, use_global_device_ids=true | all-gather | bytes 66048 | tf_op jit(solution)/shard_map/while/body/eval_jaxpr/all_gather | solution.py:104
  1608.1 76.8 %all-reduce.4 = f32[4096]{0:T(1024)S(1)} all-reduce(f32[4096]{0:T(1024)S(1)} %dynamic-update-slice.2), channel_id=1, replica_groups=mesh['gz'=16,'gy'=8] {'gz','gy'}, use_global_device_ids=true, to_apply=%add.2 | all-reduce | flops 4096 | bytes 32768 | tf_op jit(solution)/shard_map/while
  1686.7 1.5 gather_fusion.1
  1698.0 1.3 pad_maximum_fusion.11
  1699.4 1.3 fusion.82
  1702.8 3.5 collective-permute-start.2
  1712.4 1.3 gather_fusion.2
  1713.7 1.5 pad_maximum_fusion.13
  1718.8 1.9 collective-permute-start
  1721.9 1.3 slice.340
  1725.4 1.9 broadcast_subtract_fusion.4
  1727.3 300.7 %all-gather.2 = f32[128,1,128]{2,1,0:T(1,128)S(1)} all-gather(f32[1,1,128]{2,1,0:T(1,128)S(1)} %bitcast.168), channel_id=1, replica_groups=mesh['gz'=16,'gy'=8] {'gz','gy'}, dimensions={0}, use_global_device_ids=true | all-gather | bytes 66048 | tf_op jit(solution)/shard_map/while/body/eval_jaxpr/all_gather | solution.py:104
  2032.9 76.8 %all-reduce.4 = f32[4096]{0:T(1024)S(1)} all-reduce(f32[4096]{0:T(1024)S(1)} %dynamic-update-slice.2), channel_id=1, replica_groups=mesh['gz'=16,'gy'=8] {'gz','gy'}, use_global_device_ids=true, to_apply=%add.2 | all-reduce | flops 4096 | bytes 32768 | tf_op jit(solution)/shard_map/while
  2111.5 1.5 gather_fusion.1
  2122.9 1.3 pad_maximum_fusion.11
  2124.3 1.3 fusion.82
  2126.2 1.3 collective-permute-start.3
  2127.7 3.5 collective-permute-start.2
  2137.2 1.3 gather_fusion.2
  2138.6 1.5 pad_maximum_fusion.13
  (454 shorter events, 156.6 us)
Async XLA Ops:
  2.0 2.6 copy-start.18
  3.5 7.5 copy-start.2
  3.5 7.5 copy-start.7
  3.6 7.5 copy-start.15
  11.0 317.6 %copy-start.20 = (s32[32]{0:T(128)}, s32[32]{0:T(128)S(1)}, u32[]{:S(2)}) copy-start(s32[32]{0:T(128)S(1)} %get-tuple-element.465) | copy-start | bytes 388 | tf_op jit(solution)/shard_map/while
  12.6 410.0 %collective-permute-start.1 = (f32[2,32,256]{2,1,0:T(8,128)}, f32[2,32,256]{2,1,0:T(8,128)}, u32[]{:S(2)}, u32[]{:S(2)}) collective-permute-start(f32[2,32,256]{2,1,0:T(8,128)} %pad_maximum_fusion.10), channel_id=1, source_target_pairs={{1,0},{2,1},{3,2},{4,3},{5,4},{6,5},{7,6},{9,8},{10,9},{11,10},{12... | collective-permute-start | bytes 196616 | tf_op jit(solution)/shard_map/while/body/eval_jaxpr/ppermute | solution.py:22
  14.5 410.3 %collective-permute-start = (f32[2,16,256]{2,1,0:T(8,128)}, f32[2,16,256]{2,1,0:T(8,128)}, u32[]{:S(2)}, u32[]{:S(2)}) collective-permute-start(f32[2,16,256]{2,1,0:T(8,128)} %slice_bitcast_fusion.7), channel_id=1, source_target_pairs={{8,0},{16,8},{24,16},{32,24},{40,32},{48,40},{56,48},{64,56},{72,6... | collective-permute-start | bytes 98312 | tf_op jit(solution)/shard_map/while/body/eval_jaxpr/ppermute | solution.py:22
  331.9 89.5 %copy-start.12 = (f32[32]{0:T(128)S(1)}, f32[32]{0:T(128)}, u32[]{:S(2)}) copy-start(f32[32]{0:T(128)} %get-tuple-element.438) | copy-start | bytes 388 | tf_op jit(solution)/shard_map/while
  331.9 89.5 %copy-start.16 = (f32[32]{0:T(128)S(1)}, f32[32]{0:T(128)}, u32[]{:S(2)}) copy-start(f32[32]{0:T(128)} %get-tuple-element.466) | copy-start | bytes 388 | tf_op jit(solution)/shard_map/while
  331.9 89.5 %copy-start.17 = (f32[32]{0:T(128)S(1)}, f32[32]{0:T(128)}, u32[]{:S(2)}) copy-start(f32[32]{0:T(128)} %get-tuple-element.467) | copy-start | bytes 388 | tf_op jit(solution)/shard_map/while
  331.9 90.1 %copy-start.9 = (s32[32]{0:T(128)S(1)}, s32[32]{0:T(128)}, u32[]{:S(2)}) copy-start(s32[32]{0:T(128)} %get-tuple-element.409) | copy-start | bytes 388 | tf_op jit(solution)/shard_map/while
  421.4 3.4 copy-start.3
  421.4 3.4 copy-start.4
  426.8 5.0 collective-permute-start.3
  428.3 4.5 collective-permute-start.2
  439.2 1.5 copy-start.21
  440.7 312.7 %copy-start.20 = (s32[32]{0:T(128)}, s32[32]{0:T(128)S(1)}, u32[]{:S(2)}) copy-start(s32[32]{0:T(128)S(1)} %get-tuple-element.465) | copy-start | bytes 388 | tf_op jit(solution)/shard_map/while
  442.3 405.1 %collective-permute-start.1 = (f32[2,32,256]{2,1,0:T(8,128)}, f32[2,32,256]{2,1,0:T(8,128)}, u32[]{:S(2)}, u32[]{:S(2)}) collective-permute-start(f32[2,32,256]{2,1,0:T(8,128)} %pad_maximum_fusion.10), channel_id=1, source_target_pairs={{1,0},{2,1},{3,2},{4,3},{5,4},{6,5},{7,6},{9,8},{10,9},{11,10},{12... | collective-permute-start | bytes 196616 | tf_op jit(solution)/shard_map/while/body/eval_jaxpr/ppermute | solution.py:22
  444.2 405.4 %collective-permute-start = (f32[2,16,256]{2,1,0:T(8,128)}, f32[2,16,256]{2,1,0:T(8,128)}, u32[]{:S(2)}, u32[]{:S(2)}) collective-permute-start(f32[2,16,256]{2,1,0:T(8,128)} %slice_bitcast_fusion.7), channel_id=1, source_target_pairs={{8,0},{16,8},{24,16},{32,24},{40,32},{48,40},{56,48},{64,56},{72,6... | collective-permute-start | bytes 98312 | tf_op jit(solution)/shard_map/while/body/eval_jaxpr/ppermute | solution.py:22
  756.8 89.5 %copy-start.12 = (f32[32]{0:T(128)S(1)}, f32[32]{0:T(128)}, u32[]{:S(2)}) copy-start(f32[32]{0:T(128)} %get-tuple-element.438) | copy-start | bytes 388 | tf_op jit(solution)/shard_map/while
  756.8 89.5 %copy-start.16 = (f32[32]{0:T(128)S(1)}, f32[32]{0:T(128)}, u32[]{:S(2)}) copy-start(f32[32]{0:T(128)} %get-tuple-element.466) | copy-start | bytes 388 | tf_op jit(solution)/shard_map/while
  756.8 89.5 %copy-start.17 = (f32[32]{0:T(128)S(1)}, f32[32]{0:T(128)}, u32[]{:S(2)}) copy-start(f32[32]{0:T(128)} %get-tuple-element.467) | copy-start | bytes 388 | tf_op jit(solution)/shard_map/while
  756.8 90.1 %copy-start.9 = (s32[32]{0:T(128)S(1)}, s32[32]{0:T(128)}, u32[]{:S(2)}) copy-start(s32[32]{0:T(128)} %get-tuple-element.409) | copy-start | bytes 388 | tf_op jit(solution)/shard_map/while
  846.3 3.4 copy-start.3
  846.3 3.4 copy-start.4
  851.7 5.0 collective-permute-start.3
  853.1 4.5 collective-permute-start.2
  864.0 1.5 copy-start.21
  865.6 312.7 %copy-start.20 = (s32[32]{0:T(128)}, s32[32]{0:T(128)S(1)}, u32[]{:S(2)}) copy-start(s32[32]{0:T(128)S(1)} %get-tuple-element.465) | copy-start | bytes 388 | tf_op jit(solution)/shard_map/while
  867.2 405.1 %collective-permute-start.1 = (f32[2,32,256]{2,1,0:T(8,128)}, f32[2,32,256]{2,1,0:T(8,128)}, u32[]{:S(2)}, u32[]{:S(2)}) collective-permute-start(f32[2,32,256]{2,1,0:T(8,128)} %pad_maximum_fusion.10), channel_id=1, source_target_pairs={{1,0},{2,1},{3,2},{4,3},{5,4},{6,5},{7,6},{9,8},{10,9},{11,10},{12... | collective-permute-start | bytes 196616 | tf_op jit(solution)/shard_map/while/body/eval_jaxpr/ppermute | solution.py:22
  869.1 405.4 %collective-permute-start = (f32[2,16,256]{2,1,0:T(8,128)}, f32[2,16,256]{2,1,0:T(8,128)}, u32[]{:S(2)}, u32[]{:S(2)}) collective-permute-start(f32[2,16,256]{2,1,0:T(8,128)} %slice_bitcast_fusion.7), channel_id=1, source_target_pairs={{8,0},{16,8},{24,16},{32,24},{40,32},{48,40},{56,48},{64,56},{72,6... | collective-permute-start | bytes 98312 | tf_op jit(solution)/shard_map/while/body/eval_jaxpr/ppermute | solution.py:22
  1181.6 89.5 %copy-start.12 = (f32[32]{0:T(128)S(1)}, f32[32]{0:T(128)}, u32[]{:S(2)}) copy-start(f32[32]{0:T(128)} %get-tuple-element.438) | copy-start | bytes 388 | tf_op jit(solution)/shard_map/while
  1181.6 89.5 %copy-start.16 = (f32[32]{0:T(128)S(1)}, f32[32]{0:T(128)}, u32[]{:S(2)}) copy-start(f32[32]{0:T(128)} %get-tuple-element.466) | copy-start | bytes 388 | tf_op jit(solution)/shard_map/while
  1181.6 89.5 %copy-start.17 = (f32[32]{0:T(128)S(1)}, f32[32]{0:T(128)}, u32[]{:S(2)}) copy-start(f32[32]{0:T(128)} %get-tuple-element.467) | copy-start | bytes 388 | tf_op jit(solution)/shard_map/while
  1181.6 90.1 %copy-start.9 = (s32[32]{0:T(128)S(1)}, s32[32]{0:T(128)}, u32[]{:S(2)}) copy-start(s32[32]{0:T(128)} %get-tuple-element.409) | copy-start | bytes 388 | tf_op jit(solution)/shard_map/while
  1271.1 3.4 copy-start.3
  1271.1 3.4 copy-start.4
  1276.5 5.0 collective-permute-start.3
  1278.0 4.5 collective-permute-start.2
  1290.4 312.7 %copy-start.20 = (s32[32]{0:T(128)}, s32[32]{0:T(128)S(1)}, u32[]{:S(2)}) copy-start(s32[32]{0:T(128)S(1)} %get-tuple-element.465) | copy-start | bytes 388 | tf_op jit(solution)/shard_map/while
  1292.0 405.1 %collective-permute-start.1 = (f32[2,32,256]{2,1,0:T(8,128)}, f32[2,32,256]{2,1,0:T(8,128)}, u32[]{:S(2)}, u32[]{:S(2)}) collective-permute-start(f32[2,32,256]{2,1,0:T(8,128)} %pad_maximum_fusion.10), channel_id=1, source_target_pairs={{1,0},{2,1},{3,2},{4,3},{5,4},{6,5},{7,6},{9,8},{10,9},{11,10},{12... | collective-permute-start | bytes 196616 | tf_op jit(solution)/shard_map/while/body/eval_jaxpr/ppermute | solution.py:22
  1293.9 405.4 %collective-permute-start = (f32[2,16,256]{2,1,0:T(8,128)}, f32[2,16,256]{2,1,0:T(8,128)}, u32[]{:S(2)}, u32[]{:S(2)}) collective-permute-start(f32[2,16,256]{2,1,0:T(8,128)} %slice_bitcast_fusion.7), channel_id=1, source_target_pairs={{8,0},{16,8},{24,16},{32,24},{40,32},{48,40},{56,48},{64,56},{72,6... | collective-permute-start | bytes 98312 | tf_op jit(solution)/shard_map/while/body/eval_jaxpr/ppermute | solution.py:22
  1606.5 89.5 %copy-start.12 = (f32[32]{0:T(128)S(1)}, f32[32]{0:T(128)}, u32[]{:S(2)}) copy-start(f32[32]{0:T(128)} %get-tuple-element.438) | copy-start | bytes 388 | tf_op jit(solution)/shard_map/while
  1606.5 89.5 %copy-start.16 = (f32[32]{0:T(128)S(1)}, f32[32]{0:T(128)}, u32[]{:S(2)}) copy-start(f32[32]{0:T(128)} %get-tuple-element.466) | copy-start | bytes 388 | tf_op jit(solution)/shard_map/while
  1606.5 89.5 %copy-start.17 = (f32[32]{0:T(128)S(1)}, f32[32]{0:T(128)}, u32[]{:S(2)}) copy-start(f32[32]{0:T(128)} %get-tuple-element.467) | copy-start | bytes 388 | tf_op jit(solution)/shard_map/while
  1606.5 90.1 %copy-start.9 = (s32[32]{0:T(128)S(1)}, s32[32]{0:T(128)}, u32[]{:S(2)}) copy-start(s32[32]{0:T(128)} %get-tuple-element.409) | copy-start | bytes 388 | tf_op jit(solution)/shard_map/while
  1696.0 3.4 copy-start.3
  1696.0 3.4 copy-start.4
  1701.4 5.0 collective-permute-start.3
  1702.8 4.5 collective-permute-start.2
  1713.7 1.5 copy-start.21
  1715.3 312.7 %copy-start.20 = (s32[32]{0:T(128)}, s32[32]{0:T(128)S(1)}, u32[]{:S(2)}) copy-start(s32[32]{0:T(128)S(1)} %get-tuple-element.465) | copy-start | bytes 388 | tf_op jit(solution)/shard_map/while
  1716.9 405.1 %collective-permute-start.1 = (f32[2,32,256]{2,1,0:T(8,128)}, f32[2,32,256]{2,1,0:T(8,128)}, u32[]{:S(2)}, u32[]{:S(2)}) collective-permute-start(f32[2,32,256]{2,1,0:T(8,128)} %pad_maximum_fusion.10), channel_id=1, source_target_pairs={{1,0},{2,1},{3,2},{4,3},{5,4},{6,5},{7,6},{9,8},{10,9},{11,10},{12... | collective-permute-start | bytes 196616 | tf_op jit(solution)/shard_map/while/body/eval_jaxpr/ppermute | solution.py:22
  1718.8 405.4 %collective-permute-start = (f32[2,16,256]{2,1,0:T(8,128)}, f32[2,16,256]{2,1,0:T(8,128)}, u32[]{:S(2)}, u32[]{:S(2)}) collective-permute-start(f32[2,16,256]{2,1,0:T(8,128)} %slice_bitcast_fusion.7), channel_id=1, source_target_pairs={{8,0},{16,8},{24,16},{32,24},{40,32},{48,40},{56,48},{64,56},{72,6... | collective-permute-start | bytes 98312 | tf_op jit(solution)/shard_map/while/body/eval_jaxpr/ppermute | solution.py:22
  2031.3 89.5 %copy-start.12 = (f32[32]{0:T(128)S(1)}, f32[32]{0:T(128)}, u32[]{:S(2)}) copy-start(f32[32]{0:T(128)} %get-tuple-element.438) | copy-start | bytes 388 | tf_op jit(solution)/shard_map/while
  2031.3 89.5 %copy-start.16 = (f32[32]{0:T(128)S(1)}, f32[32]{0:T(128)}, u32[]{:S(2)}) copy-start(f32[32]{0:T(128)} %get-tuple-element.466) | copy-start | bytes 388 | tf_op jit(solution)/shard_map/while
  2031.3 89.5 %copy-start.17 = (f32[32]{0:T(128)S(1)}, f32[32]{0:T(128)}, u32[]{:S(2)}) copy-start(f32[32]{0:T(128)} %get-tuple-element.467) | copy-start | bytes 388 | tf_op jit(solution)/shard_map/while
  2031.3 90.1 %copy-start.9 = (s32[32]{0:T(128)S(1)}, s32[32]{0:T(128)}, u32[]{:S(2)}) copy-start(s32[32]{0:T(128)} %get-tuple-element.409) | copy-start | bytes 388 | tf_op jit(solution)/shard_map/while
  2120.8 3.4 copy-start.3
  2120.8 3.4 copy-start.4
  2126.2 5.0 collective-permute-start.3
  2127.7 4.5 collective-permute-start.2
  2140.2 1.7 copy-start.1
  2140.2 1.6 copy-start.14
  (34 other events, 44.9 us)
where the time goes:
time: 2150 us; the launch traced here: 2140 us
  blocking collectives  1890 us (88%)
  local copies, waits for them, and re-layouts  95.5 us (4%)
  other arithmetic  80.4 us (4%)
  starting transfers between devices  41.5 us (2%)
  matrix products  27.2 us (1%)
    all_gather x5, blocking collectives, circuit_inputs(): lax.all_gather(volts, ('gz', 'gy'), axis=0, tiled=True)  1510 us
    while x5, blocking collectives  384 us
  transfers between devices with their start and end apart: 20, of which 5 were waited for; matrix products, arithmetic and copies ran while one was open for 6% of the time, Pallas kernels for 0%

commit v1 on v0

v1 whole, which is shorter than its diff:
```python
import functools

import jax
import jax.numpy as jnp
from jax import lax
from jax.experimental import pallas as pl
from jax.experimental.pallas import tpu as pltpu
from jax.sharding import PartitionSpec as P

STEPS = 5
NEWTON = 2
BS = 64
NB_DEV = 2
OFF = 4
PORT_DEV = 32
NODE_DEV = NB_DEV * BS
DEPTH = 5
CZ, CY, NX = 32, 16, 256
LAYERS = CZ + 2 * DEPTH
ROWS = LAYERS * CY
OWN_LO, OWN_HI = DEPTH * CY, (DEPTH + CZ) * CY
EDGE = DEPTH * CY
PACK = 8 * EDGE + CY
TALL = 48
ND = 128
REACH = 3 * PORT_DEV

time_step = 0.55
charge_scale = 4.0
diode_weight = 0.5

f32 = jnp.float32
VM = pl.BlockSpec(memory_space=pltpu.VMEM)
SM = pl.BlockSpec(memory_space=pltpu.SMEM)
HBM = pl.BlockSpec(memory_space=pltpu.HBM)
DMA = pltpu.SemaphoreType.DMA


def onchip(shape):
    return pltpu.VMEM(shape, f32)


def keep(value):
    return pltpu.with_memory_space_constraint(value, pltpu.VMEM)


def away(value):
    return pltpu.with_memory_space_constraint(value, pltpu.HBM)


def params():
    return pltpu.CompilerParams(vmem_limit_bytes=8 << 20)


def lanes_of(count, width):
    return lax.broadcasted_iota(jnp.int32, (count, width), 1)


def pick(rows, lane):
    hit = lanes_of(rows.shape[0], rows.shape[1]) == lane
    return jnp.sum(jnp.where(hit, rows, 0.0), axis=1, keepdims=True)


def spread(column, lane, width):
    hit = lanes_of(column.shape[0], width) == lane
    return jnp.where(hit, column, 0.0)


def write_outgoing(out, volts_row, inject_rows, table, first, rows_ref):
    parity = lax.broadcasted_iota(jnp.int32, out.shape, 0) % 2
    out[...] = jnp.where(parity == 0, jnp.broadcast_to(volts_row, out.shape), 0.0)
    rows_ref[...] = inject_rows
    for port in range(PORT_DEV):
        spot = pl.ds(table[first + port] + 1, 1)
        out[spot, :] = out[spot, :] + rows_ref[port : port + 1, :]


def write_edges(up, down, e_xy, e_z, h=None):
    upper = [(e_xy, (0,)), (e_xy, (1,)), (e_z, ())] + ([(h, (0,)), (h, (2,))] if h is not None else [])
    for slot, (source, part) in enumerate(upper):
        for layer in range(LAYERS):
            spot = layer * CY + CY - 1
            up[slot, layer : layer + 1, :] = source[part + (slice(spot, spot + 1), slice(None))]
        up[slot, LAYERS:TALL, :] = jnp.zeros((TALL - LAYERS, NX), f32)
    for slot, (source, part) in enumerate((upper[0], upper[2])):
        for layer in range(LAYERS):
            spot = layer * CY
            down[slot, layer : layer + 1, :] = source[part + (slice(spot, spot + 1), slice(None))]
        down[slot, LAYERS:TALL, :] = jnp.zeros((TALL - LAYERS, NX), f32)


def copier(sems):
    copies = []

    def copy(source, target):
        job = pltpu.make_async_copy(source, target, sems.at[len(copies)])
        job.start()
        copies.append(job)

    return copies, copy


def begin_kernel(
    table, e_in, h_in, coef_in, loss_in, cell_rows, columns, volts, diag, inv, off,
    up, down, out, m_off, m_diag, m_inv, e_z, picked, spread_rows, sems,
):
    copies, copy = copier(sems)
    copy(e_in.at[2], e_z)
    top = pl.ds(CZ * CY - EDGE, EDGE)
    bottom = pl.ds(0, EDGE)
    sources = [e_in.at[k] for k in range(3)] + [h_in.at[k] for k in range(3)] + [coef_in, loss_in]
    for slot, source in enumerate(sources):
        copy(source.at[top], up.at[pl.ds(slot * EDGE, EDGE)])
        copy(source.at[bottom], down.at[pl.ds(slot * EDGE, EDGE)])
    copy(cell_rows, up.at[pl.ds(8 * EDGE, CY)])
    copy(cell_rows, down.at[pl.ds(8 * EDGE, CY)])

    m_diag[...] = jnp.zeros_like(m_diag)
    m_inv[...] = jnp.zeros_like(m_inv)
    for j in range(NB_DEV):
        part = slice(j * BS, (j + 1) * BS)
        m_diag[part, part] = diag[j]
        m_inv[part, part] = inv[j].T
        for k in range(OFF):
            m_off[part, k * BS : (k + 1) * BS] = off[j, k]

    copies[0].wait()
    for port in range(PORT_DEV):
        picked[port : port + 1, :] = e_z[pl.ds(table[port], 1), :]
    gain = columns[0:PORT_DEV, 0:1]
    place = columns[0:PORT_DEV, 1:2].astype(jnp.int32)
    lane = columns[0:PORT_DEV, 2:3].astype(jnp.int32)
    sample = pick(picked[...], place)
    rows = spread(gain * sample, lane, NODE_DEV)
    write_outgoing(out, volts[...], rows, table, PORT_DEV, spread_rows)
    for job in copies[1:]:
        job.wait()


def begin(table, e_in, h_in, coef, loss, cell_rows, columns, volts, diag, inv, off):
    return pl.pallas_call(
        begin_kernel,
        name="begin",
        out_shape=(
            jax.ShapeDtypeStruct((PACK, NX), f32),
            jax.ShapeDtypeStruct((PACK, NX), f32),
            jax.ShapeDtypeStruct((2 * ND, NODE_DEV), f32),
            onchip((NODE_DEV, OFF * BS)),
            onchip((NODE_DEV, NODE_DEV)),
            onchip((NODE_DEV, NODE_DEV)),
        ),
        in_specs=[SM, HBM, HBM, HBM, HBM, HBM, VM, VM, VM, VM, VM],
        out_specs=(HBM, HBM, VM, VM, VM, VM),
        scratch_shapes=[
            pltpu.VMEM((CZ * CY, NX), f32),
            pltpu.VMEM((PORT_DEV, NX), f32),
            pltpu.VMEM((PORT_DEV, NODE_DEV), f32),
            DMA((19,)),
        ],
        compiler_params=params(),
    )(table, *map(away, (e_in, h_in, coef, loss, cell_rows)), columns, volts, diag, inv, off)


def halo_kernel(
    table, columns, lower, upper, e_in, h_in, coef_in, loss_in,
    e_xy, e_z, h, media, up, down, sample, coef, picked, sems,
):
    copies, copy = copier(sems)
    targets = [
        e_xy.at[0], e_xy.at[1], e_z, h.at[0], h.at[1], h.at[2], media.at[0], media.at[1],
    ]
    sources = [e_in.at[k] for k in range(3)] + [h_in.at[k] for k in range(3)] + [coef_in, loss_in]
    own = pl.ds(OWN_LO, CZ * CY)
    for slot, (source, target) in enumerate(zip(sources, targets)):
        part = pl.ds(slot * EDGE, EDGE)
        copy(source, target.at[own])
        copy(lower.at[part], target.at[pl.ds(0, EDGE)])
        copy(upper.at[part], target.at[pl.ds(OWN_HI, EDGE)])
    for job in copies:
        job.wait()

    @pl.loop(0, LAYERS)
    def _(layer):
        part = pl.ds(pl.multiple_of(layer * CY, CY), CY)
        media[1, part, :] = 1.0 - media[1, part, :]

    place = columns[:, 1:2].astype(jnp.int32)
    for port in range(REACH):
        picked[port : port + 1, :] = e_z[pl.ds(table[port], 1), :]
    sample[...] = pick(picked[...], place)
    for port in range(REACH):
        picked[port : port + 1, :] = media[0, pl.ds(table[port], 1), :]
    coef[...] = pick(picked[...], place)
    write_edges(up, down, e_xy, e_z, h)


def halo(table, columns, lower, upper, e_in, h_in, coef, loss):
    return pl.pallas_call(
        halo_kernel,
        name="halo",
        out_shape=(
            onchip((2, ROWS, NX)),
            onchip((ROWS, NX)),
            onchip((3, ROWS, NX)),
            onchip((2, ROWS, NX)),
            jax.ShapeDtypeStruct((5, TALL, NX), f32),
            jax.ShapeDtypeStruct((2, TALL, NX), f32),
            onchip((REACH, 1)),
            onchip((REACH, 1)),
        ),
        in_specs=[SM, VM] + [HBM] * 6,
        out_specs=(VM,) * 8,
        scratch_shapes=[pltpu.VMEM((REACH, NX), f32), DMA((24,))],
        compiler_params=params(),
    )(table, columns, *map(away, (lower, upper, e_in, h_in, coef, loss)))


def field_kernel(step, first, bounds, front, back, near, media, edge_in, e_xy, e_z, h, to_xy, to_z, to_h, edge):
    base = 3 if first else 0
    low_z, low_y = bounds[0], bounds[1]
    lane = lanes_of(CY, NX)
    row = lax.broadcasted_iota(jnp.int32, (CY, NX), 0)
    last_lane, first_lane = lane == NX - 1, lane == 0
    last_row, first_row = row == CY - 1, row == 0

    def next_x(value):
        return jnp.where(last_lane, 0.0, pltpu.roll(value, NX - 1, 1))

    def prior_x(value):
        return jnp.where(first_lane, 0.0, pltpu.roll(value, 1, 1))

    def next_y(value, beyond):
        return jnp.where(last_row, beyond, pltpu.roll(value, CY - 1, 0))

    def prior_y(value, beyond):
        return jnp.where(first_row, beyond, pltpu.roll(value, 1, 0))

    span = pl.ds(0, LAYERS)
    out_x, out_y, out_z = front[0, span, :], front[1, span, :], front[2, span, :]
    out_y_above = front[1, pl.ds(1, LAYERS), :]
    tall_lane = lanes_of(LAYERS, NX)
    out_y_next = jnp.where(tall_lane == NX - 1, 0.0, pltpu.roll(out_y, NX - 1, 1))
    near_x, near_z = near[0, span, :], near[1, span, :]
    edge_x, edge_z = edge_in[base, span, :], edge_in[base + 1, span, :]
    edge[0, span, :] = edge_x - low_y * ((near_z - out_z) - (out_y_above - out_y))
    edge[1, span, :] = edge_z - low_y * ((out_y_next - out_y) - (near_x - out_x))

    def magnetic(layer):
        here = pl.ds(pl.multiple_of(layer * CY, CY), CY)
        above = pl.ds(pl.multiple_of(layer * CY + CY, CY), CY)
        e_x, e_y, e_zz = e_xy[0, here, :], e_xy[1, here, :], e_z[here, :]
        rate = jnp.where(layer < DEPTH, low_z, time_step)
        curl_x = (next_y(e_zz, back[1, pl.ds(layer, 1), :]) - e_zz) - (e_xy[1, above, :] - e_y)
        curl_y = (e_xy[0, above, :] - e_x) - (next_x(e_zz) - e_zz)
        curl_z = (next_x(e_y) - e_y) - (next_y(e_x, back[0, pl.ds(layer, 1), :]) - e_x)
        h_x = h[0, here, :] - rate * curl_x
        h_y = h[1, here, :] - rate * curl_y
        h_z = h[2, here, :] - rate * curl_z
        to_h[0, here, :] = h_x
        to_h[1, here, :] = h_y
        to_h[2, here, :] = h_z
        return here, e_x, e_y, e_zz, h_x, h_y, h_z

    magnetic(step - 1)

    @pl.loop(step, LAYERS - step)
    def _(layer):
        here, e_x, e_y, e_zz, h_x, h_y, h_z = magnetic(layer)
        below = pl.ds(pl.multiple_of(layer * CY - CY, CY), CY)
        coef, kept = media[0, here, :], media[1, here, :]
        back_x = (h_z - prior_y(h_z, edge[1, pl.ds(layer, 1), :])) - (h_y - to_h[1, below, :])
        back_y = (h_x - to_h[0, below, :]) - (h_z - prior_x(h_z))
        back_z = (h_y - prior_x(h_y)) - (h_x - prior_y(h_x, edge[0, pl.ds(layer, 1), :]))
        to_xy[0, here, :] = kept * e_x + coef * back_x
        to_xy[1, here, :] = kept * e_y + coef * back_y
        to_z[here, :] = kept * e_zz + coef * back_z


def field(step, bounds, front, back, near, media, edge, e_xy, e_z, h):
    first = step == 1
    return pl.pallas_call(
        functools.partial(field_kernel, step, first),
        name="field",
        out_shape=(
            onchip((2, ROWS, NX)), onchip((ROWS, NX)), onchip((3, ROWS, NX)), onchip((2, TALL, NX)),
        ),
        in_specs=[SM] + [VM] * 8,
        out_specs=(VM,) * 4,
        compiler_params=params(),
    )(
        bounds, front, back, near, keep(media), front if first else keep(edge),
        keep(e_xy), keep(e_z), keep(h),
    )


NODES_AT, ACTIVE_AT, OFF_AT, SWAP_AT = REACH, 2 * REACH, 3 * REACH, 3 * REACH + NB_DEV * OFF


def solve(arrived, table, volts, m_off, m_diag, m_inv):
    lane = lanes_of(1, NODE_DEV)
    halves = []
    for j in range(NB_DEV):
        pieces = []
        for half in range(OFF // 2):
            total = None
            for side in range(2):
                spot = j * OFF + half * 2 + side
                row = arrived[pl.ds(table[OFF_AT + spot], 1), :]
                row = jnp.where(table[SWAP_AT + spot] == side, row, pltpu.roll(row, BS, 1))
                row = jnp.where((lane < BS) == (side == 0), row, 0.0)
                total = row if total is None else total + row
            pieces.append(jnp.broadcast_to(total, (BS, NODE_DEV)))
        halves.append(pieces)
    first = jnp.concatenate([halves[0][0], halves[1][0]], axis=0)
    second = jnp.concatenate([halves[0][1], halves[1][1]], axis=0)
    product = m_off[:, 0:NODE_DEV] * first + m_off[:, NODE_DEV : 2 * NODE_DEV] * second
    offsum = jnp.sum(product, axis=1, keepdims=True)
    parity = lax.broadcasted_iota(jnp.int32, arrived.shape, 0) % 2
    inject = jnp.sum(jnp.where(parity == 1, arrived[...], 0.0), axis=0, keepdims=True)
    start = volts[...]
    target = charge_scale * start + inject
    diagonal = lax.broadcasted_iota(jnp.int32, (NODE_DEV, NODE_DEV), 0) == lanes_of(NODE_DEV, NODE_DEV)
    iterate = start
    for newton_round in range(NEWTON):
        local = diode_weight * jnp.tanh(iterate) - target
        terms = m_diag[...] * iterate + jnp.where(diagonal, local, 0.0)
        resid = jnp.sum(terms, axis=1, keepdims=True) + offsum
        iterate = iterate - jnp.sum(m_inv[...] * resid, axis=0, keepdims=True)
    return iterate


def apply_ports(table, arrived, columns, sample, coef, e_z, picked, deltas):
    for port in range(REACH):
        picked[port : port + 1, 0:NODE_DEV] = arrived[pl.ds(table[NODES_AT + port], 1), :]
    gain = columns[:, 0:1]
    place = columns[:, 1:2].astype(jnp.int32)
    lane = columns[:, 2:3].astype(jnp.int32)
    near = pick(picked[:, 0:NODE_DEV], lane)
    current = gain * (sample[...] - near)
    deltas[...] = spread(-coef[...] * current, place, NX)

    def add(port):
        spot = pl.ds(table[port], 1)
        e_z[spot, :] = e_z[spot, :] + deltas[port : port + 1, :]

    for port in range(PORT_DEV):
        add(port)
    for port in range(PORT_DEV, REACH):
        pl.when(table[ACTIVE_AT + port] > 0)(functools.partial(add, port))
    return gain, place, lane


def ports_kernel(
    table, arrived, columns, sample, coef, e_xy, e_in, e_z, up, down, picked, deltas,
):
    e_z[...] = e_in[...]
    apply_ports(table, arrived, columns, sample, coef, e_z, picked, deltas)
    write_edges(up, down, e_xy, e_z)


def ports(table, arrived, columns, sample, coef, e_xy, e_z):
    return pl.pallas_call(
        ports_kernel,
        name="ports",
        out_shape=(
            onchip((ROWS, NX)),
            jax.ShapeDtypeStruct((3, TALL, NX), f32),
            jax.ShapeDtypeStruct((2, TALL, NX), f32),
        ),
        in_specs=[SM] + [VM] * 6,
        out_specs=(VM,) * 3,
        scratch_shapes=[pltpu.VMEM((REACH, NX), f32), pltpu.VMEM((REACH, NX), f32)],
        compiler_params=params(),
    )(table, arrived, columns, keep(sample), keep(coef), keep(e_xy), keep(e_z))


def circuit_kernel(
    table, arrived, columns, volts, m_off, m_diag, m_inv, e_z,
    out, volts_out, sample_out, picked, spread_rows,
):
    for port in range(REACH):
        picked[port : port + 1, :] = e_z[pl.ds(table[port], 1), :]
    taken = pick(picked[...], columns[:, 1:2].astype(jnp.int32))
    sample_out[...] = taken
    solved = solve(arrived, table, volts, m_off, m_diag, m_inv)
    volts_out[...] = solved
    own = slice(0, PORT_DEV)
    lane = columns[own, 2:3].astype(jnp.int32)
    rows = spread(columns[own, 0:1] * taken[own], lane, NODE_DEV)
    write_outgoing(out, solved, rows, table, NODES_AT, spread_rows)


def circuit(table, arrived, columns, volts, mats, e_z):
    return pl.pallas_call(
        circuit_kernel,
        name="circuit",
        out_shape=(
            onchip(arrived.shape),
            onchip((1, NODE_DEV)),
            onchip((REACH, 1)),
        ),
        in_specs=[SM] + [VM] * 7,
        out_specs=(VM,) * 3,
        scratch_shapes=[pltpu.VMEM((REACH, NX), f32), pltpu.VMEM((PORT_DEV, NODE_DEV), f32)],
        compiler_params=params(),
    )(table, arrived, columns, volts, *[keep(mat) for mat in mats], keep(e_z))


def finish_kernel(
    table, arrived, columns, sample, coef, volts, m_off, m_diag, m_inv, e_xy, e_in, h,
    e_out, h_out, volts_out, e_z, picked, deltas, sems,
):
    own = pl.ds(OWN_LO, CZ * CY)
    copies, copy = copier(sems)
    for k in range(3):
        copy(h.at[k, own], h_out.at[k])
    for k in range(2):
        copy(e_xy.at[k, own], e_out.at[k])
    e_z[...] = e_in[...]
    apply_ports(table, arrived, columns, sample, coef, e_z, picked, deltas)
    copy(e_z.at[own], e_out.at[2])
    volts_out[...] = solve(arrived, table, volts, m_off, m_diag, m_inv)
    for job in copies:
        job.wait()


def finish(table, arrived, columns, sample, coef, volts, mats, e_xy, e_z, h):
    return pl.pallas_call(
        finish_kernel,
        name="finish",
        out_shape=(
            jax.ShapeDtypeStruct((3, CZ * CY, NX), f32),
            jax.ShapeDtypeStruct((3, CZ * CY, NX), f32),
            jax.ShapeDtypeStruct((1, NODE_DEV), f32),
        ),
        in_specs=[SM] + [VM] * 11,
        out_specs=(HBM, HBM, VM),
        scratch_shapes=[
            pltpu.VMEM((ROWS, NX), f32),
            pltpu.VMEM((REACH, NX), f32),
            pltpu.VMEM((REACH, NX), f32),
            DMA((6,)),
        ],
        compiler_params=params(),
    )(
        table, arrived, columns, keep(sample), keep(coef), volts,
        *[keep(mat) for mat in mats], keep(e_xy), keep(e_z), keep(h),
    )


def shifted(value, axis, steps):
    count = lax.axis_size(axis)
    first, last = (max(0, -steps), min(count, count - steps))
    return lax.ppermute(value, axis, [(source, source + steps) for source in range(first, last)])


def exchange(value):
    return lax.all_to_all(value, ("gz", "gy"), 0, 0, tiled=True)


def body(
    e_field,
    h_field,
    e_coef,
    e_loss,
    port_cell,
    port_node,
    port_gain,
    diag_blocks,
    inv_blocks,
    off_blocks,
    off_cols,
    volts_init,
):
    gz, gy = lax.axis_index("gz"), lax.axis_index("gy")
    n_gz, n_gy = lax.axis_size("gz"), lax.axis_size("gy")
    device = gz * n_gy + gy
    count = n_gz * n_gy * PORT_DEV

    def of_device(table, which):
        start = jnp.clip(which, 0, n_gz * n_gy - 1) * PORT_DEV
        return lax.dynamic_slice_in_dim(table, start, PORT_DEV)

    trio = (device, device - n_gy, device + n_gy)
    nodes = jnp.concatenate([of_device(port_node, which) for which in trio])
    gains = jnp.concatenate([of_device(port_gain, which) for which in trio])
    node_row = 2 * (nodes // NODE_DEV)

    def columns_of(gain, cells, node):
        table = jnp.stack([gain, (cells % NX).astype(f32), (node % NODE_DEV).astype(f32)], axis=1)
        return table

    own = slice(0, PORT_DEV)
    cell_rows = jnp.pad(port_cell.astype(f32)[None], ((0, CY - 1), (0, NX - PORT_DEV)))
    flat = (CZ * CY, NX)
    grids = [array.reshape(array.shape[:-3] + flat) for array in (e_field, h_field, e_coef, e_loss)]
    volts = volts_init.reshape(1, NODE_DEV)
    up, down, out, *mats = begin(
        jnp.concatenate([port_cell // NX, node_row[own]]),
        *grids,
        cell_rows,
        columns_of(gains[own], port_cell, nodes[own]),
        volts,
        diag_blocks,
        inv_blocks,
        off_blocks,
    )
    lower = shifted(up, "gz", 1)
    upper = shifted(down, "gz", -1)
    arrived = exchange(out)
    lower, upper, arrived = lax.optimization_barrier((lower, upper, arrived))

    spot = 8 * EDGE
    cells = jnp.concatenate(
        [
            port_cell,
            lower[spot, 0:PORT_DEV].astype(jnp.int32),
            upper[spot, 0:PORT_DEV].astype(jnp.int32),
        ]
    )
    group = jnp.arange(REACH, dtype=jnp.int32) // PORT_DEV
    offset = jnp.where(group == 0, 0, jnp.where(group == 1, -CZ, CZ))
    layer = cells // (CY * NX) + offset + DEPTH
    exists = (group == 0) | ((group == 1) & (gz > 0)) | ((group == 2) & (gz < n_gz - 1))
    valid = exists & (layer >= 0) & (layer < LAYERS)
    cell_row = jnp.clip(layer, 0, LAYERS - 1) * CY + (cells // NX) % CY
    active = valid.astype(jnp.int32)
    columns = columns_of(jnp.where(valid, gains, 0.0), cells, nodes)
    flat_cols = off_cols.reshape(-1)
    table = jnp.concatenate(
        [cell_row, node_row, active, 2 * (flat_cols // NB_DEV), flat_cols % NB_DEV]
    )
    bounds = jnp.stack(
        [jnp.where(gz > 0, time_step, 0.0), jnp.where(gy > 0, time_step, 0.0)]
    ).astype(f32)

    e_xy, e_z, h, media, up, down, sample, coef = halo(table, columns, lower, upper, *grids)
    edge = None
    for step in range(1, STEPS + 1):
        front = shifted(up, "gy", 1)
        back = shifted(down, "gy", -1)
        if step > 1:
            out, volts, sample = circuit(table, arrived, columns, volts, mats, e_z)
            out, front, back = lax.optimization_barrier((out, front, back))
            arrived = exchange(out)
            arrived, e_z = lax.optimization_barrier((arrived, e_z))
        e_xy, e_z, h, edge = field(step, bounds, front, back, down, media, edge, e_xy, e_z, h)
        shared = (table, arrived, columns, sample, coef)
        if step < STEPS:
            e_z, up, down = ports(*shared, e_xy, e_z)
        else:
            e_end, h_end, volts = finish(*shared, volts, mats, e_xy, e_z, h)
    return e_end.reshape(e_field.shape), h_end.reshape(h_field.shape), volts.reshape(-1)


def solution(mesh):
    placed = (
        P(None, "gz", "gy", None),
        P(None, "gz", "gy", None),
        P("gz", "gy", None),
        P("gz", "gy", None),
        P(("gz", "gy")),
        P(),
        P(),
        P(("gz", "gy"), None, None),
        P(("gz", "gy"), None, None),
        P(("gz", "gy"), None, None, None),
        P(("gz", "gy"), None),
        P(("gz", "gy")),
    )
    return jax.shard_map(
        body,
        mesh=mesh,
        in_specs=placed,
        out_specs=(P(None, "gz", "gy", None), P(None, "gz", "gy", None), P(("gz", "gy"))),
        check_vma=False,
    )
```

time: 2150 us -> 222 us (0.10)
  blocking collectives: 1890 us -> 87.5 us
  local copies, waits for them, and re-layouts: 95.5 us -> 12.2 us
  other arithmetic: 80.4 us -> 1.45 us
  Pallas kernels: 0 us -> 55.8 us
  matrix products: 27.2 us -> 0 us
    all_gather x5 -> x0, blocking collectives: 1510 us -> none  [circuit_inputs(): lax.all_gather(volts, ('gz', 'gy'), axis=0, tiled=True)]
    while x5 -> x0, blocking collectives: 384 us -> none
    all_to_all x0 -> x4, blocking collectives: none -> 87.5 us  [exchange(): return lax.all_to_all(value, ('gz', 'gy'), 0, 0, tiled=True)]
    pallas_call x0 -> x16, Pallas kernels: none -> 55.8 us  [the longest x5 32.8 us: field(): pl.pallas_call(functools.partial(field_kernel, step, first), name='field'...]
    sub x45 -> x0, other arithmetic: 35.2 us -> none  [the longest x5 9.51 us: update_electric(): return (1.0 - e_loss) * e_now + e_coef * jnp.stack([back_x, back_y, back_z])]
    dot_general x30 -> x0, matrix products: 27.2 us -> none  [the longest x10 10.5 us: newton_solve(): jnp.einsum('jab,jb->ja', diag_blocks, iterate, precision=precise)]
    slice x46 -> x0, local copies, waits for them, and re-layouts: 24.2 us -> none  [the longest x5 6.54 us: update_magnetic(): above_x = jnp.concatenate([e_now[1:3, :, :, 1:], blank], axis=3)]
    gather x17 -> x0, local copies, waits for them, and re-layouts: 21.9 us -> none  [the longest x5 7.4 us: whole_terms(): picked = blocks_all[off_cols]]
  transfers between devices with their start and end apart: 20 -> 13, of which waited for: 5 -> 6; matrix products, arithmetic and copies ran while one was open for 6% -> 0% of each run, Pallas kernels for 0% -> 2%
where the time goes in v1:
time: 222 us; the launch traced here: 221 us
  blocking collectives  87.5 us (39%)
  Pallas kernels  55.8 us (25%)
  starting transfers between devices  37.5 us (17%)
  waiting for transfers between devices  25.3 us (11%)
  local copies, waits for them, and re-layouts  12.2 us (5%)
    all_to_all x4, blocking collectives, exchange(): return lax.all_to_all(value, ('gz', 'gy'), 0, 0, tiled=True)  87.5 us
    pallas_call x5, Pallas kernels, field(): pl.pallas_call(functools.partial(field_kernel, step, first), name='field'...  32.8 us
    ppermute x12, starting transfers between devices, shifted(): lax.ppermute(value, axis, [(source, source + steps) for source in range(f...  26.2 us
    ppermute x12, waiting for transfers between devices, shifted(): lax.ppermute(value, axis, [(source, source + steps) for source in range(f...  15.4 us
    all_to_all x1, starting transfers between devices, exchange(): return lax.all_to_all(value, ('gz', 'gy'), 0, 0, tiled=True)  11.4 us
    unnamed x30, local copies, waits for them, and re-layouts  10.3 us
    all_to_all x1, waiting for transfers between devices, exchange(): return lax.all_to_all(value, ('gz', 'gy'), 0, 0, tiled=True)  9.89 us
    pallas_call x4, Pallas kernels, ports(): pl.pallas_call(ports_kernel, name='ports', out_shape=(onchip((ROWS, NX)),...  7.08 us
  transfers between devices with their start and end apart: 13, of which 6 were waited for; matrix products, arithmetic and copies ran while one was open for 0% of the time, Pallas kernels for 2%

profile of v1, /device:TPU:1, one launch (start us, length us, event | category | flops | bytes accessed | tf_op | source)
XLA Modules:
  0.0 220.7 jit_solution(6538852526227048486)
XLA Ops:
  0.6 0.9 dynamic-slice_bitcast_fusion.1
  1.5 0.9 fusion.4
  2.4 0.1 copy.27.columns
  2.5 0.1 fusion.12
  2.6 0.1 pad_add_fusion.1.table
  2.7 0.6 pad.4.cell_rows
  3.3 0.9 copy-done.4
  4.2 0.8 copy-done.7
  5.1 0.8 copy-done.8
  5.9 0.7 copy-done.9
  6.6 3.0 %begin.1 = (f32[656,256]{1,0:T(8,128)S(1)}, f32[656,256]{1,0:T(8,128)S(1)}, f32[256,128]{1,0:T(8,128)}, f32[128,256]{1,0:T(8,128)S(1)}, f32[128,128]{1,0:T(8,128)S(1)}, /*index=5*/f32[128,128]{1,0:T(8,128)S(1)}) custom-call(s32[64]{0:T(128)S(1)} %pad_add_fusion.1.table, f32[3,512,256]{2,1,0:T(8,128)} %bitcast.60, f32[3,512,256]{2,1,0:T(8,128)} %bitcast.62, ...), custom_call_target="tpu_custom_call" | custom-call | tf_op jit(solution)/shard_map/begin/pallas_call | solution.py:141
  9.6 4.6 %collective-permute-start = (f32[656,256]{1,0:T(8,128)S(1)}, f32[656,256]{1,0:T(8,128)S(1)}, u32[]{:S(2)}, u32[]{:S(2)}) collective-permute-start(f32[656,256]{1,0:T(8,128)S(1)} %get-tuple-element.86), channel_id=1, source_target_pairs={{0,8},{8,16},{16,24},{24,32},{32,40},{40,48},{48,56},{56,64},{64,7... | collective-permute-start | bytes 2015240 | tf_op jit(solution)/shard_map/ppermute | solution.py:454
  14.2 1.9 collective-permute-start.1
  16.1 11.4 %all-to-all-start = ((f32[128,2,128]{2,1,0:T(2,128)}), f32[128,2,128]{2,1,0:T(2,128)S(1)}, u32[]{:S(2)}, u32[]{:S(2)}) async-start(f32[128,2,128]{2,1,0:T(2,128)} %bitcast.9), calls=%async_computation | async-start | bytes 262144 | tf_op jit(solution)/shard_map/all_to_all | solution.py:458
  27.5 0.1 reshape.575
  27.6 0.1 fusion.8
  27.7 9.9 %all-to-all-done = f32[128,2,128]{2,1,0:T(2,128)S(1)} async-done(((f32[128,2,128]{2,1,0:T(2,128)}), f32[128,2,128]{2,1,0:T(2,128)S(1)}, u32[]{:S(2)}, u32[]{:S(2)}) %all-to-all-start) | async-done | bytes 131104 | tf_op jit(solution)/shard_map/all_to_all | solution.py:458
  37.6 0.1 and_select_fusion.2
  37.7 0.1 copy.30.columns
  37.8 0.1 and_convert_fusion
  38.0 0.4 copy-done.11
  38.4 0.2 copy-done.12
  38.6 0.1 concatenate.102.table
  38.7 4.7 %halo.1 = (f32[2,672,256]{2,1,0:T(8,128)S(1)}, f32[672,256]{1,0:T(8,128)S(1)}, f32[3,672,256]{2,1,0:T(8,128)S(1)}, f32[2,672,256]{2,1,0:T(8,128)S(1)}, f32[5,48,...) custom-call(s32[304]{0:T(512)S(1)} %concatenate.102.table, ...), custom_call_target="tpu_custom_call" | custom-call | tf_op jit(solution)/shard_map/halo/pallas_call | solution.py:198
  43.4 1.3 copy-done
  44.7 0.8 copy-done.2
  45.6 0.6 copy-done.5
  46.2 2.3 %collective-permute-start.2 = (f32[5,48,256]{2,1,0:T(8,128)}, f32[5,48,256]{2,1,0:T(8,128)S(1)}, u32[]{:S(2)}, u32[]{:S(2)}) collective-permute-start(f32[5,48,256]{2,1,0:T(8,128)} %get-tuple-element.97), channel_id=1, source_target_pairs={{0,1},{1,2},{2,3},{3,4},{4,5},{5,6},{6,7},{8,9},{9,10},{10,11},{11... | collective-permute-start | bytes 737288 | tf_op jit(solution)/shard_map/ppermute | solution.py:454
  48.5 1.3 collective-permute-start.3
  49.8 0.1 pad_maximum_fusion.2.bounds
  49.9 4.2 %collective-permute-done.3.back = f32[2,48,256]{2,1,0:T(8,128)S(1)} collective-permute-done((f32[2,48,256]{2,1,0:T(8,128)}, f32[2,48,256]{2,1,0:T(8,128)S(1)}, u32[]{:S(2)}, u32[]{:S(2)}) %collective-permute-start.3) | collective-permute-done | bytes 98336 | tf_op jit(solution)/shard_map/ppermute | solution.py:454
  54.1 1.6 copy-done.1
  55.7 1.1 copy-done.3
  56.8 0.9 copy-done.6
  57.7 7.1 %field.5 = (f32[2,672,256]{2,1,0:T(8,128)S(1)}, f32[672,256]{1,0:T(8,128)S(1)}, f32[3,672,256]{2,1,0:T(8,128)S(1)}, f32[2,48,256]{2,1,0:T(8,128)S(1)}) custom-call(f32[2]{0:T(128)S(1)} %pad_maximum_fusion.2.bounds, f32[5,48,256]{2,1,0:T(8,128)S(1)} %collective-permute-done.2.front.edge_in, f32[2,48,256]{2,1,0:T(8,128)S(1)} %collective-permute-done.3.back, ...), custom_call_target="tpu_custom_call" | custom-call | tf_op jit(solution)/shard_map/field/pallas_call | solution.py:281
  64.8 1.8 ports.4
  66.6 3.5 %collective-permute-start.4 = (f32[3,48,256]{2,1,0:T(8,128)S(1)}, f32[3,48,256]{2,1,0:T(8,128)S(1)}, u32[]{:S(2)}, u32[]{:S(2)}) collective-permute-start(f32[3,48,256]{2,1,0:T(8,128)S(1)} %get-tuple-element.107), channel_id=1, source_target_pairs={{0,1},{1,2},{2,3},{3,4},{4,5},{5,6},{6,7},{8,9},{9,10},{10,11},{11... | collective-permute-start | bytes 442376 | tf_op jit(solution)/shard_map/ppermute | solution.py:454
  70.1 1.3 collective-permute-start.5
  71.4 1.3 circuit.4
  72.7 2.8 %collective-permute-done.5.back = f32[2,48,256]{2,1,0:T(8,128)S(1)} collective-permute-done((f32[2,48,256]{2,1,0:T(8,128)S(1)}, f32[2,48,256]{2,1,0:T(8,128)S(1)}, u32[]{:S(2)}, u32[]{:S(2)}) %collective-permute-start.5) | collective-permute-done | bytes 98336 | tf_op jit(solution)/shard_map/ppermute | solution.py:454
  75.5 26.5 %all_to_all.60 = f32[128,2,128]{2,1,0:T(2,128)S(1)} all-to-all(f32[128,2,128]{2,1,0:T(2,128)S(1)} %bitcast.57), channel_id=1, replica_groups=mesh['gz'=16,'gy'=8] {'gz','gy'}, dimensions={0} | all-to-all | bytes 262144 | tf_op jit(solution)/shard_map/all_to_all | solution.py:458
  101.9 6.8 %field.6 = (f32[2,672,256]{2,1,0:T(8,128)S(1)}, f32[672,256]{1,0:T(8,128)S(1)}, f32[3,672,256]{2,1,0:T(8,128)S(1)}, f32[2,48,256]{2,1,0:T(8,128)S(1)}) custom-call(f32[2]{0:T(128)S(1)} %pad_maximum_fusion.2.bounds, f32[3,48,256]{2,1,0:T(8,128)S(1)} %collective-permute-done.4.front, f32[2,48,256]{2,1,0:T(8,128)S(1)} %collective-permute-done.5.back, ...), custom_call_target="tpu_custom_call" | custom-call | tf_op jit(solution)/shard_map/field/pallas_call | solution.py:281
  108.7 1.8 ports.5
  110.5 2.5 %collective-permute-start.6 = (f32[3,48,256]{2,1,0:T(8,128)S(1)}, f32[3,48,256]{2,1,0:T(8,128)S(1)}, u32[]{:S(2)}, u32[]{:S(2)}) collective-permute-start(f32[3,48,256]{2,1,0:T(8,128)S(1)} %get-tuple-element.122), channel_id=1, source_target_pairs={{0,1},{1,2},{2,3},{3,4},{4,5},{5,6},{6,7},{8,9},{9,10},{10,11},{11... | collective-permute-start | bytes 442376 | tf_op jit(solution)/shard_map/ppermute | solution.py:454
  113.0 1.3 collective-permute-start.7
  114.3 1.3 circuit.5
  115.5 2.8 %collective-permute-done.7.back = f32[2,48,256]{2,1,0:T(8,128)S(1)} collective-permute-done((f32[2,48,256]{2,1,0:T(8,128)S(1)}, f32[2,48,256]{2,1,0:T(8,128)S(1)}, u32[]{:S(2)}, u32[]{:S(2)}) %collective-permute-start.7) | collective-permute-done | bytes 98336 | tf_op jit(solution)/shard_map/ppermute | solution.py:454
  118.3 20.3 %all_to_all.61 = f32[128,2,128]{2,1,0:T(2,128)S(1)} all-to-all(f32[128,2,128]{2,1,0:T(2,128)S(1)} %bitcast.54), channel_id=1, replica_groups=mesh['gz'=16,'gy'=8] {'gz','gy'}, dimensions={0} | all-to-all | bytes 262144 | tf_op jit(solution)/shard_map/all_to_all | solution.py:458
  138.7 6.4 %field.7 = (f32[2,672,256]{2,1,0:T(8,128)S(1)}, f32[672,256]{1,0:T(8,128)S(1)}, f32[3,672,256]{2,1,0:T(8,128)S(1)}, f32[2,48,256]{2,1,0:T(8,128)S(1)}) custom-call(f32[2]{0:T(128)S(1)} %pad_maximum_fusion.2.bounds, f32[3,48,256]{2,1,0:T(8,128)S(1)} %collective-permute-done.6.front, f32[2,48,256]{2,1,0:T(8,128)S(1)} %collective-permute-done.7.back, ...), custom_call_target="tpu_custom_call" | custom-call | tf_op jit(solution)/shard_map/field/pallas_call | solution.py:281
  145.1 1.8 ports.6
  146.9 2.5 %collective-permute-start.8 = (f32[3,48,256]{2,1,0:T(8,128)S(1)}, f32[3,48,256]{2,1,0:T(8,128)S(1)}, u32[]{:S(2)}, u32[]{:S(2)}) collective-permute-start(f32[3,48,256]{2,1,0:T(8,128)S(1)} %get-tuple-element.137), channel_id=1, source_target_pairs={{0,1},{1,2},{2,3},{3,4},{4,5},{5,6},{6,7},{8,9},{9,10},{10,11},{11... | collective-permute-start | bytes 442376 | tf_op jit(solution)/shard_map/ppermute | solution.py:454
  149.4 1.3 collective-permute-start.9
  150.7 1.3 circuit.6
  151.9 2.8 %collective-permute-done.9.back = f32[2,48,256]{2,1,0:T(8,128)S(1)} collective-permute-done((f32[2,48,256]{2,1,0:T(8,128)S(1)}, f32[2,48,256]{2,1,0:T(8,128)S(1)}, u32[]{:S(2)}, u32[]{:S(2)}) %collective-permute-start.9) | collective-permute-done | bytes 98336 | tf_op jit(solution)/shard_map/ppermute | solution.py:454
  154.7 20.3 %all_to_all.62 = f32[128,2,128]{2,1,0:T(2,128)S(1)} all-to-all(f32[128,2,128]{2,1,0:T(2,128)S(1)} %bitcast.55), channel_id=1, replica_groups=mesh['gz'=16,'gy'=8] {'gz','gy'}, dimensions={0} | all-to-all | bytes 262144 | tf_op jit(solution)/shard_map/all_to_all | solution.py:458
  175.1 6.1 %field.8 = (f32[2,672,256]{2,1,0:T(8,128)S(1)}, f32[672,256]{1,0:T(8,128)S(1)}, f32[3,672,256]{2,1,0:T(8,128)S(1)}, f32[2,48,256]{2,1,0:T(8,128)S(1)}) custom-call(f32[2]{0:T(128)S(1)} %pad_maximum_fusion.2.bounds, f32[3,48,256]{2,1,0:T(8,128)S(1)} %collective-permute-done.8.front, f32[2,48,256]{2,1,0:T(8,128)S(1)} %collective-permute-done.9.back, ...), custom_call_target="tpu_custom_call" | custom-call | tf_op jit(solution)/shard_map/field/pallas_call | solution.py:281
  181.2 1.8 ports.7
  183.0 2.5 %collective-permute-start.10 = (f32[3,48,256]{2,1,0:T(8,128)S(1)}, f32[3,48,256]{2,1,0:T(8,128)S(1)}, u32[]{:S(2)}, u32[]{:S(2)}) collective-permute-start(f32[3,48,256]{2,1,0:T(8,128)S(1)} %get-tuple-element.152), channel_id=1, source_target_pairs={{0,1},{1,2},{2,3},{3,4},{4,5},{5,6},{6,7},{8,9},{9,10},{10,11},{11... | collective-permute-start | bytes 442376 | tf_op jit(solution)/shard_map/ppermute | solution.py:454
  185.5 1.3 collective-permute-start.11
  186.8 1.3 circuit.7
  188.0 2.8 %collective-permute-done.11.back = f32[2,48,256]{2,1,0:T(8,128)S(1)} collective-permute-done((f32[2,48,256]{2,1,0:T(8,128)S(1)}, f32[2,48,256]{2,1,0:T(8,128)S(1)}, u32[]{:S(2)}, u32[]{:S(2)}) %collective-permute-start.11) | collective-permute-done | bytes 98336 | tf_op jit(solution)/shard_map/ppermute | solution.py:454
  190.8 20.3 %all_to_all.63 = f32[128,2,128]{2,1,0:T(2,128)S(1)} all-to-all(f32[128,2,128]{2,1,0:T(2,128)S(1)} %bitcast.56), channel_id=1, replica_groups=mesh['gz'=16,'gy'=8] {'gz','gy'}, dimensions={0} | all-to-all | bytes 262144 | tf_op jit(solution)/shard_map/all_to_all | solution.py:458
  211.2 6.4 %field.9 = (f32[2,672,256]{2,1,0:T(8,128)S(1)}, f32[672,256]{1,0:T(8,128)S(1)}, f32[3,672,256]{2,1,0:T(8,128)S(1)}, f32[2,48,256]{2,1,0:T(8,128)}) custom-call(f32[2]{0:T(128)S(1)} %pad_maximum_fusion.2.bounds, f32[3,48,256]{2,1,0:T(8,128)S(1)} %collective-permute-done.10.front, f32[2,48,256]{2,1,0:T(8,128)S(1)} %collective-permute-done.11.back, ...), custom_call_target="tpu_custom_call" | custom-call | tf_op jit(solution)/shard_map/field/pallas_call | solution.py:281
  217.5 3.2 %finish.1 = (f32[3,512,256]{2,1,0:T(8,128)}, f32[3,512,256]{2,1,0:T(8,128)}, f32[1,128]{1,0:T(1,128)}) custom-call(s32[304]{0:T(512)S(1)} %concatenate.102.table, f32[256,128]{1,0:T(8,128)S(1)} %bitcast.53, f32[96,3]{1,0:T(8,128)S(1)} %copy.30.columns, f32[96,1]{1,0:T(8,128)S(1)} %get-tuple-element.156.sample, f32[96,1]{1,0:T(8,128)S(1)} %get-tuple-element.96.coef, ...), custom_call_target="tpu_custom_call" | custom-call | tf_op jit(solution)/shard_map/finish/pallas_call | solution.py:428
  (32 shorter events, 0.1 us)
Async XLA Ops:
  3.3 0.9 copy-start.4
  4.2 0.8 copy-start.7
  5.1 0.8 copy-start.8
  5.9 0.7 copy-start.9
  6.6 20.9 %copy-start.14 = (s32[2,4]{1,0:T(2,128)S(1)}, s32[2,4]{1,0:T(2,128)}, u32[]{:S(2)}) copy-start(s32[2,4]{1,0:T(2,128)} %param.22) | copy-start | bytes 100
  6.6 31.0 %copy-start.13 = (s32[32]{0:T(128)S(1)}, s32[32]{0:T(128)}, u32[]{:S(2)}) copy-start(s32[32]{0:T(128)} %param.16) | copy-start | bytes 388
  9.6 28.0 %collective-permute-start = (f32[656,256]{1,0:T(8,128)S(1)}, f32[656,256]{1,0:T(8,128)S(1)}, u32[]{:S(2)}, u32[]{:S(2)}) collective-permute-start(f32[656,256]{1,0:T(8,128)S(1)} %get-tuple-element.86), channel_id=1, source_target_pairs={{0,8},{8,16},{16,24},{24,32},{32,40},{40,48},{48,56},{56,64},{64,7... | collective-permute-start | bytes 2015240 | tf_op jit(solution)/shard_map/ppermute | solution.py:454
  14.2 23.4 %collective-permute-start.1 = (f32[656,256]{1,0:T(8,128)S(1)}, f32[656,256]{1,0:T(8,128)S(1)}, u32[]{:S(2)}, u32[]{:S(2)}) collective-permute-start(f32[656,256]{1,0:T(8,128)S(1)} %get-tuple-element.87), channel_id=1, source_target_pairs={{8,0},{16,8},{24,16},{32,24},{40,32},{48,40},{56,48},{64,56},{72,6... | collective-permute-start | bytes 2015240 | tf_op jit(solution)/shard_map/ppermute | solution.py:454
  16.1 21.5 %all-to-all-start = ((f32[128,2,128]{2,1,0:T(2,128)}), f32[128,2,128]{2,1,0:T(2,128)S(1)}, u32[]{:S(2)}, u32[]{:S(2)}) async-start(f32[128,2,128]{2,1,0:T(2,128)} %bitcast.9), calls=%async_computation | async-start | bytes 262144 | tf_op jit(solution)/shard_map/all_to_all | solution.py:458
  37.6 0.8 copy-start.11
  37.6 1.1 copy-start.12
  43.4 1.3 copy-start
  44.7 0.8 copy-start.2
  45.6 0.6 copy-start.5
  46.2 7.9 %collective-permute-start.2 = (f32[5,48,256]{2,1,0:T(8,128)}, f32[5,48,256]{2,1,0:T(8,128)S(1)}, u32[]{:S(2)}, u32[]{:S(2)}) collective-permute-start(f32[5,48,256]{2,1,0:T(8,128)} %get-tuple-element.97), channel_id=1, source_target_pairs={{0,1},{1,2},{2,3},{3,4},{4,5},{5,6},{6,7},{8,9},{9,10},{10,11},{11... | collective-permute-start | bytes 737288 | tf_op jit(solution)/shard_map/ppermute | solution.py:454
  48.5 5.6 %collective-permute-start.3 = (f32[2,48,256]{2,1,0:T(8,128)}, f32[2,48,256]{2,1,0:T(8,128)S(1)}, u32[]{:S(2)}, u32[]{:S(2)}) collective-permute-start(f32[2,48,256]{2,1,0:T(8,128)} %copy-done.5), channel_id=1, source_target_pairs={{1,0},{2,1},{3,2},{4,3},{5,4},{6,5},{7,6},{9,8},{10,9},{11,10},{12... | collective-permute-start | bytes 294920 | tf_op jit(solution)/shard_map/ppermute | solution.py:454
  54.1 1.6 copy-start.1
  55.7 1.1 copy-start.3
  56.8 0.9 copy-start.6
  64.8 6.6 %copy-start.10 = (f32[128]{0:T(128)S(1)}, f32[128]{0:T(128)}, u32[]{:S(2)}) copy-start(f32[128]{0:T(128)} %param.23) | copy-start | bytes 1540
  66.6 8.8 %collective-permute-start.4 = (f32[3,48,256]{2,1,0:T(8,128)S(1)}, f32[3,48,256]{2,1,0:T(8,128)S(1)}, u32[]{:S(2)}, u32[]{:S(2)}) collective-permute-start(f32[3,48,256]{2,1,0:T(8,128)S(1)} %get-tuple-element.107), channel_id=1, source_target_pairs={{0,1},{1,2},{2,3},{3,4},{4,5},{5,6},{6,7},{8,9},{9,10},{10,11},{11... | collective-permute-start | bytes 442376 | tf_op jit(solution)/shard_map/ppermute | solution.py:454
  70.1 5.4 %collective-permute-start.5 = (f32[2,48,256]{2,1,0:T(8,128)S(1)}, f32[2,48,256]{2,1,0:T(8,128)S(1)}, u32[]{:S(2)}, u32[]{:S(2)}) collective-permute-start(f32[2,48,256]{2,1,0:T(8,128)S(1)} %get-tuple-element.108.near), channel_id=1, source_target_pairs={{1,0},{2,1},{3,2},{4,3},{5,4},{6,5},{7,6},{9,8},{10,9},{11,10},{12... | collective-permute-start | bytes 294920 | tf_op jit(solution)/shard_map/ppermute | solution.py:454
  110.5 7.8 %collective-permute-start.6 = (f32[3,48,256]{2,1,0:T(8,128)S(1)}, f32[3,48,256]{2,1,0:T(8,128)S(1)}, u32[]{:S(2)}, u32[]{:S(2)}) collective-permute-start(f32[3,48,256]{2,1,0:T(8,128)S(1)} %get-tuple-element.122), channel_id=1, source_target_pairs={{0,1},{1,2},{2,3},{3,4},{4,5},{5,6},{6,7},{8,9},{9,10},{10,11},{11... | collective-permute-start | bytes 442376 | tf_op jit(solution)/shard_map/ppermute | solution.py:454
  113.0 5.4 %collective-permute-start.7 = (f32[2,48,256]{2,1,0:T(8,128)S(1)}, f32[2,48,256]{2,1,0:T(8,128)S(1)}, u32[]{:S(2)}, u32[]{:S(2)}) collective-permute-start(f32[2,48,256]{2,1,0:T(8,128)S(1)} %get-tuple-element.123.near), channel_id=1, source_target_pairs={{1,0},{2,1},{3,2},{4,3},{5,4},{6,5},{7,6},{9,8},{10,9},{11,10},{12... | collective-permute-start | bytes 294920 | tf_op jit(solution)/shard_map/ppermute | solution.py:454
  146.9 7.8 %collective-permute-start.8 = (f32[3,48,256]{2,1,0:T(8,128)S(1)}, f32[3,48,256]{2,1,0:T(8,128)S(1)}, u32[]{:S(2)}, u32[]{:S(2)}) collective-permute-start(f32[3,48,256]{2,1,0:T(8,128)S(1)} %get-tuple-element.137), channel_id=1, source_target_pairs={{0,1},{1,2},{2,3},{3,4},{4,5},{5,6},{6,7},{8,9},{9,10},{10,11},{11... | collective-permute-start | bytes 442376 | tf_op jit(solution)/shard_map/ppermute | solution.py:454
  149.4 5.4 %collective-permute-start.9 = (f32[2,48,256]{2,1,0:T(8,128)S(1)}, f32[2,48,256]{2,1,0:T(8,128)S(1)}, u32[]{:S(2)}, u32[]{:S(2)}) collective-permute-start(f32[2,48,256]{2,1,0:T(8,128)S(1)} %get-tuple-element.138.near), channel_id=1, source_target_pairs={{1,0},{2,1},{3,2},{4,3},{5,4},{6,5},{7,6},{9,8},{10,9},{11,10},{12... | collective-permute-start | bytes 294920 | tf_op jit(solution)/shard_map/ppermute | solution.py:454
  183.0 7.8 %collective-permute-start.10 = (f32[3,48,256]{2,1,0:T(8,128)S(1)}, f32[3,48,256]{2,1,0:T(8,128)S(1)}, u32[]{:S(2)}, u32[]{:S(2)}) collective-permute-start(f32[3,48,256]{2,1,0:T(8,128)S(1)} %get-tuple-element.152), channel_id=1, source_target_pairs={{0,1},{1,2},{2,3},{3,4},{4,5},{5,6},{6,7},{8,9},{9,10},{10,11},{11... | collective-permute-start | bytes 442376 | tf_op jit(solution)/shard_map/ppermute | solution.py:454
  185.5 5.4 %collective-permute-start.11 = (f32[2,48,256]{2,1,0:T(8,128)S(1)}, f32[2,48,256]{2,1,0:T(8,128)S(1)}, u32[]{:S(2)}, u32[]{:S(2)}) collective-permute-start(f32[2,48,256]{2,1,0:T(8,128)S(1)} %get-tuple-element.153.near), channel_id=1, source_target_pairs={{1,0},{2,1},{3,2},{4,3},{5,4},{6,5},{7,6},{9,8},{10,9},{11,10},{12... | collective-permute-start | bytes 294920 | tf_op jit(solution)/shard_map/ppermute | solution.py:454

commit v2 on v1

v2 whole, which is shorter than its diff:
```python
import functools

import jax
import jax.numpy as jnp
from jax import lax
from jax.experimental import pallas as pl
from jax.experimental.pallas import tpu as pltpu
from jax.sharding import PartitionSpec as P

STEPS = 5
NEWTON = 2
BS = 64
NB_DEV = 2
OFF = 4
PORT_DEV = 32
ND = 128
NODE_DEV = NB_DEV * BS
DEPTH = 5
CZ, CY, NX = 32, 16, 256
LAYERS = CZ + 2 * DEPTH
PAD = 8
TALL = CY + 2 * PAD
PARTS = 8
STRIP = PARTS * DEPTH
SIDES = ((0, 0), (-1, 0), (1, 0), (0, -1), (-1, -1), (1, -1), (0, 1), (-1, 1), (1, 1))
REACH = len(SIDES) * PORT_DEV
NODES_AT, COUNT_AT, OFF_AT = REACH, 2 * REACH, 2 * REACH + 1
SWAP_AT = OFF_AT + NB_DEV * OFF

time_step = 0.55
charge_scale = 4.0
diode_weight = 0.5

f32 = jnp.float32
VM = pl.BlockSpec(memory_space=pltpu.VMEM)
SM = pl.BlockSpec(memory_space=pltpu.SMEM)
HBM = pl.BlockSpec(memory_space=pltpu.HBM)
DMA = pltpu.SemaphoreType.DMA
CUBE = (LAYERS, TALL, NX)


def onchip(shape):
    return pltpu.VMEM(shape, f32)


def keep(value):
    return pltpu.with_memory_space_constraint(value, pltpu.VMEM)


def away(value):
    return pltpu.with_memory_space_constraint(value, pltpu.HBM)


def params():
    return pltpu.CompilerParams(vmem_limit_bytes=12 << 20)


def lanes_of(count, width):
    return lax.broadcasted_iota(jnp.int32, (count, width), 1)


def pick(rows, lane):
    hit = lanes_of(rows.shape[0], rows.shape[1]) == lane
    return jnp.sum(jnp.where(hit, rows, 0.0), axis=1, keepdims=True)


def spread(column, lane, width):
    hit = lanes_of(column.shape[0], width) == lane
    return jnp.where(hit, column, 0.0)


def columns_at(columns, part):
    block = columns[part, :]
    return block[:, 0:1], block[:, 1:2].astype(jnp.int32), block[:, 2:3].astype(jnp.int32)


def write_outgoing(out, volts_row, inject_rows, table, first, rows_ref):
    parity = lax.broadcasted_iota(jnp.int32, out.shape, 0) % 2
    out[...] = jnp.where(parity == 0, jnp.broadcast_to(volts_row, out.shape), 0.0)
    rows_ref[...] = inject_rows
    for port in range(PORT_DEV):
        spot = pl.ds(table[first + port] + 1, 1)
        out[spot, :] = out[spot, :] + rows_ref[port : port + 1, :]


def copier(sems):
    copies = []

    def copy(source, target):
        job = pltpu.make_async_copy(source, target, sems.at[len(copies)])
        job.start()
        copies.append(job)

    return copies, copy


def strip_of(block, rows):
    return jnp.concatenate([block(part)[rows] for part in range(PARTS)], axis=0)


def begin_kernel(
    table, e_in, h_in, coef_in, loss_in, cell_rows, columns, volts, diag, inv, off,
    up, down, front, back, out, m_off, m_diag, m_inv, fields, picked, spread_rows, sems,
):
    copies, copy = copier(sems)
    sources = [e_in.at[k] for k in range(3)] + [h_in.at[k] for k in range(3)] + [coef_in, loss_in]
    for part in (2, 0, 1, 3, 4, 5, 6, 7):
        copy(sources[part], fields.at[part])
    for part, source in enumerate(sources):
        to = pl.ds(part * DEPTH, DEPTH)
        copy(source.at[pl.ds(CZ - DEPTH, DEPTH)], up.at[to])
        copy(source.at[pl.ds(0, DEPTH)], down.at[to])
    copy(cell_rows, up.at[PARTS * DEPTH])
    copy(cell_rows, down.at[PARTS * DEPTH])

    m_diag[...] = jnp.zeros_like(m_diag)
    m_inv[...] = jnp.zeros_like(m_inv)
    for j in range(NB_DEV):
        part = slice(j * BS, (j + 1) * BS)
        m_diag[part, part] = diag[j]
        m_inv[part, part] = inv[j].T
        for k in range(OFF):
            m_off[part, k * BS : (k + 1) * BS] = off[j, k]

    copies[0].wait()
    for port in range(PORT_DEV):
        spot = table[port]
        picked[port : port + 1, :] = fields[2, spot // CY, pl.ds(spot % CY, 1), :]
    gain, place, lane = columns_at(columns, slice(0, PORT_DEV))
    sample = pick(picked[...], place)
    rows = spread(gain * sample, lane, NODE_DEV)
    write_outgoing(out, volts[...], rows, table, PORT_DEV, spread_rows)
    for job in copies[1:8]:
        job.wait()

    @pl.loop(0, CZ)
    def _(layer):
        to = pl.ds(pl.multiple_of(layer * STRIP, 8), STRIP)
        front[to, :] = strip_of(lambda part: fields[part, layer, 8:CY, :], slice(8 - DEPTH, 8))
        back[to, :] = strip_of(lambda part: fields[part, layer, 0:8, :], slice(0, DEPTH))

    front[CZ * STRIP :, :] = cell_rows[0:8, :]
    back[CZ * STRIP :, :] = cell_rows[0:8, :]
    for job in copies[8:]:
        job.wait()


def begin(table, e_in, h_in, coef, loss, cell_rows, columns, volts, diag, inv, off):
    return pl.pallas_call(
        begin_kernel,
        name="begin",
        out_shape=(
            jax.ShapeDtypeStruct((PARTS * DEPTH + 1, CY, NX), f32),
            jax.ShapeDtypeStruct((PARTS * DEPTH + 1, CY, NX), f32),
            jax.ShapeDtypeStruct((CZ * STRIP + 8, NX), f32),
            jax.ShapeDtypeStruct((CZ * STRIP + 8, NX), f32),
            jax.ShapeDtypeStruct((2 * ND, NODE_DEV), f32),
            onchip((NODE_DEV, OFF * BS)),
            onchip((NODE_DEV, NODE_DEV)),
            onchip((NODE_DEV, NODE_DEV)),
        ),
        in_specs=[SM, HBM, HBM, HBM, HBM, VM, VM, VM, VM, VM, VM],
        out_specs=(HBM, HBM, VM, VM, VM, VM, VM, VM),
        scratch_shapes=[
            pltpu.VMEM((PARTS, CZ, CY, NX), f32),
            pltpu.VMEM((PORT_DEV, NX), f32),
            pltpu.VMEM((PORT_DEV, NODE_DEV), f32),
            DMA((26,)),
        ],
        compiler_params=params(),
    )(table, *map(away, (e_in, h_in, coef, loss)), cell_rows, columns, volts, diag, inv, off)


def corners_kernel(lower, upper, front, back):
    for side, source in enumerate((lower, upper)):
        for layer in range(DEPTH):
            to = pl.ds((side * DEPTH + layer) * STRIP, STRIP)
            front[to, :] = strip_of(
                lambda part: source[part * DEPTH + layer, 8:CY, :], slice(8 - DEPTH, 8)
            )
            back[to, :] = strip_of(
                lambda part: source[part * DEPTH + layer, 0:8, :], slice(0, DEPTH)
            )
    row = lax.broadcasted_iota(jnp.int32, (8, NX), 0)
    last = PARTS * DEPTH
    cells = jnp.where(row == 0, lower[last, 0:8, :], pltpu.roll(upper[last, 0:8, :], 1, 0))
    front[2 * DEPTH * STRIP :, :] = cells
    back[2 * DEPTH * STRIP :, :] = cells


def corners(lower, upper):
    shape = jax.ShapeDtypeStruct((2 * DEPTH * STRIP + 8, NX), f32)
    return pl.pallas_call(
        corners_kernel,
        name="corners",
        out_shape=(shape, shape),
        in_specs=[VM, VM],
        out_specs=(VM, VM),
        compiler_params=params(),
    )(lower, upper)


def halo_kernel(
    spots, active, node_row, columns, lower, upper, before, after, before_ends, after_ends,
    e_in, h_in, coef_in, loss_in,
    e_xy, e_z, h, media, found, columns_out, sample, coef, picked, sems,
):
    copies, copy = copier(sems)
    targets = [
        e_xy.at[0], e_xy.at[1], e_z, h.at[0], h.at[1], h.at[2], media.at[0], media.at[1],
    ]
    sources = [e_in.at[k] for k in range(3)] + [h_in.at[k] for k in range(3)] + [coef_in, loss_in]
    middle = pl.ds(PAD, CY)
    for part, (source, target) in enumerate(zip(sources, targets)):
        given = pl.ds(part * DEPTH, DEPTH)
        copy(source, target.at[pl.ds(DEPTH, CZ), middle])
        copy(lower.at[given], target.at[pl.ds(0, DEPTH), middle])
        copy(upper.at[given], target.at[pl.ds(DEPTH + CZ, DEPTH), middle])

    blank = jnp.zeros((8 - DEPTH, NX), f32)

    def unpack(ahead, behind, at, layer):
        given = pl.ds(pl.multiple_of(at * STRIP, 8), STRIP)
        low, high = ahead[given, :], behind[given, :]
        for part, target in enumerate(targets):
            rows = slice(part * DEPTH, (part + 1) * DEPTH)
            target[layer, 0:PAD, :] = jnp.concatenate([blank, low[rows]], axis=0)
            target[layer, PAD + CY : TALL, :] = jnp.concatenate([high[rows], blank], axis=0)

    @pl.loop(0, CZ)
    def _(layer):
        unpack(before, after, layer, layer + DEPTH)

    @pl.loop(0, 2 * DEPTH)
    def _(end):
        unpack(before_ends, after_ends, end, jnp.where(end < DEPTH, end, end + CZ))

    @pl.loop(0, REACH)
    def _(port):
        found[port] = PAD
        found[NODES_AT + port] = 0

    columns_out[...] = jnp.zeros_like(columns_out)

    def place_port(port, count):
        @pl.when(active[port] > 0)
        def _():
            found[count] = spots[port]
            found[NODES_AT + count] = node_row[port]
            columns_out[pl.ds(count, 1), :] = columns[pl.ds(port, 1), :]

        return count + active[port]

    count = lax.fori_loop(0, REACH, place_port, 0)
    groups = (count + PORT_DEV - 1) // PORT_DEV
    found[COUNT_AT] = groups
    for item in range(2 * NB_DEV * OFF):
        found[OFF_AT + item] = node_row[REACH + item]

    for job in copies:
        job.wait()

    @pl.loop(0, LAYERS)
    def _(layer):
        media[1, layer] = 1.0 - media[1, layer]

    @pl.loop(0, groups)
    def _(group):
        part = pl.ds(pl.multiple_of(group * PORT_DEV, PORT_DEV), PORT_DEV)
        _, place, _ = columns_at(columns_out, part)
        sample[part, :] = gather_cells(e_z, found, group, place, picked)
        coef[part, :] = gather_cells(media.at[0], found, group, place, picked)


def gather_cells(source, found, group, place, picked):
    for port in range(PORT_DEV):
        spot = found[group * PORT_DEV + port]
        picked[port : port + 1, :] = source[spot // TALL, pl.ds(spot % TALL, 1), :]
    return pick(picked[...], place)


def halo(spots, active, node_row, columns, lower, upper, sides, e_in, h_in, coef, loss):
    return pl.pallas_call(
        halo_kernel,
        name="halo",
        out_shape=(
            onchip((2,) + CUBE),
            onchip(CUBE),
            onchip((3,) + CUBE),
            onchip((2,) + CUBE),
            jax.ShapeDtypeStruct((SWAP_AT + NB_DEV * OFF,), jnp.int32),
            onchip(columns.shape),
            onchip((REACH, 1)),
            onchip((REACH, 1)),
        ),
        in_specs=[SM, SM, SM, VM, HBM, HBM, VM, VM, VM, VM] + [HBM] * 4,
        out_specs=(VM, VM, VM, VM, SM, VM, VM, VM),
        scratch_shapes=[pltpu.VMEM((PORT_DEV, NX), f32), DMA((24,))],
        compiler_params=params(),
    )(
        spots, active, node_row, columns, away(lower), away(upper), *sides,
        *map(away, (e_in, h_in, coef, loss)),
    )


def field_kernel(step, bounds, media, e_xy, e_z, h, to_xy, to_z, to_h):
    low_z, low_y = bounds[0], bounds[1]
    lane = lanes_of(TALL, NX)
    last_lane, first_lane = lane == NX - 1, lane == 0
    row = lax.broadcasted_iota(jnp.int32, (TALL, NX), 0)
    rate_rows = jnp.where(row < PAD, low_y, time_step)

    def next_x(value):
        return jnp.where(last_lane, 0.0, pltpu.roll(value, NX - 1, 1))

    def prior_x(value):
        return jnp.where(first_lane, 0.0, pltpu.roll(value, 1, 1))

    def next_y(value):
        return pltpu.roll(value, TALL - 1, 0)

    def prior_y(value):
        return pltpu.roll(value, 1, 0)

    def magnetic(layer):
        e_x, e_y, e_zz = e_xy[0, layer], e_xy[1, layer], e_z[layer]
        rate = rate_rows * jnp.where(layer < DEPTH, low_z, 1.0)
        curl_x = (next_y(e_zz) - e_zz) - (e_xy[1, layer + 1] - e_y)
        curl_y = (e_xy[0, layer + 1] - e_x) - (next_x(e_zz) - e_zz)
        curl_z = (next_x(e_y) - e_y) - (next_y(e_x) - e_x)
        return (h[0, layer] - rate * curl_x, h[1, layer] - rate * curl_y, h[2, layer] - rate * curl_z)

    def electric(layer):
        h_x, h_y, h_z = to_h[0, layer], to_h[1, layer], to_h[2, layer]
        coef, kept = media[0, layer], media[1, layer]
        back_x = (h_z - prior_y(h_z)) - (h_y - to_h[1, layer - 1])
        back_y = (h_x - to_h[0, layer - 1]) - (h_z - prior_x(h_z))
        back_z = (h_y - prior_x(h_y)) - (h_x - prior_y(h_x))
        return (
            kept * e_xy[0, layer] + coef * back_x,
            kept * e_xy[1, layer] + coef * back_y,
            kept * e_z[layer] + coef * back_z,
        )

    def put_h(layer, values):
        to_h[0, layer], to_h[1, layer], to_h[2, layer] = values

    def put_e(layer, values):
        to_xy[0, layer], to_xy[1, layer], to_z[layer] = values

    put_h(step - 1, magnetic(step - 1))
    put_h(step, magnetic(step))
    last = LAYERS - step - 1

    @pl.loop(step, last)
    def _(layer):
        electric_values = electric(layer)
        magnetic_values = magnetic(layer + 1)
        put_e(layer, electric_values)
        put_h(layer + 1, magnetic_values)

    put_e(last, electric(last))


def field(step, bounds, media, e_xy, e_z, h):
    return pl.pallas_call(
        functools.partial(field_kernel, step),
        name="field",
        out_shape=(onchip((2,) + CUBE), onchip(CUBE), onchip((3,) + CUBE)),
        in_specs=[SM] + [VM] * 4,
        out_specs=(VM,) * 3,
        compiler_params=params(),
    )(bounds, keep(media), keep(e_xy), keep(e_z), keep(h))


def solve(arrived, table, volts, m_off, m_diag, m_inv):
    lane = lanes_of(1, NODE_DEV)
    halves = []
    for j in range(NB_DEV):
        pieces = []
        for half in range(OFF // 2):
            total = None
            for side in range(2):
                spot = j * OFF + half * 2 + side
                row = arrived[pl.ds(table[OFF_AT + spot], 1), :]
                row = jnp.where(table[SWAP_AT + spot] == side, row, pltpu.roll(row, BS, 1))
                row = jnp.where((lane < BS) == (side == 0), row, 0.0)
                total = row if total is None else total + row
            pieces.append(jnp.broadcast_to(total, (BS, NODE_DEV)))
        halves.append(pieces)
    first = jnp.concatenate([halves[0][0], halves[1][0]], axis=0)
    second = jnp.concatenate([halves[0][1], halves[1][1]], axis=0)
    product = m_off[:, 0:NODE_DEV] * first + m_off[:, NODE_DEV : 2 * NODE_DEV] * second
    offsum = jnp.sum(product, axis=1, keepdims=True)
    parity = lax.broadcasted_iota(jnp.int32, arrived.shape, 0) % 2
    inject = jnp.sum(jnp.where(parity == 1, arrived[...], 0.0), axis=0, keepdims=True)
    start = volts[...]
    target = charge_scale * start + inject
    diagonal = lax.broadcasted_iota(jnp.int32, (NODE_DEV, NODE_DEV), 0) == lanes_of(NODE_DEV, NODE_DEV)
    iterate = start
    for newton_round in range(NEWTON):
        local = diode_weight * jnp.tanh(iterate) - target
        terms = m_diag[...] * iterate + jnp.where(diagonal, local, 0.0)
        resid = jnp.sum(terms, axis=1, keepdims=True) + offsum
        iterate = iterate - jnp.sum(m_inv[...] * resid, axis=0, keepdims=True)
    return iterate


def apply_ports(table, arrived, columns, sample, coef, e_z, near_rows, deltas):
    @pl.loop(0, table[COUNT_AT])
    def _(group):
        first = group * PORT_DEV
        part = pl.ds(pl.multiple_of(first, PORT_DEV), PORT_DEV)
        for port in range(PORT_DEV):
            near_rows[port : port + 1, :] = arrived[pl.ds(table[NODES_AT + first + port], 1), :]
        gain, place, lane = columns_at(columns, part)
        current = gain * (sample[part, :] - pick(near_rows[...], lane))
        deltas[...] = spread(-coef[part, :] * current, place, NX)
        for port in range(PORT_DEV):
            spot = table[first + port]
            layer, row = spot // TALL, pl.ds(spot % TALL, 1)
            e_z[layer, row, :] = e_z[layer, row, :] + deltas[port : port + 1, :]


def circuit_kernel(
    table, arrived, columns, sample, coef, volts, m_off, m_diag, m_inv, e_in,
    e_z, out, volts_out, sample_out, near_rows, deltas, picked, spread_rows,
):
    e_z[...] = e_in[...]
    apply_ports(table, arrived, columns, sample, coef, e_z, near_rows, deltas)

    @pl.loop(0, table[COUNT_AT])
    def _(group):
        part = pl.ds(pl.multiple_of(group * PORT_DEV, PORT_DEV), PORT_DEV)
        _, place, _ = columns_at(columns, part)
        sample_out[part, :] = gather_cells(e_z, table, group, place, picked)

    solved = solve(arrived, table, volts, m_off, m_diag, m_inv)
    volts_out[...] = solved
    own = slice(0, PORT_DEV)
    gain, _, lane = columns_at(columns, own)
    rows = spread(gain * sample_out[own, :], lane, NODE_DEV)
    write_outgoing(out, solved, rows, table, NODES_AT, spread_rows)


def circuit(table, arrived, columns, sample, coef, volts, mats, e_z):
    return pl.pallas_call(
        circuit_kernel,
        name="circuit",
        out_shape=(
            onchip(CUBE),
            onchip(arrived.shape),
            onchip((1, NODE_DEV)),
            onchip((REACH, 1)),
        ),
        in_specs=[SM] + [VM] * 9,
        out_specs=(VM,) * 4,
        scratch_shapes=[
            pltpu.VMEM((PORT_DEV, NODE_DEV), f32),
            pltpu.VMEM((PORT_DEV, NX), f32),
            pltpu.VMEM((PORT_DEV, NX), f32),
            pltpu.VMEM((PORT_DEV, NODE_DEV), f32),
        ],
        compiler_params=params(),
    )(
        table, arrived, keep(columns), keep(sample), keep(coef), volts,
        *[keep(mat) for mat in mats], keep(e_z),
    )


def finish_kernel(
    table, arrived, columns, sample, coef, volts, m_off, m_diag, m_inv, e_xy, e_in, h,
    e_out, h_out, volts_out, e_z, near_rows, deltas, sems,
):
    copies, copy = copier(sems)
    layers, rows = pl.ds(DEPTH, CZ), pl.ds(PAD, CY)
    for k in range(3):
        copy(h.at[k, layers, rows], h_out.at[k])
    for k in range(2):
        copy(e_xy.at[k, layers, rows], e_out.at[k])
    e_z[...] = e_in[...]
    apply_ports(table, arrived, columns, sample, coef, e_z, near_rows, deltas)
    copy(e_z.at[layers, rows], e_out.at[2])
    volts_out[...] = solve(arrived, table, volts, m_off, m_diag, m_inv)
    for job in copies:
        job.wait()


def finish(table, arrived, columns, sample, coef, volts, mats, e_xy, e_z, h):
    return pl.pallas_call(
        finish_kernel,
        name="finish",
        out_shape=(
            jax.ShapeDtypeStruct((3, CZ, CY, NX), f32),
            jax.ShapeDtypeStruct((3, CZ, CY, NX), f32),
            jax.ShapeDtypeStruct((1, NODE_DEV), f32),
        ),
        in_specs=[SM] + [VM] * 11,
        out_specs=(HBM, HBM, VM),
        scratch_shapes=[
            pltpu.VMEM(CUBE, f32),
            pltpu.VMEM((PORT_DEV, NODE_DEV), f32),
            pltpu.VMEM((PORT_DEV, NX), f32),
            DMA((6,)),
        ],
        compiler_params=params(),
    )(
        table, arrived, keep(columns), keep(sample), keep(coef), volts,
        *[keep(mat) for mat in mats], keep(e_xy), keep(e_z), keep(h),
    )


def shifted(value, axis, steps):
    count = lax.axis_size(axis)
    first, last = (max(0, -steps), min(count, count - steps))
    return lax.ppermute(value, axis, [(source, source + steps) for source in range(first, last)])


def exchange(value):
    return lax.all_to_all(value, ("gz", "gy"), 0, 0, tiled=True)


def body(
    e_field,
    h_field,
    e_coef,
    e_loss,
    port_cell,
    port_node,
    port_gain,
    diag_blocks,
    inv_blocks,
    off_blocks,
    off_cols,
    volts_init,
):
    gz, gy = lax.axis_index("gz"), lax.axis_index("gy")
    n_gz, n_gy = lax.axis_size("gz"), lax.axis_size("gy")
    device = gz * n_gy + gy
    own = slice(0, PORT_DEV)

    def columns_of(gain, cells, node):
        return jnp.stack([gain, (cells % NX).astype(f32), (node % NODE_DEV).astype(f32)], axis=1)

    own_node = lax.dynamic_slice_in_dim(port_node, device * PORT_DEV, PORT_DEV)
    own_gain = lax.dynamic_slice_in_dim(port_gain, device * PORT_DEV, PORT_DEV)
    cell_rows = jnp.pad(port_cell.astype(f32)[None], ((0, CY - 1), (0, NX - PORT_DEV)))
    grids = (e_field, h_field, e_coef, e_loss)
    volts = volts_init.reshape(1, NODE_DEV)
    up, down, front, back, out, *mats = begin(
        jnp.concatenate([port_cell // NX, 2 * (own_node // NODE_DEV)]),
        *grids,
        cell_rows,
        columns_of(own_gain, port_cell, own_node),
        volts,
        diag_blocks,
        inv_blocks,
        off_blocks,
    )
    before = shifted(front, "gy", 1)
    after = shifted(back, "gy", -1)
    lower = shifted(up, "gz", 1)
    upper = shifted(down, "gz", -1)
    arrived = exchange(out)
    front_ends, back_ends = corners(lower, upper)
    before_ends = shifted(front_ends, "gy", 1)
    after_ends = shifted(back_ends, "gy", -1)
    sides = (before, after, before_ends, after_ends)

    def cells_in(value, row):
        return value[row, own].astype(jnp.int32)

    last, end = CZ * STRIP, 2 * DEPTH * STRIP
    cells = jnp.stack(
        [
            port_cell,
            lower[PARTS * DEPTH, 0, own].astype(jnp.int32),
            upper[PARTS * DEPTH, 0, own].astype(jnp.int32),
            cells_in(before, last),
            cells_in(before_ends, end),
            cells_in(before_ends, end + 1),
            cells_in(after, last),
            cells_in(after_ends, end),
            cells_in(after_ends, end + 1),
        ]
    )
    shift_z = jnp.array([side[0] for side in SIDES], jnp.int32)[:, None]
    shift_y = jnp.array([side[1] for side in SIDES], jnp.int32)[:, None]
    at_z, at_y = gz + shift_z, gy + shift_y
    exists = (at_z >= 0) & (at_z < n_gz) & (at_y >= 0) & (at_y < n_gy)
    ids = jnp.where(exists, at_z * n_gy + at_y, 0)[:, 0]
    nodes = port_node.reshape(-1, PORT_DEV)[ids].reshape(-1)
    gains = port_gain.reshape(-1, PORT_DEV)[ids].reshape(-1)
    layer = cells // (CY * NX) + shift_z * CZ + DEPTH
    row = (cells // NX) % CY + shift_y * CY + PAD
    inside = (layer >= 1) & (layer < LAYERS - 1) & (row >= PAD - DEPTH + 1) & (row < PAD + CY + DEPTH - 1)
    valid = exists & inside
    spots = jnp.where(valid, layer * TALL + row, PAD).reshape(-1)
    active = valid.astype(jnp.int32).reshape(-1)
    columns = columns_of(gains, cells.reshape(-1), nodes)
    flat_cols = off_cols.reshape(-1)
    node_row = jnp.concatenate(
        [2 * (nodes // NODE_DEV), 2 * (flat_cols // NB_DEV), flat_cols % NB_DEV]
    )
    bounds = jnp.stack([jnp.where(gz > 0, 1.0, 0.0), jnp.where(gy > 0, time_step, 0.0)]).astype(f32)

    e_xy, e_z, h, media, table, columns, sample, coef = halo(
        spots, active, node_row, columns, lower, upper, sides, *grids
    )
    for step in range(1, STEPS + 1):
        if step > 1:
            arrived = exchange(out)
            arrived, e_z = lax.optimization_barrier((arrived, e_z))
        e_xy, e_z, h = field(step, bounds, media, e_xy, e_z, h)
        shared = (table, arrived, columns, sample, coef, volts, mats)
        if step < STEPS:
            e_z, out, volts, sample = circuit(*shared, e_z)
        else:
            e_end, h_end, volts = finish(*shared, e_xy, e_z, h)
    return e_end, h_end, volts.reshape(-1)


def solution(mesh):
    placed = (
        P(None, "gz", "gy", None),
        P(None, "gz", "gy", None),
        P("gz", "gy", None),
        P("gz", "gy", None),
        P(("gz", "gy")),
        P(),
        P(),
        P(("gz", "gy"), None, None),
        P(("gz", "gy"), None, None),
        P(("gz", "gy"), None, None, None),
        P(("gz", "gy"), None),
        P(("gz", "gy")),
    )
    return jax.shard_map(
        body,
        mesh=mesh,
        in_specs=placed,
        out_specs=(P(None, "gz", "gy", None), P(None, "gz", "gy", None), P(("gz", "gy"))),
        check_vma=False,
    )
```

time: 222 us -> 243 us (1.095)
  Pallas kernels: 55.8 us -> 92.7 us
  blocking collectives: 87.5 us -> 74.7 us
  local copies, waits for them, and re-layouts: 12.2 us -> 23 us
  starting transfers between devices: 37.5 us -> 30.1 us
  waiting for transfers between devices: 25.3 us -> 18.7 us
    pallas_call x1, Pallas kernels: 2.97 us -> 43.1 us  [begin(): pl.pallas_call(begin_kernel, name='begin', out_shape=(jax.ShapeDtypeStruc...]
    all_to_all x4, blocking collectives: 87.5 us -> 74.7 us  [exchange(): return lax.all_to_all(value, ('gz', 'gy'), 0, 0, tiled=True)]
    ppermute x12 -> x6, starting transfers between devices: 26.2 us -> 16.2 us  [shifted(): lax.ppermute(value, axis, [(source, source + steps) for source in range(f...]
    all_to_all x1, waiting for transfers between devices: 9.89 us -> 0.01 us  [exchange(): return lax.all_to_all(value, ('gz', 'gy'), 0, 0, tiled=True)]
    unnamed x30 -> x58, local copies, waits for them, and re-layouts: 10.3 us -> 19.7 us
    ppermute x12 -> x6, waiting for transfers between devices: 15.4 us -> 18.7 us  [shifted(): lax.ppermute(value, axis, [(source, source + steps) for source in range(f...]
    pallas_call x14 -> x11, Pallas kernels: 49.6 us -> 46.4 us  [the longest x5 24.1 us: field(): pl.pallas_call(functools.partial(field_kernel, step), name='field', out_s...]
    all_to_all x1, starting transfers between devices: 11.4 us -> 13.9 us  [exchange(): return lax.all_to_all(value, ('gz', 'gy'), 0, 0, tiled=True)]
  transfers between devices with their start and end apart: 13 -> 7, of which waited for: 6 -> 2; matrix products, arithmetic and copies ran while one was open for 0% -> 1% of each run, Pallas kernels for 2% -> 7%
where the time goes in v2:
time: 243 us
  Pallas kernels  92.7 us (38%)
  blocking collectives  74.7 us (31%)
  starting transfers between devices  30.1 us (12%)
  local copies, waits for them, and re-layouts  23 us (9%)
  waiting for transfers between devices  18.7 us (8%)
  other arithmetic  2.65 us (1%)
    all_to_all x4, blocking collectives, exchange(): return lax.all_to_all(value, ('gz', 'gy'), 0, 0, tiled=True)  74.7 us
    pallas_call x1, Pallas kernels, begin(): pl.pallas_call(begin_kernel, name='begin', out_shape=(jax.ShapeDtypeStruc...  43.1 us
    pallas_call x5, Pallas kernels, field(): pl.pallas_call(functools.partial(field_kernel, step), name='field', out_s...  24.1 us
    unnamed x58, local copies, waits for them, and re-layouts  19.7 us
    ppermute x6, waiting for transfers between devices, shifted(): lax.ppermute(value, axis, [(source, source + steps) for source in range(f...  18.7 us
    ppermute x6, starting transfers between devices, shifted(): lax.ppermute(value, axis, [(source, source + steps) for source in range(f...  16.2 us
    all_to_all x1, starting transfers between devices, exchange(): return lax.all_to_all(value, ('gz', 'gy'), 0, 0, tiled=True)  13.9 us
    pallas_call x4, Pallas kernels, circuit(): pl.pallas_call(circuit_kernel, name='circuit', out_shape=(onchip(CUBE), o...  11.6 us
  transfers between devices with their start and end apart: 7, of which 2 were waited for; matrix products, arithmetic and copies ran while one was open for 1% of the time, Pallas kernels for 7%

profile of v2, /device:TPU:1, one launch (start us, length us, event | category | flops | bytes accessed | tf_op | source)
XLA Modules:
  0.0 242.8 jit_solution(14234836647257638700)
XLA Ops:
  0.6 0.8 fusion.18
  1.4 0.8 dynamic-slice_bitcast_fusion
  2.2 0.8 fusion.16
  3.0 0.1 copy.33.columns
  3.1 0.1 pad_add_fusion.1.table
  3.2 0.9 copy-done.14
  4.1 0.8 copy-done.17
  5.0 0.8 copy-done.18
  5.8 0.7 copy-done.19
  6.5 43.1 %begin.1 = (f32[41,16,256]{2,1,0:T(8,128)}, f32[41,16,256]{2,1,0:T(8,128)}, f32[1288,256]{1,0:T(8,128)}, f32[1288,256]{1,0:T(8,128)}, f32[256,128]{1,0:T(8,128)}...) custom-call(s32[64]{0:T(128)S(1)} %pad_add_fusion.1.table, f32[3,32,16,256]{3,2,1,0:T(8,128)} %e_in.3, ...), custom_call_target="tpu_custom_call" | custom-call | tf_op jit(solution)/shard_map/begin/pallas_call | solution.py:149
  49.6 4.6 %collective-permute-start = (f32[41,16,256]{2,1,0:T(8,128)}, f32[41,16,256]{2,1,0:T(8,128)S(1)}, u32[]{:S(2)}, u32[]{:S(2)}) collective-permute-start(f32[41,16,256]{2,1,0:T(8,128)} %get-tuple-element.63), channel_id=1, source_target_pairs={{0,8},{8,16},{16,24},{24,32},{32,40},{40,48},{48,56},{56,64},{64,7... | collective-permute-start | bytes 2015240 | tf_op jit(solution)/shard_map/ppermute | solution.py:516
  54.2 1.9 collective-permute-start.1
  56.2 3.6 %collective-permute-start.2 = (f32[1288,256]{1,0:T(8,128)}, f32[1288,256]{1,0:T(8,128)S(1)}, u32[]{:S(2)}, u32[]{:S(2)}) collective-permute-start(f32[1288,256]{1,0:T(8,128)} %get-tuple-element.65), channel_id=1, source_target_pairs={{0,1},{1,2},{2,3},{3,4},{4,5},{5,6},{6,7},{8,9},{9,10},{10,11},{11... | collective-permute-start | bytes 3956744 | tf_op jit(solution)/shard_map/ppermute | solution.py:516
  59.8 1.3 collective-permute-start.4
  61.1 13.9 %all-to-all-start = ((f32[128,2,128]{2,1,0:T(2,128)}), f32[128,2,128]{2,1,0:T(2,128)}, u32[]{:S(2)}, u32[]{:S(2)}) async-start(f32[128,2,128]{2,1,0:T(2,128)} %bitcast.8), calls=%async_computation | async-start | bytes 262144 | tf_op jit(solution)/shard_map/all_to_all | solution.py:520
  75.1 0.1 reshape.202
  75.2 0.6 gather_fusion
  75.7 0.1 reshape.203
  75.8 0.1 reshape.207
  76.0 0.1 and.137
  76.2 0.1 add.142
  76.4 0.1 add.148
  76.4 0.1 reshape.204
  76.6 0.6 gather_fusion.1
  77.1 0.1 stack_reshape.3
  77.2 0.1 pad_maximum_fusion.2.bounds
  77.3 0.1 pad_add_fusion.node_row
  77.4 0.1 corners.1
  77.5 3.4 %collective-permute-start.3 = (f32[408,256]{1,0:T(8,128)S(1)}, f32[408,256]{1,0:T(8,128)S(1)}, u32[]{:S(2)}, u32[]{:S(2)}) collective-permute-start(f32[408,256]{1,0:T(8,128)S(1)} %get-tuple-element.66), channel_id=1, source_target_pairs={{0,1},{1,2},{2,3},{3,4},{4,5},{5,6},{6,7},{8,9},{9,10},{10,11},{11... | collective-permute-start | bytes 1253384 | tf_op jit(solution)/shard_map/ppermute | solution.py:516
  81.0 1.3 collective-permute-start.5
  82.3 15.2 %collective-permute-done.3.before_ends = f32[408,256]{1,0:T(8,128)S(1)} collective-permute-done((f32[408,256]{1,0:T(8,128)S(1)}, f32[408,256]{1,0:T(8,128)S(1)}, u32[]{:S(2)}, u32[]{:S(2)}) %collective-permute-start.3) | collective-permute-done | bytes 417824 | tf_op jit(solution)/shard_map/ppermute | solution.py:516
  97.5 0.7 copy-done.10
  98.2 3.5 %collective-permute-done.5.after_ends = f32[408,256]{1,0:T(8,128)S(1)} collective-permute-done((f32[408,256]{1,0:T(8,128)S(1)}, f32[408,256]{1,0:T(8,128)S(1)}, u32[]{:S(2)}, u32[]{:S(2)}) %collective-permute-start.5) | collective-permute-done | bytes 417824 | tf_op jit(solution)/shard_map/ppermute | solution.py:516
  101.8 0.8 copy-done.12
  102.5 1.1 copy-done.8
  103.6 0.7 slice_convert_fusion.2
  104.3 0.1 stack.48
  104.4 0.1 reshape.206
  104.5 0.1 copy.34.columns
  104.7 1.3 copy-done.9
  106.0 1.0 copy-done.11
  107.1 1.0 copy-done.13
  108.1 10.6 %halo.1 = (f32[2,42,32,256]{3,2,1,0:T(8,128)S(1)}, f32[42,32,256]{2,1,0:T(8,128)S(1)}, f32[3,42,32,256]{3,2,1,0:T(8,128)S(1)}, f32[2,42,32,256]{3,2,1,0:T(8,128)...) custom-call(s32[288]{0:T(512)S(1)} %add_select_fusion.4.spots, ...), custom_call_target="tpu_custom_call" | custom-call | tf_op jit(solution)/shard_map/halo/pallas_call | solution.py:283
  118.6 0.7 copy-done.15
  119.3 5.3 %field.5 = (f32[2,42,32,256]{3,2,1,0:T(8,128)S(1)}, f32[42,32,256]{2,1,0:T(8,128)S(1)}, f32[3,42,32,256]{3,2,1,0:T(8,128)S(1)}) custom-call(f32[2]{0:T(128)S(1)} %pad_maximum_fusion.2.bounds, f32[2,42,32,256]{3,2,1,0:T(8,128)S(1)} %get-tuple-element.77.media, f32[2,42,32,256]{3,2,1,0:T(8,128)S(1)} %get-tuple-element.78.e_xy, ...), custom_call_target="tpu_custom_call" | custom-call | tf_op jit(solution)/shard_map/field/pallas_call | solution.py:366
  124.6 1.9 copy-done
  126.6 1.6 copy-done.2
  128.1 1.1 copy-done.6
  129.2 1.3 copy-done.7
  130.6 3.2 %circuit.4 = (f32[42,32,256]{2,1,0:T(8,128)S(1)}, f32[256,128]{1,0:T(8,128)S(1)}, f32[1,128]{1,0:T(1,128)S(1)}, f32[288,1]{1,0:T(8,128)S(1)}) custom-call(s32[593]{0:T(1024)S(1)} %get-tuple-element.69.table, f32[256,128]{1,0:T(8,128)} %bitcast.9.arrived, f32[288,3]{1,0:T(8,128)S(1)} %get-tuple-element.71.columns, f32[288,1]{1,0:T(8,128)S(1)} %copy-done.16, ...), custom_call_target="tpu_custom_call" | custom-call | tf_op jit(solution)/shard_map/circuit/pallas_call | solution.py:447
  133.7 29.7 %all_to_all.59 = f32[128,2,128]{2,1,0:T(2,128)S(1)} all-to-all(f32[128,2,128]{2,1,0:T(2,128)S(1)} %bitcast.34), channel_id=1, replica_groups=mesh['gz'=16,'gy'=8] {'gz','gy'}, dimensions={0} | all-to-all | bytes 262144 | tf_op jit(solution)/shard_map/all_to_all | solution.py:520
  163.4 2.2 copy-done.1
  165.6 1.8 copy-done.3
  167.4 5.1 %field.6 = (f32[2,42,32,256]{3,2,1,0:T(8,128)S(1)}, f32[42,32,256]{2,1,0:T(8,128)S(1)}, f32[3,42,32,256]{3,2,1,0:T(8,128)S(1)}) custom-call(f32[2]{0:T(128)S(1)} %pad_maximum_fusion.2.bounds, f32[2,42,32,256]{3,2,1,0:T(8,128)S(1)} %get-tuple-element.77.media, f32[2,42,32,256]{3,2,1,0:T(8,128)S(1)} %copy-done.3, f32[42,32,256]{2,1,0:T(8,128)S(1)} %get-tuple-element.88.e_z, ...), custom_call_target="tpu_custom_call" | custom-call | tf_op jit(solution)/shard_map/field/pallas_call | solution.py:366
  172.4 2.8 %circuit.5 = (f32[42,32,256]{2,1,0:T(8,128)S(1)}, f32[256,128]{1,0:T(8,128)S(1)}, f32[1,128]{1,0:T(1,128)S(1)}, f32[288,1]{1,0:T(8,128)S(1)}) custom-call(s32[593]{0:T(1024)S(1)} %get-tuple-element.69.table, f32[256,128]{1,0:T(8,128)S(1)} %bitcast.28, f32[288,3]{1,0:T(8,128)S(1)} %get-tuple-element.71.columns, f32[288,1]{1,0:T(8,128)S(1)} %get-tuple-element.85.sample, ...), custom_call_target="tpu_custom_call" | custom-call | tf_op jit(solution)/shard_map/circuit/pallas_call | solution.py:447
  175.3 15.0 %all_to_all.60 = f32[128,2,128]{2,1,0:T(2,128)S(1)} all-to-all(f32[128,2,128]{2,1,0:T(2,128)S(1)} %bitcast.31), channel_id=1, replica_groups=mesh['gz'=16,'gy'=8] {'gz','gy'}, dimensions={0} | all-to-all | bytes 262144 | tf_op jit(solution)/shard_map/all_to_all | solution.py:520
  190.3 4.8 %field.7 = (f32[2,42,32,256]{3,2,1,0:T(8,128)S(1)}, f32[42,32,256]{2,1,0:T(8,128)S(1)}, f32[3,42,32,256]{3,2,1,0:T(8,128)S(1)}) custom-call(f32[2]{0:T(128)S(1)} %pad_maximum_fusion.2.bounds, f32[2,42,32,256]{3,2,1,0:T(8,128)S(1)} %get-tuple-element.77.media, f32[2,42,32,256]{3,2,1,0:T(8,128)S(1)} %get-tuple-element.96.e_xy, ...), custom_call_target="tpu_custom_call" | custom-call | tf_op jit(solution)/shard_map/field/pallas_call | solution.py:366
  195.1 2.8 %circuit.6 = (f32[42,32,256]{2,1,0:T(8,128)S(1)}, f32[256,128]{1,0:T(8,128)S(1)}, f32[1,128]{1,0:T(1,128)S(1)}, f32[288,1]{1,0:T(8,128)S(1)}) custom-call(s32[593]{0:T(1024)S(1)} %get-tuple-element.69.table, f32[256,128]{1,0:T(8,128)S(1)} %bitcast.29, f32[288,3]{1,0:T(8,128)S(1)} %get-tuple-element.71.columns, f32[288,1]{1,0:T(8,128)S(1)} %get-tuple-element.94.sample, ...), custom_call_target="tpu_custom_call" | custom-call | tf_op jit(solution)/shard_map/circuit/pallas_call | solution.py:447
  197.9 15.0 %all_to_all.61 = f32[128,2,128]{2,1,0:T(2,128)S(1)} all-to-all(f32[128,2,128]{2,1,0:T(2,128)S(1)} %bitcast.32), channel_id=1, replica_groups=mesh['gz'=16,'gy'=8] {'gz','gy'}, dimensions={0} | all-to-all | bytes 262144 | tf_op jit(solution)/shard_map/all_to_all | solution.py:520
  212.9 4.6 %field.8 = (f32[2,42,32,256]{3,2,1,0:T(8,128)S(1)}, f32[42,32,256]{2,1,0:T(8,128)S(1)}, f32[3,42,32,256]{3,2,1,0:T(8,128)S(1)}) custom-call(f32[2]{0:T(128)S(1)} %pad_maximum_fusion.2.bounds, f32[2,42,32,256]{3,2,1,0:T(8,128)S(1)} %get-tuple-element.77.media, f32[2,42,32,256]{3,2,1,0:T(8,128)S(1)} %get-tuple-element.105.e_xy, ...), custom_call_target="tpu_custom_call" | custom-call | tf_op jit(solution)/shard_map/field/pallas_call | solution.py:366
  217.5 2.8 %circuit.7 = (f32[42,32,256]{2,1,0:T(8,128)S(1)}, f32[256,128]{1,0:T(8,128)S(1)}, f32[1,128]{1,0:T(1,128)S(1)}, f32[288,1]{1,0:T(8,128)S(1)}) custom-call(s32[593]{0:T(1024)S(1)} %get-tuple-element.69.table, f32[256,128]{1,0:T(8,128)S(1)} %bitcast.30, f32[288,3]{1,0:T(8,128)S(1)} %get-tuple-element.71.columns, f32[288,1]{1,0:T(8,128)S(1)} %get-tuple-element.103.sample, ...), custom_call_target="tpu_custom_call" | custom-call | tf_op jit(solution)/shard_map/circuit/pallas_call | solution.py:447
  220.3 15.0 %all_to_all.62 = f32[128,2,128]{2,1,0:T(2,128)S(1)} all-to-all(f32[128,2,128]{2,1,0:T(2,128)S(1)} %bitcast.33), channel_id=1, replica_groups=mesh['gz'=16,'gy'=8] {'gz','gy'}, dimensions={0} | all-to-all | bytes 262144 | tf_op jit(solution)/shard_map/all_to_all | solution.py:520
  235.3 4.3 %field.9 = (f32[2,42,32,256]{3,2,1,0:T(8,128)S(1)}, f32[42,32,256]{2,1,0:T(8,128)S(1)}, f32[3,42,32,256]{3,2,1,0:T(8,128)S(1)}) custom-call(f32[2]{0:T(128)S(1)} %pad_maximum_fusion.2.bounds, f32[2,42,32,256]{3,2,1,0:T(8,128)S(1)} %get-tuple-element.77.media, f32[2,42,32,256]{3,2,1,0:T(8,128)S(1)} %get-tuple-element.114.e_xy, ...), custom_call_target="tpu_custom_call" | custom-call | tf_op jit(solution)/shard_map/field/pallas_call | solution.py:366
  239.7 3.2 %finish.1 = (f32[3,32,16,256]{3,2,1,0:T(8,128)}, f32[3,32,16,256]{3,2,1,0:T(8,128)}, f32[1,128]{1,0:T(1,128)}) custom-call(s32[593]{0:T(1024)S(1)} %get-tuple-element.69.table, f32[256,128]{1,0:T(8,128)S(1)} %bitcast.27, f32[288,3]{1,0:T(8,128)S(1)} %get-tuple-element.71.columns, f32[288,1]{1,0:T(8,128)S(1)} %get-tuple-element.112.sample, ...), custom_call_target="tpu_custom_call" | custom-call | tf_op jit(solution)/shard_map/finish/pallas_call | solution.py:490
  (67 shorter events, 0.6 us)
Async XLA Ops:
  3.2 1.0 copy-start.14
  4.1 0.8 copy-start.17
  5.0 0.8 copy-start.18
  5.8 0.7 copy-start.19
  6.5 68.6 %copy-start.21 = (s32[4096]{0:T(1024)S(1)}, s32[4096]{0:T(1024)}, u32[]{:S(2)}) copy-start(s32[4096]{0:T(1024)} %param.19) | copy-start | bytes 49156
  6.5 68.7 %copy-start.26 = (s32[9]{0:T(128)S(1)}, s32[9]{0:T(128)}, u32[]{:S(2)}) copy-start(s32[9]{0:T(128)} %constant.173.clone) | copy-start | bytes 112
  6.5 68.7 %copy-start.27 = (s32[9]{0:T(128)S(1)}, s32[9]{0:T(128)}, u32[]{:S(2)}) copy-start(s32[9]{0:T(128)} %constant.172.clone) | copy-start | bytes 112
  6.5 69.4 %copy-start.22 = (f32[4096]{0:T(1024)S(1)}, f32[4096]{0:T(1024)}, u32[]{:S(2)}) copy-start(f32[4096]{0:T(1024)} %param.20) | copy-start | bytes 49156
  6.5 69.7 %copy-start.25 = (s32[9]{0:T(128)S(1)}, s32[9]{0:T(128)}, u32[]{:S(2)}) copy-start(s32[9]{0:T(128)} %constant.181) | copy-start | bytes 112
  6.5 69.8 %copy-start.24 = (s32[9]{0:T(128)S(1)}, s32[9]{0:T(128)}, u32[]{:S(2)}) copy-start(s32[9]{0:T(128)} %constant.182) | copy-start | bytes 112
  6.5 70.0 %copy-start.28 = (s32[2,4]{1,0:T(2,128)S(1)}, s32[2,4]{1,0:T(2,128)}, u32[]{:S(2)}) copy-start(s32[2,4]{1,0:T(2,128)} %param.24) | copy-start | bytes 100
  49.6 54.6 %copy-start.23 = (s32[32]{0:T(128)S(1)}, s32[32]{0:T(128)}, u32[]{:S(2)}) copy-start(s32[32]{0:T(128)} %param.18) | copy-start | bytes 388
  49.6 27.7 %collective-permute-start = (f32[41,16,256]{2,1,0:T(8,128)}, f32[41,16,256]{2,1,0:T(8,128)S(1)}, u32[]{:S(2)}, u32[]{:S(2)}) collective-permute-start(f32[41,16,256]{2,1,0:T(8,128)} %get-tuple-element.63), channel_id=1, source_target_pairs={{0,8},{8,16},{16,24},{24,32},{32,40},{40,48},{48,56},{56,64},{64,7... | collective-permute-start | bytes 2015240 | tf_op jit(solution)/shard_map/ppermute | solution.py:516
  54.2 23.2 %collective-permute-start.1 = (f32[41,16,256]{2,1,0:T(8,128)}, f32[41,16,256]{2,1,0:T(8,128)S(1)}, u32[]{:S(2)}, u32[]{:S(2)}) collective-permute-start(f32[41,16,256]{2,1,0:T(8,128)} %get-tuple-element.64), channel_id=1, source_target_pairs={{8,0},{16,8},{24,16},{32,24},{40,32},{48,40},{56,48},{64,56},{72,6... | collective-permute-start | bytes 2015240 | tf_op jit(solution)/shard_map/ppermute | solution.py:516
  56.2 46.3 %collective-permute-start.2 = (f32[1288,256]{1,0:T(8,128)}, f32[1288,256]{1,0:T(8,128)S(1)}, u32[]{:S(2)}, u32[]{:S(2)}) collective-permute-start(f32[1288,256]{1,0:T(8,128)} %get-tuple-element.65), channel_id=1, source_target_pairs={{0,1},{1,2},{2,3},{3,4},{4,5},{5,6},{6,7},{8,9},{9,10},{10,11},{11... | collective-permute-start | bytes 3956744 | tf_op jit(solution)/shard_map/ppermute | solution.py:516
  59.8 43.8 %collective-permute-start.4 = (f32[1288,256]{1,0:T(8,128)}, f32[1288,256]{1,0:T(8,128)}, u32[]{:S(2)}, u32[]{:S(2)}) collective-permute-start(f32[1288,256]{1,0:T(8,128)} %get-tuple-element.67), channel_id=1, source_target_pairs={{1,0},{2,1},{3,2},{4,3},{5,4},{6,5},{7,6},{9,8},{10,9},{11,10},{12... | collective-permute-start | bytes 3956744 | tf_op jit(solution)/shard_map/ppermute | solution.py:516
  61.1 68.1 %all-to-all-start = ((f32[128,2,128]{2,1,0:T(2,128)}), f32[128,2,128]{2,1,0:T(2,128)}, u32[]{:S(2)}, u32[]{:S(2)}) async-start(f32[128,2,128]{2,1,0:T(2,128)} %bitcast.8), calls=%async_computation | async-start | bytes 262144 | tf_op jit(solution)/shard_map/all_to_all | solution.py:520
  77.4 27.3 %copy-start.4 = (f32[41,16,256]{2,1,0:T(8,128)}, f32[41,16,256]{2,1,0:T(8,128)S(1)}, u32[]{:S(2)}) copy-start(f32[41,16,256]{2,1,0:T(8,128)S(1)} %collective-permute-done.lower) | copy-start | bytes 2015236
  77.4 27.3 %copy-start.5 = (f32[41,16,256]{2,1,0:T(8,128)}, f32[41,16,256]{2,1,0:T(8,128)S(1)}, u32[]{:S(2)}) copy-start(f32[41,16,256]{2,1,0:T(8,128)S(1)} %collective-permute-done.1.upper) | copy-start | bytes 2015236
  77.5 20.0 %collective-permute-start.3 = (f32[408,256]{1,0:T(8,128)S(1)}, f32[408,256]{1,0:T(8,128)S(1)}, u32[]{:S(2)}, u32[]{:S(2)}) collective-permute-start(f32[408,256]{1,0:T(8,128)S(1)} %get-tuple-element.66), channel_id=1, source_target_pairs={{0,1},{1,2},{2,3},{3,4},{4,5},{5,6},{6,7},{8,9},{9,10},{10,11},{11... | collective-permute-start | bytes 1253384 | tf_op jit(solution)/shard_map/ppermute | solution.py:516
  81.0 20.8 %collective-permute-start.5 = (f32[408,256]{1,0:T(8,128)S(1)}, f32[408,256]{1,0:T(8,128)S(1)}, u32[]{:S(2)}, u32[]{:S(2)}) collective-permute-start(f32[408,256]{1,0:T(8,128)S(1)} %get-tuple-element.68), channel_id=1, source_target_pairs={{1,0},{2,1},{3,2},{4,3},{5,4},{6,5},{7,6},{9,8},{10,9},{11,10},{12... | collective-permute-start | bytes 1253384 | tf_op jit(solution)/shard_map/ppermute | solution.py:516
  97.5 0.7 copy-start.10
  101.8 0.8 copy-start.12
  102.5 1.1 copy-start.8
  104.7 1.3 copy-start.9
  106.0 1.0 copy-start.11
  107.1 1.0 copy-start.13
  118.6 0.7 copy-start.15
  119.3 9.9 %copy-start.16 = (f32[288,1]{1,0:T(8,128)S(1)}, f32[288,1]{1,0:T(8,128)}, u32[]{:S(2)}) copy-start(f32[288,1]{1,0:T(8,128)} %copy-done.15) | copy-start | bytes 3460
  119.3 9.9 %copy-start.20 = (f32[128]{0:T(128)S(1)}, f32[128]{0:T(128)}, u32[]{:S(2)}) copy-start(f32[128]{0:T(128)} %param.25) | copy-start | bytes 1540
  124.6 1.9 copy-start
  126.6 1.6 copy-start.2
  128.1 1.1 copy-start.6
  129.2 1.3 copy-start.7
  163.4 2.2 copy-start.1
  165.6 1.8 copy-start.3

commit v3 on v2

v3 whole, which is shorter than its diff:
```python
import functools

import jax
import jax.numpy as jnp
from jax import lax
from jax.experimental import pallas as pl
from jax.experimental.pallas import tpu as pltpu
from jax.sharding import PartitionSpec as P

STEPS = 5
NEWTON = 2
BS = 64
NB_DEV = 2
OFF = 4
PORT_DEV = 32
ND = 128
NODE_DEV = NB_DEV * BS
DEPTH = 5
CZ, CY, NX = 32, 16, 256
LAYERS = CZ + 2 * DEPTH
PAD = 8
TALL = CY + 2 * PAD
PARTS = 8
STRIP = PARTS * DEPTH
SIDES = ((0, 0), (-1, 0), (1, 0), (0, -1), (-1, -1), (1, -1), (0, 1), (-1, 1), (1, 1))
REACH = len(SIDES) * PORT_DEV
NODES_AT, COUNT_AT, OFF_AT = REACH, 2 * REACH, 2 * REACH + 1
SWAP_AT = OFF_AT + NB_DEV * OFF

time_step = 0.55
charge_scale = 4.0
diode_weight = 0.5

f32 = jnp.float32
VM = pl.BlockSpec(memory_space=pltpu.VMEM)
SM = pl.BlockSpec(memory_space=pltpu.SMEM)
HBM = pl.BlockSpec(memory_space=pltpu.HBM)
DMA = pltpu.SemaphoreType.DMA
CUBE = (LAYERS, TALL, NX)


def onchip(shape):
    return pltpu.VMEM(shape, f32)


def keep(value):
    return pltpu.with_memory_space_constraint(value, pltpu.VMEM)


def away(value):
    return pltpu.with_memory_space_constraint(value, pltpu.HBM)


def params():
    return pltpu.CompilerParams(vmem_limit_bytes=12 << 20)


def lanes_of(count, width):
    return lax.broadcasted_iota(jnp.int32, (count, width), 1)


def pick(rows, lane):
    hit = lanes_of(rows.shape[0], rows.shape[1]) == lane
    return jnp.sum(jnp.where(hit, rows, 0.0), axis=1, keepdims=True)


def spread(column, lane, width):
    hit = lanes_of(column.shape[0], width) == lane
    return jnp.where(hit, column, 0.0)


def columns_at(columns, part):
    block = columns[part, :]
    return block[:, 0:1], block[:, 1:2].astype(jnp.int32), block[:, 2:3].astype(jnp.int32)


def row_kind(shape, stride):
    return lax.broadcasted_iota(jnp.int32, shape, 0) % stride


def add_rows(out, stride, devices, rows_ref):
    for port, device in enumerate(devices):
        spot = pl.ds(device * stride + 1, 1)
        out[spot, :] = out[spot, :] + rows_ref[port : port + 1, :]


def copier(sems):
    copies = []

    def copy(source, target):
        job = pltpu.make_async_copy(source, target, sems.at[len(copies)])
        job.start()
        copies.append(job)

    return copies, copy


def begin_kernel(
    n_gy, cells, nodes, gains, e_in, h_in, coef_in, loss_in, cell_row, volts,
    up, down, front, back, out, fields, picked, hits, rows_ref, sems,
):
    copies, copy = copier(sems)
    sources = [e_in.at[k] for k in range(3)] + [h_in.at[k] for k in range(3)] + [coef_in, loss_in]
    for part in (2, 0, 1, 3, 4, 5, 6, 7):
        copy(sources[part], fields.at[part])
    for part, source in enumerate(sources):
        to = pl.ds(part * DEPTH, DEPTH)
        copy(source.at[pl.ds(CZ - DEPTH, DEPTH)], up.at[to])
        copy(source.at[pl.ds(0, DEPTH)], down.at[to])

    first = (lax.axis_index("gz") * n_gy + lax.axis_index("gy")) * PORT_DEV
    wide, narrow = lanes_of(1, NX), lanes_of(1, NODE_DEV)
    own_nodes = [nodes[first + port] for port in range(PORT_DEV)]
    for port, node in enumerate(own_nodes):
        hits[port : port + 1, :] = jnp.where(narrow == node % NODE_DEV, 1.0, 0.0)
    kind = row_kind(out.shape, 4)
    rows_ref[0:1, :] = jnp.zeros((1, NODE_DEV), f32)
    rows_ref[0:1, 0:PORT_DEV] = cell_row[...].astype(f32)
    out[...] = jnp.where(kind == 0, volts[...], jnp.where(kind == 2, rows_ref[0:1, :], 0.0))

    copies[0].wait()
    for port in range(PORT_DEV):
        cell = cells[port]
        line = cell // NX
        value = fields[2, line // CY, pl.ds(line % CY, 1), :] * gains[first + port]
        picked[port : port + 1, :] = jnp.where(wide == cell % NX, value, 0.0)
    rows_ref[...] = hits[...] * jnp.sum(picked[...], axis=1, keepdims=True)
    add_rows(out, 4, [node // NODE_DEV for node in own_nodes], rows_ref)
    for job in copies[1:8]:
        job.wait()

    @pl.loop(0, CZ)
    def _(layer):
        for part in range(PARTS):
            to = slice(part * DEPTH, (part + 1) * DEPTH)
            front[layer, to, :] = fields[part, layer, CY - DEPTH : CY, :]
            back[layer, to, :] = fields[part, layer, 0:DEPTH, :]

    for job in copies[8:]:
        job.wait()


def begin(n_gy, cells, nodes, gains, e_in, h_in, coef, loss, volts):
    thick = jax.ShapeDtypeStruct((PARTS * DEPTH, CY, NX), f32)
    strips = jax.ShapeDtypeStruct((CZ, STRIP, NX), f32)
    return pl.pallas_call(
        functools.partial(begin_kernel, n_gy),
        name="begin",
        out_shape=(thick, thick, strips, strips, jax.ShapeDtypeStruct((4 * ND, NODE_DEV), f32)),
        in_specs=[SM, SM, SM, HBM, HBM, HBM, HBM, VM, VM],
        out_specs=(HBM, HBM, VM, VM, VM),
        scratch_shapes=[
            pltpu.VMEM((PARTS, CZ, CY, NX), f32),
            pltpu.VMEM((PORT_DEV, NX), f32),
            pltpu.VMEM((PORT_DEV, NODE_DEV), f32),
            pltpu.VMEM((PORT_DEV, NODE_DEV), f32),
            DMA((24,)),
        ],
        compiler_params=params(),
    )(cells, nodes, gains, *map(away, (e_in, h_in, coef, loss)), cells.reshape(1, -1), volts)


def matrices_kernel(diag, inv, off, m_off, m_diag, m_inv):
    m_diag[...] = jnp.zeros_like(m_diag)
    m_inv[...] = jnp.zeros_like(m_inv)
    for j in range(NB_DEV):
        part = slice(j * BS, (j + 1) * BS)
        m_diag[part, part] = diag[j]
        m_inv[part, part] = inv[j].T
        for k in range(OFF):
            m_off[part, k * BS : (k + 1) * BS] = off[j, k]


def matrices(diag, inv, off):
    square = onchip((NODE_DEV, NODE_DEV))
    return pl.pallas_call(
        matrices_kernel,
        name="matrices",
        out_shape=(onchip((NODE_DEV, OFF * BS)), square, square),
        in_specs=[VM, VM, VM],
        out_specs=(VM, VM, VM),
        compiler_params=params(),
    )(diag, inv, off)


def corners_kernel(lower, upper, front, back):
    for side, source in enumerate((lower, upper)):
        for layer in range(DEPTH):
            for part in range(PARTS):
                to = slice(part * DEPTH, (part + 1) * DEPTH)
                given = part * DEPTH + layer
                front[side * DEPTH + layer, to, :] = source[given, CY - DEPTH : CY, :]
                back[side * DEPTH + layer, to, :] = source[given, 0:DEPTH, :]


def corners(lower, upper):
    shape = jax.ShapeDtypeStruct((2 * DEPTH, STRIP, NX), f32)
    return pl.pallas_call(
        corners_kernel,
        name="corners",
        out_shape=(shape, shape),
        in_specs=[VM, VM],
        out_specs=(VM, VM),
        compiler_params=params(),
    )(lower, upper)


def plan_kernel(spots, active, node_at, columns, found, columns_out):
    @pl.loop(0, REACH)
    def _(port):
        found[port] = PAD
        found[NODES_AT + port] = 0

    columns_out[...] = jnp.zeros_like(columns_out)

    def place_port(port, count):
        @pl.when(active[port] > 0)
        def _():
            found[count] = spots[port]
            found[NODES_AT + count] = node_at[port]
            columns_out[pl.ds(count, 1), :] = columns[pl.ds(port, 1), :]

        return count + active[port]

    count = lax.fori_loop(0, REACH, place_port, 0)
    found[COUNT_AT] = (count + PORT_DEV - 1) // PORT_DEV
    for item in range(2 * NB_DEV * OFF):
        found[OFF_AT + item] = node_at[REACH + item]


def plan(spots, active, node_at, columns):
    return pl.pallas_call(
        plan_kernel,
        name="plan",
        out_shape=(
            jax.ShapeDtypeStruct((SWAP_AT + NB_DEV * OFF,), jnp.int32),
            jax.ShapeDtypeStruct(columns.shape, f32),
        ),
        in_specs=[SM, SM, SM, VM],
        out_specs=(SM, VM),
        compiler_params=params(),
    )(spots, active, node_at, columns)


def halo_kernel(
    found, columns, lower, upper, before, after, before_ends, after_ends,
    e_in, h_in, coef_in, loss_in, e_xy, e_z, h, media, sample, coef, picked, sems,
):
    copies, copy = copier(sems)
    targets = [
        e_xy.at[0], e_xy.at[1], e_z, h.at[0], h.at[1], h.at[2], media.at[0], media.at[1],
    ]
    sources = [e_in.at[k] for k in range(3)] + [h_in.at[k] for k in range(3)] + [coef_in, loss_in]
    middle = pl.ds(PAD, CY)
    for part, (source, target) in enumerate(zip(sources, targets)):
        given = pl.ds(part * DEPTH, DEPTH)
        copy(source, target.at[pl.ds(DEPTH, CZ), middle])
        copy(lower.at[given], target.at[pl.ds(0, DEPTH), middle])
        copy(upper.at[given], target.at[pl.ds(DEPTH + CZ, DEPTH), middle])

    def unpack(ahead, behind, at, layer):
        for part, target in enumerate(targets):
            rows = slice(part * DEPTH, (part + 1) * DEPTH)
            target[layer, PAD - DEPTH : PAD, :] = ahead[at, rows, :]
            target[layer, PAD + CY : PAD + CY + DEPTH, :] = behind[at, rows, :]

    @pl.loop(0, CZ)
    def _(layer):
        unpack(before, after, layer, layer + DEPTH)

    @pl.loop(0, 2 * DEPTH)
    def _(end):
        unpack(before_ends, after_ends, end, jnp.where(end < DEPTH, end, end + CZ))

    for job in copies:
        job.wait()

    @pl.loop(0, LAYERS)
    def _(layer):
        media[1, layer] = 1.0 - media[1, layer]

    @pl.loop(0, found[COUNT_AT])
    def _(group):
        part = pl.ds(pl.multiple_of(group * PORT_DEV, PORT_DEV), PORT_DEV)
        _, place, _ = columns_at(columns, part)
        sample[part, :] = gather_cells(e_z, found, group, place, picked)
        coef[part, :] = gather_cells(media.at[0], found, group, place, picked)


def gather_cells(source, found, group, place, picked):
    for port in range(PORT_DEV):
        spot = found[group * PORT_DEV + port]
        picked[port : port + 1, :] = source[spot // TALL, pl.ds(spot % TALL, 1), :]
    return pick(picked[...], place)


def halo(found, columns, lower, upper, sides, e_in, h_in, coef, loss):
    return pl.pallas_call(
        halo_kernel,
        name="halo",
        out_shape=(
            onchip((2,) + CUBE),
            onchip(CUBE),
            onchip((3,) + CUBE),
            onchip((2,) + CUBE),
            onchip((REACH, 1)),
            onchip((REACH, 1)),
        ),
        in_specs=[SM, VM, HBM, HBM, VM, VM, VM, VM] + [HBM] * 4,
        out_specs=(VM,) * 6,
        scratch_shapes=[pltpu.VMEM((PORT_DEV, NX), f32), DMA((24,))],
        compiler_params=params(),
    )(found, columns, away(lower), away(upper), *sides, *map(away, (e_in, h_in, coef, loss)))


def field_kernel(step, bounds, media, e_xy, e_z, h, to_xy, to_z, to_h):
    low_z, low_y = bounds[0], bounds[1]
    lane = lanes_of(TALL, NX)
    last_lane, first_lane = lane == NX - 1, lane == 0
    row = lax.broadcasted_iota(jnp.int32, (TALL, NX), 0)
    rate_rows = jnp.where(row < PAD, low_y, time_step)

    def next_x(value):
        return jnp.where(last_lane, 0.0, pltpu.roll(value, NX - 1, 1))

    def prior_x(value):
        return jnp.where(first_lane, 0.0, pltpu.roll(value, 1, 1))

    def next_y(value):
        return pltpu.roll(value, TALL - 1, 0)

    def prior_y(value):
        return pltpu.roll(value, 1, 0)

    def magnetic(layer):
        e_x, e_y, e_zz = e_xy[0, layer], e_xy[1, layer], e_z[layer]
        rate = rate_rows * jnp.where(layer < DEPTH, low_z, 1.0)
        curl_x = (next_y(e_zz) - e_zz) - (e_xy[1, layer + 1] - e_y)
        curl_y = (e_xy[0, layer + 1] - e_x) - (next_x(e_zz) - e_zz)
        curl_z = (next_x(e_y) - e_y) - (next_y(e_x) - e_x)
        return (h[0, layer] - rate * curl_x, h[1, layer] - rate * curl_y, h[2, layer] - rate * curl_z)

    def electric(layer):
        h_x, h_y, h_z = to_h[0, layer], to_h[1, layer], to_h[2, layer]
        coef, kept = media[0, layer], media[1, layer]
        back_x = (h_z - prior_y(h_z)) - (h_y - to_h[1, layer - 1])
        back_y = (h_x - to_h[0, layer - 1]) - (h_z - prior_x(h_z))
        back_z = (h_y - prior_x(h_y)) - (h_x - prior_y(h_x))
        return (
            kept * e_xy[0, layer] + coef * back_x,
            kept * e_xy[1, layer] + coef * back_y,
            kept * e_z[layer] + coef * back_z,
        )

    def put_h(layer, values):
        to_h[0, layer], to_h[1, layer], to_h[2, layer] = values

    def put_e(layer, values):
        to_xy[0, layer], to_xy[1, layer], to_z[layer] = values

    put_h(step - 1, magnetic(step - 1))
    put_h(step, magnetic(step))
    last = LAYERS - step - 1

    @pl.loop(step, last)
    def _(layer):
        electric_values = electric(layer)
        magnetic_values = magnetic(layer + 1)
        put_e(layer, electric_values)
        put_h(layer + 1, magnetic_values)

    put_e(last, electric(last))


def field(step, bounds, media, e_xy, e_z, h):
    return pl.pallas_call(
        functools.partial(field_kernel, step),
        name="field",
        out_shape=(onchip((2,) + CUBE), onchip(CUBE), onchip((3,) + CUBE)),
        in_specs=[SM] + [VM] * 4,
        out_specs=(VM,) * 3,
        compiler_params=params(),
    )(bounds, keep(media), keep(e_xy), keep(e_z), keep(h))


def solve(stride, arrived, table, volts, m_off, m_diag, m_inv):
    lane = lanes_of(1, NODE_DEV)
    halves = []
    for j in range(NB_DEV):
        pieces = []
        for half in range(OFF // 2):
            total = None
            for side in range(2):
                spot = j * OFF + half * 2 + side
                row = arrived[pl.ds(table[OFF_AT + spot] * stride, 1), :]
                row = jnp.where(table[SWAP_AT + spot] == side, row, pltpu.roll(row, BS, 1))
                row = jnp.where((lane < BS) == (side == 0), row, 0.0)
                total = row if total is None else total + row
            pieces.append(jnp.broadcast_to(total, (BS, NODE_DEV)))
        halves.append(pieces)
    first = jnp.concatenate([halves[0][0], halves[1][0]], axis=0)
    second = jnp.concatenate([halves[0][1], halves[1][1]], axis=0)
    product = m_off[:, 0:NODE_DEV] * first + m_off[:, NODE_DEV : 2 * NODE_DEV] * second
    offsum = jnp.sum(product, axis=1, keepdims=True)
    kind = row_kind(arrived.shape, stride)
    inject = jnp.sum(jnp.where(kind == 1, arrived[...], 0.0), axis=0, keepdims=True)
    start = volts[...]
    target = charge_scale * start + inject
    diagonal = lax.broadcasted_iota(jnp.int32, (NODE_DEV, NODE_DEV), 0) == lanes_of(NODE_DEV, NODE_DEV)
    iterate = start
    for newton_round in range(NEWTON):
        local = diode_weight * jnp.tanh(iterate) - target
        terms = m_diag[...] * iterate + jnp.where(diagonal, local, 0.0)
        resid = jnp.sum(terms, axis=1, keepdims=True) + offsum
        iterate = iterate - jnp.sum(m_inv[...] * resid, axis=0, keepdims=True)
    return iterate


def apply_ports(stride, table, arrived, columns, sample, coef, e_z, near_rows, deltas):
    @pl.loop(0, table[COUNT_AT])
    def _(group):
        first = group * PORT_DEV
        part = pl.ds(pl.multiple_of(first, PORT_DEV), PORT_DEV)
        for port in range(PORT_DEV):
            near_at = table[NODES_AT + first + port] * stride
            near_rows[port : port + 1, :] = arrived[pl.ds(near_at, 1), :]
        gain, place, lane = columns_at(columns, part)
        current = gain * (sample[part, :] - pick(near_rows[...], lane))
        deltas[...] = spread(-coef[part, :] * current, place, NX)
        for port in range(PORT_DEV):
            spot = table[first + port]
            layer, row = spot // TALL, pl.ds(spot % TALL, 1)
            e_z[layer, row, :] = e_z[layer, row, :] + deltas[port : port + 1, :]


def circuit_kernel(
    stride, table, arrived, columns, sample, coef, volts, m_off, m_diag, m_inv, e_in,
    e_z, out, volts_out, sample_out, near_rows, deltas, picked, spread_rows,
):
    e_z[...] = e_in[...]
    apply_ports(stride, table, arrived, columns, sample, coef, e_z, near_rows, deltas)

    @pl.loop(0, table[COUNT_AT])
    def _(group):
        part = pl.ds(pl.multiple_of(group * PORT_DEV, PORT_DEV), PORT_DEV)
        _, place, _ = columns_at(columns, part)
        sample_out[part, :] = gather_cells(e_z, table, group, place, picked)

    solved = solve(stride, arrived, table, volts, m_off, m_diag, m_inv)
    volts_out[...] = solved
    own = slice(0, PORT_DEV)
    gain, _, lane = columns_at(columns, own)
    spread_rows[...] = spread(gain * sample_out[own, :], lane, NODE_DEV)
    out[...] = jnp.where(row_kind(out.shape, 2) == 0, solved, 0.0)
    add_rows(out, 2, [table[NODES_AT + port] for port in range(PORT_DEV)], spread_rows)


def circuit(table, arrived, columns, sample, coef, volts, mats, e_z):
    return pl.pallas_call(
        functools.partial(circuit_kernel, arrived.shape[0] // ND),
        name="circuit",
        out_shape=(
            onchip(CUBE),
            onchip((2 * ND, NODE_DEV)),
            onchip((1, NODE_DEV)),
            onchip((REACH, 1)),
        ),
        in_specs=[SM] + [VM] * 9,
        out_specs=(VM,) * 4,
        scratch_shapes=[
            pltpu.VMEM((PORT_DEV, NODE_DEV), f32),
            pltpu.VMEM((PORT_DEV, NX), f32),
            pltpu.VMEM((PORT_DEV, NX), f32),
            pltpu.VMEM((PORT_DEV, NODE_DEV), f32),
        ],
        compiler_params=params(),
    )(
        table, arrived, columns, keep(sample), keep(coef), volts,
        *[keep(mat) for mat in mats], keep(e_z),
    )


def finish_kernel(
    stride, table, arrived, columns, sample, coef, volts, m_off, m_diag, m_inv, e_xy, e_in, h,
    e_out, h_out, volts_out, e_z, near_rows, deltas, sems,
):
    copies, copy = copier(sems)
    layers, rows = pl.ds(DEPTH, CZ), pl.ds(PAD, CY)
    for k in range(3):
        copy(h.at[k, layers, rows], h_out.at[k])
    for k in range(2):
        copy(e_xy.at[k, layers, rows], e_out.at[k])
    e_z[...] = e_in[...]
    apply_ports(stride, table, arrived, columns, sample, coef, e_z, near_rows, deltas)
    copy(e_z.at[layers, rows], e_out.at[2])
    volts_out[...] = solve(stride, arrived, table, volts, m_off, m_diag, m_inv)
    for job in copies:
        job.wait()


def finish(table, arrived, columns, sample, coef, volts, mats, e_xy, e_z, h):
    return pl.pallas_call(
        functools.partial(finish_kernel, arrived.shape[0] // ND),
        name="finish",
        out_shape=(
            jax.ShapeDtypeStruct((3, CZ, CY, NX), f32),
            jax.ShapeDtypeStruct((3, CZ, CY, NX), f32),
            jax.ShapeDtypeStruct((1, NODE_DEV), f32),
        ),
        in_specs=[SM] + [VM] * 11,
        out_specs=(HBM, HBM, VM),
        scratch_shapes=[
            pltpu.VMEM(CUBE, f32),
            pltpu.VMEM((PORT_DEV, NODE_DEV), f32),
            pltpu.VMEM((PORT_DEV, NX), f32),
            DMA((6,)),
        ],
        compiler_params=params(),
    )(
        table, arrived, columns, keep(sample), keep(coef), volts,
        *[keep(mat) for mat in mats], keep(e_xy), keep(e_z), keep(h),
    )


def shifted(value, axis, steps):
    count = lax.axis_size(axis)
    first, last = (max(0, -steps), min(count, count - steps))
    return lax.ppermute(value, axis, [(source, source + steps) for source in range(first, last)])


def exchange(value):
    return lax.all_to_all(value, ("gz", "gy"), 0, 0, tiled=True)


def body(
    e_field,
    h_field,
    e_coef,
    e_loss,
    port_cell,
    port_node,
    port_gain,
    diag_blocks,
    inv_blocks,
    off_blocks,
    off_cols,
    volts_init,
):
    gz, gy = lax.axis_index("gz"), lax.axis_index("gy")
    n_gz, n_gy = lax.axis_size("gz"), lax.axis_size("gy")
    grids = (e_field, h_field, e_coef, e_loss)
    volts = volts_init.reshape(1, NODE_DEV)
    up, down, front, back, out = begin(n_gy, port_cell, port_node, port_gain, *grids, volts)
    before = shifted(front, "gy", 1)
    after = shifted(back, "gy", -1)
    lower = shifted(up, "gz", 1)
    upper = shifted(down, "gz", -1)
    arrived = exchange(out)
    front_ends, back_ends = corners(lower, upper)
    before_ends = shifted(front_ends, "gy", 1)
    after_ends = shifted(back_ends, "gy", -1)
    sides = (before, after, before_ends, after_ends)
    mats = matrices(diag_blocks, inv_blocks, off_blocks)

    shift_z = jnp.array([side[0] for side in SIDES], jnp.int32)[:, None]
    shift_y = jnp.array([side[1] for side in SIDES], jnp.int32)[:, None]
    at_z, at_y = gz + shift_z, gy + shift_y
    exists = (at_z >= 0) & (at_z < n_gz) & (at_y >= 0) & (at_y < n_gy)
    ids = jnp.where(exists, at_z * n_gy + at_y, 0)[:, 0]
    cells = arrived[4 * ids + 2][:, 0:PORT_DEV].astype(jnp.int32)
    nodes = port_node.reshape(-1, PORT_DEV)[ids].reshape(-1)
    gains = port_gain.reshape(-1, PORT_DEV)[ids].reshape(-1)
    layer = cells // (CY * NX) + shift_z * CZ + DEPTH
    row = (cells // NX) % CY + shift_y * CY + PAD
    inside = (layer >= 1) & (layer < LAYERS - 1) & (row >= PAD - DEPTH + 1) & (row < PAD + CY + DEPTH - 1)
    valid = exists & inside
    spots = jnp.where(valid, layer * TALL + row, PAD).reshape(-1)
    columns = jnp.stack(
        [gains, (cells % NX).astype(f32).reshape(-1), (nodes % NODE_DEV).astype(f32)], axis=1
    )
    flat_cols = off_cols.reshape(-1)
    node_at = jnp.concatenate([nodes // NODE_DEV, flat_cols // NB_DEV, flat_cols % NB_DEV])
    table, columns = plan(spots, valid.astype(jnp.int32).reshape(-1), node_at, columns)
    bounds = jnp.stack([jnp.where(gz > 0, 1.0, 0.0), jnp.where(gy > 0, time_step, 0.0)]).astype(f32)

    e_xy, e_z, h, media, sample, coef = halo(table, columns, lower, upper, sides, *grids)
    for step in range(1, STEPS + 1):
        if step > 1:
            arrived = exchange(out)
            arrived, e_z = lax.optimization_barrier((arrived, e_z))
        e_xy, e_z, h = field(step, bounds, media, e_xy, e_z, h)
        shared = (table, arrived, columns, sample, coef, volts, mats)
        if step < STEPS:
            e_z, out, volts, sample = circuit(*shared, e_z)
        else:
            e_end, h_end, volts = finish(*shared, e_xy, e_z, h)
    return e_end, h_end, volts.reshape(-1)


def solution(mesh):
    placed = (
        P(None, "gz", "gy", None),
        P(None, "gz", "gy", None),
        P("gz", "gy", None),
        P("gz", "gy", None),
        P(("gz", "gy")),
        P(),
        P(),
        P(("gz", "gy"), None, None),
        P(("gz", "gy"), None, None),
        P(("gz", "gy"), None, None, None),
        P(("gz", "gy"), None),
        P(("gz", "gy")),
    )
    return jax.shard_map(
        body,
        mesh=mesh,
        in_specs=placed,
        out_specs=(P(None, "gz", "gy", None), P(None, "gz", "gy", None), P(("gz", "gy"))),
        check_vma=False,
    )
```

time: 243 us -> 225 us (0.926)
  local copies, waits for them, and re-layouts: 23 us -> 7.52 us
  starting transfers between devices: 30.1 us -> 26.9 us
  Pallas kernels: 92.7 us -> 95.4 us
  blocking collectives: 74.7 us -> 72.1 us
    unnamed x58 -> x34, local copies, waits for them, and re-layouts: 19.7 us -> 4.89 us
    pallas_call x6 -> x8, Pallas kernels: 57.9 us -> 64.7 us  [the longest x1 42.8 us: begin(): pl.pallas_call(functools.partial(begin_kernel, n_gy), name='begin', out_s...]
    pallas_call x1, Pallas kernels: 10.6 us -> 5.68 us  [halo(): pl.pallas_call(halo_kernel, name='halo', out_shape=(onchip((2,) + CUBE),...]
    all_to_all x4, blocking collectives: 74.7 us -> 72.1 us  [exchange(): return lax.all_to_all(value, ('gz', 'gy'), 0, 0, tiled=True)]
    all_to_all x1, starting transfers between devices: 13.9 us -> 11.5 us  [exchange(): return lax.all_to_all(value, ('gz', 'gy'), 0, 0, tiled=True)]
  transfers between devices with their start and end apart: 7 -> 7, of which waited for: 2 -> 3; matrix products, arithmetic and copies ran while one was open for 1% -> 2% of each run, Pallas kernels for 7% -> 4%
where the time goes in v3:
time: 225 us
  Pallas kernels  95.4 us (42%)
  blocking collectives  72.1 us (32%)
  starting transfers between devices  26.9 us (12%)
  waiting for transfers between devices  19.7 us (9%)
  local copies, waits for them, and re-layouts  7.52 us (3%)
  other arithmetic  2.86 us (1%)
    all_to_all x4, blocking collectives, exchange(): return lax.all_to_all(value, ('gz', 'gy'), 0, 0, tiled=True)  72.1 us
    pallas_call x1, Pallas kernels, begin(): pl.pallas_call(functools.partial(begin_kernel, n_gy), name='begin', out_s...  42.8 us
    pallas_call x5, Pallas kernels, field(): pl.pallas_call(functools.partial(field_kernel, step), name='field', out_s...  23.8 us
    ppermute x6, waiting for transfers between devices, shifted(): lax.ppermute(value, axis, [(source, source + steps) for source in range(f...  19.7 us
    ppermute x6, starting transfers between devices, shifted(): lax.ppermute(value, axis, [(source, source + steps) for source in range(f...  15.4 us
    all_to_all x1, starting transfers between devices, exchange(): return lax.all_to_all(value, ('gz', 'gy'), 0, 0, tiled=True)  11.5 us
    pallas_call x4, Pallas kernels, circuit(): pl.pallas_call(functools.partial(circuit_kernel, arrived.shape[0] // ND),...  11.3 us
    pallas_call x1, Pallas kernels, plan(): pl.pallas_call(plan_kernel, name='plan', out_shape=(jax.ShapeDtypeStruct(...  7.31 us
  transfers between devices with their start and end apart: 7, of which 3 were waited for; matrix products, arithmetic and copies ran while one was open for 2% of the time, Pallas kernels for 4%

profile of v3, /device:TPU:1, one launch (start us, length us, event | category | flops | bytes accessed | tf_op | source)
XLA Modules:
  0.0 225.4 jit_solution(11469938014358977653)
XLA Ops:
  0.6 0.0 copy-start.3
  0.6 0.7 copy-done.3
  1.4 0.7 copy-done.5
  2.1 0.7 copy-done.9
  2.7 0.7 copy-done.10
  3.4 0.0 copy-start.6
  3.4 42.8 %begin.1 = (f32[40,16,256]{2,1,0:T(8,128)}, f32[40,16,256]{2,1,0:T(8,128)}, f32[32,40,256]{2,1,0:T(8,128)S(1)}, f32[32,40,256]{2,1,0:T(8,128)S(1)}, f32[512,128]{1,0:T(8,128)}) custom-call(s32[32]{0:T(128)S(1)} %copy-done.9, s32[4096]{0:T(1024)S(1)} %copy-done.3, f32[4096]{0:T(1024)S(1)} %copy-done.5, f32[3,32,16,256]{3,2,1,0:T(8,128)} %e_in.3, ...), custom_call_target="tpu_custom_call" | custom-call | tf_op jit(solution)/shard_map/begin/pallas_call | solution.py:146
  46.3 0.0 copy-start.12
  46.3 1.0 copy-done.12
  47.3 1.1 copy-done.13
  48.4 11.5 %all-to-all-start = ((f32[128,4,128]{2,1,0:T(4,128)}), f32[128,4,128]{2,1,0:T(4,128)S(1)}, u32[]{:S(2)}, u32[]{:S(2)}) async-start(f32[128,4,128]{2,1,0:T(4,128)} %bitcast.2), calls=%async_computation | async-start | bytes 524288 | tf_op jit(solution)/shard_map/all_to_all | solution.py:532
  59.9 3.5 %collective-permute-start = (f32[40,16,256]{2,1,0:T(8,128)}, f32[40,16,256]{2,1,0:T(8,128)S(1)}, u32[]{:S(2)}, u32[]{:S(2)}) collective-permute-start(f32[40,16,256]{2,1,0:T(8,128)} %get-tuple-element.66), channel_id=1, source_target_pairs={{0,8},{8,16},{16,24},{24,32},{32,40},{40,48},{48,56},{56,64},{64,7... | collective-permute-start | bytes 1966088 | tf_op jit(solution)/shard_map/ppermute | solution.py:528
  63.4 1.9 collective-permute-start.1
  65.4 3.4 %collective-permute-start.2 = (f32[32,40,256]{2,1,0:T(8,128)}, f32[32,40,256]{2,1,0:T(8,128)S(1)}, u32[]{:S(2)}, u32[]{:S(2)}) collective-permute-start(f32[32,40,256]{2,1,0:T(8,128)} %copy-done.13), channel_id=1, source_target_pairs={{0,1},{1,2},{2,3},{3,4},{4,5},{5,6},{6,7},{8,9},{9,10},{10,11},{11... | collective-permute-start | bytes 3932168 | tf_op jit(solution)/shard_map/ppermute | solution.py:528
  68.7 1.3 collective-permute-start.3
  70.0 0.0 copy-done.4
  70.0 0.1 reshape.132
  70.1 0.5 compare_select_fusion.2
  70.7 0.6 gather_fusion.1
  71.2 0.1 reshape.133
  71.3 0.1 reshape.134
  71.4 0.6 pad_clamp_fusion.1
  72.0 0.1 pad_add_fusion.node_at
  72.1 0.1 pad_maximum_fusion.1.bounds
  72.2 0.1 reshape.136
  72.2 0.0 copy-done.6
  72.2 0.1 reshape.135
  72.3 0.6 gather_fusion.2
  72.9 0.1 stack_reshape.6
  73.0 0.2 matrices.1
  73.2 0.0 all-to-all-done
  73.2 0.7 gather_fusion
  73.9 4.8 %collective-permute-done.lower = f32[40,16,256]{2,1,0:T(8,128)S(1)} collective-permute-done((f32[40,16,256]{2,1,0:T(8,128)}, f32[40,16,256]{2,1,0:T(8,128)S(1)}, u32[]{:S(2)}, u32[]{:S(2)}) %collective-permute-start) | collective-permute-done | bytes 655392 | tf_op jit(solution)/shard_map/ppermute | solution.py:528
  78.6 0.0 collective-permute-done.1.upper
  78.6 1.2 corners.1
  79.8 4.0 %collective-permute-start.4 = (f32[10,40,256]{2,1,0:T(8,128)}, f32[10,40,256]{2,1,0:T(8,128)}, u32[]{:S(2)}, u32[]{:S(2)}) collective-permute-start(f32[10,40,256]{2,1,0:T(8,128)} %get-tuple-element.70), channel_id=1, source_target_pairs={{0,1},{1,2},{2,3},{3,4},{4,5},{5,6},{6,7},{8,9},{9,10},{10,11},{11... | collective-permute-start | bytes 1228808 | tf_op jit(solution)/shard_map/ppermute | solution.py:528
  83.9 1.3 collective-permute-start.5
  85.2 0.8 fusion.16
  85.9 0.8 add_select_fusion.4
  86.7 0.1 reshape.129.spots
  86.8 0.1 reshape.139.active
  86.8 0.1 stack_reshape.7
  86.9 0.1 copy.22.columns
  87.1 7.3 %plan.1 = (s32[593]{0:T(1024)S(1)}, f32[288,3]{1,0:T(8,128)S(1)}) custom-call(s32[288]{0:T(512)S(1)} %reshape.129.spots, s32[288]{0:T(512)S(1)} %reshape.139.active, s32[304]{0:T(512)S(1)} %pad_add_fusion.node_at, f32[288,3]{1,0:T(8,128)S(1)} %copy.22.columns), custom_call_target="tpu_custom_call" | custom-call | tf_op jit(solution)/shard_map/plan/pallas_call | solution.py:232
  94.4 10.8 %collective-permute-done.4.before_ends = f32[10,40,256]{2,1,0:T(8,128)} collective-permute-done((f32[10,40,256]{2,1,0:T(8,128)}, f32[10,40,256]{2,1,0:T(8,128)}, u32[]{:S(2)}, u32[]{:S(2)}) %collective-permute-start.4) | collective-permute-done | bytes 409632 | tf_op jit(solution)/shard_map/ppermute | solution.py:528
  105.2 4.2 %collective-permute-done.5.after_ends = f32[10,40,256]{2,1,0:T(8,128)} collective-permute-done((f32[10,40,256]{2,1,0:T(8,128)}, f32[10,40,256]{2,1,0:T(8,128)}, u32[]{:S(2)}, u32[]{:S(2)}) %collective-permute-start.5) | collective-permute-done | bytes 409632 | tf_op jit(solution)/shard_map/ppermute | solution.py:528
  109.4 0.0 collective-permute-done.2.before
  109.4 0.0 collective-permute-done.3.after
  109.4 5.7 %halo.1 = (f32[2,42,32,256]{3,2,1,0:T(8,128)S(1)}, f32[42,32,256]{2,1,0:T(8,128)S(1)}, f32[3,42,32,256]{3,2,1,0:T(8,128)S(1)}, f32[2,42,32,256]{3,2,1,0:T(8,128)...) custom-call(s32[593]{0:T(1024)S(1)} %get-tuple-element.64.found.table, f32[288,3]{1,0:T(8,128)S(1)} %get-tuple-element.65.columns, ...), custom_call_target="tpu_custom_call" | custom-call | tf_op jit(solution)/shard_map/halo/pallas_call | solution.py:298
  115.1 0.0 copy-start.11
  115.1 5.2 %field.5 = (f32[2,42,32,256]{3,2,1,0:T(8,128)S(1)}, f32[42,32,256]{2,1,0:T(8,128)S(1)}, f32[3,42,32,256]{3,2,1,0:T(8,128)S(1)}) custom-call(f32[2]{0:T(128)S(1)} %pad_maximum_fusion.1.bounds, f32[2,42,32,256]{3,2,1,0:T(8,128)S(1)} %get-tuple-element.77.media, f32[2,42,32,256]{3,2,1,0:T(8,128)S(1)} %get-tuple-element.78.e_xy, ...), custom_call_target="tpu_custom_call" | custom-call | tf_op jit(solution)/shard_map/field/pallas_call | solution.py:376
  120.3 2.8 %circuit.4 = (f32[42,32,256]{2,1,0:T(8,128)S(1)}, f32[256,128]{1,0:T(8,128)S(1)}, f32[1,128]{1,0:T(1,128)S(1)}, f32[288,1]{1,0:T(8,128)S(1)}) custom-call(s32[593]{0:T(1024)S(1)} %get-tuple-element.64.found.table, f32[512,128]{1,0:T(8,128)S(1)} %bitcast.16, f32[288,3]{1,0:T(8,128)S(1)} %get-tuple-element.65.columns, f32[288,1]{1,0:T(8,128)S(1)} %get-tuple-element.72.sample, ...), custom_call_target="tpu_custom_call" | custom-call | tf_op jit(solution)/shard_map/circuit/pallas_call | solution.py:459
  123.2 27.0 %all_to_all.59 = f32[128,2,128]{2,1,0:T(2,128)S(1)} all-to-all(f32[128,2,128]{2,1,0:T(2,128)S(1)} %bitcast.24), channel_id=1, replica_groups=mesh['gz'=16,'gy'=8] {'gz','gy'}, dimensions={0} | all-to-all | bytes 262144 | tf_op jit(solution)/shard_map/all_to_all | solution.py:532
  150.2 5.0 %field.6 = (f32[2,42,32,256]{3,2,1,0:T(8,128)S(1)}, f32[42,32,256]{2,1,0:T(8,128)S(1)}, f32[3,42,32,256]{3,2,1,0:T(8,128)S(1)}) custom-call(f32[2]{0:T(128)S(1)} %pad_maximum_fusion.1.bounds, f32[2,42,32,256]{3,2,1,0:T(8,128)S(1)} %get-tuple-element.77.media, f32[2,42,32,256]{3,2,1,0:T(8,128)S(1)} %get-tuple-element.87.e_xy, ...), custom_call_target="tpu_custom_call" | custom-call | tf_op jit(solution)/shard_map/field/pallas_call | solution.py:376
  155.2 2.8 %circuit.5 = (f32[42,32,256]{2,1,0:T(8,128)S(1)}, f32[256,128]{1,0:T(8,128)S(1)}, f32[1,128]{1,0:T(1,128)S(1)}, f32[288,1]{1,0:T(8,128)S(1)}) custom-call(s32[593]{0:T(1024)S(1)} %get-tuple-element.64.found.table, f32[256,128]{1,0:T(8,128)S(1)} %bitcast.18, f32[288,3]{1,0:T(8,128)S(1)} %get-tuple-element.65.columns, f32[288,1]{1,0:T(8,128)S(1)} %get-tuple-element.85.sample, ...), custom_call_target="tpu_custom_call" | custom-call | tf_op jit(solution)/shard_map/circuit/pallas_call | solution.py:459
  158.0 15.0 %all_to_all.60 = f32[128,2,128]{2,1,0:T(2,128)S(1)} all-to-all(f32[128,2,128]{2,1,0:T(2,128)S(1)} %bitcast.21), channel_id=1, replica_groups=mesh['gz'=16,'gy'=8] {'gz','gy'}, dimensions={0} | all-to-all | bytes 262144 | tf_op jit(solution)/shard_map/all_to_all | solution.py:532
  173.1 4.7 %field.7 = (f32[2,42,32,256]{3,2,1,0:T(8,128)S(1)}, f32[42,32,256]{2,1,0:T(8,128)S(1)}, f32[3,42,32,256]{3,2,1,0:T(8,128)S(1)}) custom-call(f32[2]{0:T(128)S(1)} %pad_maximum_fusion.1.bounds, f32[2,42,32,256]{3,2,1,0:T(8,128)S(1)} %get-tuple-element.77.media, f32[2,42,32,256]{3,2,1,0:T(8,128)S(1)} %get-tuple-element.96.e_xy, ...), custom_call_target="tpu_custom_call" | custom-call | tf_op jit(solution)/shard_map/field/pallas_call | solution.py:376
  177.8 2.8 %circuit.6 = (f32[42,32,256]{2,1,0:T(8,128)S(1)}, f32[256,128]{1,0:T(8,128)S(1)}, f32[1,128]{1,0:T(1,128)S(1)}, f32[288,1]{1,0:T(8,128)S(1)}) custom-call(s32[593]{0:T(1024)S(1)} %get-tuple-element.64.found.table, f32[256,128]{1,0:T(8,128)S(1)} %bitcast.19, f32[288,3]{1,0:T(8,128)S(1)} %get-tuple-element.65.columns, f32[288,1]{1,0:T(8,128)S(1)} %get-tuple-element.94.sample, ...), custom_call_target="tpu_custom_call" | custom-call | tf_op jit(solution)/shard_map/circuit/pallas_call | solution.py:459
  180.6 15.0 %all_to_all.61 = f32[128,2,128]{2,1,0:T(2,128)S(1)} all-to-all(f32[128,2,128]{2,1,0:T(2,128)S(1)} %bitcast.22), channel_id=1, replica_groups=mesh['gz'=16,'gy'=8] {'gz','gy'}, dimensions={0} | all-to-all | bytes 262144 | tf_op jit(solution)/shard_map/all_to_all | solution.py:532
  195.6 4.5 %field.8 = (f32[2,42,32,256]{3,2,1,0:T(8,128)S(1)}, f32[42,32,256]{2,1,0:T(8,128)S(1)}, f32[3,42,32,256]{3,2,1,0:T(8,128)S(1)}) custom-call(f32[2]{0:T(128)S(1)} %pad_maximum_fusion.1.bounds, f32[2,42,32,256]{3,2,1,0:T(8,128)S(1)} %get-tuple-element.77.media, f32[2,42,32,256]{3,2,1,0:T(8,128)S(1)} %get-tuple-element.105.e_xy, ...), custom_call_target="tpu_custom_call" | custom-call | tf_op jit(solution)/shard_map/field/pallas_call | solution.py:376
  200.2 2.8 %circuit.7 = (f32[42,32,256]{2,1,0:T(8,128)S(1)}, f32[256,128]{1,0:T(8,128)S(1)}, f32[1,128]{1,0:T(1,128)S(1)}, f32[288,1]{1,0:T(8,128)S(1)}) custom-call(s32[593]{0:T(1024)S(1)} %get-tuple-element.64.found.table, f32[256,128]{1,0:T(8,128)S(1)} %bitcast.20, f32[288,3]{1,0:T(8,128)S(1)} %get-tuple-element.65.columns, f32[288,1]{1,0:T(8,128)S(1)} %get-tuple-element.103.sample, ...), custom_call_target="tpu_custom_call" | custom-call | tf_op jit(solution)/shard_map/circuit/pallas_call | solution.py:459
  203.0 15.0 %all_to_all.62 = f32[128,2,128]{2,1,0:T(2,128)S(1)} all-to-all(f32[128,2,128]{2,1,0:T(2,128)S(1)} %bitcast.23), channel_id=1, replica_groups=mesh['gz'=16,'gy'=8] {'gz','gy'}, dimensions={0} | all-to-all | bytes 262144 | tf_op jit(solution)/shard_map/all_to_all | solution.py:532
  218.0 4.3 %field.9 = (f32[2,42,32,256]{3,2,1,0:T(8,128)S(1)}, f32[42,32,256]{2,1,0:T(8,128)S(1)}, f32[3,42,32,256]{3,2,1,0:T(8,128)S(1)}) custom-call(f32[2]{0:T(128)S(1)} %pad_maximum_fusion.1.bounds, f32[2,42,32,256]{3,2,1,0:T(8,128)S(1)} %get-tuple-element.77.media, f32[2,42,32,256]{3,2,1,0:T(8,128)S(1)} %get-tuple-element.114.e_xy, ...), custom_call_target="tpu_custom_call" | custom-call | tf_op jit(solution)/shard_map/field/pallas_call | solution.py:376
  222.3 3.2 %finish.1 = (f32[3,32,16,256]{3,2,1,0:T(8,128)}, f32[3,32,16,256]{3,2,1,0:T(8,128)}, f32[1,128]{1,0:T(1,128)}) custom-call(s32[593]{0:T(1024)S(1)} %get-tuple-element.64.found.table, f32[256,128]{1,0:T(8,128)S(1)} %bitcast.17, f32[288,3]{1,0:T(8,128)S(1)} %get-tuple-element.65.columns, f32[288,1]{1,0:T(8,128)S(1)} %get-tuple-element.112.sample, ...), custom_call_target="tpu_custom_call" | custom-call | tf_op jit(solution)/shard_map/finish/pallas_call | solution.py:502
  (29 shorter events, 0.1 us)
Async XLA Ops:
  0.6 0.7 copy-start.3
  1.4 0.7 copy-start.5
  2.1 0.7 copy-start.9
  2.7 0.7 copy-start.10
  3.4 66.6 %copy-start.4 = (s32[4096]{0:T(1024)S(1)}, s32[4096]{0:T(1024)}, u32[]{:S(2)}) copy-start(s32[4096]{0:T(1024)} %nodes.1) | copy-start | bytes 49156
  3.4 66.7 %copy-start.14 = (s32[9]{0:T(128)S(1)}, s32[9]{0:T(128)}, u32[]{:S(2)}) copy-start(s32[9]{0:T(128)} %constant.142.clone) | copy-start | bytes 112
  3.4 66.7 %copy-start.15 = (s32[9]{0:T(128)S(1)}, s32[9]{0:T(128)}, u32[]{:S(2)}) copy-start(s32[9]{0:T(128)} %constant.143.clone) | copy-start | bytes 112
  3.4 67.9 %copy-start.16 = (s32[2,4]{1,0:T(2,128)S(1)}, s32[2,4]{1,0:T(2,128)}, u32[]{:S(2)}) copy-start(s32[2,4]{1,0:T(2,128)} %param.24) | copy-start | bytes 100
  3.4 68.8 %copy-start.6 = (f32[4096]{0:T(1024)S(1)}, f32[4096]{0:T(1024)}, u32[]{:S(2)}) copy-start(f32[4096]{0:T(1024)} %gains.1) | copy-start | bytes 49156
  3.4 69.6 %copy-start.2 = (f32[2,4,64,64]{3,2,1,0:T(8,128)S(1)}, f32[2,4,64,64]{3,2,1,0:T(8,128)}, u32[]{:S(2)}) copy-start(f32[2,4,64,64]{3,2,1,0:T(8,128)} %off.1) | copy-start | bytes 393220
  3.4 69.6 %copy-start.7 = (f32[2,64,64]{2,1,0:T(8,128)S(1)}, f32[2,64,64]{2,1,0:T(8,128)}, u32[]{:S(2)}) copy-start(f32[2,64,64]{2,1,0:T(8,128)} %diag.1) | copy-start | bytes 98308
  3.4 69.5 %copy-start.8 = (f32[2,64,64]{2,1,0:T(8,128)S(1)}, f32[2,64,64]{2,1,0:T(8,128)}, u32[]{:S(2)}) copy-start(f32[2,64,64]{2,1,0:T(8,128)} %inv.1) | copy-start | bytes 98308
  46.3 1.1 copy-start.12
  47.3 1.1 copy-start.13
  48.4 24.8 %all-to-all-start = ((f32[128,4,128]{2,1,0:T(4,128)}), f32[128,4,128]{2,1,0:T(4,128)S(1)}, u32[]{:S(2)}, u32[]{:S(2)}) async-start(f32[128,4,128]{2,1,0:T(4,128)} %bitcast.2), calls=%async_computation | async-start | bytes 524288 | tf_op jit(solution)/shard_map/all_to_all | solution.py:532
  59.9 18.7 %collective-permute-start = (f32[40,16,256]{2,1,0:T(8,128)}, f32[40,16,256]{2,1,0:T(8,128)S(1)}, u32[]{:S(2)}, u32[]{:S(2)}) collective-permute-start(f32[40,16,256]{2,1,0:T(8,128)} %get-tuple-element.66), channel_id=1, source_target_pairs={{0,8},{8,16},{16,24},{24,32},{32,40},{40,48},{48,56},{56,64},{64,7... | collective-permute-start | bytes 1966088 | tf_op jit(solution)/shard_map/ppermute | solution.py:528
  63.4 15.2 %collective-permute-start.1 = (f32[40,16,256]{2,1,0:T(8,128)}, f32[40,16,256]{2,1,0:T(8,128)S(1)}, u32[]{:S(2)}, u32[]{:S(2)}) collective-permute-start(f32[40,16,256]{2,1,0:T(8,128)} %get-tuple-element.67), channel_id=1, source_target_pairs={{8,0},{16,8},{24,16},{32,24},{40,32},{48,40},{56,48},{64,56},{72,6... | collective-permute-start | bytes 1966088 | tf_op jit(solution)/shard_map/ppermute | solution.py:528
  65.4 44.0 %collective-permute-start.2 = (f32[32,40,256]{2,1,0:T(8,128)}, f32[32,40,256]{2,1,0:T(8,128)S(1)}, u32[]{:S(2)}, u32[]{:S(2)}) collective-permute-start(f32[32,40,256]{2,1,0:T(8,128)} %copy-done.13), channel_id=1, source_target_pairs={{0,1},{1,2},{2,3},{3,4},{4,5},{5,6},{6,7},{8,9},{9,10},{10,11},{11... | collective-permute-start | bytes 3932168 | tf_op jit(solution)/shard_map/ppermute | solution.py:528
  68.7 40.7 %collective-permute-start.3 = (f32[32,40,256]{2,1,0:T(8,128)}, f32[32,40,256]{2,1,0:T(8,128)}, u32[]{:S(2)}, u32[]{:S(2)}) collective-permute-start(f32[32,40,256]{2,1,0:T(8,128)} %copy-done.12), channel_id=1, source_target_pairs={{1,0},{2,1},{3,2},{4,3},{5,4},{6,5},{7,6},{9,8},{10,9},{11,10},{12... | collective-permute-start | bytes 3932168 | tf_op jit(solution)/shard_map/ppermute | solution.py:528
  78.6 30.8 %copy-start = (f32[40,16,256]{2,1,0:T(8,128)}, f32[40,16,256]{2,1,0:T(8,128)S(1)}, u32[]{:S(2)}) copy-start(f32[40,16,256]{2,1,0:T(8,128)S(1)} %collective-permute-done.lower) | copy-start | bytes 1966084
  78.6 30.8 %copy-start.1 = (f32[40,16,256]{2,1,0:T(8,128)}, f32[40,16,256]{2,1,0:T(8,128)S(1)}, u32[]{:S(2)}) copy-start(f32[40,16,256]{2,1,0:T(8,128)S(1)} %collective-permute-done.1.upper) | copy-start | bytes 1966084
  79.8 25.4 %collective-permute-start.4 = (f32[10,40,256]{2,1,0:T(8,128)}, f32[10,40,256]{2,1,0:T(8,128)}, u32[]{:S(2)}, u32[]{:S(2)}) collective-permute-start(f32[10,40,256]{2,1,0:T(8,128)} %get-tuple-element.70), channel_id=1, source_target_pairs={{0,1},{1,2},{2,3},{3,4},{4,5},{5,6},{6,7},{8,9},{9,10},{10,11},{11... | collective-permute-start | bytes 1228808 | tf_op jit(solution)/shard_map/ppermute | solution.py:528
  83.9 25.5 %collective-permute-start.5 = (f32[10,40,256]{2,1,0:T(8,128)}, f32[10,40,256]{2,1,0:T(8,128)}, u32[]{:S(2)}, u32[]{:S(2)}) collective-permute-start(f32[10,40,256]{2,1,0:T(8,128)} %get-tuple-element.71), channel_id=1, source_target_pairs={{1,0},{2,1},{3,2},{4,3},{5,4},{6,5},{7,6},{9,8},{10,9},{11,10},{12... | collective-permute-start | bytes 1228808 | tf_op jit(solution)/shard_map/ppermute | solution.py:528
  115.1 5.2 %copy-start.11 = (f32[128]{0:T(128)S(1)}, f32[128]{0:T(128)}, u32[]{:S(2)}) copy-start(f32[128]{0:T(128)} %param.25) | copy-start | bytes 1540

commit v4 on v3

--- a/solution.py
+++ b/solution.py
@@ -35,6 +35,7 @@
 VM = pl.BlockSpec(memory_space=pltpu.VMEM)
 SM = pl.BlockSpec(memory_space=pltpu.SMEM)
 HBM = pl.BlockSpec(memory_space=pltpu.HBM)
+ANY = pl.BlockSpec(memory_space=pl.ANY)
 DMA = pltpu.SemaphoreType.DMA
 CUBE = (LAYERS, TALL, NX)
 
@@ -95,19 +96,63 @@
     return copies, copy
 
 
+def sources_of(e_in, h_in, coef_in, loss_in):
+    return [e_in.at[k] for k in range(3)] + [h_in.at[k] for k in range(3)] + [coef_in, loss_in]
+
+
+def strip_kernel(top, e_in, h_in, coef_in, loss_in, after, strip, fields, sems):
+    copies, copy = copier(sems)
+    rows = pl.ds(CY - 8 if top else 0, 8)
+    for part, source in enumerate(sources_of(e_in, h_in, coef_in, loss_in)):
+        copy(source.at[:, rows], fields.at[part])
+    for job in copies:
+        job.wait()
+    given = slice(8 - DEPTH, 8) if top else slice(0, DEPTH)
+
+    @pl.loop(0, CZ)
+    def _(layer):
+        for part in range(PARTS):
+            strip[layer, part * DEPTH : (part + 1) * DEPTH, :] = fields[part, layer, given, :]
+
+
+def strip_of(top, grids, after):
+    return pl.pallas_call(
+        functools.partial(strip_kernel, top),
+        name="strip",
+        out_shape=jax.ShapeDtypeStruct((CZ, STRIP, NX), f32),
+        in_specs=[HBM] * 4 + [ANY],
+        out_specs=VM,
+        scratch_shapes=[pltpu.VMEM((PARTS, CZ, 8, NX), f32), DMA((PARTS,))],
+        compiler_params=params(),
+    )(*map(away, grids), after)
+
+
+def slab_kernel(top, e_in, h_in, coef_in, loss_in, after, slab, sems):
+    copies, copy = copier(sems)
+    layers = pl.ds(CZ - DEPTH if top else 0, DEPTH)
+    for part, source in enumerate(sources_of(e_in, h_in, coef_in, loss_in)):
+        copy(source.at[layers], slab.at[pl.ds(part * DEPTH, DEPTH)])
+    for job in copies:
+        job.wait()
+
+
+def slab_of(top, grids, after):
+    return pl.pallas_call(
+        functools.partial(slab_kernel, top),
+        name="slab",
+        out_shape=jax.ShapeDtypeStruct((PARTS * DEPTH, CY, NX), f32),
+        in_specs=[HBM] * 4 + [ANY],
+        out_specs=VM,
+        scratch_shapes=[DMA((PARTS,))],
+        compiler_params=params(),
+    )(*map(away, grids), after)
+
+
 def begin_kernel(
-    n_gy, cells, nodes, gains, e_in, h_in, coef_in, loss_in, cell_row, volts,
-    up, down, front, back, out, fields, picked, hits, rows_ref, sems,
+    n_gy, cells, nodes, gains, e_in, cell_row, volts, after, out, e_z, picked, hits, rows_ref, sem,
 ):
-    copies, copy = copier(sems)
-    sources = [e_in.at[k] for k in range(3)] + [h_in.at[k] for k in range(3)] + [coef_in, loss_in]
-    for part in (2, 0, 1, 3, 4, 5, 6, 7):
-        copy(sources[part], fields.at[part])
-    for part, source in enumerate(sources):
-        to = pl.ds(part * DEPTH, DEPTH)
-        copy(source.at[pl.ds(CZ - DEPTH, DEPTH)], up.at[to])
-        copy(source.at[pl.ds(0, DEPTH)], down.at[to])
-
+    load = pltpu.make_async_copy(e_in.at[2], e_z, sem)
+    load.start()
     first = (lax.axis_index("gz") * n_gy + lax.axis_index("gy")) * PORT_DEV
     wide, narrow = lanes_of(1, NX), lanes_of(1, NODE_DEV)
     own_nodes = [nodes[first + port] for port in range(PORT_DEV)]
@@ -118,46 +163,32 @@
     rows_ref[0:1, 0:PORT_DEV] = cell_row[...].astype(f32)
     out[...] = jnp.where(kind == 0, volts[...], jnp.where(kind == 2, rows_ref[0:1, :], 0.0))
 
-    copies[0].wait()
+    load.wait()
     for port in range(PORT_DEV):
         cell = cells[port]
         line = cell // NX
-        value = fields[2, line // CY, pl.ds(line % CY, 1), :] * gains[first + port]
+        value = e_z[line // CY, pl.ds(line % CY, 1), :] * gains[first + port]
         picked[port : port + 1, :] = jnp.where(wide == cell % NX, value, 0.0)
     rows_ref[...] = hits[...] * jnp.sum(picked[...], axis=1, keepdims=True)
     add_rows(out, 4, [node // NODE_DEV for node in own_nodes], rows_ref)
-    for job in copies[1:8]:
-        job.wait()
-
-    @pl.loop(0, CZ)
-    def _(layer):
-        for part in range(PARTS):
-            to = slice(part * DEPTH, (part + 1) * DEPTH)
-            front[layer, to, :] = fields[part, layer, CY - DEPTH : CY, :]
-            back[layer, to, :] = fields[part, layer, 0:DEPTH, :]
-
-    for job in copies[8:]:
-        job.wait()
-
-
-def begin(n_gy, cells, nodes, gains, e_in, h_in, coef, loss, volts):
-    thick = jax.ShapeDtypeStruct((PARTS * DEPTH, CY, NX), f32)
-    strips = jax.ShapeDtypeStruct((CZ, STRIP, NX), f32)
+
+
+def begin(n_gy, cells, nodes, gains, e_in, volts, after):
     return pl.pallas_call(
         functools.partial(begin_kernel, n_gy),
         name="begin",
-        out_shape=(thick, thick, strips, strips, jax.ShapeDtypeStruct((4 * ND, NODE_DEV), f32)),
-        in_specs=[SM, SM, SM, HBM, HBM, HBM, HBM, VM, VM],
-        out_specs=(HBM, HBM, VM, VM, VM),
+        out_shape=jax.ShapeDtypeStruct((4 * ND, NODE_DEV), f32),
+        in_specs=[SM, SM, SM, HBM, VM, VM, ANY],
+        out_specs=VM,
         scratch_shapes=[
-            pltpu.VMEM((PARTS, CZ, CY, NX), f32),
+            pltpu.VMEM((CZ, CY, NX), f32),
             pltpu.VMEM((PORT_DEV, NX), f32),
             pltpu.VMEM((PORT_DEV, NODE_DEV), f32),
             pltpu.VMEM((PORT_DEV, NODE_DEV), f32),
-            DMA((24,)),
+            DMA,
         ],
         compiler_params=params(),
-    )(cells, nodes, gains, *map(away, (e_in, h_in, coef, loss)), cells.reshape(1, -1), volts)
+    )(cells, nodes, gains, away(e_in), cells.reshape(1, -1), volts, after)
 
 
 def matrices_kernel(diag, inv, off, m_off, m_diag, m_inv):
@@ -550,11 +581,15 @@
     n_gz, n_gy = lax.axis_size("gz"), lax.axis_size("gy")
     grids = (e_field, h_field, e_coef, e_loss)
     volts = volts_init.reshape(1, NODE_DEV)
-    up, down, front, back, out = begin(n_gy, port_cell, port_node, port_gain, *grids, volts)
+    front = strip_of(True, grids, volts)
     before = shifted(front, "gy", 1)
+    back = strip_of(False, grids, front)
     after = shifted(back, "gy", -1)
+    up = slab_of(True, grids, back)
     lower = shifted(up, "gz", 1)
+    down = slab_of(False, grids, up)
     upper = shifted(down, "gz", -1)
+    out = begin(n_gy, port_cell, port_node, port_gain, e_field, volts, down)
     arrived = exchange(out)
     front_ends, back_ends = corners(lower, upper)
     before_ends = shifted(front_ends, "gy", 1)

time: 225 us -> 200 us (0.89)
  Pallas kernels: 95.4 us -> 66.2 us
  blocking collectives: 72.1 us -> 64 us
  local copies, waits for them, and re-layouts: 7.52 us -> 12.4 us
  starting transfers between devices: 26.9 us -> 30.6 us
  other arithmetic: 2.86 us -> 6.44 us
    pallas_call x1, Pallas kernels: 42.8 us -> 3.37 us  [begin(): pl.pallas_call(functools.partial(begin_kernel, n_gy), name='begin', out_s...]
    ppermute x6, waiting for transfers between devices: 19.7 us -> 0.02 us  [shifted(): lax.ppermute(value, axis, [(source, source + steps) for source in range(f...]
    all_to_all x1, waiting for transfers between devices: 0.01 us -> 18.8 us  [exchange(): return lax.all_to_all(value, ('gz', 'gy'), 0, 0, tiled=True)]
    all_to_all x4, blocking collectives: 72.1 us -> 64 us  [exchange(): return lax.all_to_all(value, ('gz', 'gy'), 0, 0, tiled=True)]
    pallas_call x0 -> x4, Pallas kernels: none -> 8.01 us  [the longest x2 4.15 us: slab_of(): pl.pallas_call(functools.partial(slab_kernel, top), name='slab', out_shap...]
    another operation x3, local copies, waits for them, and re-layouts: 0.3 us -> 3.48 us  [body(): jnp.stack([gains, (cells % NX).astype(f32).reshape(-1), (nodes % NODE_DEV...]
    ppermute x6, starting transfers between devices: 15.4 us -> 18 us  [shifted(): lax.ppermute(value, axis, [(source, source + steps) for source in range(f...]
    unnamed x34 -> x28, local copies, waits for them, and re-layouts: 4.89 us -> 4.24 us
  transfers between devices with their start and end apart: 7 -> 7, of which waited for: 3 -> 1; matrix products, arithmetic and copies ran while one was open for 2% -> 7% of each run, Pallas kernels for 4% -> 10%
where the time goes in v4:
time: 200 us
  Pallas kernels  66.2 us (33%)
  blocking collectives  64 us (32%)
  starting transfers between devices  30.6 us (15%)
  waiting for transfers between devices  18.8 us (9%)
  local copies, waits for them, and re-layouts  12.4 us (6%)
  other arithmetic  6.44 us (3%)
    all_to_all x4, blocking collectives, exchange(): return lax.all_to_all(value, ('gz', 'gy'), 0, 0, tiled=True)  64 us
    pallas_call x5, Pallas kernels, field(): pl.pallas_call(functools.partial(field_kernel, step), name='field', out_s...  24 us
    all_to_all x1, waiting for transfers between devices, exchange(): return lax.all_to_all(value, ('gz', 'gy'), 0, 0, tiled=True)  18.8 us
    ppermute x6, starting transfers between devices, shifted(): lax.ppermute(value, axis, [(source, source + steps) for source in range(f...  18 us
    all_to_all x1, starting transfers between devices, exchange(): return lax.all_to_all(value, ('gz', 'gy'), 0, 0, tiled=True)  12.6 us
    pallas_call x4, Pallas kernels, circuit(): pl.pallas_call(functools.partial(circuit_kernel, arrived.shape[0] // ND),...  11.7 us
    pallas_call x1, Pallas kernels, plan(): pl.pallas_call(plan_kernel, name='plan', out_shape=(jax.ShapeDtypeStruct(...  7.31 us
    pallas_call x1, Pallas kernels, halo(): pl.pallas_call(halo_kernel, name='halo', out_shape=(onchip((2,) + CUBE),...  6.07 us
  transfers between devices with their start and end apart: 7, of which 1 were waited for; matrix products, arithmetic and copies ran while one was open for 7% of the time, Pallas kernels for 10%

profile of v4, /device:TPU:1, one launch (start us, length us, event | category | flops | bytes accessed | tf_op | source)
XLA Modules:
  0.0 199.5 jit_solution(17695404794981665926)
XLA Ops:
  0.6 0.0 copy-start.7
  0.6 0.6 copy-done.7
  1.3 1.9 strip.2.after
  3.2 5.5 %collective-permute-start.2 = (f32[32,40,256]{2,1,0:T(8,128)S(1)}, f32[32,40,256]{2,1,0:T(8,128)}, u32[]{:S(2)}, u32[]{:S(2)}) collective-permute-start(f32[32,40,256]{2,1,0:T(8,128)S(1)} %strip.2.after), channel_id=1, source_target_pairs={{0,1},{1,2},{2,3},{3,4},{4,5},{5,6},{6,7},{8,9},{9,10},{10,11},{11... | collective-permute-start | bytes 3932168 | tf_op jit(solution)/shard_map/ppermute | solution.py:559
  8.7 1.9 strip.3.after
  10.6 1.3 collective-permute-start.3
  11.9 2.1 %slab.2.after = f32[40,16,256]{2,1,0:T(8,128)} custom-call(f32[3,32,16,256]{3,2,1,0:T(8,128)} %e_in.11, f32[3,32,16,256]{3,2,1,0:T(8,128)} %h_in.9, f32[32,16,256]{2,1,0:T(8,128)} %coef_in.9, f32[32,16,256]{2,1,0:T(8,128)} %loss_in.9, f32[32,40,256]{2,1,0:T(8,128)S(1)} %strip.3.after), custom_call_target="tpu_custom_call" | custom-call | tf_op jit(solution)/shard_map/slab/pallas_call | solution.py:140
  14.0 0.0 copy-start.3
  14.0 0.0 copy-start.4
  14.0 0.0 copy-start.10
  14.1 4.2 %collective-permute-start = (f32[40,16,256]{2,1,0:T(8,128)}, f32[40,16,256]{2,1,0:T(8,128)S(1)}, u32[]{:S(2)}, u32[]{:S(2)}) collective-permute-start(f32[40,16,256]{2,1,0:T(8,128)} %slab.2.after), channel_id=1, source_target_pairs={{0,8},{8,16},{16,24},{24,32},{32,40},{40,48},{48,56},{56,64},{64,7... | collective-permute-start | bytes 1966088 | tf_op jit(solution)/shard_map/ppermute | solution.py:559
  18.2 2.1 %slab.3.after = f32[40,16,256]{2,1,0:T(8,128)} custom-call(f32[3,32,16,256]{3,2,1,0:T(8,128)} %e_in.11, f32[3,32,16,256]{3,2,1,0:T(8,128)} %h_in.9, f32[32,16,256]{2,1,0:T(8,128)} %coef_in.9, f32[32,16,256]{2,1,0:T(8,128)} %loss_in.9, f32[40,16,256]{2,1,0:T(8,128)} %slab.2.after), custom_call_target="tpu_custom_call" | custom-call | tf_op jit(solution)/shard_map/slab/pallas_call | solution.py:140
  20.3 1.9 collective-permute-start.1
  22.3 0.0 copy-start.11
  22.3 0.0 copy-start.12
  22.3 3.4 %begin.1 = f32[512,128]{1,0:T(8,128)} custom-call(s32[32]{0:T(128)S(1)} %copy-done.10, s32[4096]{0:T(1024)S(1)} %copy-done.3, f32[4096]{0:T(1024)S(1)} %copy-done.4, f32[3,32,16,256]{3,2,1,0:T(8,128)} %e_in.11, s32[1,32]{1,0:T(1,128)S(1)} %bitcast.26, f32[1,128]{1,0:T(1,128)S(1)} %bitcast.24, f32[40,16,256]{2,1,0:T(8,128)} %slab.3.after), custom_call_target="tpu_custom_call" | custom-call | tf_op jit(solution)/shard_map/begin/pallas_call | solution.py:177
  25.7 12.6 %all-to-all-start = ((f32[128,4,128]{2,1,0:T(4,128)}), f32[128,4,128]{2,1,0:T(4,128)}, u32[]{:S(2)}, u32[]{:S(2)}) async-start(f32[128,4,128]{2,1,0:T(4,128)} %bitcast.2), calls=%async_computation | async-start | bytes 524288 | tf_op jit(solution)/shard_map/all_to_all | solution.py:563
  38.4 0.1 reshape.132
  38.4 0.5 compare_select_fusion.2
  39.0 0.6 gather_fusion.1
  39.5 0.1 reshape.133
  39.6 0.1 reshape.134
  39.7 0.6 pad_clamp_fusion.1
  40.3 0.1 pad_add_fusion.node_at
  40.4 0.1 pad_maximum_fusion.1.bounds
  40.5 0.1 reshape.136
  40.6 0.1 reshape.135
  40.6 0.6 gather_fusion.2
  41.2 0.6 stack_reshape.6
  41.9 0.9 copy-done.2
  42.8 0.8 copy-done.5
  43.6 0.8 copy-done.6
  44.5 0.2 matrices.1
  44.6 0.6 fusion.11
  45.2 18.8 %all-to-all-done = f32[128,4,128]{2,1,0:T(4,128)} async-done(((f32[128,4,128]{2,1,0:T(4,128)}), f32[128,4,128]{2,1,0:T(4,128)}, u32[]{:S(2)}, u32[]{:S(2)}) %all-to-all-start) | async-done | bytes 262176 | tf_op jit(solution)/shard_map/all_to_all | solution.py:563
  64.0 1.6 gather_fusion
  65.7 0.6 fusion.6
  66.3 2.4 %corners.1 = (f32[10,40,256]{2,1,0:T(8,128)}, f32[10,40,256]{2,1,0:T(8,128)}) custom-call(f32[40,16,256]{2,1,0:T(8,128)S(1)} %collective-permute-done.lower, f32[40,16,256]{2,1,0:T(8,128)} %collective-permute-done.1.upper), custom_call_target="tpu_custom_call" | custom-call | tf_op jit(solution)/shard_map/corners/pallas_call | solution.py:229
  68.7 3.9 %collective-permute-start.4 = (f32[10,40,256]{2,1,0:T(8,128)}, f32[10,40,256]{2,1,0:T(8,128)}, u32[]{:S(2)}, u32[]{:S(2)}) collective-permute-start(f32[10,40,256]{2,1,0:T(8,128)} %get-tuple-element.60), channel_id=1, source_target_pairs={{0,1},{1,2},{2,3},{3,4},{4,5},{5,6},{6,7},{8,9},{9,10},{10,11},{11... | collective-permute-start | bytes 1228808 | tf_op jit(solution)/shard_map/ppermute | solution.py:559
  72.5 1.3 collective-permute-start.5
  73.8 1.4 fusion.16
  75.2 1.3 add_select_fusion.4
  76.5 0.8 reshape.129.spots
  77.3 0.8 reshape.139.active
  78.1 1.4 stack_reshape.7
  79.4 1.3 pad_maximum_fusion
  80.7 1.5 copy.22.columns
  82.2 0.9 copy-done.1
  83.1 7.3 %plan.1 = (s32[593]{0:T(1024)S(1)}, f32[288,3]{1,0:T(8,128)S(1)}) custom-call(s32[288]{0:T(512)S(1)} %reshape.129.spots, s32[288]{0:T(512)S(1)} %reshape.139.active, s32[304]{0:T(512)S(1)} %pad_add_fusion.node_at, f32[288,3]{1,0:T(8,128)S(1)} %copy-done.1), custom_call_target="tpu_custom_call" | custom-call | tf_op jit(solution)/shard_map/plan/pallas_call | solution.py:263
  90.4 6.1 %halo.1 = (f32[2,42,32,256]{3,2,1,0:T(8,128)S(1)}, f32[42,32,256]{2,1,0:T(8,128)S(1)}, f32[3,42,32,256]{3,2,1,0:T(8,128)S(1)}, f32[2,42,32,256]{3,2,1,0:T(8,128)...) custom-call(s32[593]{0:T(1024)S(1)} %get-tuple-element.58.found.table, f32[288,3]{1,0:T(8,128)S(1)} %get-tuple-element.59.columns, ...), custom_call_target="tpu_custom_call" | custom-call | tf_op jit(solution)/shard_map/halo/pallas_call | solution.py:329
  96.5 5.2 %field.5 = (f32[2,42,32,256]{3,2,1,0:T(8,128)S(1)}, f32[42,32,256]{2,1,0:T(8,128)S(1)}, f32[3,42,32,256]{3,2,1,0:T(8,128)S(1)}) custom-call(f32[2]{0:T(128)S(1)} %pad_maximum_fusion.1.bounds, f32[2,42,32,256]{3,2,1,0:T(8,128)S(1)} %get-tuple-element.67.media, f32[2,42,32,256]{3,2,1,0:T(8,128)S(1)} %get-tuple-element.68.e_xy, ...), custom_call_target="tpu_custom_call" | custom-call | tf_op jit(solution)/shard_map/field/pallas_call | solution.py:407
  101.8 3.2 %circuit.4 = (f32[42,32,256]{2,1,0:T(8,128)S(1)}, f32[256,128]{1,0:T(8,128)S(1)}, f32[1,128]{1,0:T(1,128)S(1)}, f32[288,1]{1,0:T(8,128)S(1)}) custom-call(s32[593]{0:T(1024)S(1)} %get-tuple-element.58.found.table, f32[512,128]{1,0:T(8,128)} %bitcast.3.arrived, f32[288,3]{1,0:T(8,128)S(1)} %get-tuple-element.59.columns, ...), custom_call_target="tpu_custom_call" | custom-call | tf_op jit(solution)/shard_map/circuit/pallas_call | solution.py:490
  105.0 20.8 %all_to_all.59 = f32[128,2,128]{2,1,0:T(2,128)S(1)} all-to-all(f32[128,2,128]{2,1,0:T(2,128)S(1)} %bitcast.22), channel_id=1, replica_groups=mesh['gz'=16,'gy'=8] {'gz','gy'}, dimensions={0} | all-to-all | bytes 262144 | tf_op jit(solution)/shard_map/all_to_all | solution.py:563
  125.8 5.0 %field.6 = (f32[2,42,32,256]{3,2,1,0:T(8,128)S(1)}, f32[42,32,256]{2,1,0:T(8,128)S(1)}, f32[3,42,32,256]{3,2,1,0:T(8,128)S(1)}) custom-call(f32[2]{0:T(128)S(1)} %pad_maximum_fusion.1.bounds, f32[2,42,32,256]{3,2,1,0:T(8,128)S(1)} %get-tuple-element.67.media, f32[2,42,32,256]{3,2,1,0:T(8,128)S(1)} %get-tuple-element.77.e_xy, ...), custom_call_target="tpu_custom_call" | custom-call | tf_op jit(solution)/shard_map/field/pallas_call | solution.py:407
  130.8 2.8 %circuit.5 = (f32[42,32,256]{2,1,0:T(8,128)S(1)}, f32[256,128]{1,0:T(8,128)S(1)}, f32[1,128]{1,0:T(1,128)S(1)}, f32[288,1]{1,0:T(8,128)S(1)}) custom-call(s32[593]{0:T(1024)S(1)} %get-tuple-element.58.found.table, f32[256,128]{1,0:T(8,128)S(1)} %bitcast.16, f32[288,3]{1,0:T(8,128)S(1)} %get-tuple-element.59.columns, f32[288,1]{1,0:T(8,128)S(1)} %get-tuple-element.75.sample, ...), custom_call_target="tpu_custom_call" | custom-call | tf_op jit(solution)/shard_map/circuit/pallas_call | solution.py:490
  133.6 14.4 %all_to_all.60 = f32[128,2,128]{2,1,0:T(2,128)S(1)} all-to-all(f32[128,2,128]{2,1,0:T(2,128)S(1)} %bitcast.19), channel_id=1, replica_groups=mesh['gz'=16,'gy'=8] {'gz','gy'}, dimensions={0} | all-to-all | bytes 262144 | tf_op jit(solution)/shard_map/all_to_all | solution.py:563
  148.0 4.8 %field.7 = (f32[2,42,32,256]{3,2,1,0:T(8,128)S(1)}, f32[42,32,256]{2,1,0:T(8,128)S(1)}, f32[3,42,32,256]{3,2,1,0:T(8,128)S(1)}) custom-call(f32[2]{0:T(128)S(1)} %pad_maximum_fusion.1.bounds, f32[2,42,32,256]{3,2,1,0:T(8,128)S(1)} %get-tuple-element.67.media, f32[2,42,32,256]{3,2,1,0:T(8,128)S(1)} %get-tuple-element.86.e_xy, ...), custom_call_target="tpu_custom_call" | custom-call | tf_op jit(solution)/shard_map/field/pallas_call | solution.py:407
  152.8 2.8 %circuit.6 = (f32[42,32,256]{2,1,0:T(8,128)S(1)}, f32[256,128]{1,0:T(8,128)S(1)}, f32[1,128]{1,0:T(1,128)S(1)}, f32[288,1]{1,0:T(8,128)S(1)}) custom-call(s32[593]{0:T(1024)S(1)} %get-tuple-element.58.found.table, f32[256,128]{1,0:T(8,128)S(1)} %bitcast.17, f32[288,3]{1,0:T(8,128)S(1)} %get-tuple-element.59.columns, f32[288,1]{1,0:T(8,128)S(1)} %get-tuple-element.84.sample, ...), custom_call_target="tpu_custom_call" | custom-call | tf_op jit(solution)/shard_map/circuit/pallas_call | solution.py:490
  155.7 14.4 %all_to_all.61 = f32[128,2,128]{2,1,0:T(2,128)S(1)} all-to-all(f32[128,2,128]{2,1,0:T(2,128)S(1)} %bitcast.20), channel_id=1, replica_groups=mesh['gz'=16,'gy'=8] {'gz','gy'}, dimensions={0} | all-to-all | bytes 262144 | tf_op jit(solution)/shard_map/all_to_all | solution.py:563
  170.1 4.6 %field.8 = (f32[2,42,32,256]{3,2,1,0:T(8,128)S(1)}, f32[42,32,256]{2,1,0:T(8,128)S(1)}, f32[3,42,32,256]{3,2,1,0:T(8,128)S(1)}) custom-call(f32[2]{0:T(128)S(1)} %pad_maximum_fusion.1.bounds, f32[2,42,32,256]{3,2,1,0:T(8,128)S(1)} %get-tuple-element.67.media, f32[2,42,32,256]{3,2,1,0:T(8,128)S(1)} %get-tuple-element.95.e_xy, ...), custom_call_target="tpu_custom_call" | custom-call | tf_op jit(solution)/shard_map/field/pallas_call | solution.py:407
  174.7 2.8 %circuit.7 = (f32[42,32,256]{2,1,0:T(8,128)S(1)}, f32[256,128]{1,0:T(8,128)S(1)}, f32[1,128]{1,0:T(1,128)S(1)}, f32[288,1]{1,0:T(8,128)S(1)}) custom-call(s32[593]{0:T(1024)S(1)} %get-tuple-element.58.found.table, f32[256,128]{1,0:T(8,128)S(1)} %bitcast.18, f32[288,3]{1,0:T(8,128)S(1)} %get-tuple-element.59.columns, f32[288,1]{1,0:T(8,128)S(1)} %get-tuple-element.93.sample, ...), custom_call_target="tpu_custom_call" | custom-call | tf_op jit(solution)/shard_map/circuit/pallas_call | solution.py:490
  177.5 14.4 %all_to_all.62 = f32[128,2,128]{2,1,0:T(2,128)S(1)} all-to-all(f32[128,2,128]{2,1,0:T(2,128)S(1)} %bitcast.21), channel_id=1, replica_groups=mesh['gz'=16,'gy'=8] {'gz','gy'}, dimensions={0} | all-to-all | bytes 262144 | tf_op jit(solution)/shard_map/all_to_all | solution.py:563
  191.9 4.4 %field.9 = (f32[2,42,32,256]{3,2,1,0:T(8,128)S(1)}, f32[42,32,256]{2,1,0:T(8,128)S(1)}, f32[3,42,32,256]{3,2,1,0:T(8,128)S(1)}) custom-call(f32[2]{0:T(128)S(1)} %pad_maximum_fusion.1.bounds, f32[2,42,32,256]{3,2,1,0:T(8,128)S(1)} %get-tuple-element.67.media, f32[2,42,32,256]{3,2,1,0:T(8,128)S(1)} %get-tuple-element.104.e_xy, ...), custom_call_target="tpu_custom_call" | custom-call | tf_op jit(solution)/shard_map/field/pallas_call | solution.py:407
  196.4 3.2 %finish.1 = (f32[3,32,16,256]{3,2,1,0:T(8,128)}, f32[3,32,16,256]{3,2,1,0:T(8,128)}, f32[1,128]{1,0:T(1,128)}) custom-call(s32[593]{0:T(1024)S(1)} %get-tuple-element.58.found.table, f32[256,128]{1,0:T(8,128)S(1)} %bitcast.15, f32[288,3]{1,0:T(8,128)S(1)} %get-tuple-element.59.columns, f32[288,1]{1,0:T(8,128)S(1)} %get-tuple-element.102.sample, ...), custom_call_target="tpu_custom_call" | custom-call | tf_op jit(solution)/shard_map/finish/pallas_call | solution.py:533
  (27 shorter events, 0.1 us)
Async XLA Ops:
  0.6 0.7 copy-start.7
  3.2 87.2 %collective-permute-start.2 = (f32[32,40,256]{2,1,0:T(8,128)S(1)}, f32[32,40,256]{2,1,0:T(8,128)}, u32[]{:S(2)}, u32[]{:S(2)}) collective-permute-start(f32[32,40,256]{2,1,0:T(8,128)S(1)} %strip.2.after), channel_id=1, source_target_pairs={{0,1},{1,2},{2,3},{3,4},{4,5},{5,6},{6,7},{8,9},{9,10},{10,11},{11... | collective-permute-start | bytes 3932168 | tf_op jit(solution)/shard_map/ppermute | solution.py:559
  10.6 79.8 %collective-permute-start.3 = (f32[32,40,256]{2,1,0:T(8,128)S(1)}, f32[32,40,256]{2,1,0:T(8,128)}, u32[]{:S(2)}, u32[]{:S(2)}) collective-permute-start(f32[32,40,256]{2,1,0:T(8,128)S(1)} %strip.3.after), channel_id=1, source_target_pairs={{1,0},{2,1},{3,2},{4,3},{5,4},{6,5},{7,6},{9,8},{10,9},{11,10},{12... | collective-permute-start | bytes 3932168 | tf_op jit(solution)/shard_map/ppermute | solution.py:559
  14.0 8.2 %copy-start.3 = (s32[4096]{0:T(1024)S(1)}, s32[4096]{0:T(1024)}, u32[]{:S(2)}) copy-start(s32[4096]{0:T(1024)} %nodes.1) | copy-start | bytes 49156
  14.0 8.2 %copy-start.4 = (f32[4096]{0:T(1024)S(1)}, f32[4096]{0:T(1024)}, u32[]{:S(2)}) copy-start(f32[4096]{0:T(1024)} %gains.1) | copy-start | bytes 49156
  14.0 8.2 %copy-start.8 = (f32[128]{0:T(128)S(1)}, f32[128]{0:T(128)}, u32[]{:S(2)}) copy-start(f32[128]{0:T(128)} %param.25) | copy-start | bytes 1540
  14.0 8.2 %copy-start.10 = (s32[32]{0:T(128)S(1)}, s32[32]{0:T(128)}, u32[]{:S(2)}) copy-start(s32[32]{0:T(128)} %cells.1) | copy-start | bytes 388
  14.1 52.2 %collective-permute-start = (f32[40,16,256]{2,1,0:T(8,128)}, f32[40,16,256]{2,1,0:T(8,128)S(1)}, u32[]{:S(2)}, u32[]{:S(2)}) collective-permute-start(f32[40,16,256]{2,1,0:T(8,128)} %slab.2.after), channel_id=1, source_target_pairs={{0,8},{8,16},{16,24},{24,32},{32,40},{40,48},{48,56},{56,64},{64,7... | collective-permute-start | bytes 1966088 | tf_op jit(solution)/shard_map/ppermute | solution.py:559
  20.3 45.9 %collective-permute-start.1 = (f32[40,16,256]{2,1,0:T(8,128)}, f32[40,16,256]{2,1,0:T(8,128)}, u32[]{:S(2)}, u32[]{:S(2)}) collective-permute-start(f32[40,16,256]{2,1,0:T(8,128)} %slab.3.after), channel_id=1, source_target_pairs={{8,0},{16,8},{24,16},{32,24},{40,32},{48,40},{56,48},{64,56},{72,6... | collective-permute-start | bytes 1966088 | tf_op jit(solution)/shard_map/ppermute | solution.py:559
  22.3 16.1 %copy-start.11 = (s32[9]{0:T(128)S(1)}, s32[9]{0:T(128)}, u32[]{:S(2)}) copy-start(s32[9]{0:T(128)} %constant.142.clone) | copy-start | bytes 112
  22.3 16.1 %copy-start.12 = (s32[9]{0:T(128)S(1)}, s32[9]{0:T(128)}, u32[]{:S(2)}) copy-start(s32[9]{0:T(128)} %constant.143.clone) | copy-start | bytes 112
  22.3 17.3 %copy-start.13 = (s32[2,4]{1,0:T(2,128)S(1)}, s32[2,4]{1,0:T(2,128)}, u32[]{:S(2)}) copy-start(s32[2,4]{1,0:T(2,128)} %param.24) | copy-start | bytes 100
  25.7 38.3 %all-to-all-start = ((f32[128,4,128]{2,1,0:T(4,128)}), f32[128,4,128]{2,1,0:T(4,128)}, u32[]{:S(2)}, u32[]{:S(2)}) async-start(f32[128,4,128]{2,1,0:T(4,128)} %bitcast.2), calls=%async_computation | async-start | bytes 524288 | tf_op jit(solution)/shard_map/all_to_all | solution.py:563
  41.8 0.9 copy-start.2
  42.8 0.8 copy-start.5
  43.6 0.8 copy-start.6
  66.3 24.2 %copy-start = (f32[40,16,256]{2,1,0:T(8,128)}, f32[40,16,256]{2,1,0:T(8,128)S(1)}, u32[]{:S(2)}) copy-start(f32[40,16,256]{2,1,0:T(8,128)S(1)} %collective-permute-done.lower) | copy-start | bytes 1966084
  68.7 21.7 %collective-permute-start.4 = (f32[10,40,256]{2,1,0:T(8,128)}, f32[10,40,256]{2,1,0:T(8,128)}, u32[]{:S(2)}, u32[]{:S(2)}) collective-permute-start(f32[10,40,256]{2,1,0:T(8,128)} %get-tuple-element.60), channel_id=1, source_target_pairs={{0,1},{1,2},{2,3},{3,4},{4,5},{5,6},{6,7},{8,9},{9,10},{10,11},{11... | collective-permute-start | bytes 1228808 | tf_op jit(solution)/shard_map/ppermute | solution.py:559
  72.5 17.9 %collective-permute-start.5 = (f32[10,40,256]{2,1,0:T(8,128)}, f32[10,40,256]{2,1,0:T(8,128)}, u32[]{:S(2)}, u32[]{:S(2)}) collective-permute-start(f32[10,40,256]{2,1,0:T(8,128)} %get-tuple-element.61), channel_id=1, source_target_pairs={{1,0},{2,1},{3,2},{4,3},{5,4},{6,5},{7,6},{9,8},{10,9},{11,10},{12... | collective-permute-start | bytes 1228808 | tf_op jit(solution)/shard_map/ppermute | solution.py:559
  82.2 0.9 copy-start.1
  96.5 5.2 %copy-start.9 = (f32[128]{0:T(128)S(1)}, f32[128]{0:T(128)}, u32[]{:S(2)}) copy-start(f32[128]{0:T(128)} %param.25) | copy-start | bytes 1540

commit v5 on v4

--- a/solution.py
+++ b/solution.py
@@ -24,8 +24,7 @@
 STRIP = PARTS * DEPTH
 SIDES = ((0, 0), (-1, 0), (1, 0), (0, -1), (-1, -1), (1, -1), (0, 1), (-1, 1), (1, 1))
 REACH = len(SIDES) * PORT_DEV
-NODES_AT, COUNT_AT, OFF_AT = REACH, 2 * REACH, 2 * REACH + 1
-SWAP_AT = OFF_AT + NB_DEV * OFF
+SPOTS, NODES, COUNT = 0, 1, 7
 
 time_step = 0.55
 charge_scale = 4.0
@@ -72,7 +71,7 @@
 
 def columns_at(columns, part):
     block = columns[part, :]
-    return block[:, 0:1], block[:, 1:2].astype(jnp.int32), block[:, 2:3].astype(jnp.int32)
+    return block[:, 2:3], block[:, 3:4].astype(jnp.int32), block[:, 4:5].astype(jnp.int32)
 
 
 def row_kind(shape, stride):
@@ -214,7 +213,7 @@
     )(diag, inv, off)
 
 
-def corners_kernel(lower, upper, front, back):
+def corners_kernel(lower, upper, after, front, back):
     for side, source in enumerate((lower, upper)):
         for layer in range(DEPTH):
             for part in range(PARTS):
@@ -224,53 +223,79 @@
                 back[side * DEPTH + layer, to, :] = source[given, 0:DEPTH, :]
 
 
-def corners(lower, upper):
+def corners(lower, upper, after):
     shape = jax.ShapeDtypeStruct((2 * DEPTH, STRIP, NX), f32)
     return pl.pallas_call(
         corners_kernel,
         name="corners",
         out_shape=(shape, shape),
-        in_specs=[VM, VM],
+        in_specs=[VM, VM, ANY],
         out_specs=(VM, VM),
         compiler_params=params(),
-    )(lower, upper)
-
-
-def plan_kernel(spots, active, node_at, columns, found, columns_out):
-    @pl.loop(0, REACH)
-    def _(port):
-        found[port] = PAD
-        found[NODES_AT + port] = 0
-
-    columns_out[...] = jnp.zeros_like(columns_out)
-
-    def place_port(port, count):
-        @pl.when(active[port] > 0)
-        def _():
-            found[count] = spots[port]
-            found[NODES_AT + count] = node_at[port]
-            columns_out[pl.ds(count, 1), :] = columns[pl.ds(port, 1), :]
-
-        return count + active[port]
-
-    count = lax.fori_loop(0, REACH, place_port, 0)
-    found[COUNT_AT] = (count + PORT_DEV - 1) // PORT_DEV
-    for item in range(2 * NB_DEV * OFF):
-        found[OFF_AT + item] = node_at[REACH + item]
-
-
-def plan(spots, active, node_at, columns):
-    return pl.pallas_call(
-        plan_kernel,
+    )(lower, upper, after)
+
+
+def plan_kernel(n_gz, n_gy, arrived, nodes, gains, found, columns, facts):
+    gz, gy = lax.axis_index("gz"), lax.axis_index("gy")
+    lane = lanes_of(1, NODE_DEV)
+    width = NODE_DEV // PORT_DEV
+    facts[...] = jnp.zeros_like(facts)
+    for group, (side_z, side_y) in enumerate(SIDES):
+        at_z, at_y = gz + side_z, gy + side_y
+        exists = (at_z >= 0) & (at_z < n_gz) & (at_y >= 0) & (at_y < n_gy)
+        device = jnp.where(exists, at_z * n_gy + at_y, 0)
+        slot = group % width
+        turn = (slot - device % width + width) % width * PORT_DEV
+        row = pl.ds(device // width, 1)
+        node, gain = pltpu.roll(nodes[row, :], turn, 1), pltpu.roll(gains[row, :], turn, 1)
+        cell = pltpu.roll(arrived[pl.ds(4 * device + 2, 1), :], slot * PORT_DEV, 1).astype(jnp.int32)
+        layer = cell // (CY * NX) + (side_z * CZ + DEPTH)
+        line = (cell // NX) % CY + (side_y * CY + PAD)
+        valid = (layer >= 1) & (layer < LAYERS - 1)
+        valid &= (line > PAD - DEPTH) & (line < PAD + CY + DEPTH - 1)
+        valid &= (lane // PORT_DEV == slot) & (jnp.where(exists, 1, 0) > 0)
+        values = (layer * TALL + line, node // NODE_DEV, gain, cell % NX, node % NODE_DEV, 1)
+        part = slice(group // width * NODE_DEV, (group // width + 1) * NODE_DEV)
+        for kind, value in enumerate(values):
+            fact = jnp.where(valid, jnp.asarray(value).astype(f32), 0.0)
+            facts[kind : kind + 1, part] = facts[kind : kind + 1, part] + fact
+
+    used = facts[5:6, :]
+    total = used.shape[1]
+    upper = lax.broadcasted_iota(jnp.int32, (total, total), 0) <= lanes_of(total, total)
+    ones = jnp.broadcast_to(used, (8, total))
+    order = jnp.dot(ones, upper.astype(f32), preferred_element_type=f32)[0:1, :] - 1.0
+    spot = lax.broadcasted_iota(jnp.int32, (REACH, total), 0)
+    chosen = jnp.where((spot == order.astype(jnp.int32)) & (used > 0.0), 1.0, 0.0)
+    across = (((1,), (1,)), ((), ()))
+    columns[...] = lax.dot_general(
+        chosen, facts[...], across, precision=lax.Precision.HIGHEST, preferred_element_type=f32
+    )
+    rows = lax.dot_general(
+        facts[...], chosen, across, precision=lax.Precision.HIGHEST, preferred_element_type=f32
+    )
+    count = jnp.sum(used, axis=1, keepdims=True)
+    groups = ((count + (PORT_DEV - 1)) / PORT_DEV).astype(jnp.int32)
+    kind = lax.broadcasted_iota(jnp.int32, rows.shape, 0)
+    unused = (kind == 0) & (lanes_of(8, REACH) >= count.astype(jnp.int32))
+    whole = jnp.where(unused, PAD, (rows + 0.5).astype(jnp.int32))
+    found[...] = jnp.where(kind == 7, groups, whole)
+
+
+def plan(n_gz, n_gy, arrived, nodes, gains):
+    lanes = -(-REACH // NODE_DEV) * NODE_DEV
+    return pl.pallas_call(
+        functools.partial(plan_kernel, n_gz, n_gy),
         name="plan",
         out_shape=(
-            jax.ShapeDtypeStruct((SWAP_AT + NB_DEV * OFF,), jnp.int32),
-            jax.ShapeDtypeStruct(columns.shape, f32),
+            jax.ShapeDtypeStruct((8, REACH), jnp.int32),
+            jax.ShapeDtypeStruct((REACH, 8), f32),
         ),
-        in_specs=[SM, SM, SM, VM],
-        out_specs=(SM, VM),
-        compiler_params=params(),
-    )(spots, active, node_at, columns)
+        in_specs=[VM, VM, VM],
+        out_specs=(VM, VM),
+        scratch_shapes=[pltpu.VMEM((8, lanes), f32)],
+        compiler_params=params(),
+    )(arrived, nodes.reshape(-1, NODE_DEV), gains.reshape(-1, NODE_DEV))
 
 
 def halo_kernel(
@@ -310,7 +335,7 @@
     def _(layer):
         media[1, layer] = 1.0 - media[1, layer]
 
-    @pl.loop(0, found[COUNT_AT])
+    @pl.loop(0, found[COUNT, 0])
     def _(group):
         part = pl.ds(pl.multiple_of(group * PORT_DEV, PORT_DEV), PORT_DEV)
         _, place, _ = columns_at(columns, part)
@@ -320,7 +345,7 @@
 
 def gather_cells(source, found, group, place, picked):
     for port in range(PORT_DEV):
-        spot = found[group * PORT_DEV + port]
+        spot = found[SPOTS, group * PORT_DEV + port]
         picked[port : port + 1, :] = source[spot // TALL, pl.ds(spot % TALL, 1), :]
     return pick(picked[...], place)
 
@@ -344,8 +369,9 @@
     )(found, columns, away(lower), away(upper), *sides, *map(away, (e_in, h_in, coef, loss)))
 
 
-def field_kernel(step, bounds, media, e_xy, e_z, h, to_xy, to_z, to_h):
-    low_z, low_y = bounds[0], bounds[1]
+def field_kernel(step, media, e_xy, e_z, h, to_xy, to_z, to_h):
+    low_z = jnp.where(lax.axis_index("gz") > 0, 1.0, 0.0)
+    low_y = jnp.where(lax.axis_index("gy") > 0, time_step, 0.0)
     lane = lanes_of(TALL, NX)
     last_lane, first_lane = lane == NX - 1, lane == 0
     row = lax.broadcasted_iota(jnp.int32, (TALL, NX), 0)
@@ -403,18 +429,18 @@
     put_e(last, electric(last))
 
 
-def field(step, bounds, media, e_xy, e_z, h):
+def field(step, media, e_xy, e_z, h):
     return pl.pallas_call(
         functools.partial(field_kernel, step),
         name="field",
         out_shape=(onchip((2,) + CUBE), onchip(CUBE), onchip((3,) + CUBE)),
-        in_specs=[SM] + [VM] * 4,
+        in_specs=[VM] * 4,
         out_specs=(VM,) * 3,
         compiler_params=params(),
-    )(bounds, keep(media), keep(e_xy), keep(e_z), keep(h))
-
-
-def solve(stride, arrived, table, volts, m_off, m_diag, m_inv):
+    )(keep(media), keep(e_xy), keep(e_z), keep(h))
+
+
+def solve(stride, arrived, off_cols, volts, m_off, m_diag, m_inv):
     lane = lanes_of(1, NODE_DEV)
     halves = []
     for j in range(NB_DEV):
@@ -422,9 +448,9 @@
         for half in range(OFF // 2):
             total = None
             for side in range(2):
-                spot = j * OFF + half * 2 + side
-                row = arrived[pl.ds(table[OFF_AT + spot] * stride, 1), :]
-                row = jnp.where(table[SWAP_AT + spot] == side, row, pltpu.roll(row, BS, 1))
+                column = off_cols[j, half * 2 + side]
+                row = arrived[pl.ds(column // NB_DEV * stride, 1), :]
+                row = jnp.where(column % NB_DEV == side, row, pltpu.roll(row, BS, 1))
                 row = jnp.where((lane < BS) == (side == 0), row, 0.0)
                 total = row if total is None else total + row
             pieces.append(jnp.broadcast_to(total, (BS, NODE_DEV)))
@@ -448,45 +474,45 @@
 
 
 def apply_ports(stride, table, arrived, columns, sample, coef, e_z, near_rows, deltas):
-    @pl.loop(0, table[COUNT_AT])
+    @pl.loop(0, table[COUNT, 0])
     def _(group):
         first = group * PORT_DEV
         part = pl.ds(pl.multiple_of(first, PORT_DEV), PORT_DEV)
         for port in range(PORT_DEV):
-            near_at = table[NODES_AT + first + port] * stride
+            near_at = table[NODES, first + port] * stride
             near_rows[port : port + 1, :] = arrived[pl.ds(near_at, 1), :]
         gain, place, lane = columns_at(columns, part)
         current = gain * (sample[part, :] - pick(near_rows[...], lane))
         deltas[...] = spread(-coef[part, :] * current, place, NX)
         for port in range(PORT_DEV):
-            spot = table[first + port]
+            spot = table[SPOTS, first + port]
             layer, row = spot // TALL, pl.ds(spot % TALL, 1)
             e_z[layer, row, :] = e_z[layer, row, :] + deltas[port : port + 1, :]
 
 
 def circuit_kernel(
-    stride, table, arrived, columns, sample, coef, volts, m_off, m_diag, m_inv, e_in,
+    stride, table, off_cols, arrived, columns, sample, coef, volts, m_off, m_diag, m_inv, e_in,
     e_z, out, volts_out, sample_out, near_rows, deltas, picked, spread_rows,
 ):
     e_z[...] = e_in[...]
     apply_ports(stride, table, arrived, columns, sample, coef, e_z, near_rows, deltas)
 
-    @pl.loop(0, table[COUNT_AT])
+    @pl.loop(0, table[COUNT, 0])
     def _(group):
         part = pl.ds(pl.multiple_of(group * PORT_DEV, PORT_DEV), PORT_DEV)
         _, place, _ = columns_at(columns, part)
         sample_out[part, :] = gather_cells(e_z, table, group, place, picked)
 
-    solved = solve(stride, arrived, table, volts, m_off, m_diag, m_inv)
+    solved = solve(stride, arrived, off_cols, volts, m_off, m_diag, m_inv)
     volts_out[...] = solved
     own = slice(0, PORT_DEV)
     gain, _, lane = columns_at(columns, own)
     spread_rows[...] = spread(gain * sample_out[own, :], lane, NODE_DEV)
     out[...] = jnp.where(row_kind(out.shape, 2) == 0, solved, 0.0)
-    add_rows(out, 2, [table[NODES_AT + port] for port in range(PORT_DEV)], spread_rows)
-
-
-def circuit(table, arrived, columns, sample, coef, volts, mats, e_z):
+    add_rows(out, 2, [table[NODES, port] for port in range(PORT_DEV)], spread_rows)
+
+
+def circuit(table, off_cols, arrived, columns, sample, coef, volts, mats, e_z):
     return pl.pallas_call(
         functools.partial(circuit_kernel, arrived.shape[0] // ND),
         name="circuit",
@@ -496,7 +522,7 @@
             onchip((1, NODE_DEV)),
             onchip((REACH, 1)),
         ),
-        in_specs=[SM] + [VM] * 9,
+        in_specs=[SM, SM] + [VM] * 9,
         out_specs=(VM,) * 4,
         scratch_shapes=[
             pltpu.VMEM((PORT_DEV, NODE_DEV), f32),
@@ -506,13 +532,13 @@
         ],
         compiler_params=params(),
     )(
-        table, arrived, columns, keep(sample), keep(coef), volts,
+        table, off_cols, arrived, columns, keep(sample), keep(coef), volts,
         *[keep(mat) for mat in mats], keep(e_z),
     )
 
 
 def finish_kernel(
-    stride, table, arrived, columns, sample, coef, volts, m_off, m_diag, m_inv, e_xy, e_in, h,
+    stride, table, off_cols, arrived, columns, sample, coef, volts, m_off, m_diag, m_inv, e_xy, e_in, h,
     e_out, h_out, volts_out, e_z, near_rows, deltas, sems,
 ):
     copies, copy = copier(sems)
@@ -524,12 +550,12 @@
     e_z[...] = e_in[...]
     apply_ports(stride, table, arrived, columns, sample, coef, e_z, near_rows, deltas)
     copy(e_z.at[layers, rows], e_out.at[2])
-    volts_out[...] = solve(stride, arrived, table, volts, m_off, m_diag, m_inv)
+    volts_out[...] = solve(stride, arrived, off_cols, volts, m_off, m_diag, m_inv)
     for job in copies:
         job.wait()
 
 
-def finish(table, arrived, columns, sample, coef, volts, mats, e_xy, e_z, h):
+def finish(table, off_cols, arrived, columns, sample, coef, volts, mats, e_xy, e_z, h):
     return pl.pallas_call(
         functools.partial(finish_kernel, arrived.shape[0] // ND),
         name="finish",
@@ -538,7 +564,7 @@
             jax.ShapeDtypeStruct((3, CZ, CY, NX), f32),
             jax.ShapeDtypeStruct((1, NODE_DEV), f32),
         ),
-        in_specs=[SM] + [VM] * 11,
+        in_specs=[SM, SM] + [VM] * 11,
         out_specs=(HBM, HBM, VM),
         scratch_shapes=[
             pltpu.VMEM(CUBE, f32),
@@ -548,7 +574,7 @@
         ],
         compiler_params=params(),
     )(
-        table, arrived, columns, keep(sample), keep(coef), volts,
+        table, off_cols, arrived, columns, keep(sample), keep(coef), volts,
         *[keep(mat) for mat in mats], keep(e_xy), keep(e_z), keep(h),
     )
 
@@ -577,7 +603,6 @@
     off_cols,
     volts_init,
 ):
-    gz, gy = lax.axis_index("gz"), lax.axis_index("gy")
     n_gz, n_gy = lax.axis_size("gz"), lax.axis_size("gy")
     grids = (e_field, h_field, e_coef, e_loss)
     volts = volts_init.reshape(1, NODE_DEV)
@@ -591,40 +616,22 @@
     upper = shifted(down, "gz", -1)
     out = begin(n_gy, port_cell, port_node, port_gain, e_field, volts, down)
     arrived = exchange(out)
-    front_ends, back_ends = corners(lower, upper)
+    front_ends, back_ends = corners(lower, upper, out)
     before_ends = shifted(front_ends, "gy", 1)
     after_ends = shifted(back_ends, "gy", -1)
+    arrived, front_ends, back_ends = lax.optimization_barrier((arrived, front_ends, back_ends))
     sides = (before, after, before_ends, after_ends)
     mats = matrices(diag_blocks, inv_blocks, off_blocks)
 
-    shift_z = jnp.array([side[0] for side in SIDES], jnp.int32)[:, None]
-    shift_y = jnp.array([side[1] for side in SIDES], jnp.int32)[:, None]
-    at_z, at_y = gz + shift_z, gy + shift_y
-    exists = (at_z >= 0) & (at_z < n_gz) & (at_y >= 0) & (at_y < n_gy)
-    ids = jnp.where(exists, at_z * n_gy + at_y, 0)[:, 0]
-    cells = arrived[4 * ids + 2][:, 0:PORT_DEV].astype(jnp.int32)
-    nodes = port_node.reshape(-1, PORT_DEV)[ids].reshape(-1)
-    gains = port_gain.reshape(-1, PORT_DEV)[ids].reshape(-1)
-    layer = cells // (CY * NX) + shift_z * CZ + DEPTH
-    row = (cells // NX) % CY + shift_y * CY + PAD
-    inside = (layer >= 1) & (layer < LAYERS - 1) & (row >= PAD - DEPTH + 1) & (row < PAD + CY + DEPTH - 1)
-    valid = exists & inside
-    spots = jnp.where(valid, layer * TALL + row, PAD).reshape(-1)
-    columns = jnp.stack(
-        [gains, (cells % NX).astype(f32).reshape(-1), (nodes % NODE_DEV).astype(f32)], axis=1
-    )
-    flat_cols = off_cols.reshape(-1)
-    node_at = jnp.concatenate([nodes // NODE_DEV, flat_cols // NB_DEV, flat_cols % NB_DEV])
-    table, columns = plan(spots, valid.astype(jnp.int32).reshape(-1), node_at, columns)
-    bounds = jnp.stack([jnp.where(gz > 0, 1.0, 0.0), jnp.where(gy > 0, time_step, 0.0)]).astype(f32)
+    table, columns = plan(n_gz, n_gy, arrived, port_node, port_gain)
 
     e_xy, e_z, h, media, sample, coef = halo(table, columns, lower, upper, sides, *grids)
     for step in range(1, STEPS + 1):
         if step > 1:
             arrived = exchange(out)
             arrived, e_z = lax.optimization_barrier((arrived, e_z))
-        e_xy, e_z, h = field(step, bounds, media, e_xy, e_z, h)
-        shared = (table, arrived, columns, sample, coef, volts, mats)
+        e_xy, e_z, h = field(step, media, e_xy, e_z, h)
+        shared = (table, off_cols, arrived, columns, sample, coef, volts, mats)
         if step < STEPS:
             e_z, out, volts, sample = circuit(*shared, e_z)
         else:

time: 200 us -> 199 us (level)
  starting transfers between devices: 30.6 us -> 57.7 us
  Pallas kernels: 66.2 us -> 56.8 us
  local copies, waits for them, and re-layouts: 12.4 us -> 4.87 us
  other arithmetic: 6.44 us -> 0 us
  blocking collectives: 64 us -> 59.2 us
    all_to_all x1, starting transfers between devices: 12.6 us -> 39.7 us  [exchange(): return lax.all_to_all(value, ('gz', 'gy'), 0, 0, tiled=True)]
    all_to_all x1, waiting for transfers between devices: 18.8 us -> 8.02 us  [exchange(): return lax.all_to_all(value, ('gz', 'gy'), 0, 0, tiled=True)]
    ppermute x6, waiting for transfers between devices: 0.02 us -> 10.5 us  [shifted(): lax.ppermute(value, axis, [(source, source + steps) for source in range(f...]
    pallas_call x1, Pallas kernels: 7.31 us -> 2.11 us  [plan(): pl.pallas_call(functools.partial(plan_kernel, n_gz, n_gy), name='plan', o...]
    all_to_all x4, blocking collectives: 64 us -> 59.2 us  [exchange(): return lax.all_to_all(value, ('gz', 'gy'), 0, 0, tiled=True)]
    another operation x3 -> x0, local copies, waits for them, and re-layouts: 3.48 us -> none  [body(): jnp.stack([gains, (cells % NX).astype(f32).reshape(-1), (nodes % NODE_DEV...]
    pallas_call x5, Pallas kernels: 24 us -> 20.7 us  [field(): pl.pallas_call(functools.partial(field_kernel, step), name='field', out_s...]
    gather x3 -> x0, local copies, waits for them, and re-layouts: 2.75 us -> none  [the longest x1 1.63 us: body(): cells = arrived[4 * ids + 2][:, 0:PORT_DEV].astype(jnp.int32)]
  transfers between devices with their start and end apart: 7 -> 7, of which waited for: 1 -> 3; matrix products, arithmetic and copies ran while one was open for 7% -> 0% of each run, Pallas kernels for 10% -> 4%
where the time goes in v5:
time: 199 us; the launch traced here: 198 us
  blocking collectives  59.2 us (30%)
  starting transfers between devices  57.7 us (29%)
  Pallas kernels  56.8 us (29%)
  waiting for transfers between devices  18.5 us (9%)
  local copies, waits for them, and re-layouts  4.87 us (2%)
    all_to_all x4, blocking collectives, exchange(): return lax.all_to_all(value, ('gz', 'gy'), 0, 0, tiled=True)  59.2 us
    all_to_all x1, starting transfers between devices, exchange(): return lax.all_to_all(value, ('gz', 'gy'), 0, 0, tiled=True)  39.7 us
    pallas_call x5, Pallas kernels, field(): pl.pallas_call(functools.partial(field_kernel, step), name='field', out_s...  20.7 us
    ppermute x6, starting transfers between devices, shifted(): lax.ppermute(value, axis, [(source, source + steps) for source in range(f...  17.9 us
    pallas_call x4, Pallas kernels, circuit(): pl.pallas_call(functools.partial(circuit_kernel, arrived.shape[0] // ND),...  14 us
    ppermute x6, waiting for transfers between devices, shifted(): lax.ppermute(value, axis, [(source, source + steps) for source in range(f...  10.5 us
    all_to_all x1, waiting for transfers between devices, exchange(): return lax.all_to_all(value, ('gz', 'gy'), 0, 0, tiled=True)  8.02 us
    pallas_call x1, Pallas kernels, halo(): pl.pallas_call(halo_kernel, name='halo', out_shape=(onchip((2,) + CUBE),...  6.15 us
  transfers between devices with their start and end apart: 7, of which 3 were waited for; matrix products, arithmetic and copies ran while one was open for 0% of the time, Pallas kernels for 4%

profile of v5, /device:TPU:1, one launch (start us, length us, event | category | flops | bytes accessed | tf_op | source)
XLA Modules:
  0.0 197.9 jit_solution(12427686888132106290)
XLA Ops:
  0.6 0.0 copy-start.10
  0.6 0.6 copy-done.10
  1.3 1.9 strip.2.after
  3.2 1.9 strip.3.after
  5.2 1.3 collective-permute-start.3
  6.5 6.1 %collective-permute-start.2 = (f32[32,40,256]{2,1,0:T(8,128)S(1)}, f32[32,40,256]{2,1,0:T(8,128)}, u32[]{:S(2)}, u32[]{:S(2)}) collective-permute-start(f32[32,40,256]{2,1,0:T(8,128)S(1)} %strip.2.after), channel_id=1, source_target_pairs={{0,1},{1,2},{2,3},{3,4},{4,5},{5,6},{6,7},{8,9},{9,10},{10,11},{11... | collective-permute-start | bytes 3932168 | tf_op jit(solution)/shard_map/ppermute | solution.py:585
  12.6 1.2 slab.2.after
  13.8 0.0 copy-start.4
  13.8 0.0 copy-start.5
  13.8 0.0 copy-start.11
  13.8 0.0 copy-start.13
  13.8 1.3 slab.3.after
  15.1 2.9 %collective-permute-start.1 = (f32[40,16,256]{2,1,0:T(8,128)S(1)}, f32[40,16,256]{2,1,0:T(8,128)S(1)}, u32[]{:S(2)}, u32[]{:S(2)}) collective-permute-start(f32[40,16,256]{2,1,0:T(8,128)S(1)} %slab.3.after), channel_id=1, source_target_pairs={{8,0},{16,8},{24,16},{32,24},{40,32},{48,40},{56,48},{64,56},{72,6... | collective-permute-start | bytes 1966088 | tf_op jit(solution)/shard_map/ppermute | solution.py:585
  18.0 3.2 %collective-permute-start = (f32[40,16,256]{2,1,0:T(8,128)S(1)}, f32[40,16,256]{2,1,0:T(8,128)S(1)}, u32[]{:S(2)}, u32[]{:S(2)}) collective-permute-start(f32[40,16,256]{2,1,0:T(8,128)S(1)} %slab.2.after), channel_id=1, source_target_pairs={{0,8},{8,16},{16,24},{24,32},{32,40},{40,48},{48,56},{56,64},{64,7... | collective-permute-start | bytes 1966088 | tf_op jit(solution)/shard_map/ppermute | solution.py:585
  21.2 0.0 copy-done.4
  21.2 0.0 copy-done.5
  21.2 0.0 copy-done.11
  21.2 0.0 copy-done.13
  21.2 2.7 %begin.1.after = f32[512,128]{1,0:T(8,128)S(1)} custom-call(s32[32]{0:T(128)S(1)} %copy-done.13, s32[4096]{0:T(1024)S(1)} %copy-done.4, f32[4096]{0:T(1024)S(1)} %copy-done.5, f32[3,32,16,256]{3,2,1,0:T(8,128)} %e_in.11, s32[1,32]{1,0:T(1,128)S(1)} %bitcast.29, f32[1,128]{1,0:T(1,128)S(1)} %bitcast.27, f32[40,16,256]{2,1,0:T(8,128)S(1)} %slab.3.after), custom_call_target="tpu_custom_call" | custom-call | tf_op jit(solution)/shard_map/begin/pallas_call | solution.py:176
  23.9 0.0 copy-start.2
  23.9 4.0 %collective-permute-done.1.upper = f32[40,16,256]{2,1,0:T(8,128)S(1)} collective-permute-done((f32[40,16,256]{2,1,0:T(8,128)S(1)}, f32[40,16,256]{2,1,0:T(8,128)S(1)}, u32[]{:S(2)}, u32[]{:S(2)}) %collective-permute-start.1) | collective-permute-done | bytes 655392 | tf_op jit(solution)/shard_map/ppermute | solution.py:585
  27.9 6.4 %collective-permute-done.lower = f32[40,16,256]{2,1,0:T(8,128)S(1)} collective-permute-done((f32[40,16,256]{2,1,0:T(8,128)S(1)}, f32[40,16,256]{2,1,0:T(8,128)S(1)}, u32[]{:S(2)}, u32[]{:S(2)}) %collective-permute-start) | collective-permute-done | bytes 655392 | tf_op jit(solution)/shard_map/ppermute | solution.py:585
  34.3 1.1 corners.1
  35.4 0.0 copy-start.1
  35.4 0.8 copy-done.1
  36.2 3.2 %collective-permute-start.4 = (f32[10,40,256]{2,1,0:T(8,128)}, f32[10,40,256]{2,1,0:T(8,128)}, u32[]{:S(2)}, u32[]{:S(2)}) collective-permute-start(f32[10,40,256]{2,1,0:T(8,128)} %get-tuple-element.59), channel_id=1, source_target_pairs={{0,1},{1,2},{2,3},{3,4},{4,5},{5,6},{6,7},{8,9},{9,10},{10,11},{11... | collective-permute-start | bytes 1228808 | tf_op jit(solution)/shard_map/ppermute | solution.py:585
  39.5 1.3 collective-permute-start.5
  40.7 0.0 copy-done.2
  40.8 39.7 %all-to-all-start = ((f32[128,4,128]{2,1,0:T(4,128)}), f32[128,4,128]{2,1,0:T(4,128)}, u32[]{:S(2)}, u32[]{:S(2)}) async-start(f32[128,4,128]{2,1,0:T(4,128)} %bitcast.15), calls=%async_computation | async-start | bytes 524288 | tf_op jit(solution)/shard_map/all_to_all | solution.py:589
  80.5 0.0 copy-start.3
  80.5 0.9 copy-done.3
  81.5 0.0 copy-start.7
  81.5 0.8 copy-done.7
  82.3 0.0 copy-start.8
  82.3 0.8 copy-done.8
  83.1 0.2 matrices.1
  83.3 8.0 %all-to-all-done = f32[128,4,128]{2,1,0:T(4,128)} async-done(((f32[128,4,128]{2,1,0:T(4,128)}), f32[128,4,128]{2,1,0:T(4,128)}, u32[]{:S(2)}, u32[]{:S(2)}) %all-to-all-start) | async-done | bytes 262176 | tf_op jit(solution)/shard_map/all_to_all | solution.py:589
  91.3 0.0 copy-start.6
  91.3 0.7 copy-done.6
  92.0 2.1 %plan.1 = (s32[8,288]{1,0:T(8,128)S(1)}, f32[288,8]{1,0:T(8,128)S(1)}) custom-call(f32[512,128]{1,0:T(8,128)} %bitcast.3.arrived, s32[32,128]{1,0:T(8,128)S(1)} %bitcast.24, f32[32,128]{1,0:T(8,128)S(1)} %bitcast.25), custom_call_target="tpu_custom_call" | custom-call | tf_op jit(solution)/shard_map/plan/pallas_call | solution.py:287
  94.2 0.0 collective-permute-done.4.before_ends
  94.2 0.0 collective-permute-done.5.after_ends
  94.2 0.0 collective-permute-done.3.after
  94.2 0.0 collective-permute-done.2.before
  94.2 0.0 copy-done
  94.2 6.2 %halo.1 = (f32[2,42,32,256]{3,2,1,0:T(8,128)S(1)}, f32[42,32,256]{2,1,0:T(8,128)S(1)}, f32[3,42,32,256]{3,2,1,0:T(8,128)S(1)}, f32[2,42,32,256]{3,2,1,0:T(8,128)...) custom-call(s32[8,288]{1,0:T(8,128)S(1)} %get-tuple-element.62.found.table, f32[288,8]{1,0:T(8,128)S(1)} %get-tuple-element.63.columns, ...), custom_call_target="tpu_custom_call" | custom-call | tf_op jit(solution)/shard_map/halo/pallas_call | solution.py:354
  100.4 0.0 copy-start.9
  100.4 0.0 copy-start.12
  100.4 4.6 %field.5 = (f32[2,42,32,256]{3,2,1,0:T(8,128)S(1)}, f32[42,32,256]{2,1,0:T(8,128)S(1)}, f32[3,42,32,256]{3,2,1,0:T(8,128)S(1)}) custom-call(f32[2,42,32,256]{3,2,1,0:T(8,128)S(1)} %get-tuple-element.69.media, f32[2,42,32,256]{3,2,1,0:T(8,128)S(1)} %get-tuple-element.70.e_xy, f32[42,32,256]{2,1,0:T(8,128)S(1)} %get-tuple-element.71.e_z, ...), custom_call_target="tpu_custom_call" | custom-call | tf_op jit(solution)/shard_map/field/pallas_call | solution.py:433
  105.0 0.0 copy-done.9
  105.0 0.0 copy-done.12
  105.0 3.7 %circuit.4 = (f32[42,32,256]{2,1,0:T(8,128)S(1)}, f32[256,128]{1,0:T(8,128)S(1)}, f32[1,128]{1,0:T(1,128)S(1)}, f32[288,1]{1,0:T(8,128)S(1)}) custom-call(s32[8,288]{1,0:T(8,128)S(1)} %get-tuple-element.62.found.table, s32[2,4]{1,0:T(2,128)S(1)} %copy-done.9, f32[512,128]{1,0:T(8,128)} %bitcast.3.arrived, f32[288,8]{1,0:T(8,128)S(1)} %get-tuple-element.63.columns, ...), custom_call_target="tpu_custom_call" | custom-call | tf_op jit(solution)/shard_map/circuit/pallas_call | solution.py:516
  108.7 15.2 %all_to_all.60 = f32[128,2,128]{2,1,0:T(2,128)S(1)} all-to-all(f32[128,2,128]{2,1,0:T(2,128)S(1)} %bitcast.23), channel_id=1, replica_groups=mesh['gz'=16,'gy'=8] {'gz','gy'}, dimensions={0} | all-to-all | bytes 262144 | tf_op jit(solution)/shard_map/all_to_all | solution.py:589
  123.9 4.4 %field.6 = (f32[2,42,32,256]{3,2,1,0:T(8,128)S(1)}, f32[42,32,256]{2,1,0:T(8,128)S(1)}, f32[3,42,32,256]{3,2,1,0:T(8,128)S(1)}) custom-call(f32[2,42,32,256]{3,2,1,0:T(8,128)S(1)} %get-tuple-element.69.media, f32[2,42,32,256]{3,2,1,0:T(8,128)S(1)} %get-tuple-element.79.e_xy, f32[42,32,256]{2,1,0:T(8,128)S(1)} %get-tuple-element.80.e_z, ...), custom_call_target="tpu_custom_call" | custom-call | tf_op jit(solution)/shard_map/field/pallas_call | solution.py:433
  128.3 3.4 %circuit.5 = (f32[42,32,256]{2,1,0:T(8,128)S(1)}, f32[256,128]{1,0:T(8,128)S(1)}, f32[1,128]{1,0:T(1,128)S(1)}, f32[288,1]{1,0:T(8,128)S(1)}) custom-call(s32[8,288]{1,0:T(8,128)S(1)} %get-tuple-element.62.found.table, s32[2,4]{1,0:T(2,128)S(1)} %copy-done.9, f32[256,128]{1,0:T(8,128)S(1)} %bitcast.16, f32[288,8]{1,0:T(8,128)S(1)} %get-tuple-element.63.columns, ...), custom_call_target="tpu_custom_call" | custom-call | tf_op jit(solution)/shard_map/circuit/pallas_call | solution.py:516
  131.7 14.7 %all_to_all.61 = f32[128,2,128]{2,1,0:T(2,128)S(1)} all-to-all(f32[128,2,128]{2,1,0:T(2,128)S(1)} %bitcast.20), channel_id=1, replica_groups=mesh['gz'=16,'gy'=8] {'gz','gy'}, dimensions={0} | all-to-all | bytes 262144 | tf_op jit(solution)/shard_map/all_to_all | solution.py:589
  146.4 4.1 %field.7 = (f32[2,42,32,256]{3,2,1,0:T(8,128)S(1)}, f32[42,32,256]{2,1,0:T(8,128)S(1)}, f32[3,42,32,256]{3,2,1,0:T(8,128)S(1)}) custom-call(f32[2,42,32,256]{3,2,1,0:T(8,128)S(1)} %get-tuple-element.69.media, f32[2,42,32,256]{3,2,1,0:T(8,128)S(1)} %get-tuple-element.88.e_xy, f32[42,32,256]{2,1,0:T(8,128)S(1)} %get-tuple-element.89.e_z, ...), custom_call_target="tpu_custom_call" | custom-call | tf_op jit(solution)/shard_map/field/pallas_call | solution.py:433
  150.5 3.4 %circuit.6 = (f32[42,32,256]{2,1,0:T(8,128)S(1)}, f32[256,128]{1,0:T(8,128)S(1)}, f32[1,128]{1,0:T(1,128)S(1)}, f32[288,1]{1,0:T(8,128)S(1)}) custom-call(s32[8,288]{1,0:T(8,128)S(1)} %get-tuple-element.62.found.table, s32[2,4]{1,0:T(2,128)S(1)} %copy-done.9, f32[256,128]{1,0:T(8,128)S(1)} %bitcast.17, f32[288,8]{1,0:T(8,128)S(1)} %get-tuple-element.63.columns, ...), custom_call_target="tpu_custom_call" | custom-call | tf_op jit(solution)/shard_map/circuit/pallas_call | solution.py:516
  154.0 14.7 %all_to_all.62 = f32[128,2,128]{2,1,0:T(2,128)S(1)} all-to-all(f32[128,2,128]{2,1,0:T(2,128)S(1)} %bitcast.21), channel_id=1, replica_groups=mesh['gz'=16,'gy'=8] {'gz','gy'}, dimensions={0} | all-to-all | bytes 262144 | tf_op jit(solution)/shard_map/all_to_all | solution.py:589
  168.6 3.9 %field.8 = (f32[2,42,32,256]{3,2,1,0:T(8,128)S(1)}, f32[42,32,256]{2,1,0:T(8,128)S(1)}, f32[3,42,32,256]{3,2,1,0:T(8,128)S(1)}) custom-call(f32[2,42,32,256]{3,2,1,0:T(8,128)S(1)} %get-tuple-element.69.media, f32[2,42,32,256]{3,2,1,0:T(8,128)S(1)} %get-tuple-element.97.e_xy, f32[42,32,256]{2,1,0:T(8,128)S(1)} %get-tuple-element.98.e_z, ...), custom_call_target="tpu_custom_call" | custom-call | tf_op jit(solution)/shard_map/field/pallas_call | solution.py:433
  172.5 3.4 %circuit.7 = (f32[42,32,256]{2,1,0:T(8,128)S(1)}, f32[256,128]{1,0:T(8,128)S(1)}, f32[1,128]{1,0:T(1,128)S(1)}, f32[288,1]{1,0:T(8,128)S(1)}) custom-call(s32[8,288]{1,0:T(8,128)S(1)} %get-tuple-element.62.found.table, s32[2,4]{1,0:T(2,128)S(1)} %copy-done.9, f32[256,128]{1,0:T(8,128)S(1)} %bitcast.18, f32[288,8]{1,0:T(8,128)S(1)} %get-tuple-element.63.columns, ...), custom_call_target="tpu_custom_call" | custom-call | tf_op jit(solution)/shard_map/circuit/pallas_call | solution.py:516
  176.0 14.7 %all_to_all.63 = f32[128,2,128]{2,1,0:T(2,128)S(1)} all-to-all(f32[128,2,128]{2,1,0:T(2,128)S(1)} %bitcast.22), channel_id=1, replica_groups=mesh['gz'=16,'gy'=8] {'gz','gy'}, dimensions={0} | all-to-all | bytes 262144 | tf_op jit(solution)/shard_map/all_to_all | solution.py:589
  190.6 3.7 %field.9 = (f32[2,42,32,256]{3,2,1,0:T(8,128)S(1)}, f32[42,32,256]{2,1,0:T(8,128)S(1)}, f32[3,42,32,256]{3,2,1,0:T(8,128)S(1)}) custom-call(f32[2,42,32,256]{3,2,1,0:T(8,128)S(1)} %get-tuple-element.69.media, f32[2,42,32,256]{3,2,1,0:T(8,128)S(1)} %get-tuple-element.106.e_xy, f32[42,32,256]{2,1,0:T(8,128)S(1)} %get-tuple-element.107.e_z, ...), custom_call_target="tpu_custom_call" | custom-call | tf_op jit(solution)/shard_map/field/pallas_call | solution.py:433
  194.3 3.6 %finish.1 = (f32[3,32,16,256]{3,2,1,0:T(8,128)}, f32[3,32,16,256]{3,2,1,0:T(8,128)}, f32[1,128]{1,0:T(1,128)}) custom-call(s32[8,288]{1,0:T(8,128)S(1)} %get-tuple-element.62.found.table, s32[2,4]{1,0:T(2,128)S(1)} %copy-done.9, f32[256,128]{1,0:T(8,128)S(1)} %bitcast.19, f32[288,8]{1,0:T(8,128)S(1)} %get-tuple-element.63.columns, ...), custom_call_target="tpu_custom_call" | custom-call | tf_op jit(solution)/shard_map/finish/pallas_call | solution.py:559
  (1 shorter events, 0.0 us)
Async XLA Ops:
  0.6 0.7 copy-start.10
  5.2 89.0 %collective-permute-start.3 = (f32[32,40,256]{2,1,0:T(8,128)S(1)}, f32[32,40,256]{2,1,0:T(8,128)}, u32[]{:S(2)}, u32[]{:S(2)}) collective-permute-start(f32[32,40,256]{2,1,0:T(8,128)S(1)} %strip.3.after), channel_id=1, source_target_pairs={{1,0},{2,1},{3,2},{4,3},{5,4},{6,5},{7,6},{9,8},{10,9},{11,10},{12... | collective-permute-start | bytes 3932168 | tf_op jit(solution)/shard_map/ppermute | solution.py:585
  6.5 87.7 %collective-permute-start.2 = (f32[32,40,256]{2,1,0:T(8,128)S(1)}, f32[32,40,256]{2,1,0:T(8,128)}, u32[]{:S(2)}, u32[]{:S(2)}) collective-permute-start(f32[32,40,256]{2,1,0:T(8,128)S(1)} %strip.2.after), channel_id=1, source_target_pairs={{0,1},{1,2},{2,3},{3,4},{4,5},{5,6},{6,7},{8,9},{9,10},{10,11},{11... | collective-permute-start | bytes 3932168 | tf_op jit(solution)/shard_map/ppermute | solution.py:585
  13.8 7.4 %copy-start.4 = (s32[4096]{0:T(1024)S(1)}, s32[4096]{0:T(1024)}, u32[]{:S(2)}) copy-start(s32[4096]{0:T(1024)} %nodes.1) | copy-start | bytes 49156
  13.8 7.4 %copy-start.5 = (f32[4096]{0:T(1024)S(1)}, f32[4096]{0:T(1024)}, u32[]{:S(2)}) copy-start(f32[4096]{0:T(1024)} %gains.1) | copy-start | bytes 49156
  13.8 7.4 %copy-start.11 = (f32[128]{0:T(128)S(1)}, f32[128]{0:T(128)}, u32[]{:S(2)}) copy-start(f32[128]{0:T(128)} %param.23) | copy-start | bytes 1540
  13.8 7.4 %copy-start.13 = (s32[32]{0:T(128)S(1)}, s32[32]{0:T(128)}, u32[]{:S(2)}) copy-start(s32[32]{0:T(128)} %cells.1) | copy-start | bytes 388
  15.1 12.8 %collective-permute-start.1 = (f32[40,16,256]{2,1,0:T(8,128)S(1)}, f32[40,16,256]{2,1,0:T(8,128)S(1)}, u32[]{:S(2)}, u32[]{:S(2)}) collective-permute-start(f32[40,16,256]{2,1,0:T(8,128)S(1)} %slab.3.after), channel_id=1, source_target_pairs={{8,0},{16,8},{24,16},{32,24},{40,32},{48,40},{56,48},{64,56},{72,6... | collective-permute-start | bytes 1966088 | tf_op jit(solution)/shard_map/ppermute | solution.py:585
  18.0 16.3 %collective-permute-start = (f32[40,16,256]{2,1,0:T(8,128)S(1)}, f32[40,16,256]{2,1,0:T(8,128)S(1)}, u32[]{:S(2)}, u32[]{:S(2)}) collective-permute-start(f32[40,16,256]{2,1,0:T(8,128)S(1)} %slab.2.after), channel_id=1, source_target_pairs={{0,8},{8,16},{16,24},{24,32},{32,40},{40,48},{48,56},{56,64},{64,7... | collective-permute-start | bytes 1966088 | tf_op jit(solution)/shard_map/ppermute | solution.py:585
  23.9 16.9 %copy-start.2 = (f32[512,128]{1,0:T(8,128)}, f32[512,128]{1,0:T(8,128)S(1)}, u32[]{:S(2)}) copy-start(f32[512,128]{1,0:T(8,128)S(1)} %begin.1.after) | copy-start | bytes 786436
  27.9 66.3 %copy-start = (f32[40,16,256]{2,1,0:T(8,128)}, f32[40,16,256]{2,1,0:T(8,128)S(1)}, u32[]{:S(2)}) copy-start(f32[40,16,256]{2,1,0:T(8,128)S(1)} %collective-permute-done.1.upper) | copy-start | bytes 1966084
  35.4 0.8 copy-start.1
  36.2 58.0 %collective-permute-start.4 = (f32[10,40,256]{2,1,0:T(8,128)}, f32[10,40,256]{2,1,0:T(8,128)}, u32[]{:S(2)}, u32[]{:S(2)}) collective-permute-start(f32[10,40,256]{2,1,0:T(8,128)} %get-tuple-element.59), channel_id=1, source_target_pairs={{0,1},{1,2},{2,3},{3,4},{4,5},{5,6},{6,7},{8,9},{9,10},{10,11},{11... | collective-permute-start | bytes 1228808 | tf_op jit(solution)/shard_map/ppermute | solution.py:585
  39.5 54.7 %collective-permute-start.5 = (f32[10,40,256]{2,1,0:T(8,128)}, f32[10,40,256]{2,1,0:T(8,128)}, u32[]{:S(2)}, u32[]{:S(2)}) collective-permute-start(f32[10,40,256]{2,1,0:T(8,128)} %get-tuple-element.60), channel_id=1, source_target_pairs={{1,0},{2,1},{3,2},{4,3},{5,4},{6,5},{7,6},{9,8},{10,9},{11,10},{12... | collective-permute-start | bytes 1228808 | tf_op jit(solution)/shard_map/ppermute | solution.py:585
  40.8 50.6 %all-to-all-start = ((f32[128,4,128]{2,1,0:T(4,128)}), f32[128,4,128]{2,1,0:T(4,128)}, u32[]{:S(2)}, u32[]{:S(2)}) async-start(f32[128,4,128]{2,1,0:T(4,128)} %bitcast.15), calls=%async_computation | async-start | bytes 524288 | tf_op jit(solution)/shard_map/all_to_all | solution.py:589
  80.5 1.0 copy-start.3
  81.5 0.8 copy-start.7
  82.3 0.8 copy-start.8
  91.3 0.7 copy-start.6
  100.4 4.6 %copy-start.9 = (s32[2,4]{1,0:T(2,128)S(1)}, s32[2,4]{1,0:T(2,128)}, u32[]{:S(2)}) copy-start(s32[2,4]{1,0:T(2,128)} %off_cols.9) | copy-start | bytes 100
  100.4 4.6 %copy-start.12 = (f32[128]{0:T(128)S(1)}, f32[128]{0:T(128)}, u32[]{:S(2)}) copy-start(f32[128]{0:T(128)} %param.23) | copy-start | bytes 1540

commit v6 on v5

--- a/solution.py
+++ b/solution.py
@@ -24,7 +24,7 @@
 STRIP = PARTS * DEPTH
 SIDES = ((0, 0), (-1, 0), (1, 0), (0, -1), (-1, -1), (1, -1), (0, 1), (-1, 1), (1, 1))
 REACH = len(SIDES) * PORT_DEV
-SPOTS, NODES, COUNT = 0, 1, 7
+NODES, COUNT = REACH, 2 * REACH
 
 time_step = 0.55
 charge_scale = 4.0
@@ -335,7 +335,7 @@
     def _(layer):
         media[1, layer] = 1.0 - media[1, layer]
 
-    @pl.loop(0, found[COUNT, 0])
+    @pl.loop(0, found[COUNT])
     def _(group):
         part = pl.ds(pl.multiple_of(group * PORT_DEV, PORT_DEV), PORT_DEV)
         _, place, _ = columns_at(columns, part)
@@ -345,7 +345,7 @@
 
 def gather_cells(source, found, group, place, picked):
     for port in range(PORT_DEV):
-        spot = found[SPOTS, group * PORT_DEV + port]
+        spot = found[group * PORT_DEV + port]
         picked[port : port + 1, :] = source[spot // TALL, pl.ds(spot % TALL, 1), :]
     return pick(picked[...], place)
 
@@ -474,18 +474,18 @@
 
 
 def apply_ports(stride, table, arrived, columns, sample, coef, e_z, near_rows, deltas):
-    @pl.loop(0, table[COUNT, 0])
+    @pl.loop(0, table[COUNT])
     def _(group):
         first = group * PORT_DEV
         part = pl.ds(pl.multiple_of(first, PORT_DEV), PORT_DEV)
         for port in range(PORT_DEV):
-            near_at = table[NODES, first + port] * stride
+            near_at = table[NODES + first + port] * stride
             near_rows[port : port + 1, :] = arrived[pl.ds(near_at, 1), :]
         gain, place, lane = columns_at(columns, part)
         current = gain * (sample[part, :] - pick(near_rows[...], lane))
         deltas[...] = spread(-coef[part, :] * current, place, NX)
         for port in range(PORT_DEV):
-            spot = table[SPOTS, first + port]
+            spot = table[first + port]
             layer, row = spot // TALL, pl.ds(spot % TALL, 1)
             e_z[layer, row, :] = e_z[layer, row, :] + deltas[port : port + 1, :]
 
@@ -497,7 +497,7 @@
     e_z[...] = e_in[...]
     apply_ports(stride, table, arrived, columns, sample, coef, e_z, near_rows, deltas)
 
-    @pl.loop(0, table[COUNT, 0])
+    @pl.loop(0, table[COUNT])
     def _(group):
         part = pl.ds(pl.multiple_of(group * PORT_DEV, PORT_DEV), PORT_DEV)
         _, place, _ = columns_at(columns, part)
@@ -509,7 +509,7 @@
     gain, _, lane = columns_at(columns, own)
     spread_rows[...] = spread(gain * sample_out[own, :], lane, NODE_DEV)
     out[...] = jnp.where(row_kind(out.shape, 2) == 0, solved, 0.0)
-    add_rows(out, 2, [table[NODES, port] for port in range(PORT_DEV)], spread_rows)
+    add_rows(out, 2, [table[NODES + port] for port in range(PORT_DEV)], spread_rows)
 
 
 def circuit(table, off_cols, arrived, columns, sample, coef, volts, mats, e_z):
@@ -606,15 +606,15 @@
     n_gz, n_gy = lax.axis_size("gz"), lax.axis_size("gy")
     grids = (e_field, h_field, e_coef, e_loss)
     volts = volts_init.reshape(1, NODE_DEV)
-    front = strip_of(True, grids, volts)
+    up = slab_of(True, grids, volts)
+    lower = shifted(up, "gz", 1)
+    down = slab_of(False, grids, up)
+    upper = shifted(down, "gz", -1)
+    front = strip_of(True, grids, down)
     before = shifted(front, "gy", 1)
     back = strip_of(False, grids, front)
     after = shifted(back, "gy", -1)
-    up = slab_of(True, grids, back)
-    lower = shifted(up, "gz", 1)
-    down = slab_of(False, grids, up)
-    upper = shifted(down, "gz", -1)
-    out = begin(n_gy, port_cell, port_node, port_gain, e_field, volts, down)
+    out = begin(n_gy, port_cell, port_node, port_gain, e_field, volts, back)
     arrived = exchange(out)
     front_ends, back_ends = corners(lower, upper, out)
     before_ends = shifted(front_ends, "gy", 1)
@@ -623,7 +623,8 @@
     sides = (before, after, before_ends, after_ends)
     mats = matrices(diag_blocks, inv_blocks, off_blocks)
 
-    table, columns = plan(n_gz, n_gy, arrived, port_node, port_gain)
+    found, columns = plan(n_gz, n_gy, arrived, port_node, port_gain)
+    table = jnp.concatenate([found[0], found[1], found[7, 0:1]])
 
     e_xy, e_z, h, media, sample, coef = halo(table, columns, lower, upper, sides, *grids)
     for step in range(1, STEPS + 1):

time: 199 us -> 196 us (0.985)
  starting transfers between devices: 57.7 us -> 30.6 us
  blocking collectives: 59.2 us -> 77.2 us
    all_to_all x1, starting transfers between devices: 39.7 us -> 11.7 us  [exchange(): return lax.all_to_all(value, ('gz', 'gy'), 0, 0, tiled=True)]
    all_to_all x4, blocking collectives: 59.2 us -> 77.2 us  [exchange(): return lax.all_to_all(value, ('gz', 'gy'), 0, 0, tiled=True)]
    all_to_all x1, waiting for transfers between devices: 8.02 us -> 19.6 us  [exchange(): return lax.all_to_all(value, ('gz', 'gy'), 0, 0, tiled=True)]
    ppermute x6, waiting for transfers between devices: 10.5 us -> 0.02 us  [shifted(): lax.ppermute(value, axis, [(source, source + steps) for source in range(f...]
  transfers between devices with their start and end apart: 7 -> 7, of which waited for: 3 -> 1; matrix products, arithmetic and copies ran while one was open for 0% -> 1% of each run, Pallas kernels for 4% -> 4%
where the time goes in v6:
time: 196 us; the launch traced here: 194 us
  blocking collectives  77.2 us (39%)
  Pallas kernels  58.6 us (30%)
  starting transfers between devices  30.6 us (16%)
  waiting for transfers between devices  19.6 us (10%)
  local copies, waits for them, and re-layouts  6.46 us (3%)
    all_to_all x4, blocking collectives, exchange(): return lax.all_to_all(value, ('gz', 'gy'), 0, 0, tiled=True)  77.2 us
    pallas_call x5, Pallas kernels, field(): pl.pallas_call(functools.partial(field_kernel, step), name='field', out_s...  20.7 us
    all_to_all x1, waiting for transfers between devices, exchange(): return lax.all_to_all(value, ('gz', 'gy'), 0, 0, tiled=True)  19.6 us
    ppermute x6, starting transfers between devices, shifted(): lax.ppermute(value, axis, [(source, source + steps) for source in range(f...  18.9 us
    pallas_call x4, Pallas kernels, circuit(): pl.pallas_call(functools.partial(circuit_kernel, arrived.shape[0] // ND),...  13.2 us
    all_to_all x1, starting transfers between devices, exchange(): return lax.all_to_all(value, ('gz', 'gy'), 0, 0, tiled=True)  11.7 us
    pallas_call x1, Pallas kernels, halo(): pl.pallas_call(halo_kernel, name='halo', out_shape=(onchip((2,) + CUBE),...  6.07 us
    unnamed x28, local copies, waits for them, and re-layouts  5.89 us
  transfers between devices with their start and end apart: 7, of which 1 were waited for; matrix products, arithmetic and copies ran while one was open for 1% of the time, Pallas kernels for 4%

profile of v6, /device:TPU:1, one launch (start us, length us, event | category | flops | bytes accessed | tf_op | source)
XLA Modules:
  0.0 194.1 jit_solution(9793836227365595124)
XLA Ops:
  0.6 0.0 copy-start.10
  0.6 0.6 copy-done.10
  1.3 2.1 %slab.2.after = f32[40,16,256]{2,1,0:T(8,128)} custom-call(f32[3,32,16,256]{3,2,1,0:T(8,128)} %e_in.11, f32[3,32,16,256]{3,2,1,0:T(8,128)} %h_in.9, f32[32,16,256]{2,1,0:T(8,128)} %coef_in.9, f32[32,16,256]{2,1,0:T(8,128)} %loss_in.9, f32[1,128]{1,0:T(1,128)S(1)} %bitcast.27), custom_call_target="tpu_custom_call" | custom-call | tf_op jit(solution)/shard_map/slab/pallas_call | solution.py:139
  3.4 2.1 %slab.3.after = f32[40,16,256]{2,1,0:T(8,128)} custom-call(f32[3,32,16,256]{3,2,1,0:T(8,128)} %e_in.11, f32[3,32,16,256]{3,2,1,0:T(8,128)} %h_in.9, f32[32,16,256]{2,1,0:T(8,128)} %coef_in.9, f32[32,16,256]{2,1,0:T(8,128)} %loss_in.9, f32[40,16,256]{2,1,0:T(8,128)} %slab.2.after), custom_call_target="tpu_custom_call" | custom-call | tf_op jit(solution)/shard_map/slab/pallas_call | solution.py:139
  5.4 1.9 strip.2.after
  7.4 0.0 copy-start.4
  7.4 0.0 copy-start.5
  7.4 0.0 copy-start.11
  7.4 0.0 copy-start.13
  7.4 1.9 %strip.3.after = f32[32,40,256]{2,1,0:T(8,128)S(1)} custom-call(f32[3,32,16,256]{3,2,1,0:T(8,128)} %e_in.11, f32[3,32,16,256]{3,2,1,0:T(8,128)} %h_in.9, f32[32,16,256]{2,1,0:T(8,128)} %coef_in.9, f32[32,16,256]{2,1,0:T(8,128)} %loss_in.9, f32[32,40,256]{2,1,0:T(8,128)S(1)} %strip.2.after), custom_call_target="tpu_custom_call" | custom-call | tf_op jit(solution)/shard_map/strip/pallas_call | solution.py:118
  9.4 1.3 collective-permute-start.3
  10.7 6.1 %collective-permute-start.2 = (f32[32,40,256]{2,1,0:T(8,128)S(1)}, f32[32,40,256]{2,1,0:T(8,128)}, u32[]{:S(2)}, u32[]{:S(2)}) collective-permute-start(f32[32,40,256]{2,1,0:T(8,128)S(1)} %strip.2.after), channel_id=1, source_target_pairs={{0,1},{1,2},{2,3},{3,4},{4,5},{5,6},{6,7},{8,9},{9,10},{10,11},{11... | collective-permute-start | bytes 3932168 | tf_op jit(solution)/shard_map/ppermute | solution.py:585
  16.8 2.9 %collective-permute-start.1 = (f32[40,16,256]{2,1,0:T(8,128)}, f32[40,16,256]{2,1,0:T(8,128)S(1)}, u32[]{:S(2)}, u32[]{:S(2)}) collective-permute-start(f32[40,16,256]{2,1,0:T(8,128)} %slab.3.after), channel_id=1, source_target_pairs={{8,0},{16,8},{24,16},{32,24},{40,32},{48,40},{56,48},{64,56},{72,6... | collective-permute-start | bytes 1966088 | tf_op jit(solution)/shard_map/ppermute | solution.py:585
  19.7 3.2 %collective-permute-start = (f32[40,16,256]{2,1,0:T(8,128)}, f32[40,16,256]{2,1,0:T(8,128)}, u32[]{:S(2)}, u32[]{:S(2)}) collective-permute-start(f32[40,16,256]{2,1,0:T(8,128)} %slab.2.after), channel_id=1, source_target_pairs={{0,8},{8,16},{16,24},{24,32},{32,40},{40,48},{48,56},{56,64},{64,7... | collective-permute-start | bytes 1966088 | tf_op jit(solution)/shard_map/ppermute | solution.py:585
  22.9 0.0 copy-done.4
  22.9 0.0 copy-done.5
  22.9 0.0 copy-done.11
  22.9 0.0 copy-done.13
  22.9 2.7 %begin.1.after = f32[512,128]{1,0:T(8,128)S(1)} custom-call(s32[32]{0:T(128)S(1)} %copy-done.13, s32[4096]{0:T(1024)S(1)} %copy-done.4, f32[4096]{0:T(1024)S(1)} %copy-done.5, f32[3,32,16,256]{3,2,1,0:T(8,128)} %e_in.11, s32[1,32]{1,0:T(1,128)S(1)} %bitcast.30, f32[1,128]{1,0:T(1,128)S(1)} %bitcast.28, f32[32,40,256]{2,1,0:T(8,128)S(1)} %strip.3.after), custom_call_target="tpu_custom_call" | custom-call | tf_op jit(solution)/shard_map/begin/pallas_call | solution.py:176
  25.6 0.0 copy-start.1
  25.6 0.7 copy-done.1
  26.3 11.7 %all-to-all-start = ((f32[128,4,128]{2,1,0:T(4,128)}), f32[128,4,128]{2,1,0:T(4,128)}, u32[]{:S(2)}, u32[]{:S(2)}) async-start(f32[128,4,128]{2,1,0:T(4,128)} %bitcast.16), calls=%async_computation | async-start | bytes 524288 | tf_op jit(solution)/shard_map/all_to_all | solution.py:589
  38.0 0.0 collective-permute-done.1.upper
  38.0 0.0 copy-start
  38.0 0.0 collective-permute-done.lower
  38.0 0.0 copy-start.2
  38.0 1.2 copy-done.2
  39.2 2.1 %corners.1 = (f32[10,40,256]{2,1,0:T(8,128)}, f32[10,40,256]{2,1,0:T(8,128)}) custom-call(f32[40,16,256]{2,1,0:T(8,128)} %collective-permute-done.lower, f32[40,16,256]{2,1,0:T(8,128)S(1)} %collective-permute-done.1.upper, f32[512,128]{1,0:T(8,128)S(1)} %copy-done.2), custom_call_target="tpu_custom_call" | custom-call | tf_op jit(solution)/shard_map/corners/pallas_call | solution.py:228
  41.3 4.2 %collective-permute-start.4 = (f32[10,40,256]{2,1,0:T(8,128)}, f32[10,40,256]{2,1,0:T(8,128)}, u32[]{:S(2)}, u32[]{:S(2)}) collective-permute-start(f32[10,40,256]{2,1,0:T(8,128)} %get-tuple-element.59), channel_id=1, source_target_pairs={{0,1},{1,2},{2,3},{3,4},{4,5},{5,6},{6,7},{8,9},{9,10},{10,11},{11... | collective-permute-start | bytes 1228808 | tf_op jit(solution)/shard_map/ppermute | solution.py:585
  45.5 1.3 collective-permute-start.5
  46.8 0.0 copy-start.3
  46.8 0.9 copy-done.3
  47.7 0.8 copy-done.7
  48.6 0.8 copy-done.8
  49.4 0.2 matrices.1
  49.6 19.6 %all-to-all-done = f32[128,4,128]{2,1,0:T(4,128)} async-done(((f32[128,4,128]{2,1,0:T(4,128)}), f32[128,4,128]{2,1,0:T(4,128)}, u32[]{:S(2)}, u32[]{:S(2)}) %all-to-all-start) | async-done | bytes 262176 | tf_op jit(solution)/shard_map/all_to_all | solution.py:589
  69.2 0.7 copy-done.6
  69.9 2.1 %plan.1 = (s32[8,288]{1,0:T(8,128)S(1)}, f32[288,8]{1,0:T(8,128)S(1)}) custom-call(f32[512,128]{1,0:T(8,128)} %bitcast.3.arrived, s32[32,128]{1,0:T(8,128)S(1)} %bitcast.25, f32[32,128]{1,0:T(8,128)S(1)} %bitcast.26), custom_call_target="tpu_custom_call" | custom-call | tf_op jit(solution)/shard_map/plan/pallas_call | solution.py:287
  72.0 0.5 slice.11
  72.6 0.7 pad_add_fusion.found.table
  73.3 0.0 collective-permute-done.4.before_ends
  73.3 0.0 collective-permute-done.5.after_ends
  73.3 0.0 collective-permute-done.3.after
  73.3 0.0 collective-permute-done.2.before
  73.3 0.0 copy-done
  73.4 6.1 %halo.1 = (f32[2,42,32,256]{3,2,1,0:T(8,128)S(1)}, f32[42,32,256]{2,1,0:T(8,128)S(1)}, f32[3,42,32,256]{3,2,1,0:T(8,128)S(1)}, f32[2,42,32,256]{3,2,1,0:T(8,128)...) custom-call(s32[577]{0:T(1024)S(1)} %pad_add_fusion.found.table, f32[288,8]{1,0:T(8,128)S(1)} %get-tuple-element.63.columns, ...), custom_call_target="tpu_custom_call" | custom-call | tf_op jit(solution)/shard_map/halo/pallas_call | solution.py:354
  79.4 0.0 copy-start.9
  79.4 0.0 copy-start.12
  79.5 4.6 %field.5 = (f32[2,42,32,256]{3,2,1,0:T(8,128)S(1)}, f32[42,32,256]{2,1,0:T(8,128)S(1)}, f32[3,42,32,256]{3,2,1,0:T(8,128)S(1)}) custom-call(f32[2,42,32,256]{3,2,1,0:T(8,128)S(1)} %get-tuple-element.69.media, f32[2,42,32,256]{3,2,1,0:T(8,128)S(1)} %get-tuple-element.70.e_xy, f32[42,32,256]{2,1,0:T(8,128)S(1)} %get-tuple-element.71.e_z, ...), custom_call_target="tpu_custom_call" | custom-call | tf_op jit(solution)/shard_map/field/pallas_call | solution.py:433
  84.1 0.0 copy-done.9
  84.1 0.0 copy-done.12
  84.1 3.6 %circuit.4 = (f32[42,32,256]{2,1,0:T(8,128)S(1)}, f32[256,128]{1,0:T(8,128)S(1)}, f32[1,128]{1,0:T(1,128)S(1)}, f32[288,1]{1,0:T(8,128)S(1)}) custom-call(s32[577]{0:T(1024)S(1)} %pad_add_fusion.found.table, s32[2,4]{1,0:T(2,128)S(1)} %copy-done.9, f32[512,128]{1,0:T(8,128)} %bitcast.3.arrived, f32[288,8]{1,0:T(8,128)S(1)} %get-tuple-element.63.columns, ...), custom_call_target="tpu_custom_call" | custom-call | tf_op jit(solution)/shard_map/circuit/pallas_call | solution.py:516
  87.7 34.4 %all_to_all.60 = f32[128,2,128]{2,1,0:T(2,128)S(1)} all-to-all(f32[128,2,128]{2,1,0:T(2,128)S(1)} %bitcast.24), channel_id=1, replica_groups=mesh['gz'=16,'gy'=8] {'gz','gy'}, dimensions={0} | all-to-all | bytes 262144 | tf_op jit(solution)/shard_map/all_to_all | solution.py:589
  122.1 4.4 %field.6 = (f32[2,42,32,256]{3,2,1,0:T(8,128)S(1)}, f32[42,32,256]{2,1,0:T(8,128)S(1)}, f32[3,42,32,256]{3,2,1,0:T(8,128)S(1)}) custom-call(f32[2,42,32,256]{3,2,1,0:T(8,128)S(1)} %get-tuple-element.69.media, f32[2,42,32,256]{3,2,1,0:T(8,128)S(1)} %get-tuple-element.79.e_xy, f32[42,32,256]{2,1,0:T(8,128)S(1)} %get-tuple-element.80.e_z, ...), custom_call_target="tpu_custom_call" | custom-call | tf_op jit(solution)/shard_map/field/pallas_call | solution.py:433
  126.5 3.2 %circuit.5 = (f32[42,32,256]{2,1,0:T(8,128)S(1)}, f32[256,128]{1,0:T(8,128)S(1)}, f32[1,128]{1,0:T(1,128)S(1)}, f32[288,1]{1,0:T(8,128)S(1)}) custom-call(s32[577]{0:T(1024)S(1)} %pad_add_fusion.found.table, s32[2,4]{1,0:T(2,128)S(1)} %copy-done.9, f32[256,128]{1,0:T(8,128)S(1)} %bitcast.18, f32[288,8]{1,0:T(8,128)S(1)} %get-tuple-element.63.columns, ...), custom_call_target="tpu_custom_call" | custom-call | tf_op jit(solution)/shard_map/circuit/pallas_call | solution.py:516
  129.7 14.2 %all_to_all.61 = f32[128,2,128]{2,1,0:T(2,128)S(1)} all-to-all(f32[128,2,128]{2,1,0:T(2,128)S(1)} %bitcast.21), channel_id=1, replica_groups=mesh['gz'=16,'gy'=8] {'gz','gy'}, dimensions={0} | all-to-all | bytes 262144 | tf_op jit(solution)/shard_map/all_to_all | solution.py:589
  143.9 4.1 %field.7 = (f32[2,42,32,256]{3,2,1,0:T(8,128)S(1)}, f32[42,32,256]{2,1,0:T(8,128)S(1)}, f32[3,42,32,256]{3,2,1,0:T(8,128)S(1)}) custom-call(f32[2,42,32,256]{3,2,1,0:T(8,128)S(1)} %get-tuple-element.69.media, f32[2,42,32,256]{3,2,1,0:T(8,128)S(1)} %get-tuple-element.88.e_xy, f32[42,32,256]{2,1,0:T(8,128)S(1)} %get-tuple-element.89.e_z, ...), custom_call_target="tpu_custom_call" | custom-call | tf_op jit(solution)/shard_map/field/pallas_call | solution.py:433
  148.1 3.2 %circuit.6 = (f32[42,32,256]{2,1,0:T(8,128)S(1)}, f32[256,128]{1,0:T(8,128)S(1)}, f32[1,128]{1,0:T(1,128)S(1)}, f32[288,1]{1,0:T(8,128)S(1)}) custom-call(s32[577]{0:T(1024)S(1)} %pad_add_fusion.found.table, s32[2,4]{1,0:T(2,128)S(1)} %copy-done.9, f32[256,128]{1,0:T(8,128)S(1)} %bitcast.19, f32[288,8]{1,0:T(8,128)S(1)} %get-tuple-element.63.columns, ...), custom_call_target="tpu_custom_call" | custom-call | tf_op jit(solution)/shard_map/circuit/pallas_call | solution.py:516
  151.3 14.2 %all_to_all.62 = f32[128,2,128]{2,1,0:T(2,128)S(1)} all-to-all(f32[128,2,128]{2,1,0:T(2,128)S(1)} %bitcast.22), channel_id=1, replica_groups=mesh['gz'=16,'gy'=8] {'gz','gy'}, dimensions={0} | all-to-all | bytes 262144 | tf_op jit(solution)/shard_map/all_to_all | solution.py:589
  165.5 3.9 %field.8 = (f32[2,42,32,256]{3,2,1,0:T(8,128)S(1)}, f32[42,32,256]{2,1,0:T(8,128)S(1)}, f32[3,42,32,256]{3,2,1,0:T(8,128)S(1)}) custom-call(f32[2,42,32,256]{3,2,1,0:T(8,128)S(1)} %get-tuple-element.69.media, f32[2,42,32,256]{3,2,1,0:T(8,128)S(1)} %get-tuple-element.97.e_xy, f32[42,32,256]{2,1,0:T(8,128)S(1)} %get-tuple-element.98.e_z, ...), custom_call_target="tpu_custom_call" | custom-call | tf_op jit(solution)/shard_map/field/pallas_call | solution.py:433
  169.5 3.2 %circuit.7 = (f32[42,32,256]{2,1,0:T(8,128)S(1)}, f32[256,128]{1,0:T(8,128)S(1)}, f32[1,128]{1,0:T(1,128)S(1)}, f32[288,1]{1,0:T(8,128)S(1)}) custom-call(s32[577]{0:T(1024)S(1)} %pad_add_fusion.found.table, s32[2,4]{1,0:T(2,128)S(1)} %copy-done.9, f32[256,128]{1,0:T(8,128)S(1)} %bitcast.20, f32[288,8]{1,0:T(8,128)S(1)} %get-tuple-element.63.columns, ...), custom_call_target="tpu_custom_call" | custom-call | tf_op jit(solution)/shard_map/circuit/pallas_call | solution.py:516
  172.7 14.2 %all_to_all.63 = f32[128,2,128]{2,1,0:T(2,128)S(1)} all-to-all(f32[128,2,128]{2,1,0:T(2,128)S(1)} %bitcast.23), channel_id=1, replica_groups=mesh['gz'=16,'gy'=8] {'gz','gy'}, dimensions={0} | all-to-all | bytes 262144 | tf_op jit(solution)/shard_map/all_to_all | solution.py:589
  186.9 3.7 %field.9 = (f32[2,42,32,256]{3,2,1,0:T(8,128)S(1)}, f32[42,32,256]{2,1,0:T(8,128)S(1)}, f32[3,42,32,256]{3,2,1,0:T(8,128)S(1)}) custom-call(f32[2,42,32,256]{3,2,1,0:T(8,128)S(1)} %get-tuple-element.69.media, f32[2,42,32,256]{3,2,1,0:T(8,128)S(1)} %get-tuple-element.106.e_xy, f32[42,32,256]{2,1,0:T(8,128)S(1)} %get-tuple-element.107.e_z, ...), custom_call_target="tpu_custom_call" | custom-call | tf_op jit(solution)/shard_map/field/pallas_call | solution.py:433
  190.6 3.4 %finish.1 = (f32[3,32,16,256]{3,2,1,0:T(8,128)}, f32[3,32,16,256]{3,2,1,0:T(8,128)}, f32[1,128]{1,0:T(1,128)}) custom-call(s32[577]{0:T(1024)S(1)} %pad_add_fusion.found.table, s32[2,4]{1,0:T(2,128)S(1)} %copy-done.9, f32[256,128]{1,0:T(8,128)S(1)} %bitcast.17, f32[288,8]{1,0:T(8,128)S(1)} %get-tuple-element.63.columns, ...), custom_call_target="tpu_custom_call" | custom-call | tf_op jit(solution)/shard_map/finish/pallas_call | solution.py:559
  (4 shorter events, 0.0 us)
Async XLA Ops:
  0.6 0.7 copy-start.10
  7.4 15.5 %copy-start.4 = (s32[4096]{0:T(1024)S(1)}, s32[4096]{0:T(1024)}, u32[]{:S(2)}) copy-start(s32[4096]{0:T(1024)} %nodes.1) | copy-start | bytes 49156
  7.4 15.5 %copy-start.5 = (f32[4096]{0:T(1024)S(1)}, f32[4096]{0:T(1024)}, u32[]{:S(2)}) copy-start(f32[4096]{0:T(1024)} %gains.1) | copy-start | bytes 49156
  7.4 15.5 %copy-start.11 = (f32[128]{0:T(128)S(1)}, f32[128]{0:T(128)}, u32[]{:S(2)}) copy-start(f32[128]{0:T(128)} %param.23) | copy-start | bytes 1540
  7.4 15.5 %copy-start.13 = (s32[32]{0:T(128)S(1)}, s32[32]{0:T(128)}, u32[]{:S(2)}) copy-start(s32[32]{0:T(128)} %cells.1) | copy-start | bytes 388
  9.4 63.9 %collective-permute-start.3 = (f32[32,40,256]{2,1,0:T(8,128)S(1)}, f32[32,40,256]{2,1,0:T(8,128)}, u32[]{:S(2)}, u32[]{:S(2)}) collective-permute-start(f32[32,40,256]{2,1,0:T(8,128)S(1)} %strip.3.after), channel_id=1, source_target_pairs={{1,0},{2,1},{3,2},{4,3},{5,4},{6,5},{7,6},{9,8},{10,9},{11,10},{12... | collective-permute-start | bytes 3932168 | tf_op jit(solution)/shard_map/ppermute | solution.py:585
  10.7 62.6 %collective-permute-start.2 = (f32[32,40,256]{2,1,0:T(8,128)S(1)}, f32[32,40,256]{2,1,0:T(8,128)}, u32[]{:S(2)}, u32[]{:S(2)}) collective-permute-start(f32[32,40,256]{2,1,0:T(8,128)S(1)} %strip.2.after), channel_id=1, source_target_pairs={{0,1},{1,2},{2,3},{3,4},{4,5},{5,6},{6,7},{8,9},{9,10},{10,11},{11... | collective-permute-start | bytes 3932168 | tf_op jit(solution)/shard_map/ppermute | solution.py:585
  16.8 21.2 %collective-permute-start.1 = (f32[40,16,256]{2,1,0:T(8,128)}, f32[40,16,256]{2,1,0:T(8,128)S(1)}, u32[]{:S(2)}, u32[]{:S(2)}) collective-permute-start(f32[40,16,256]{2,1,0:T(8,128)} %slab.3.after), channel_id=1, source_target_pairs={{8,0},{16,8},{24,16},{32,24},{40,32},{48,40},{56,48},{64,56},{72,6... | collective-permute-start | bytes 1966088 | tf_op jit(solution)/shard_map/ppermute | solution.py:585
  19.7 18.4 %collective-permute-start = (f32[40,16,256]{2,1,0:T(8,128)}, f32[40,16,256]{2,1,0:T(8,128)}, u32[]{:S(2)}, u32[]{:S(2)}) collective-permute-start(f32[40,16,256]{2,1,0:T(8,128)} %slab.2.after), channel_id=1, source_target_pairs={{0,8},{8,16},{16,24},{24,32},{32,40},{40,48},{48,56},{56,64},{64,7... | collective-permute-start | bytes 1966088 | tf_op jit(solution)/shard_map/ppermute | solution.py:585
  25.6 0.7 copy-start.1
  26.3 42.9 %all-to-all-start = ((f32[128,4,128]{2,1,0:T(4,128)}), f32[128,4,128]{2,1,0:T(4,128)}, u32[]{:S(2)}, u32[]{:S(2)}) async-start(f32[128,4,128]{2,1,0:T(4,128)} %bitcast.16), calls=%async_computation | async-start | bytes 524288 | tf_op jit(solution)/shard_map/all_to_all | solution.py:589
  38.0 35.3 %copy-start = (f32[40,16,256]{2,1,0:T(8,128)}, f32[40,16,256]{2,1,0:T(8,128)S(1)}, u32[]{:S(2)}) copy-start(f32[40,16,256]{2,1,0:T(8,128)S(1)} %collective-permute-done.1.upper) | copy-start | bytes 1966084
  38.0 1.2 copy-start.2
  41.3 32.0 %collective-permute-start.4 = (f32[10,40,256]{2,1,0:T(8,128)}, f32[10,40,256]{2,1,0:T(8,128)}, u32[]{:S(2)}, u32[]{:S(2)}) collective-permute-start(f32[10,40,256]{2,1,0:T(8,128)} %get-tuple-element.59), channel_id=1, source_target_pairs={{0,1},{1,2},{2,3},{3,4},{4,5},{5,6},{6,7},{8,9},{9,10},{10,11},{11... | collective-permute-start | bytes 1228808 | tf_op jit(solution)/shard_map/ppermute | solution.py:585
  45.5 27.8 %collective-permute-start.5 = (f32[10,40,256]{2,1,0:T(8,128)}, f32[10,40,256]{2,1,0:T(8,128)}, u32[]{:S(2)}, u32[]{:S(2)}) collective-permute-start(f32[10,40,256]{2,1,0:T(8,128)} %get-tuple-element.60), channel_id=1, source_target_pairs={{1,0},{2,1},{3,2},{4,3},{5,4},{6,5},{7,6},{9,8},{10,9},{11,10},{12... | collective-permute-start | bytes 1228808 | tf_op jit(solution)/shard_map/ppermute | solution.py:585
  46.8 1.0 copy-start.3
  47.7 0.8 copy-start.7
  48.6 0.8 copy-start.8
  69.2 0.7 copy-start.6
  79.4 4.6 %copy-start.9 = (s32[2,4]{1,0:T(2,128)S(1)}, s32[2,4]{1,0:T(2,128)}, u32[]{:S(2)}) copy-start(s32[2,4]{1,0:T(2,128)} %off_cols.9) | copy-start | bytes 100
  79.4 4.6 %copy-start.12 = (f32[128]{0:T(128)S(1)}, f32[128]{0:T(128)}, u32[]{:S(2)}) copy-start(f32[128]{0:T(128)} %param.23) | copy-start | bytes 1540

commit v7 on v6

--- a/solution.py
+++ b/solution.py
@@ -13,6 +13,7 @@
 NB_DEV = 2
 OFF = 4
 PORT_DEV = 32
+GROUP = 16
 ND = 128
 NODE_DEV = NB_DEV * BS
 DEPTH = 5
@@ -99,31 +100,34 @@
     return [e_in.at[k] for k in range(3)] + [h_in.at[k] for k in range(3)] + [coef_in, loss_in]
 
 
-def strip_kernel(top, e_in, h_in, coef_in, loss_in, after, strip, fields, sems):
+def strip_kernel(top, e_in, h_in, coef_in, loss_in, lower, upper, after, strip, fields, sems):
     copies, copy = copier(sems)
     rows = pl.ds(CY - 8 if top else 0, 8)
     for part, source in enumerate(sources_of(e_in, h_in, coef_in, loss_in)):
-        copy(source.at[:, rows], fields.at[part])
+        slab = pl.ds(part * DEPTH, DEPTH)
+        copy(source.at[:, rows], fields.at[part, pl.ds(DEPTH, CZ)])
+        copy(lower.at[slab, rows], fields.at[part, pl.ds(0, DEPTH)])
+        copy(upper.at[slab, rows], fields.at[part, pl.ds(DEPTH + CZ, DEPTH)])
     for job in copies:
         job.wait()
     given = slice(8 - DEPTH, 8) if top else slice(0, DEPTH)
 
-    @pl.loop(0, CZ)
+    @pl.loop(0, LAYERS)
     def _(layer):
         for part in range(PARTS):
             strip[layer, part * DEPTH : (part + 1) * DEPTH, :] = fields[part, layer, given, :]
 
 
-def strip_of(top, grids, after):
+def strip_of(top, grids, lower, upper, after):
     return pl.pallas_call(
         functools.partial(strip_kernel, top),
         name="strip",
-        out_shape=jax.ShapeDtypeStruct((CZ, STRIP, NX), f32),
-        in_specs=[HBM] * 4 + [ANY],
+        out_shape=jax.ShapeDtypeStruct((LAYERS, STRIP, NX), f32),
+        in_specs=[HBM] * 6 + [ANY],
         out_specs=VM,
-        scratch_shapes=[pltpu.VMEM((PARTS, CZ, 8, NX), f32), DMA((PARTS,))],
-        compiler_params=params(),
-    )(*map(away, grids), after)
+        scratch_shapes=[pltpu.VMEM((PARTS, LAYERS, 8, NX), f32), DMA((3 * PARTS,))],
+        compiler_params=params(),
+    )(*map(away, (*grids, lower, upper)), after)
 
 
 def slab_kernel(top, e_in, h_in, coef_in, loss_in, after, slab, sems):
@@ -211,28 +215,6 @@
         out_specs=(VM, VM, VM),
         compiler_params=params(),
     )(diag, inv, off)
-
-
-def corners_kernel(lower, upper, after, front, back):
-    for side, source in enumerate((lower, upper)):
-        for layer in range(DEPTH):
-            for part in range(PARTS):
-                to = slice(part * DEPTH, (part + 1) * DEPTH)
-                given = part * DEPTH + layer
-                front[side * DEPTH + layer, to, :] = source[given, CY - DEPTH : CY, :]
-                back[side * DEPTH + layer, to, :] = source[given, 0:DEPTH, :]
-
-
-def corners(lower, upper, after):
-    shape = jax.ShapeDtypeStruct((2 * DEPTH, STRIP, NX), f32)
-    return pl.pallas_call(
-        corners_kernel,
-        name="corners",
-        out_shape=(shape, shape),
-        in_specs=[VM, VM, ANY],
-        out_specs=(VM, VM),
-        compiler_params=params(),
-    )(lower, upper, after)
 
 
 def plan_kernel(n_gz, n_gy, arrived, nodes, gains, found, columns, facts):
@@ -275,7 +257,7 @@
         facts[...], chosen, across, precision=lax.Precision.HIGHEST, preferred_element_type=f32
     )
     count = jnp.sum(used, axis=1, keepdims=True)
-    groups = ((count + (PORT_DEV - 1)) / PORT_DEV).astype(jnp.int32)
+    groups = ((count + (GROUP - 1)) * (1.0 / GROUP)).astype(jnp.int32)
     kind = lax.broadcasted_iota(jnp.int32, rows.shape, 0)
     unused = (kind == 0) & (lanes_of(8, REACH) >= count.astype(jnp.int32))
     whole = jnp.where(unused, PAD, (rows + 0.5).astype(jnp.int32))
@@ -299,7 +281,7 @@
 
 
 def halo_kernel(
-    found, columns, lower, upper, before, after, before_ends, after_ends,
+    found, columns, lower, upper, before, after,
     e_in, h_in, coef_in, loss_in, e_xy, e_z, h, media, sample, coef, picked, sems,
 ):
     copies, copy = copier(sems)
@@ -314,19 +296,12 @@
         copy(lower.at[given], target.at[pl.ds(0, DEPTH), middle])
         copy(upper.at[given], target.at[pl.ds(DEPTH + CZ, DEPTH), middle])
 
-    def unpack(ahead, behind, at, layer):
+    @pl.loop(0, LAYERS)
+    def _(layer):
         for part, target in enumerate(targets):
             rows = slice(part * DEPTH, (part + 1) * DEPTH)
-            target[layer, PAD - DEPTH : PAD, :] = ahead[at, rows, :]
-            target[layer, PAD + CY : PAD + CY + DEPTH, :] = behind[at, rows, :]
-
-    @pl.loop(0, CZ)
-    def _(layer):
-        unpack(before, after, layer, layer + DEPTH)
-
-    @pl.loop(0, 2 * DEPTH)
-    def _(end):
-        unpack(before_ends, after_ends, end, jnp.where(end < DEPTH, end, end + CZ))
+            target[layer, PAD - DEPTH : PAD, :] = before[layer, rows, :]
+            target[layer, PAD + CY : PAD + CY + DEPTH, :] = after[layer, rows, :]
 
     for job in copies:
         job.wait()
@@ -337,20 +312,20 @@
 
     @pl.loop(0, found[COUNT])
     def _(group):
-        part = pl.ds(pl.multiple_of(group * PORT_DEV, PORT_DEV), PORT_DEV)
+        part = pl.ds(pl.multiple_of(group * GROUP, GROUP), GROUP)
         _, place, _ = columns_at(columns, part)
         sample[part, :] = gather_cells(e_z, found, group, place, picked)
         coef[part, :] = gather_cells(media.at[0], found, group, place, picked)
 
 
 def gather_cells(source, found, group, place, picked):
-    for port in range(PORT_DEV):
-        spot = found[group * PORT_DEV + port]
+    for port in range(GROUP):
+        spot = found[group * GROUP + port]
         picked[port : port + 1, :] = source[spot // TALL, pl.ds(spot % TALL, 1), :]
     return pick(picked[...], place)
 
 
-def halo(found, columns, lower, upper, sides, e_in, h_in, coef, loss):
+def halo(found, columns, lower, upper, before, after, e_in, h_in, coef, loss):
     return pl.pallas_call(
         halo_kernel,
         name="halo",
@@ -362,11 +337,11 @@
             onchip((REACH, 1)),
             onchip((REACH, 1)),
         ),
-        in_specs=[SM, VM, HBM, HBM, VM, VM, VM, VM] + [HBM] * 4,
+        in_specs=[SM, VM, HBM, HBM, VM, VM] + [HBM] * 4,
         out_specs=(VM,) * 6,
-        scratch_shapes=[pltpu.VMEM((PORT_DEV, NX), f32), DMA((24,))],
-        compiler_params=params(),
-    )(found, columns, away(lower), away(upper), *sides, *map(away, (e_in, h_in, coef, loss)))
+        scratch_shapes=[pltpu.VMEM((GROUP, NX), f32), DMA((24,))],
+        compiler_params=params(),
+    )(found, columns, away(lower), away(upper), before, after, *map(away, (e_in, h_in, coef, loss)))
 
 
 def field_kernel(step, media, e_xy, e_z, h, to_xy, to_z, to_h):
@@ -476,15 +451,15 @@
 def apply_ports(stride, table, arrived, columns, sample, coef, e_z, near_rows, deltas):
     @pl.loop(0, table[COUNT])
     def _(group):
-        first = group * PORT_DEV
-        part = pl.ds(pl.multiple_of(first, PORT_DEV), PORT_DEV)
-        for port in range(PORT_DEV):
+        first = group * GROUP
+        part = pl.ds(pl.multiple_of(first, GROUP), GROUP)
+        for port in range(GROUP):
             near_at = table[NODES + first + port] * stride
             near_rows[port : port + 1, :] = arrived[pl.ds(near_at, 1), :]
         gain, place, lane = columns_at(columns, part)
         current = gain * (sample[part, :] - pick(near_rows[...], lane))
         deltas[...] = spread(-coef[part, :] * current, place, NX)
-        for port in range(PORT_DEV):
+        for port in range(GROUP):
             spot = table[first + port]
             layer, row = spot // TALL, pl.ds(spot % TALL, 1)
             e_z[layer, row, :] = e_z[layer, row, :] + deltas[port : port + 1, :]
@@ -499,7 +474,7 @@
 
     @pl.loop(0, table[COUNT])
     def _(group):
-        part = pl.ds(pl.multiple_of(group * PORT_DEV, PORT_DEV), PORT_DEV)
+        part = pl.ds(pl.multiple_of(group * GROUP, GROUP), GROUP)
         _, place, _ = columns_at(columns, part)
         sample_out[part, :] = gather_cells(e_z, table, group, place, picked)
 
@@ -525,9 +500,9 @@
         in_specs=[SM, SM] + [VM] * 9,
         out_specs=(VM,) * 4,
         scratch_shapes=[
-            pltpu.VMEM((PORT_DEV, NODE_DEV), f32),
-            pltpu.VMEM((PORT_DEV, NX), f32),
-            pltpu.VMEM((PORT_DEV, NX), f32),
+            pltpu.VMEM((GROUP, NODE_DEV), f32),
+            pltpu.VMEM((GROUP, NX), f32),
+            pltpu.VMEM((GROUP, NX), f32),
             pltpu.VMEM((PORT_DEV, NODE_DEV), f32),
         ],
         compiler_params=params(),
@@ -568,8 +543,8 @@
         out_specs=(HBM, HBM, VM),
         scratch_shapes=[
             pltpu.VMEM(CUBE, f32),
-            pltpu.VMEM((PORT_DEV, NODE_DEV), f32),
-            pltpu.VMEM((PORT_DEV, NX), f32),
+            pltpu.VMEM((GROUP, NODE_DEV), f32),
+            pltpu.VMEM((GROUP, NX), f32),
             DMA((6,)),
         ],
         compiler_params=params(),
@@ -610,23 +585,19 @@
     lower = shifted(up, "gz", 1)
     down = slab_of(False, grids, up)
     upper = shifted(down, "gz", -1)
-    front = strip_of(True, grids, down)
+    out = begin(n_gy, port_cell, port_node, port_gain, e_field, volts, down)
+    arrived = exchange(out)
+    front = strip_of(True, grids, lower, upper, out)
     before = shifted(front, "gy", 1)
-    back = strip_of(False, grids, front)
+    back = strip_of(False, grids, lower, upper, front)
     after = shifted(back, "gy", -1)
-    out = begin(n_gy, port_cell, port_node, port_gain, e_field, volts, back)
-    arrived = exchange(out)
-    front_ends, back_ends = corners(lower, upper, out)
-    before_ends = shifted(front_ends, "gy", 1)
-    after_ends = shifted(back_ends, "gy", -1)
-    arrived, front_ends, back_ends = lax.optimization_barrier((arrived, front_ends, back_ends))
-    sides = (before, after, before_ends, after_ends)
+    arrived, front, back = lax.optimization_barrier((arrived, front, back))
     mats = matrices(diag_blocks, inv_blocks, off_blocks)
 
     found, columns = plan(n_gz, n_gy, arrived, port_node, port_gain)
     table = jnp.concatenate([found[0], found[1], found[7, 0:1]])
 
-    e_xy, e_z, h, media, sample, coef = halo(table, columns, lower, upper, sides, *grids)
+    e_xy, e_z, h, media, sample, coef = halo(table, columns, lower, upper, before, after, *grids)
     for step in range(1, STEPS + 1):
         if step > 1:
             arrived = exchange(out)

time: 196 us -> 195 us (level)
  waiting for transfers between devices: 19.6 us -> 40.2 us
  blocking collectives: 77.2 us -> 65.1 us
  starting transfers between devices: 30.6 us -> 25.7 us
  local copies, waits for them, and re-layouts: 6.46 us -> 2.11 us
    all_to_all x4, blocking collectives: 77.2 us -> 65.1 us  [exchange(): return lax.all_to_all(value, ('gz', 'gy'), 0, 0, tiled=True)]
    all_to_all x1, waiting for transfers between devices: 19.6 us -> 30.1 us  [exchange(): return lax.all_to_all(value, ('gz', 'gy'), 0, 0, tiled=True)]
    ppermute x6 -> x4, waiting for transfers between devices: 0.02 us -> 10.1 us  [shifted(): lax.ppermute(value, axis, [(source, source + steps) for source in range(f...]
    ppermute x6 -> x4, starting transfers between devices: 18.9 us -> 13.2 us  [shifted(): lax.ppermute(value, axis, [(source, source + steps) for source in range(f...]
    unnamed x28 -> x22, local copies, waits for them, and re-layouts: 5.89 us -> 1.54 us
    pallas_call x4, Pallas kernels: 13.2 us -> 15.5 us  [circuit(): pl.pallas_call(functools.partial(circuit_kernel, arrived.shape[0] // ND),...]
    pallas_call x2, Pallas kernels: 3.89 us -> 6.07 us  [strip_of(): pl.pallas_call(functools.partial(strip_kernel, top), name='strip', out_sh...]
    pallas_call x1 -> x0, Pallas kernels: 2.14 us -> none  [corners(): pl.pallas_call(corners_kernel, name='corners', out_shape=(shape, shape),...]
  transfers between devices with their start and end apart: 7 -> 5, of which waited for: 1 -> 3; matrix products, arithmetic and copies ran while one was open for 1% -> 1% of each run, Pallas kernels for 4% -> 2%
where the time goes in v7:
time: 195 us
  blocking collectives  65.1 us (33%)
  Pallas kernels  60.1 us (31%)
  waiting for transfers between devices  40.2 us (21%)
  starting transfers between devices  25.7 us (13%)
  local copies, waits for them, and re-layouts  2.11 us (1%)
    all_to_all x4, blocking collectives, exchange(): return lax.all_to_all(value, ('gz', 'gy'), 0, 0, tiled=True)  65.1 us
    all_to_all x1, waiting for transfers between devices, exchange(): return lax.all_to_all(value, ('gz', 'gy'), 0, 0, tiled=True)  30.1 us
    pallas_call x5, Pallas kernels, field(): pl.pallas_call(functools.partial(field_kernel, step), name='field', out_s...  21.1 us
    pallas_call x4, Pallas kernels, circuit(): pl.pallas_call(functools.partial(circuit_kernel, arrived.shape[0] // ND),...  15.5 us
    ppermute x4, starting transfers between devices, shifted(): lax.ppermute(value, axis, [(source, source + steps) for source in range(f...  13.2 us
    all_to_all x1, starting transfers between devices, exchange(): return lax.all_to_all(value, ('gz', 'gy'), 0, 0, tiled=True)  12.4 us
    ppermute x4, waiting for transfers between devices, shifted(): lax.ppermute(value, axis, [(source, source + steps) for source in range(f...  10.1 us
    pallas_call x1, Pallas kernels, halo(): pl.pallas_call(halo_kernel, name='halo', out_shape=(onchip((2,) + CUBE),...  6.21 us
  transfers between devices with their start and end apart: 5, of which 3 were waited for; matrix products, arithmetic and copies ran while one was open for 1% of the time, Pallas kernels for 2%

profile of v7, /device:TPU:1, one launch (start us, length us, event | category | flops | bytes accessed | tf_op | source)
XLA Modules:
  0.0 194.9 jit_solution(2548772074648108435)
XLA Ops:
  0.6 0.0 copy-start.6
  0.6 0.6 copy-done.6
  1.3 1.2 slab.2.after
  2.5 0.0 copy-start.1
  2.5 0.0 copy-start.2
  2.6 0.0 copy-start.8
  2.6 1.2 slab.3.after
  3.8 3.3 %collective-permute-start.1 = (f32[40,16,256]{2,1,0:T(8,128)S(1)}, f32[40,16,256]{2,1,0:T(8,128)S(1)}, u32[]{:S(2)}, u32[]{:S(2)}) collective-permute-start(f32[40,16,256]{2,1,0:T(8,128)S(1)} %slab.3.after), channel_id=1, source_target_pairs={{8,0},{16,8},{24,16},{32,24},{40,32},{48,40},{56,48},{64,56},{72,6... | collective-permute-start | bytes 1966088 | tf_op jit(solution)/shard_map/ppermute | solution.py:560
  7.2 3.2 %collective-permute-start = (f32[40,16,256]{2,1,0:T(8,128)S(1)}, f32[40,16,256]{2,1,0:T(8,128)S(1)}, u32[]{:S(2)}, u32[]{:S(2)}) collective-permute-start(f32[40,16,256]{2,1,0:T(8,128)S(1)} %slab.2.after), channel_id=1, source_target_pairs={{0,8},{8,16},{16,24},{24,32},{32,40},{40,48},{48,56},{56,64},{64,7... | collective-permute-start | bytes 1966088 | tf_op jit(solution)/shard_map/ppermute | solution.py:560
  10.4 0.0 copy-done.1
  10.4 0.0 copy-done.2
  10.4 0.0 copy-done.8
  10.4 3.4 %begin.1.after = f32[512,128]{1,0:T(8,128)} custom-call(s32[32]{0:T(128)S(1)} %copy-done.8, s32[4096]{0:T(1024)S(1)} %copy-done.1, f32[4096]{0:T(1024)S(1)} %copy-done.2, f32[3,32,16,256]{3,2,1,0:T(8,128)} %e_in.11, s32[1,32]{1,0:T(1,128)S(1)} %bitcast.31, f32[1,128]{1,0:T(1,128)S(1)} %bitcast.29, f32[40,16,256]{2,1,0:T(8,128)S(1)} %slab.3.after), custom_call_target="tpu_custom_call" | custom-call | tf_op jit(solution)/shard_map/begin/pallas_call | solution.py:180
  13.8 2.9 %collective-permute-done.1.upper = f32[40,16,256]{2,1,0:T(8,128)S(1)} collective-permute-done((f32[40,16,256]{2,1,0:T(8,128)S(1)}, f32[40,16,256]{2,1,0:T(8,128)S(1)}, u32[]{:S(2)}, u32[]{:S(2)}) %collective-permute-start.1) | collective-permute-done | bytes 655392 | tf_op jit(solution)/shard_map/ppermute | solution.py:560
  16.7 0.0 copy-start.9
  16.7 7.2 %collective-permute-done.lower = f32[40,16,256]{2,1,0:T(8,128)S(1)} collective-permute-done((f32[40,16,256]{2,1,0:T(8,128)S(1)}, f32[40,16,256]{2,1,0:T(8,128)S(1)}, u32[]{:S(2)}, u32[]{:S(2)}) %collective-permute-start) | collective-permute-done | bytes 655392 | tf_op jit(solution)/shard_map/ppermute | solution.py:560
  23.9 0.0 copy-done.9
  23.9 0.0 copy-start.10
  23.9 0.8 copy-done.10
  24.7 2.4 %strip.2.after = f32[42,40,256]{2,1,0:T(8,128)S(1)} custom-call(f32[3,32,16,256]{3,2,1,0:T(8,128)} %e_in.11, f32[3,32,16,256]{3,2,1,0:T(8,128)} %h_in.9, f32[32,16,256]{2,1,0:T(8,128)} %coef_in.9, f32[32,16,256]{2,1,0:T(8,128)} %loss_in.9, f32[40,16,256]{2,1,0:T(8,128)} %copy-done.10, f32[40,16,256]{2,1,0:T(8,128)} %copy-done.9, f32[512,128]{1,0:T(8,128)} %begin.1.after), custom_call_target="tpu_custom_call" | custom-call | tf_op jit(solution)/shard_map/strip/pallas_call | solution.py:122
  27.1 0.0 copy-start
  27.1 0.0 copy-start.3
  27.1 0.0 copy-start.4
  27.2 3.7 %strip.3 = f32[42,40,256]{2,1,0:T(8,128)} custom-call(f32[3,32,16,256]{3,2,1,0:T(8,128)} %e_in.11, f32[3,32,16,256]{3,2,1,0:T(8,128)} %h_in.9, f32[32,16,256]{2,1,0:T(8,128)} %coef_in.9, f32[32,16,256]{2,1,0:T(8,128)} %loss_in.9, f32[40,16,256]{2,1,0:T(8,128)} %copy-done.10, f32[40,16,256]{2,1,0:T(8,128)} %copy-done.9, f32[42,40,256]{2,1,0:T(8,128)S(1)} %strip.2.after), custom_call_target="tpu_custom_call" | custom-call | tf_op jit(solution)/shard_map/strip/pallas_call | solution.py:122
  30.8 1.3 collective-permute-start.3
  32.1 5.4 %collective-permute-start.2 = (f32[42,40,256]{2,1,0:T(8,128)S(1)}, f32[42,40,256]{2,1,0:T(8,128)}, u32[]{:S(2)}, u32[]{:S(2)}) collective-permute-start(f32[42,40,256]{2,1,0:T(8,128)S(1)} %strip.2.after), channel_id=1, source_target_pairs={{0,1},{1,2},{2,3},{3,4},{4,5},{5,6},{6,7},{8,9},{9,10},{10,11},{11... | collective-permute-start | bytes 5160968 | tf_op jit(solution)/shard_map/ppermute | solution.py:560
  37.5 12.4 %all-to-all-start = ((f32[128,4,128]{2,1,0:T(4,128)}), f32[128,4,128]{2,1,0:T(4,128)S(1)}, u32[]{:S(2)}, u32[]{:S(2)}) async-start(f32[128,4,128]{2,1,0:T(4,128)} %bitcast.2), calls=%async_computation | async-start | bytes 524288 | tf_op jit(solution)/shard_map/all_to_all | solution.py:564
  50.0 0.0 copy-done
  50.0 0.0 copy-done.3
  50.0 0.0 copy-done.4
  50.0 0.2 matrices.1
  50.2 30.1 %all-to-all-done = f32[128,4,128]{2,1,0:T(4,128)S(1)} async-done(((f32[128,4,128]{2,1,0:T(4,128)}), f32[128,4,128]{2,1,0:T(4,128)S(1)}, u32[]{:S(2)}, u32[]{:S(2)}) %all-to-all-start) | async-done | bytes 262176 | tf_op jit(solution)/shard_map/all_to_all | solution.py:564
  80.3 1.2 plan.1
  81.5 0.5 slice.11
  82.0 0.7 pad_add_fusion.found.table
  82.8 0.0 collective-permute-done.3.after
  82.8 0.0 collective-permute-done.2.before
  82.8 6.2 %halo.1 = (f32[2,42,32,256]{3,2,1,0:T(8,128)S(1)}, f32[42,32,256]{2,1,0:T(8,128)S(1)}, f32[3,42,32,256]{3,2,1,0:T(8,128)S(1)}, f32[2,42,32,256]{3,2,1,0:T(8,128)...) custom-call(s32[577]{0:T(1024)S(1)} %pad_add_fusion.found.table, f32[288,8]{1,0:T(8,128)S(1)} %get-tuple-element.59.columns, ...), custom_call_target="tpu_custom_call" | custom-call | tf_op jit(solution)/shard_map/halo/pallas_call | solution.py:329
  89.0 0.0 copy-start.5
  89.0 0.0 copy-start.7
  89.0 4.8 %field.5 = (f32[2,42,32,256]{3,2,1,0:T(8,128)S(1)}, f32[42,32,256]{2,1,0:T(8,128)S(1)}, f32[3,42,32,256]{3,2,1,0:T(8,128)S(1)}) custom-call(f32[2,42,32,256]{3,2,1,0:T(8,128)S(1)} %get-tuple-element.65.media, f32[2,42,32,256]{3,2,1,0:T(8,128)S(1)} %get-tuple-element.66.e_xy, f32[42,32,256]{2,1,0:T(8,128)S(1)} %get-tuple-element.67.e_z, ...), custom_call_target="tpu_custom_call" | custom-call | tf_op jit(solution)/shard_map/field/pallas_call | solution.py:408
  93.8 0.0 copy-done.5
  93.8 0.0 copy-done.7
  93.9 3.9 %circuit.4 = (f32[42,32,256]{2,1,0:T(8,128)S(1)}, f32[256,128]{1,0:T(8,128)S(1)}, f32[1,128]{1,0:T(1,128)S(1)}, f32[288,1]{1,0:T(8,128)S(1)}) custom-call(s32[577]{0:T(1024)S(1)} %pad_add_fusion.found.table, s32[2,4]{1,0:T(2,128)S(1)} %copy-done.5, f32[512,128]{1,0:T(8,128)S(1)} %bitcast.17, f32[288,8]{1,0:T(8,128)S(1)} %get-tuple-element.59.columns, ...), custom_call_target="tpu_custom_call" | custom-call | tf_op jit(solution)/shard_map/circuit/pallas_call | solution.py:491
  97.7 20.6 %all_to_all.60 = f32[128,2,128]{2,1,0:T(2,128)S(1)} all-to-all(f32[128,2,128]{2,1,0:T(2,128)S(1)} %bitcast.25), channel_id=1, replica_groups=mesh['gz'=16,'gy'=8] {'gz','gy'}, dimensions={0} | all-to-all | bytes 262144 | tf_op jit(solution)/shard_map/all_to_all | solution.py:564
  118.4 4.4 %field.6 = (f32[2,42,32,256]{3,2,1,0:T(8,128)S(1)}, f32[42,32,256]{2,1,0:T(8,128)S(1)}, f32[3,42,32,256]{3,2,1,0:T(8,128)S(1)}) custom-call(f32[2,42,32,256]{3,2,1,0:T(8,128)S(1)} %get-tuple-element.65.media, f32[2,42,32,256]{3,2,1,0:T(8,128)S(1)} %get-tuple-element.75.e_xy, f32[42,32,256]{2,1,0:T(8,128)S(1)} %get-tuple-element.76.e_z, ...), custom_call_target="tpu_custom_call" | custom-call | tf_op jit(solution)/shard_map/field/pallas_call | solution.py:408
  122.8 3.9 %circuit.5 = (f32[42,32,256]{2,1,0:T(8,128)S(1)}, f32[256,128]{1,0:T(8,128)S(1)}, f32[1,128]{1,0:T(1,128)S(1)}, f32[288,1]{1,0:T(8,128)S(1)}) custom-call(s32[577]{0:T(1024)S(1)} %pad_add_fusion.found.table, s32[2,4]{1,0:T(2,128)S(1)} %copy-done.5, f32[256,128]{1,0:T(8,128)S(1)} %bitcast.19, f32[288,8]{1,0:T(8,128)S(1)} %get-tuple-element.59.columns, ...), custom_call_target="tpu_custom_call" | custom-call | tf_op jit(solution)/shard_map/circuit/pallas_call | solution.py:491
  126.7 14.8 %all_to_all.61 = f32[128,2,128]{2,1,0:T(2,128)S(1)} all-to-all(f32[128,2,128]{2,1,0:T(2,128)S(1)} %bitcast.22), channel_id=1, replica_groups=mesh['gz'=16,'gy'=8] {'gz','gy'}, dimensions={0} | all-to-all | bytes 262144 | tf_op jit(solution)/shard_map/all_to_all | solution.py:564
  141.5 4.2 %field.7 = (f32[2,42,32,256]{3,2,1,0:T(8,128)S(1)}, f32[42,32,256]{2,1,0:T(8,128)S(1)}, f32[3,42,32,256]{3,2,1,0:T(8,128)S(1)}) custom-call(f32[2,42,32,256]{3,2,1,0:T(8,128)S(1)} %get-tuple-element.65.media, f32[2,42,32,256]{3,2,1,0:T(8,128)S(1)} %get-tuple-element.84.e_xy, f32[42,32,256]{2,1,0:T(8,128)S(1)} %get-tuple-element.85.e_z, ...), custom_call_target="tpu_custom_call" | custom-call | tf_op jit(solution)/shard_map/field/pallas_call | solution.py:408
  145.8 3.9 %circuit.6 = (f32[42,32,256]{2,1,0:T(8,128)S(1)}, f32[256,128]{1,0:T(8,128)S(1)}, f32[1,128]{1,0:T(1,128)S(1)}, f32[288,1]{1,0:T(8,128)S(1)}) custom-call(s32[577]{0:T(1024)S(1)} %pad_add_fusion.found.table, s32[2,4]{1,0:T(2,128)S(1)} %copy-done.5, f32[256,128]{1,0:T(8,128)S(1)} %bitcast.20, f32[288,8]{1,0:T(8,128)S(1)} %get-tuple-element.59.columns, ...), custom_call_target="tpu_custom_call" | custom-call | tf_op jit(solution)/shard_map/circuit/pallas_call | solution.py:491
  149.6 14.8 %all_to_all.62 = f32[128,2,128]{2,1,0:T(2,128)S(1)} all-to-all(f32[128,2,128]{2,1,0:T(2,128)S(1)} %bitcast.23), channel_id=1, replica_groups=mesh['gz'=16,'gy'=8] {'gz','gy'}, dimensions={0} | all-to-all | bytes 262144 | tf_op jit(solution)/shard_map/all_to_all | solution.py:564
  164.5 4.0 %field.8 = (f32[2,42,32,256]{3,2,1,0:T(8,128)S(1)}, f32[42,32,256]{2,1,0:T(8,128)S(1)}, f32[3,42,32,256]{3,2,1,0:T(8,128)S(1)}) custom-call(f32[2,42,32,256]{3,2,1,0:T(8,128)S(1)} %get-tuple-element.65.media, f32[2,42,32,256]{3,2,1,0:T(8,128)S(1)} %get-tuple-element.93.e_xy, f32[42,32,256]{2,1,0:T(8,128)S(1)} %get-tuple-element.94.e_z, ...), custom_call_target="tpu_custom_call" | custom-call | tf_op jit(solution)/shard_map/field/pallas_call | solution.py:408
  168.5 3.9 %circuit.7 = (f32[42,32,256]{2,1,0:T(8,128)S(1)}, f32[256,128]{1,0:T(8,128)S(1)}, f32[1,128]{1,0:T(1,128)S(1)}, f32[288,1]{1,0:T(8,128)S(1)}) custom-call(s32[577]{0:T(1024)S(1)} %pad_add_fusion.found.table, s32[2,4]{1,0:T(2,128)S(1)} %copy-done.5, f32[256,128]{1,0:T(8,128)S(1)} %bitcast.21, f32[288,8]{1,0:T(8,128)S(1)} %get-tuple-element.59.columns, ...), custom_call_target="tpu_custom_call" | custom-call | tf_op jit(solution)/shard_map/circuit/pallas_call | solution.py:491
  172.3 14.8 %all_to_all.63 = f32[128,2,128]{2,1,0:T(2,128)S(1)} all-to-all(f32[128,2,128]{2,1,0:T(2,128)S(1)} %bitcast.24), channel_id=1, replica_groups=mesh['gz'=16,'gy'=8] {'gz','gy'}, dimensions={0} | all-to-all | bytes 262144 | tf_op jit(solution)/shard_map/all_to_all | solution.py:564
  187.2 3.7 %field.9 = (f32[2,42,32,256]{3,2,1,0:T(8,128)S(1)}, f32[42,32,256]{2,1,0:T(8,128)S(1)}, f32[3,42,32,256]{3,2,1,0:T(8,128)S(1)}) custom-call(f32[2,42,32,256]{3,2,1,0:T(8,128)S(1)} %get-tuple-element.65.media, f32[2,42,32,256]{3,2,1,0:T(8,128)S(1)} %get-tuple-element.102.e_xy, f32[42,32,256]{2,1,0:T(8,128)S(1)} %get-tuple-element.103.e_z, ...), custom_call_target="tpu_custom_call" | custom-call | tf_op jit(solution)/shard_map/field/pallas_call | solution.py:408
  190.9 4.0 %finish.1 = (f32[3,32,16,256]{3,2,1,0:T(8,128)}, f32[3,32,16,256]{3,2,1,0:T(8,128)}, f32[1,128]{1,0:T(1,128)}) custom-call(s32[577]{0:T(1024)S(1)} %pad_add_fusion.found.table, s32[2,4]{1,0:T(2,128)S(1)} %copy-done.5, f32[256,128]{1,0:T(8,128)S(1)} %bitcast.18, f32[288,8]{1,0:T(8,128)S(1)} %get-tuple-element.59.columns, ...), custom_call_target="tpu_custom_call" | custom-call | tf_op jit(solution)/shard_map/finish/pallas_call | solution.py:534
  (1 shorter events, 0.0 us)
Async XLA Ops:
  0.6 0.7 copy-start.6
  2.5 7.8 %copy-start.1 = (s32[4096]{0:T(1024)S(1)}, s32[4096]{0:T(1024)}, u32[]{:S(2)}) copy-start(s32[4096]{0:T(1024)} %nodes.1) | copy-start | bytes 49156
  2.5 7.8 %copy-start.2 = (f32[4096]{0:T(1024)S(1)}, f32[4096]{0:T(1024)}, u32[]{:S(2)}) copy-start(f32[4096]{0:T(1024)} %gains.1) | copy-start | bytes 49156
  2.6 7.8 %copy-start.8 = (s32[32]{0:T(128)S(1)}, s32[32]{0:T(128)}, u32[]{:S(2)}) copy-start(s32[32]{0:T(128)} %cells.1) | copy-start | bytes 388
  3.8 12.9 %collective-permute-start.1 = (f32[40,16,256]{2,1,0:T(8,128)S(1)}, f32[40,16,256]{2,1,0:T(8,128)S(1)}, u32[]{:S(2)}, u32[]{:S(2)}) collective-permute-start(f32[40,16,256]{2,1,0:T(8,128)S(1)} %slab.3.after), channel_id=1, source_target_pairs={{8,0},{16,8},{24,16},{32,24},{40,32},{48,40},{56,48},{64,56},{72,6... | collective-permute-start | bytes 1966088 | tf_op jit(solution)/shard_map/ppermute | solution.py:560
  7.2 16.7 %collective-permute-start = (f32[40,16,256]{2,1,0:T(8,128)S(1)}, f32[40,16,256]{2,1,0:T(8,128)S(1)}, u32[]{:S(2)}, u32[]{:S(2)}) collective-permute-start(f32[40,16,256]{2,1,0:T(8,128)S(1)} %slab.2.after), channel_id=1, source_target_pairs={{0,8},{8,16},{16,24},{24,32},{32,40},{40,48},{48,56},{56,64},{64,7... | collective-permute-start | bytes 1966088 | tf_op jit(solution)/shard_map/ppermute | solution.py:560
  16.7 7.2 %copy-start.9 = (f32[40,16,256]{2,1,0:T(8,128)}, f32[40,16,256]{2,1,0:T(8,128)S(1)}, u32[]{:S(2)}) copy-start(f32[40,16,256]{2,1,0:T(8,128)S(1)} %collective-permute-done.1.upper) | copy-start | bytes 1966084
  23.9 0.8 copy-start.10
  27.1 22.9 %copy-start = (f32[2,4,64,64]{3,2,1,0:T(8,128)S(1)}, f32[2,4,64,64]{3,2,1,0:T(8,128)}, u32[]{:S(2)}) copy-start(f32[2,4,64,64]{3,2,1,0:T(8,128)} %off.1) | copy-start | bytes 393220
  27.1 22.9 %copy-start.3 = (f32[2,64,64]{2,1,0:T(8,128)S(1)}, f32[2,64,64]{2,1,0:T(8,128)}, u32[]{:S(2)}) copy-start(f32[2,64,64]{2,1,0:T(8,128)} %diag.1) | copy-start | bytes 98308
  27.1 22.9 %copy-start.4 = (f32[2,64,64]{2,1,0:T(8,128)S(1)}, f32[2,64,64]{2,1,0:T(8,128)}, u32[]{:S(2)}) copy-start(f32[2,64,64]{2,1,0:T(8,128)} %inv.1) | copy-start | bytes 98308
  30.8 51.9 %collective-permute-start.3 = (f32[42,40,256]{2,1,0:T(8,128)}, f32[42,40,256]{2,1,0:T(8,128)}, u32[]{:S(2)}, u32[]{:S(2)}) collective-permute-start(f32[42,40,256]{2,1,0:T(8,128)} %strip.3), channel_id=1, source_target_pairs={{1,0},{2,1},{3,2},{4,3},{5,4},{6,5},{7,6},{9,8},{10,9},{11,10},{12... | collective-permute-start | bytes 5160968 | tf_op jit(solution)/shard_map/ppermute | solution.py:560
  32.1 50.7 %collective-permute-start.2 = (f32[42,40,256]{2,1,0:T(8,128)S(1)}, f32[42,40,256]{2,1,0:T(8,128)}, u32[]{:S(2)}, u32[]{:S(2)}) collective-permute-start(f32[42,40,256]{2,1,0:T(8,128)S(1)} %strip.2.after), channel_id=1, source_target_pairs={{0,1},{1,2},{2,3},{3,4},{4,5},{5,6},{6,7},{8,9},{9,10},{10,11},{11... | collective-permute-start | bytes 5160968 | tf_op jit(solution)/shard_map/ppermute | solution.py:560
  37.5 42.8 %all-to-all-start = ((f32[128,4,128]{2,1,0:T(4,128)}), f32[128,4,128]{2,1,0:T(4,128)S(1)}, u32[]{:S(2)}, u32[]{:S(2)}) async-start(f32[128,4,128]{2,1,0:T(4,128)} %bitcast.2), calls=%async_computation | async-start | bytes 524288 | tf_op jit(solution)/shard_map/all_to_all | solution.py:564
  89.0 4.8 %copy-start.5 = (s32[2,4]{1,0:T(2,128)S(1)}, s32[2,4]{1,0:T(2,128)}, u32[]{:S(2)}) copy-start(s32[2,4]{1,0:T(2,128)} %off_cols.9) | copy-start | bytes 100
  89.0 4.8 %copy-start.7 = (f32[128]{0:T(128)S(1)}, f32[128]{0:T(128)}, u32[]{:S(2)}) copy-start(f32[128]{0:T(128)} %param.23) | copy-start | bytes 1540

commit v8 on v7

--- a/solution.py
+++ b/solution.py
@@ -19,11 +19,11 @@
 DEPTH = 5
 CZ, CY, NX = 32, 16, 256
 LAYERS = CZ + 2 * DEPTH
-PAD = 8
-TALL = CY + 2 * PAD
+PAD = 0
+TALL = CY
+STACK = 48
 PARTS = 8
-STRIP = PARTS * DEPTH
-SIDES = ((0, 0), (-1, 0), (1, 0), (0, -1), (-1, -1), (1, -1), (0, 1), (-1, 1), (1, 1))
+SIDES = ((0, 0), (-1, 0), (1, 0))
 REACH = len(SIDES) * PORT_DEV
 NODES, COUNT = REACH, 2 * REACH
 
@@ -100,34 +100,15 @@
     return [e_in.at[k] for k in range(3)] + [h_in.at[k] for k in range(3)] + [coef_in, loss_in]
 
 
-def strip_kernel(top, e_in, h_in, coef_in, loss_in, lower, upper, after, strip, fields, sems):
-    copies, copy = copier(sems)
-    rows = pl.ds(CY - 8 if top else 0, 8)
-    for part, source in enumerate(sources_of(e_in, h_in, coef_in, loss_in)):
-        slab = pl.ds(part * DEPTH, DEPTH)
-        copy(source.at[:, rows], fields.at[part, pl.ds(DEPTH, CZ)])
-        copy(lower.at[slab, rows], fields.at[part, pl.ds(0, DEPTH)])
-        copy(upper.at[slab, rows], fields.at[part, pl.ds(DEPTH + CZ, DEPTH)])
-    for job in copies:
-        job.wait()
-    given = slice(8 - DEPTH, 8) if top else slice(0, DEPTH)
-
-    @pl.loop(0, LAYERS)
-    def _(layer):
-        for part in range(PARTS):
-            strip[layer, part * DEPTH : (part + 1) * DEPTH, :] = fields[part, layer, given, :]
-
-
-def strip_of(top, grids, lower, upper, after):
-    return pl.pallas_call(
-        functools.partial(strip_kernel, top),
-        name="strip",
-        out_shape=jax.ShapeDtypeStruct((LAYERS, STRIP, NX), f32),
-        in_specs=[HBM] * 6 + [ANY],
-        out_specs=VM,
-        scratch_shapes=[pltpu.VMEM((PARTS, LAYERS, 8, NX), f32), DMA((3 * PARTS,))],
-        compiler_params=params(),
-    )(*map(away, (*grids, lower, upper)), after)
+def write_rows(stack, sources, row):
+    for slot, source in enumerate(sources):
+        for layer in range(LAYERS):
+            stack[slot, layer : layer + 1, :] = source[layer, row : row + 1, :]
+        stack[slot, LAYERS:STACK, :] = jnp.zeros((STACK - LAYERS, NX), f32)
+
+
+def stack_of(count):
+    return jax.ShapeDtypeStruct((count, STACK, NX), f32)
 
 
 def slab_kernel(top, e_in, h_in, coef_in, loss_in, after, slab, sems):
@@ -281,30 +262,22 @@
 
 
 def halo_kernel(
-    found, columns, lower, upper, before, after,
-    e_in, h_in, coef_in, loss_in, e_xy, e_z, h, media, sample, coef, picked, sems,
+    found, columns, lower, upper, e_in, h_in, coef_in, loss_in,
+    e_xy, e_z, h, media, sample, coef, up, down, picked, sems,
 ):
     copies, copy = copier(sems)
     targets = [
         e_xy.at[0], e_xy.at[1], e_z, h.at[0], h.at[1], h.at[2], media.at[0], media.at[1],
     ]
-    sources = [e_in.at[k] for k in range(3)] + [h_in.at[k] for k in range(3)] + [coef_in, loss_in]
-    middle = pl.ds(PAD, CY)
-    for part, (source, target) in enumerate(zip(sources, targets)):
+    for part, source in enumerate(sources_of(e_in, h_in, coef_in, loss_in)):
         given = pl.ds(part * DEPTH, DEPTH)
-        copy(source, target.at[pl.ds(DEPTH, CZ), middle])
-        copy(lower.at[given], target.at[pl.ds(0, DEPTH), middle])
-        copy(upper.at[given], target.at[pl.ds(DEPTH + CZ, DEPTH), middle])
-
-    @pl.loop(0, LAYERS)
-    def _(layer):
-        for part, target in enumerate(targets):
-            rows = slice(part * DEPTH, (part + 1) * DEPTH)
-            target[layer, PAD - DEPTH : PAD, :] = before[layer, rows, :]
-            target[layer, PAD + CY : PAD + CY + DEPTH, :] = after[layer, rows, :]
-
+        copy(source, targets[part].at[pl.ds(DEPTH, CZ)])
+        copy(lower.at[given], targets[part].at[pl.ds(0, DEPTH)])
+        copy(upper.at[given], targets[part].at[pl.ds(DEPTH + CZ, DEPTH)])
     for job in copies:
         job.wait()
+    write_rows(up, targets[:4] + [targets[5]], CY - 1)
+    write_rows(down, (targets[0], targets[2]), 0)
 
     @pl.loop(0, LAYERS)
     def _(layer):
@@ -325,7 +298,7 @@
     return pick(picked[...], place)
 
 
-def halo(found, columns, lower, upper, before, after, e_in, h_in, coef, loss):
+def halo(found, columns, lower, upper, e_in, h_in, coef, loss):
     return pl.pallas_call(
         halo_kernel,
         name="halo",
@@ -336,21 +309,25 @@
             onchip((2,) + CUBE),
             onchip((REACH, 1)),
             onchip((REACH, 1)),
+            stack_of(5),
+            stack_of(2),
         ),
-        in_specs=[SM, VM, HBM, HBM, VM, VM] + [HBM] * 4,
-        out_specs=(VM,) * 6,
+        in_specs=[SM, VM, HBM, HBM] + [HBM] * 4,
+        out_specs=(VM,) * 8,
         scratch_shapes=[pltpu.VMEM((GROUP, NX), f32), DMA((24,))],
         compiler_params=params(),
-    )(found, columns, away(lower), away(upper), before, after, *map(away, (e_in, h_in, coef, loss)))
-
-
-def field_kernel(step, media, e_xy, e_z, h, to_xy, to_z, to_h):
-    low_z = jnp.where(lax.axis_index("gz") > 0, 1.0, 0.0)
+    )(found, columns, *map(away, (lower, upper, e_in, h_in, coef, loss)))
+
+
+def field_kernel(
+    step, base, front, back, near, edge_in, media, e_xy, e_z, h, to_xy, to_z, to_h, edge
+):
+    low_z = jnp.where(lax.axis_index("gz") > 0, time_step, 0.0)
     low_y = jnp.where(lax.axis_index("gy") > 0, time_step, 0.0)
     lane = lanes_of(TALL, NX)
     last_lane, first_lane = lane == NX - 1, lane == 0
     row = lax.broadcasted_iota(jnp.int32, (TALL, NX), 0)
-    rate_rows = jnp.where(row < PAD, low_y, time_step)
+    last_row, first_row = row == TALL - 1, row == 0
 
     def next_x(value):
         return jnp.where(last_lane, 0.0, pltpu.roll(value, NX - 1, 1))
@@ -358,26 +335,38 @@
     def prior_x(value):
         return jnp.where(first_lane, 0.0, pltpu.roll(value, 1, 1))
 
-    def next_y(value):
-        return pltpu.roll(value, TALL - 1, 0)
-
-    def prior_y(value):
-        return pltpu.roll(value, 1, 0)
+    def next_y(value, beyond):
+        return jnp.where(last_row, beyond, pltpu.roll(value, TALL - 1, 0))
+
+    def prior_y(value, beyond):
+        return jnp.where(first_row, beyond, pltpu.roll(value, 1, 0))
+
+    span = pl.ds(0, LAYERS)
+    out_x, out_y, out_z = front[0, span, :], front[1, span, :], front[2, span, :]
+    out_y_above = front[1, pl.ds(1, LAYERS), :]
+    tall_lane = lanes_of(LAYERS, NX)
+    out_y_next = jnp.where(tall_lane == NX - 1, 0.0, pltpu.roll(out_y, NX - 1, 1))
+    near_x, near_z = near[0, span, :], near[1, span, :]
+    edge_x, edge_z = edge_in[base, span, :], edge_in[base + 1, span, :]
+    edge[0, span, :] = edge_x - low_y * ((near_z - out_z) - (out_y_above - out_y))
+    edge[1, span, :] = edge_z - low_y * ((out_y_next - out_y) - (near_x - out_x))
 
     def magnetic(layer):
         e_x, e_y, e_zz = e_xy[0, layer], e_xy[1, layer], e_z[layer]
-        rate = rate_rows * jnp.where(layer < DEPTH, low_z, 1.0)
-        curl_x = (next_y(e_zz) - e_zz) - (e_xy[1, layer + 1] - e_y)
+        rate = jnp.where(layer < DEPTH, low_z, time_step)
+        beyond = pl.ds(layer, 1)
+        curl_x = (next_y(e_zz, back[1, beyond, :]) - e_zz) - (e_xy[1, layer + 1] - e_y)
         curl_y = (e_xy[0, layer + 1] - e_x) - (next_x(e_zz) - e_zz)
-        curl_z = (next_x(e_y) - e_y) - (next_y(e_x) - e_x)
+        curl_z = (next_x(e_y) - e_y) - (next_y(e_x, back[0, beyond, :]) - e_x)
         return (h[0, layer] - rate * curl_x, h[1, layer] - rate * curl_y, h[2, layer] - rate * curl_z)
 
     def electric(layer):
         h_x, h_y, h_z = to_h[0, layer], to_h[1, layer], to_h[2, layer]
         coef, kept = media[0, layer], media[1, layer]
-        back_x = (h_z - prior_y(h_z)) - (h_y - to_h[1, layer - 1])
+        beyond = pl.ds(layer, 1)
+        back_x = (h_z - prior_y(h_z, edge[1, beyond, :])) - (h_y - to_h[1, layer - 1])
         back_y = (h_x - to_h[0, layer - 1]) - (h_z - prior_x(h_z))
-        back_z = (h_y - prior_x(h_y)) - (h_x - prior_y(h_x))
+        back_z = (h_y - prior_x(h_y)) - (h_x - prior_y(h_x, edge[0, beyond, :]))
         return (
             kept * e_xy[0, layer] + coef * back_x,
             kept * e_xy[1, layer] + coef * back_y,
@@ -404,15 +393,19 @@
     put_e(last, electric(last))
 
 
-def field(step, media, e_xy, e_z, h):
-    return pl.pallas_call(
-        functools.partial(field_kernel, step),
+def field(step, front, back, near, edge, media, e_xy, e_z, h):
+    first = edge is None
+    return pl.pallas_call(
+        functools.partial(field_kernel, step, 3 if first else 0),
         name="field",
-        out_shape=(onchip((2,) + CUBE), onchip(CUBE), onchip((3,) + CUBE)),
-        in_specs=[VM] * 4,
-        out_specs=(VM,) * 3,
-        compiler_params=params(),
-    )(keep(media), keep(e_xy), keep(e_z), keep(h))
+        out_shape=(onchip((2,) + CUBE), onchip(CUBE), onchip((3,) + CUBE), onchip((2, STACK, NX))),
+        in_specs=[VM] * 8,
+        out_specs=(VM,) * 4,
+        compiler_params=params(),
+    )(
+        front, back, near, front if first else keep(edge),
+        keep(media), keep(e_xy), keep(e_z), keep(h),
+    )
 
 
 def solve(stride, arrived, off_cols, volts, m_off, m_diag, m_inv):
@@ -465,13 +458,45 @@
             e_z[layer, row, :] = e_z[layer, row, :] + deltas[port : port + 1, :]
 
 
-def circuit_kernel(
-    stride, table, off_cols, arrived, columns, sample, coef, volts, m_off, m_diag, m_inv, e_in,
-    e_z, out, volts_out, sample_out, near_rows, deltas, picked, spread_rows,
+def ports_kernel(
+    stride, table, arrived, columns, sample, coef, e_xy, e_in, e_z, up, near_rows, deltas,
 ):
     e_z[...] = e_in[...]
     apply_ports(stride, table, arrived, columns, sample, coef, e_z, near_rows, deltas)
-
+    write_rows(up, (e_xy.at[0], e_xy.at[1], e_z), CY - 1)
+
+
+def ports(table, arrived, columns, sample, coef, e_xy, e_z):
+    return pl.pallas_call(
+        functools.partial(ports_kernel, arrived.shape[0] // ND),
+        name="ports",
+        out_shape=(onchip(CUBE), stack_of(3)),
+        in_specs=[SM] + [VM] * 6,
+        out_specs=(VM, VM),
+        scratch_shapes=[pltpu.VMEM((GROUP, NODE_DEV), f32), pltpu.VMEM((GROUP, NX), f32)],
+        compiler_params=params(),
+    )(table, arrived, columns, keep(sample), keep(coef), keep(e_xy), keep(e_z))
+
+
+def base_kernel(e_xy, e_z, after, down):
+    write_rows(down, (e_xy.at[0], e_z), 0)
+
+
+def base_rows(e_xy, e_z, after):
+    return pl.pallas_call(
+        base_kernel,
+        name="base",
+        out_shape=stack_of(2),
+        in_specs=[VM, VM, ANY],
+        out_specs=VM,
+        compiler_params=params(),
+    )(keep(e_xy), keep(e_z), after)
+
+
+def circuit_kernel(
+    stride, table, off_cols, arrived, columns, volts, m_off, m_diag, m_inv, e_z, after,
+    out, volts_out, sample_out, picked, spread_rows,
+):
     @pl.loop(0, table[COUNT])
     def _(group):
         part = pl.ds(pl.multiple_of(group * GROUP, GROUP), GROUP)
@@ -487,29 +512,16 @@
     add_rows(out, 2, [table[NODES + port] for port in range(PORT_DEV)], spread_rows)
 
 
-def circuit(table, off_cols, arrived, columns, sample, coef, volts, mats, e_z):
+def circuit(table, off_cols, arrived, columns, volts, mats, e_z, after):
     return pl.pallas_call(
         functools.partial(circuit_kernel, arrived.shape[0] // ND),
         name="circuit",
-        out_shape=(
-            onchip(CUBE),
-            onchip((2 * ND, NODE_DEV)),
-            onchip((1, NODE_DEV)),
-            onchip((REACH, 1)),
-        ),
-        in_specs=[SM, SM] + [VM] * 9,
-        out_specs=(VM,) * 4,
-        scratch_shapes=[
-            pltpu.VMEM((GROUP, NODE_DEV), f32),
-            pltpu.VMEM((GROUP, NX), f32),
-            pltpu.VMEM((GROUP, NX), f32),
-            pltpu.VMEM((PORT_DEV, NODE_DEV), f32),
-        ],
-        compiler_params=params(),
-    )(
-        table, off_cols, arrived, columns, keep(sample), keep(coef), volts,
-        *[keep(mat) for mat in mats], keep(e_z),
-    )
+        out_shape=(onchip((2 * ND, NODE_DEV)), onchip((1, NODE_DEV)), onchip((REACH, 1))),
+        in_specs=[SM, SM] + [VM] * 7 + [ANY],
+        out_specs=(VM,) * 3,
+        scratch_shapes=[pltpu.VMEM((GROUP, NX), f32), pltpu.VMEM((PORT_DEV, NODE_DEV), f32)],
+        compiler_params=params(),
+    )(table, off_cols, arrived, columns, volts, *[keep(mat) for mat in mats], keep(e_z), after)
 
 
 def finish_kernel(
@@ -517,14 +529,14 @@
     e_out, h_out, volts_out, e_z, near_rows, deltas, sems,
 ):
     copies, copy = copier(sems)
-    layers, rows = pl.ds(DEPTH, CZ), pl.ds(PAD, CY)
+    layers = pl.ds(DEPTH, CZ)
     for k in range(3):
-        copy(h.at[k, layers, rows], h_out.at[k])
+        copy(h.at[k, layers], h_out.at[k])
     for k in range(2):
-        copy(e_xy.at[k, layers, rows], e_out.at[k])
+        copy(e_xy.at[k, layers], e_out.at[k])
     e_z[...] = e_in[...]
     apply_ports(stride, table, arrived, columns, sample, coef, e_z, near_rows, deltas)
-    copy(e_z.at[layers, rows], e_out.at[2])
+    copy(e_z.at[layers], e_out.at[2])
     volts_out[...] = solve(stride, arrived, off_cols, volts, m_off, m_diag, m_inv)
     for job in copies:
         job.wait()
@@ -587,27 +599,29 @@
     upper = shifted(down, "gz", -1)
     out = begin(n_gy, port_cell, port_node, port_gain, e_field, volts, down)
     arrived = exchange(out)
-    front = strip_of(True, grids, lower, upper, out)
-    before = shifted(front, "gy", 1)
-    back = strip_of(False, grids, lower, upper, front)
-    after = shifted(back, "gy", -1)
-    arrived, front, back = lax.optimization_barrier((arrived, front, back))
     mats = matrices(diag_blocks, inv_blocks, off_blocks)
 
     found, columns = plan(n_gz, n_gy, arrived, port_node, port_gain)
     table = jnp.concatenate([found[0], found[1], found[7, 0:1]])
 
-    e_xy, e_z, h, media, sample, coef = halo(table, columns, lower, upper, before, after, *grids)
+    e_xy, e_z, h, media, sample, coef, up, down = halo(table, columns, lower, upper, *grids)
+    edge = None
     for step in range(1, STEPS + 1):
+        front = shifted(up, "gy", 1)
+        back = shifted(down, "gy", -1)
         if step > 1:
+            out, volts, sample = circuit(table, off_cols, arrived, columns, volts, mats, e_z, down)
+            out, back = lax.optimization_barrier((out, back))
             arrived = exchange(out)
             arrived, e_z = lax.optimization_barrier((arrived, e_z))
-        e_xy, e_z, h = field(step, media, e_xy, e_z, h)
-        shared = (table, off_cols, arrived, columns, sample, coef, volts, mats)
+        e_xy, e_z, h, edge = field(step, front, back, down, edge, media, e_xy, e_z, h)
         if step < STEPS:
-            e_z, out, volts, sample = circuit(*shared, e_z)
+            e_z, up = ports(table, arrived, columns, sample, coef, e_xy, e_z)
+            down = base_rows(e_xy, e_z, up)
         else:
-            e_end, h_end, volts = finish(*shared, e_xy, e_z, h)
+            e_end, h_end, volts = finish(
+                table, off_cols, arrived, columns, sample, coef, volts, mats, e_xy, e_z, h
+            )
     return e_end, h_end, volts.reshape(-1)
 
 

time: 195 us -> 185 us (0.949)
  waiting for transfers between devices: 40.2 us -> 4.09 us
  blocking collectives: 65.1 us -> 97.1 us
  Pallas kernels: 60.1 us -> 47.6 us
  starting transfers between devices: 25.7 us -> 31.6 us
    all_to_all x4 -> x5, blocking collectives: 65.1 us -> 97.1 us  [exchange(): return lax.all_to_all(value, ('gz', 'gy'), 0, 0, tiled=True)]
    all_to_all x1 -> x0, waiting for transfers between devices: 30.1 us -> none  [exchange(): return lax.all_to_all(value, ('gz', 'gy'), 0, 0, tiled=True)]
    ppermute x4 -> x12, starting transfers between devices: 13.2 us -> 31.6 us  [shifted(): lax.ppermute(value, axis, [(source, source + steps) for source in range(f...]
    all_to_all x1 -> x0, starting transfers between devices: 12.4 us -> none  [exchange(): return lax.all_to_all(value, ('gz', 'gy'), 0, 0, tiled=True)]
    pallas_call x4, Pallas kernels: 15.5 us -> 6.81 us  [circuit(): pl.pallas_call(functools.partial(circuit_kernel, arrived.shape[0] // ND),...]
    ppermute x4 -> x12, waiting for transfers between devices: 10.1 us -> 4.09 us  [shifted(): lax.ppermute(value, axis, [(source, source + steps) for source in range(f...]
    pallas_call x7 -> x13, Pallas kernels: 27.2 us -> 27 us  [the longest x5 18.3 us: field(): pl.pallas_call(functools.partial(field_kernel, step, 3 if first else 0),...]
  transfers between devices with their start and end apart: 5 -> 12, of which waited for: 3 -> 1; matrix products, arithmetic and copies ran while one was open for 1% -> 1% of each run, Pallas kernels for 2% -> 5%
where the time goes in v8:
time: 185 us; the launch traced here: 184 us
  blocking collectives  97.1 us (52%)
  Pallas kernels  47.6 us (26%)
  starting transfers between devices  31.6 us (17%)
  waiting for transfers between devices  4.09 us (2%)
  local copies, waits for them, and re-layouts  2.29 us (1%)
    all_to_all x5, blocking collectives, exchange(): return lax.all_to_all(value, ('gz', 'gy'), 0, 0, tiled=True)  97.1 us
    ppermute x12, starting transfers between devices, shifted(): lax.ppermute(value, axis, [(source, source + steps) for source in range(f...  31.6 us
    pallas_call x5, Pallas kernels, field(): pl.pallas_call(functools.partial(field_kernel, step, 3 if first else 0),...  18.3 us
    pallas_call x4, Pallas kernels, ports(): pl.pallas_call(functools.partial(ports_kernel, arrived.shape[0] // ND), n...  8.47 us
    pallas_call x4, Pallas kernels, circuit(): pl.pallas_call(functools.partial(circuit_kernel, arrived.shape[0] // ND),...  6.81 us
    pallas_call x1, Pallas kernels, halo(): pl.pallas_call(halo_kernel, name='halo', out_shape=(onchip((2,) + CUBE),...  4.55 us
    ppermute x12, waiting for transfers between devices, shifted(): lax.ppermute(value, axis, [(source, source + steps) for source in range(f...  4.09 us
  transfers between devices with their start and end apart: 12, of which 1 were waited for; matrix products, arithmetic and copies ran while one was open for 1% of the time, Pallas kernels for 5%

profile of v8, /device:TPU:1, one launch (start us, length us, event | category | flops | bytes accessed | tf_op | source)
XLA Modules:
  0.0 184.4 jit_solution(10840447318129321014)
XLA Ops:
  0.6 0.0 copy-start.6
  0.6 0.6 copy-done.6
  1.3 1.2 slab.2.after
  2.5 0.0 copy-start.1
  2.5 0.0 copy-start.2
  2.6 0.0 copy-start.8
  2.6 1.2 slab.3.after
  3.8 3.3 %collective-permute-start.1 = (f32[40,16,256]{2,1,0:T(8,128)S(1)}, f32[40,16,256]{2,1,0:T(8,128)S(1)}, u32[]{:S(2)}, u32[]{:S(2)}) collective-permute-start(f32[40,16,256]{2,1,0:T(8,128)S(1)} %slab.3.after), channel_id=1, source_target_pairs={{8,0},{16,8},{24,16},{32,24},{40,32},{48,40},{56,48},{64,56},{72,6... | collective-permute-start | bytes 1966088 | tf_op jit(solution)/shard_map/ppermute | solution.py:572
  7.2 3.2 %collective-permute-start = (f32[40,16,256]{2,1,0:T(8,128)S(1)}, f32[40,16,256]{2,1,0:T(8,128)S(1)}, u32[]{:S(2)}, u32[]{:S(2)}) collective-permute-start(f32[40,16,256]{2,1,0:T(8,128)S(1)} %slab.2.after), channel_id=1, source_target_pairs={{0,8},{8,16},{16,24},{24,32},{32,40},{40,48},{48,56},{56,64},{64,7... | collective-permute-start | bytes 1966088 | tf_op jit(solution)/shard_map/ppermute | solution.py:572
  10.4 2.7 %begin.1 = f32[512,128]{1,0:T(8,128)S(1)} custom-call(s32[32]{0:T(128)S(1)} %copy-done.8, s32[4096]{0:T(1024)S(1)} %copy-done.1, f32[4096]{0:T(1024)S(1)} %copy-done.2, f32[3,32,16,256]{3,2,1,0:T(8,128)} %e_in.7, s32[1,32]{1,0:T(1,128)S(1)} %bitcast.40, f32[1,128]{1,0:T(1,128)S(1)} %bitcast.38, f32[40,16,256]{2,1,0:T(8,128)S(1)} %slab.3.after), custom_call_target="tpu_custom_call" | custom-call | tf_op jit(solution)/shard_map/begin/pallas_call | solution.py:161
  13.1 21.7 %all_to_all.59 = f32[128,4,128]{2,1,0:T(4,128)S(1)} all-to-all(f32[128,4,128]{2,1,0:T(4,128)S(1)} %bitcast.29), channel_id=1, replica_groups=mesh['gz'=16,'gy'=8] {'gz','gy'}, dimensions={0} | all-to-all | bytes 524288 | tf_op jit(solution)/shard_map/all_to_all | solution.py:576
  34.7 0.4 plan.1
  35.2 0.5 slice.11
  35.7 0.7 pad_add_fusion.found.table
  36.4 0.0 collective-permute-done.1.upper
  36.5 0.0 collective-permute-done.lower
  36.5 0.0 copy-start.10
  36.5 0.8 copy-done.9
  37.3 0.2 copy-done.10
  37.5 4.5 %halo.1 = (f32[2,42,16,256]{3,2,1,0:T(8,128)S(1)}, f32[42,16,256]{2,1,0:T(8,128)S(1)}, f32[3,42,16,256]{3,2,1,0:T(8,128)S(1)}, f32[2,42,16,256]{3,2,1,0:T(8,128)...) custom-call(s32[193]{0:T(256)S(1)} %pad_add_fusion.found.table, ...), custom_call_target="tpu_custom_call" | custom-call | tf_op jit(solution)/shard_map/halo/pallas_call | solution.py:302
  42.1 2.5 %collective-permute-start.2 = (f32[5,48,256]{2,1,0:T(8,128)S(1)}, f32[5,48,256]{2,1,0:T(8,128)S(1)}, u32[]{:S(2)}, u32[]{:S(2)}) collective-permute-start(f32[5,48,256]{2,1,0:T(8,128)S(1)} %get-tuple-element.81), channel_id=1, source_target_pairs={{0,1},{1,2},{2,3},{3,4},{4,5},{5,6},{6,7},{8,9},{9,10},{10,11},{11... | collective-permute-start | bytes 737288 | tf_op jit(solution)/shard_map/ppermute | solution.py:572
  44.5 1.3 collective-permute-start.3
  45.8 4.1 %collective-permute-done.3.back = f32[2,48,256]{2,1,0:T(8,128)S(1)} collective-permute-done((f32[2,48,256]{2,1,0:T(8,128)S(1)}, f32[2,48,256]{2,1,0:T(8,128)S(1)}, u32[]{:S(2)}, u32[]{:S(2)}) %collective-permute-start.3) | collective-permute-done | bytes 98336 | tf_op jit(solution)/shard_map/ppermute | solution.py:572
  49.9 0.0 collective-permute-done.2.front.edge_in
  49.9 4.0 %field.5 = (f32[2,42,16,256]{3,2,1,0:T(8,128)S(1)}, f32[42,16,256]{2,1,0:T(8,128)S(1)}, f32[3,42,16,256]{3,2,1,0:T(8,128)S(1)}, f32[2,48,256]{2,1,0:T(8,128)S(1)}) custom-call(f32[5,48,256]{2,1,0:T(8,128)S(1)} %collective-permute-done.2.front.edge_in, f32[2,48,256]{2,1,0:T(8,128)S(1)} %collective-permute-done.3.back, ...), custom_call_target="tpu_custom_call" | custom-call | tf_op jit(solution)/shard_map/field/pallas_call | solution.py:398
  53.9 2.1 %ports.4 = (f32[42,16,256]{2,1,0:T(8,128)S(1)}, f32[3,48,256]{2,1,0:T(8,128)S(1)}) custom-call(s32[193]{0:T(256)S(1)} %pad_add_fusion.found.table, f32[512,128]{1,0:T(8,128)S(1)} %bitcast.21, f32[96,8]{1,0:T(8,128)S(1)} %get-tuple-element.75.columns, f32[96,1]{1,0:T(8,128)S(1)} %get-tuple-element.79.sample, f32[96,1]{1,0:T(8,128)S(1)} %get-tuple-element.80.coef, ...), custom_call_target="tpu_custom_call" | custom-call | tf_op jit(solution)/shard_map/ports/pallas_call | solution.py:470
  56.0 0.0 copy-start
  56.0 0.0 copy-start.3
  56.0 0.0 copy-start.4
  56.0 0.0 copy-start.5
  56.0 0.0 copy-start.7
  56.1 1.4 collective-permute-start.4
  57.5 4.0 %collective-permute-start.5 = (f32[3,48,256]{2,1,0:T(8,128)S(1)}, f32[3,48,256]{2,1,0:T(8,128)S(1)}, u32[]{:S(2)}, u32[]{:S(2)}) collective-permute-start(f32[3,48,256]{2,1,0:T(8,128)S(1)} %get-tuple-element.90.after), channel_id=1, source_target_pairs={{0,1},{1,2},{2,3},{3,4},{4,5},{5,6},{6,7},{8,9},{9,10},{10,11},{11... | collective-permute-start | bytes 442376 | tf_op jit(solution)/shard_map/ppermute | solution.py:572
  61.6 0.2 matrices.1
  61.8 1.7 circuit.4
  63.5 0.0 collective-permute-done.4.back
  63.5 24.6 %all_to_all.60 = f32[128,2,128]{2,1,0:T(2,128)S(1)} all-to-all(f32[128,2,128]{2,1,0:T(2,128)S(1)} %bitcast.34), channel_id=1, replica_groups=mesh['gz'=16,'gy'=8] {'gz','gy'}, dimensions={0} | all-to-all | bytes 262144 | tf_op jit(solution)/shard_map/all_to_all | solution.py:576
  88.1 0.0 collective-permute-done.5.front
  88.1 3.7 %field.6 = (f32[2,42,16,256]{3,2,1,0:T(8,128)S(1)}, f32[42,16,256]{2,1,0:T(8,128)S(1)}, f32[3,42,16,256]{3,2,1,0:T(8,128)S(1)}, f32[2,48,256]{2,1,0:T(8,128)S(1)}) custom-call(f32[3,48,256]{2,1,0:T(8,128)S(1)} %collective-permute-done.5.front, f32[2,48,256]{2,1,0:T(8,128)S(1)} %collective-permute-done.4.back, f32[2,48,256]{2,1,0:T(8,128)S(1)} %base.4.after.near, ...), custom_call_target="tpu_custom_call" | custom-call | tf_op jit(solution)/shard_map/field/pallas_call | solution.py:398
  91.8 2.1 %ports.5 = (f32[42,16,256]{2,1,0:T(8,128)S(1)}, f32[3,48,256]{2,1,0:T(8,128)S(1)}) custom-call(s32[193]{0:T(256)S(1)} %pad_add_fusion.found.table, f32[256,128]{1,0:T(8,128)S(1)} %bitcast.23, f32[96,8]{1,0:T(8,128)S(1)} %get-tuple-element.75.columns, f32[96,1]{1,0:T(8,128)S(1)} %get-tuple-element.95.sample, f32[96,1]{1,0:T(8,128)S(1)} %get-tuple-element.80.coef, ...), custom_call_target="tpu_custom_call" | custom-call | tf_op jit(solution)/shard_map/ports/pallas_call | solution.py:470
  94.0 1.3 collective-permute-start.6
  95.3 4.0 %collective-permute-start.7 = (f32[3,48,256]{2,1,0:T(8,128)S(1)}, f32[3,48,256]{2,1,0:T(8,128)S(1)}, u32[]{:S(2)}, u32[]{:S(2)}) collective-permute-start(f32[3,48,256]{2,1,0:T(8,128)S(1)} %get-tuple-element.103.after), channel_id=1, source_target_pairs={{0,1},{1,2},{2,3},{3,4},{4,5},{5,6},{6,7},{8,9},{9,10},{10,11},{11... | collective-permute-start | bytes 442376 | tf_op jit(solution)/shard_map/ppermute | solution.py:572
  99.3 1.7 circuit.5
  101.0 0.0 collective-permute-done.6.back
  101.0 17.0 %all_to_all.61 = f32[128,2,128]{2,1,0:T(2,128)S(1)} all-to-all(f32[128,2,128]{2,1,0:T(2,128)S(1)} %bitcast.31), channel_id=1, replica_groups=mesh['gz'=16,'gy'=8] {'gz','gy'}, dimensions={0} | all-to-all | bytes 262144 | tf_op jit(solution)/shard_map/all_to_all | solution.py:576
  117.9 0.0 collective-permute-done.7.front
  117.9 3.5 %field.7 = (f32[2,42,16,256]{3,2,1,0:T(8,128)S(1)}, f32[42,16,256]{2,1,0:T(8,128)S(1)}, f32[3,42,16,256]{3,2,1,0:T(8,128)S(1)}, f32[2,48,256]{2,1,0:T(8,128)S(1)}) custom-call(f32[3,48,256]{2,1,0:T(8,128)S(1)} %collective-permute-done.7.front, f32[2,48,256]{2,1,0:T(8,128)S(1)} %collective-permute-done.6.back, f32[2,48,256]{2,1,0:T(8,128)S(1)} %base.5.after.near, ...), custom_call_target="tpu_custom_call" | custom-call | tf_op jit(solution)/shard_map/field/pallas_call | solution.py:398
  121.5 2.1 %ports.6 = (f32[42,16,256]{2,1,0:T(8,128)S(1)}, f32[3,48,256]{2,1,0:T(8,128)S(1)}) custom-call(s32[193]{0:T(256)S(1)} %pad_add_fusion.found.table, f32[256,128]{1,0:T(8,128)S(1)} %bitcast.25, f32[96,8]{1,0:T(8,128)S(1)} %get-tuple-element.75.columns, f32[96,1]{1,0:T(8,128)S(1)} %get-tuple-element.108.sample, f32[96,1]{1,0:T(8,128)S(1)} %get-tuple-element.80.coef, ...), custom_call_target="tpu_custom_call" | custom-call | tf_op jit(solution)/shard_map/ports/pallas_call | solution.py:470
  123.7 1.3 collective-permute-start.8
  125.0 4.0 %collective-permute-start.9 = (f32[3,48,256]{2,1,0:T(8,128)S(1)}, f32[3,48,256]{2,1,0:T(8,128)S(1)}, u32[]{:S(2)}, u32[]{:S(2)}) collective-permute-start(f32[3,48,256]{2,1,0:T(8,128)S(1)} %get-tuple-element.116.after), channel_id=1, source_target_pairs={{0,1},{1,2},{2,3},{3,4},{4,5},{5,6},{6,7},{8,9},{9,10},{10,11},{11... | collective-permute-start | bytes 442376 | tf_op jit(solution)/shard_map/ppermute | solution.py:572
  129.0 1.7 circuit.6
  130.7 0.0 collective-permute-done.8.back
  130.7 17.0 %all_to_all.62 = f32[128,2,128]{2,1,0:T(2,128)S(1)} all-to-all(f32[128,2,128]{2,1,0:T(2,128)S(1)} %bitcast.32), channel_id=1, replica_groups=mesh['gz'=16,'gy'=8] {'gz','gy'}, dimensions={0} | all-to-all | bytes 262144 | tf_op jit(solution)/shard_map/all_to_all | solution.py:576
  147.6 0.0 collective-permute-done.9.front
  147.6 3.3 %field.8 = (f32[2,42,16,256]{3,2,1,0:T(8,128)S(1)}, f32[42,16,256]{2,1,0:T(8,128)S(1)}, f32[3,42,16,256]{3,2,1,0:T(8,128)S(1)}, f32[2,48,256]{2,1,0:T(8,128)S(1)}) custom-call(f32[3,48,256]{2,1,0:T(8,128)S(1)} %collective-permute-done.9.front, f32[2,48,256]{2,1,0:T(8,128)S(1)} %collective-permute-done.8.back, f32[2,48,256]{2,1,0:T(8,128)S(1)} %base.6.after.near, ...), custom_call_target="tpu_custom_call" | custom-call | tf_op jit(solution)/shard_map/field/pallas_call | solution.py:398
  151.0 2.1 %ports.7 = (f32[42,16,256]{2,1,0:T(8,128)S(1)}, f32[3,48,256]{2,1,0:T(8,128)S(1)}) custom-call(s32[193]{0:T(256)S(1)} %pad_add_fusion.found.table, f32[256,128]{1,0:T(8,128)S(1)} %bitcast.27, f32[96,8]{1,0:T(8,128)S(1)} %get-tuple-element.75.columns, f32[96,1]{1,0:T(8,128)S(1)} %get-tuple-element.121.sample, f32[96,1]{1,0:T(8,128)S(1)} %get-tuple-element.80.coef, ...), custom_call_target="tpu_custom_call" | custom-call | tf_op jit(solution)/shard_map/ports/pallas_call | solution.py:470
  153.2 1.3 collective-permute-start.10
  154.5 4.0 %collective-permute-start.11 = (f32[3,48,256]{2,1,0:T(8,128)S(1)}, f32[3,48,256]{2,1,0:T(8,128)S(1)}, u32[]{:S(2)}, u32[]{:S(2)}) collective-permute-start(f32[3,48,256]{2,1,0:T(8,128)S(1)} %get-tuple-element.129.after), channel_id=1, source_target_pairs={{0,1},{1,2},{2,3},{3,4},{4,5},{5,6},{6,7},{8,9},{9,10},{10,11},{11... | collective-permute-start | bytes 442376 | tf_op jit(solution)/shard_map/ppermute | solution.py:572
  158.5 1.7 circuit.7
  160.2 0.0 collective-permute-done.10.back
  160.2 17.0 %all_to_all.63 = f32[128,2,128]{2,1,0:T(2,128)S(1)} all-to-all(f32[128,2,128]{2,1,0:T(2,128)S(1)} %bitcast.33), channel_id=1, replica_groups=mesh['gz'=16,'gy'=8] {'gz','gy'}, dimensions={0} | all-to-all | bytes 262144 | tf_op jit(solution)/shard_map/all_to_all | solution.py:576
  177.1 0.0 collective-permute-done.11.front
  177.1 3.8 %field.9 = (f32[2,42,16,256]{3,2,1,0:T(8,128)S(1)}, f32[42,16,256]{2,1,0:T(8,128)S(1)}, f32[3,42,16,256]{3,2,1,0:T(8,128)S(1)}, f32[2,48,256]{2,1,0:T(8,128)}) custom-call(f32[3,48,256]{2,1,0:T(8,128)S(1)} %collective-permute-done.11.front, f32[2,48,256]{2,1,0:T(8,128)S(1)} %collective-permute-done.10.back, f32[2,48,256]{2,1,0:T(8,128)S(1)} %base.7.after.near, ...), custom_call_target="tpu_custom_call" | custom-call | tf_op jit(solution)/shard_map/field/pallas_call | solution.py:398
  180.9 3.5 %finish.1 = (f32[3,32,16,256]{3,2,1,0:T(8,128)}, f32[3,32,16,256]{3,2,1,0:T(8,128)}, f32[1,128]{1,0:T(1,128)}) custom-call(s32[193]{0:T(256)S(1)} %pad_add_fusion.found.table, s32[2,4]{1,0:T(2,128)S(1)} %copy-done.5, f32[256,128]{1,0:T(8,128)S(1)} %bitcast.30, f32[96,8]{1,0:T(8,128)S(1)} %get-tuple-element.75.columns, ...), custom_call_target="tpu_custom_call" | custom-call | tf_op jit(solution)/shard_map/finish/pallas_call | solution.py:546
  (14 shorter events, 0.2 us)
Async XLA Ops:
  0.6 0.7 copy-start.6
  2.5 7.8 %copy-start.1 = (s32[4096]{0:T(1024)S(1)}, s32[4096]{0:T(1024)}, u32[]{:S(2)}) copy-start(s32[4096]{0:T(1024)} %nodes.1) | copy-start | bytes 49156
  2.5 7.8 %copy-start.2 = (f32[4096]{0:T(1024)S(1)}, f32[4096]{0:T(1024)}, u32[]{:S(2)}) copy-start(f32[4096]{0:T(1024)} %gains.1) | copy-start | bytes 49156
  2.6 7.8 %copy-start.8 = (s32[32]{0:T(128)S(1)}, s32[32]{0:T(128)}, u32[]{:S(2)}) copy-start(s32[32]{0:T(128)} %cells.1) | copy-start | bytes 388
  3.8 32.6 %collective-permute-start.1 = (f32[40,16,256]{2,1,0:T(8,128)S(1)}, f32[40,16,256]{2,1,0:T(8,128)S(1)}, u32[]{:S(2)}, u32[]{:S(2)}) collective-permute-start(f32[40,16,256]{2,1,0:T(8,128)S(1)} %slab.3.after), channel_id=1, source_target_pairs={{8,0},{16,8},{24,16},{32,24},{40,32},{48,40},{56,48},{64,56},{72,6... | collective-permute-start | bytes 1966088 | tf_op jit(solution)/shard_map/ppermute | solution.py:572
  7.2 29.3 %collective-permute-start = (f32[40,16,256]{2,1,0:T(8,128)S(1)}, f32[40,16,256]{2,1,0:T(8,128)S(1)}, u32[]{:S(2)}, u32[]{:S(2)}) collective-permute-start(f32[40,16,256]{2,1,0:T(8,128)S(1)} %slab.2.after), channel_id=1, source_target_pairs={{0,8},{8,16},{16,24},{24,32},{32,40},{40,48},{48,56},{56,64},{64,7... | collective-permute-start | bytes 1966088 | tf_op jit(solution)/shard_map/ppermute | solution.py:572
  36.5 0.8 copy-start.9
  36.5 1.0 copy-start.10
  42.1 7.8 %collective-permute-start.2 = (f32[5,48,256]{2,1,0:T(8,128)S(1)}, f32[5,48,256]{2,1,0:T(8,128)S(1)}, u32[]{:S(2)}, u32[]{:S(2)}) collective-permute-start(f32[5,48,256]{2,1,0:T(8,128)S(1)} %get-tuple-element.81), channel_id=1, source_target_pairs={{0,1},{1,2},{2,3},{3,4},{4,5},{5,6},{6,7},{8,9},{9,10},{10,11},{11... | collective-permute-start | bytes 737288 | tf_op jit(solution)/shard_map/ppermute | solution.py:572
  44.5 5.4 %collective-permute-start.3 = (f32[2,48,256]{2,1,0:T(8,128)S(1)}, f32[2,48,256]{2,1,0:T(8,128)S(1)}, u32[]{:S(2)}, u32[]{:S(2)}) collective-permute-start(f32[2,48,256]{2,1,0:T(8,128)S(1)} %get-tuple-element.82.near), channel_id=1, source_target_pairs={{1,0},{2,1},{3,2},{4,3},{5,4},{6,5},{7,6},{9,8},{10,9},{11,10},{12... | collective-permute-start | bytes 294920 | tf_op jit(solution)/shard_map/ppermute | solution.py:572
  56.0 5.6 %copy-start = (f32[2,4,64,64]{3,2,1,0:T(8,128)S(1)}, f32[2,4,64,64]{3,2,1,0:T(8,128)}, u32[]{:S(2)}) copy-start(f32[2,4,64,64]{3,2,1,0:T(8,128)} %off.1) | copy-start | bytes 393220
  56.0 5.6 %copy-start.3 = (f32[2,64,64]{2,1,0:T(8,128)S(1)}, f32[2,64,64]{2,1,0:T(8,128)}, u32[]{:S(2)}) copy-start(f32[2,64,64]{2,1,0:T(8,128)} %diag.1) | copy-start | bytes 98308
  56.0 5.6 %copy-start.4 = (f32[2,64,64]{2,1,0:T(8,128)S(1)}, f32[2,64,64]{2,1,0:T(8,128)}, u32[]{:S(2)}) copy-start(f32[2,64,64]{2,1,0:T(8,128)} %inv.1) | copy-start | bytes 98308
  56.0 5.7 %copy-start.5 = (s32[2,4]{1,0:T(2,128)S(1)}, s32[2,4]{1,0:T(2,128)}, u32[]{:S(2)}) copy-start(s32[2,4]{1,0:T(2,128)} %off_cols.9) | copy-start | bytes 100
  56.0 5.7 %copy-start.7 = (f32[128]{0:T(128)S(1)}, f32[128]{0:T(128)}, u32[]{:S(2)}) copy-start(f32[128]{0:T(128)} %param.23) | copy-start | bytes 1540
  56.1 7.4 %collective-permute-start.4 = (f32[2,48,256]{2,1,0:T(8,128)S(1)}, f32[2,48,256]{2,1,0:T(8,128)S(1)}, u32[]{:S(2)}, u32[]{:S(2)}) collective-permute-start(f32[2,48,256]{2,1,0:T(8,128)S(1)} %base.4.after.near), channel_id=1, source_target_pairs={{1,0},{2,1},{3,2},{4,3},{5,4},{6,5},{7,6},{9,8},{10,9},{11,10},{12... | collective-permute-start | bytes 294920 | tf_op jit(solution)/shard_map/ppermute | solution.py:572
  57.5 30.5 %collective-permute-start.5 = (f32[3,48,256]{2,1,0:T(8,128)S(1)}, f32[3,48,256]{2,1,0:T(8,128)S(1)}, u32[]{:S(2)}, u32[]{:S(2)}) collective-permute-start(f32[3,48,256]{2,1,0:T(8,128)S(1)} %get-tuple-element.90.after), channel_id=1, source_target_pairs={{0,1},{1,2},{2,3},{3,4},{4,5},{5,6},{6,7},{8,9},{9,10},{10,11},{11... | collective-permute-start | bytes 442376 | tf_op jit(solution)/shard_map/ppermute | solution.py:572
  94.0 7.0 %collective-permute-start.6 = (f32[2,48,256]{2,1,0:T(8,128)S(1)}, f32[2,48,256]{2,1,0:T(8,128)S(1)}, u32[]{:S(2)}, u32[]{:S(2)}) collective-permute-start(f32[2,48,256]{2,1,0:T(8,128)S(1)} %base.5.after.near), channel_id=1, source_target_pairs={{1,0},{2,1},{3,2},{4,3},{5,4},{6,5},{7,6},{9,8},{10,9},{11,10},{12... | collective-permute-start | bytes 294920 | tf_op jit(solution)/shard_map/ppermute | solution.py:572
  95.3 22.7 %collective-permute-start.7 = (f32[3,48,256]{2,1,0:T(8,128)S(1)}, f32[3,48,256]{2,1,0:T(8,128)S(1)}, u32[]{:S(2)}, u32[]{:S(2)}) collective-permute-start(f32[3,48,256]{2,1,0:T(8,128)S(1)} %get-tuple-element.103.after), channel_id=1, source_target_pairs={{0,1},{1,2},{2,3},{3,4},{4,5},{5,6},{6,7},{8,9},{9,10},{10,11},{11... | collective-permute-start | bytes 442376 | tf_op jit(solution)/shard_map/ppermute | solution.py:572
  123.7 7.0 %collective-permute-start.8 = (f32[2,48,256]{2,1,0:T(8,128)S(1)}, f32[2,48,256]{2,1,0:T(8,128)S(1)}, u32[]{:S(2)}, u32[]{:S(2)}) collective-permute-start(f32[2,48,256]{2,1,0:T(8,128)S(1)} %base.6.after.near), channel_id=1, source_target_pairs={{1,0},{2,1},{3,2},{4,3},{5,4},{6,5},{7,6},{9,8},{10,9},{11,10},{12... | collective-permute-start | bytes 294920 | tf_op jit(solution)/shard_map/ppermute | solution.py:572
  125.0 22.7 %collective-permute-start.9 = (f32[3,48,256]{2,1,0:T(8,128)S(1)}, f32[3,48,256]{2,1,0:T(8,128)S(1)}, u32[]{:S(2)}, u32[]{:S(2)}) collective-permute-start(f32[3,48,256]{2,1,0:T(8,128)S(1)} %get-tuple-element.116.after), channel_id=1, source_target_pairs={{0,1},{1,2},{2,3},{3,4},{4,5},{5,6},{6,7},{8,9},{9,10},{10,11},{11... | collective-permute-start | bytes 442376 | tf_op jit(solution)/shard_map/ppermute | solution.py:572
  153.2 7.0 %collective-permute-start.10 = (f32[2,48,256]{2,1,0:T(8,128)S(1)}, f32[2,48,256]{2,1,0:T(8,128)S(1)}, u32[]{:S(2)}, u32[]{:S(2)}) collective-permute-start(f32[2,48,256]{2,1,0:T(8,128)S(1)} %base.7.after.near), channel_id=1, source_target_pairs={{1,0},{2,1},{3,2},{4,3},{5,4},{6,5},{7,6},{9,8},{10,9},{11,10},{12... | collective-permute-start | bytes 294920 | tf_op jit(solution)/shard_map/ppermute | solution.py:572
  154.5 22.7 %collective-permute-start.11 = (f32[3,48,256]{2,1,0:T(8,128)S(1)}, f32[3,48,256]{2,1,0:T(8,128)S(1)}, u32[]{:S(2)}, u32[]{:S(2)}) collective-permute-start(f32[3,48,256]{2,1,0:T(8,128)S(1)} %get-tuple-element.129.after), channel_id=1, source_target_pairs={{0,1},{1,2},{2,3},{3,4},{4,5},{5,6},{6,7},{8,9},{9,10},{10,11},{11... | collective-permute-start | bytes 442376 | tf_op jit(solution)/shard_map/ppermute | solution.py:572

commit v9 on v8

--- a/solution.py
+++ b/solution.py
@@ -22,6 +22,7 @@
 PAD = 0
 TALL = CY
 STACK = 48
+SPARE = 3
 PARTS = 8
 SIDES = ((0, 0), (-1, 0), (1, 0))
 REACH = len(SIDES) * PORT_DEV
@@ -262,8 +263,7 @@
 
 
 def halo_kernel(
-    found, columns, lower, upper, e_in, h_in, coef_in, loss_in,
-    e_xy, e_z, h, media, sample, coef, up, down, picked, sems,
+    lower, upper, e_in, h_in, coef_in, loss_in, e_xy, e_z, h, media, up, down, sems,
 ):
     copies, copy = copier(sems)
     targets = [
@@ -283,6 +283,8 @@
     def _(layer):
         media[1, layer] = 1.0 - media[1, layer]
 
+
+def samples_kernel(found, columns, e_z, media, sample, coef, picked):
     @pl.loop(0, found[COUNT])
     def _(group):
         part = pl.ds(pl.multiple_of(group * GROUP, GROUP), GROUP)
@@ -298,7 +300,7 @@
     return pick(picked[...], place)
 
 
-def halo(found, columns, lower, upper, e_in, h_in, coef, loss):
+def halo(lower, upper, e_in, h_in, coef, loss):
     return pl.pallas_call(
         halo_kernel,
         name="halo",
@@ -307,16 +309,26 @@
             onchip(CUBE),
             onchip((3,) + CUBE),
             onchip((2,) + CUBE),
-            onchip((REACH, 1)),
-            onchip((REACH, 1)),
             stack_of(5),
             stack_of(2),
         ),
-        in_specs=[SM, VM, HBM, HBM] + [HBM] * 4,
-        out_specs=(VM,) * 8,
-        scratch_shapes=[pltpu.VMEM((GROUP, NX), f32), DMA((24,))],
-        compiler_params=params(),
-    )(found, columns, *map(away, (lower, upper, e_in, h_in, coef, loss)))
+        in_specs=[HBM] * 6,
+        out_specs=(VM,) * 6,
+        scratch_shapes=[DMA((24,))],
+        compiler_params=params(),
+    )(*map(away, (lower, upper, e_in, h_in, coef, loss)))
+
+
+def samples(found, columns, e_z, media):
+    return pl.pallas_call(
+        samples_kernel,
+        name="samples",
+        out_shape=(onchip((REACH, 1)), onchip((REACH, 1))),
+        in_specs=[SM, VM, VM, VM],
+        out_specs=(VM, VM),
+        scratch_shapes=[pltpu.VMEM((GROUP, NX), f32)],
+        compiler_params=params(),
+    )(found, columns, keep(e_z), keep(media))
 
 
 def field_kernel(
@@ -383,12 +395,20 @@
     put_h(step, magnetic(step))
     last = LAYERS - step - 1
 
-    @pl.loop(step, last)
+    electric_values = electric(step)
+    put_h(step + 1, magnetic(step + 1))
+    put_e(step, electric_values)
+
+    @pl.loop(step + 1, last, step=2)
     def _(layer):
         electric_values = electric(layer)
         magnetic_values = magnetic(layer + 1)
+        magnetic_above = magnetic(layer + 2)
         put_e(layer, electric_values)
         put_h(layer + 1, magnetic_values)
+        electric_above = electric(layer + 1)
+        put_h(layer + 2, magnetic_above)
+        put_e(layer + 1, electric_above)
 
     put_e(last, electric(last))
 
@@ -480,13 +500,15 @@
 
 def base_kernel(e_xy, e_z, after, down):
     write_rows(down, (e_xy.at[0], e_z), 0)
+    for slot in range(2, SPARE):
+        down[slot] = jnp.zeros((STACK, NX), f32)
 
 
 def base_rows(e_xy, e_z, after):
     return pl.pallas_call(
         base_kernel,
         name="base",
-        out_shape=stack_of(2),
+        out_shape=stack_of(SPARE),
         in_specs=[VM, VM, ANY],
         out_specs=VM,
         compiler_params=params(),
@@ -599,25 +621,26 @@
     upper = shifted(down, "gz", -1)
     out = begin(n_gy, port_cell, port_node, port_gain, e_field, volts, down)
     arrived = exchange(out)
+    lower, upper, arrived = lax.optimization_barrier((lower, upper, arrived))
     mats = matrices(diag_blocks, inv_blocks, off_blocks)
-
+    e_xy, e_z, h, media, up, down = halo(lower, upper, *grids)
     found, columns = plan(n_gz, n_gy, arrived, port_node, port_gain)
     table = jnp.concatenate([found[0], found[1], found[7, 0:1]])
-
-    e_xy, e_z, h, media, sample, coef, up, down = halo(table, columns, lower, upper, *grids)
+    sample, coef = samples(table, columns, e_z, media)
     edge = None
     for step in range(1, STEPS + 1):
         front = shifted(up, "gy", 1)
+        if step > 1:
+            out, volts, sample = circuit(table, off_cols, arrived, columns, volts, mats, e_z, up)
+            down = base_rows(e_xy, e_z, out)
         back = shifted(down, "gy", -1)
         if step > 1:
-            out, volts, sample = circuit(table, off_cols, arrived, columns, volts, mats, e_z, down)
-            out, back = lax.optimization_barrier((out, back))
+            out, front = lax.optimization_barrier((out, front))
             arrived = exchange(out)
             arrived, e_z = lax.optimization_barrier((arrived, e_z))
         e_xy, e_z, h, edge = field(step, front, back, down, edge, media, e_xy, e_z, h)
         if step < STEPS:
             e_z, up = ports(table, arrived, columns, sample, coef, e_xy, e_z)
-            down = base_rows(e_xy, e_z, up)
         else:
             e_end, h_end, volts = finish(
                 table, off_cols, arrived, columns, sample, coef, volts, mats, e_xy, e_z, h

time: 185 us -> 183 us (0.989)
  blocking collectives: 97.1 us -> 104 us
  starting transfers between devices: 31.6 us -> 28.4 us
  waiting for transfers between devices: 4.09 us -> 1.18 us
  Pallas kernels: 47.6 us -> 44.7 us
    all_to_all x5, blocking collectives: 97.1 us -> 104 us  [exchange(): return lax.all_to_all(value, ('gz', 'gy'), 0, 0, tiled=True)]
    ppermute x12, starting transfers between devices: 31.6 us -> 28.4 us  [shifted(): lax.ppermute(value, axis, [(source, source + steps) for source in range(f...]
    ppermute x12, waiting for transfers between devices: 4.09 us -> 1.18 us  [shifted(): lax.ppermute(value, axis, [(source, source + steps) for source in range(f...]
    pallas_call x5, Pallas kernels: 18.3 us -> 15.5 us  [field(): pl.pallas_call(functools.partial(field_kernel, step, 3 if first else 0),...]
  transfers between devices with their start and end apart: 12 -> 12, of which waited for: 1 -> 1; matrix products, arithmetic and copies ran while one was open for 1% -> 1% of each run, Pallas kernels for 5% -> 6%
where the time goes in v9:
time: 183 us; the launch traced here: 182 us
  blocking collectives  104 us (57%)
  Pallas kernels  44.7 us (24%)
  starting transfers between devices  28.4 us (16%)
  local copies, waits for them, and re-layouts  2.29 us (1%)
    all_to_all x5, blocking collectives, exchange(): return lax.all_to_all(value, ('gz', 'gy'), 0, 0, tiled=True)  104 us
    ppermute x12, starting transfers between devices, shifted(): lax.ppermute(value, axis, [(source, source + steps) for source in range(f...  28.4 us
    pallas_call x5, Pallas kernels, field(): pl.pallas_call(functools.partial(field_kernel, step, 3 if first else 0),...  15.5 us
    pallas_call x4, Pallas kernels, ports(): pl.pallas_call(functools.partial(ports_kernel, arrived.shape[0] // ND), n...  8.45 us
    pallas_call x4, Pallas kernels, circuit(): pl.pallas_call(functools.partial(circuit_kernel, arrived.shape[0] // ND),...  6.81 us
  transfers between devices with their start and end apart: 12, of which 1 were waited for; matrix products, arithmetic and copies ran while one was open for 1% of the time, Pallas kernels for 6%

profile of v9, /device:TPU:1, one launch (start us, length us, event | category | flops | bytes accessed | tf_op | source)
XLA Modules:
  0.0 182.4 jit_solution(9003723545417898230)
XLA Ops:
  0.6 0.0 copy-start.6
  0.6 0.6 copy-done.6
  1.3 1.2 slab.2.after
  2.5 0.0 copy-start.1
  2.5 0.0 copy-start.2
  2.6 0.0 copy-start.8
  2.6 1.2 slab.3.after
  3.8 3.3 %collective-permute-start.1 = (f32[40,16,256]{2,1,0:T(8,128)S(1)}, f32[40,16,256]{2,1,0:T(8,128)S(1)}, u32[]{:S(2)}, u32[]{:S(2)}) collective-permute-start(f32[40,16,256]{2,1,0:T(8,128)S(1)} %slab.3.after), channel_id=1, source_target_pairs={{8,0},{16,8},{24,16},{32,24},{40,32},{48,40},{56,48},{64,56},{72,6... | collective-permute-start | bytes 1966088 | tf_op jit(solution)/shard_map/ppermute | solution.py:594
  7.2 3.2 %collective-permute-start = (f32[40,16,256]{2,1,0:T(8,128)S(1)}, f32[40,16,256]{2,1,0:T(8,128)S(1)}, u32[]{:S(2)}, u32[]{:S(2)}) collective-permute-start(f32[40,16,256]{2,1,0:T(8,128)S(1)} %slab.2.after), channel_id=1, source_target_pairs={{0,8},{8,16},{16,24},{24,32},{32,40},{40,48},{48,56},{56,64},{64,7... | collective-permute-start | bytes 1966088 | tf_op jit(solution)/shard_map/ppermute | solution.py:594
  10.4 2.7 %begin.1 = f32[512,128]{1,0:T(8,128)S(1)} custom-call(s32[32]{0:T(128)S(1)} %copy-done.8, s32[4096]{0:T(1024)S(1)} %copy-done.1, f32[4096]{0:T(1024)S(1)} %copy-done.2, f32[3,32,16,256]{3,2,1,0:T(8,128)} %e_in.7, s32[1,32]{1,0:T(1,128)S(1)} %bitcast.40, f32[1,128]{1,0:T(1,128)S(1)} %bitcast.38, f32[40,16,256]{2,1,0:T(8,128)S(1)} %slab.3.after), custom_call_target="tpu_custom_call" | custom-call | tf_op jit(solution)/shard_map/begin/pallas_call | solution.py:162
  13.1 21.7 %all_to_all.60 = f32[128,4,128]{2,1,0:T(4,128)S(1)} all-to-all(f32[128,4,128]{2,1,0:T(4,128)S(1)} %bitcast.29), channel_id=1, replica_groups=mesh['gz'=16,'gy'=8] {'gz','gy'}, dimensions={0} | all-to-all | bytes 524288 | tf_op jit(solution)/shard_map/all_to_all | solution.py:598
  34.7 0.0 collective-permute-done.1.upper
  34.7 0.0 collective-permute-done.lower
  34.8 0.0 copy-start.10
  34.8 0.8 copy-done.9
  35.6 0.2 copy-done.10
  35.8 3.1 %halo.1 = (f32[2,42,16,256]{3,2,1,0:T(8,128)S(1)}, f32[42,16,256]{2,1,0:T(8,128)S(1)}, f32[3,42,16,256]{3,2,1,0:T(8,128)S(1)}, f32[2,42,16,256]{3,2,1,0:T(8,128)...) custom-call(f32[40,16,256]{2,1,0:T(8,128)} %copy-done.10, f32[40,16,256]{2,1,0:T(8,128)} %copy-done.9, ...), custom_call_target="tpu_custom_call" | custom-call | tf_op jit(solution)/shard_map/halo/pallas_call | solution.py:304
  38.9 1.3 collective-permute-start.3
  40.2 4.0 %collective-permute-start.2 = (f32[5,48,256]{2,1,0:T(8,128)S(1)}, f32[5,48,256]{2,1,0:T(8,128)S(1)}, u32[]{:S(2)}, u32[]{:S(2)}) collective-permute-start(f32[5,48,256]{2,1,0:T(8,128)S(1)} %get-tuple-element.89), channel_id=1, source_target_pairs={{0,1},{1,2},{2,3},{3,4},{4,5},{5,6},{6,7},{8,9},{9,10},{10,11},{11... | collective-permute-start | bytes 737288 | tf_op jit(solution)/shard_map/ppermute | solution.py:594
  44.2 0.4 plan.1
  44.7 0.5 slice.11
  45.2 0.7 pad_add_fusion.found.table
  45.9 1.4 samples.1
  47.4 0.0 collective-permute-done.3.back
  47.4 1.1 collective-permute-done.2.front.edge_in
  48.5 3.3 %field.5 = (f32[2,42,16,256]{3,2,1,0:T(8,128)S(1)}, f32[42,16,256]{2,1,0:T(8,128)S(1)}, f32[3,42,16,256]{3,2,1,0:T(8,128)S(1)}, f32[2,48,256]{2,1,0:T(8,128)S(1)}) custom-call(f32[5,48,256]{2,1,0:T(8,128)S(1)} %collective-permute-done.2.front.edge_in, f32[2,48,256]{2,1,0:T(8,128)S(1)} %collective-permute-done.3.back, ...), custom_call_target="tpu_custom_call" | custom-call | tf_op jit(solution)/shard_map/field/pallas_call | solution.py:418
  51.8 0.0 copy-start
  51.8 0.0 copy-start.3
  51.9 0.0 copy-start.4
  51.9 0.0 copy-start.5
  51.9 0.0 copy-start.7
  51.9 2.1 %ports.4 = (f32[42,16,256]{2,1,0:T(8,128)S(1)}, f32[3,48,256]{2,1,0:T(8,128)S(1)}) custom-call(s32[193]{0:T(256)S(1)} %pad_add_fusion.found.table, f32[512,128]{1,0:T(8,128)S(1)} %bitcast.21, f32[96,8]{1,0:T(8,128)S(1)} %get-tuple-element.79.columns, f32[96,1]{1,0:T(8,128)S(1)} %get-tuple-element.87.sample, f32[96,1]{1,0:T(8,128)S(1)} %get-tuple-element.88.coef, ...), custom_call_target="tpu_custom_call" | custom-call | tf_op jit(solution)/shard_map/ports/pallas_call | solution.py:490
  54.0 4.1 %collective-permute-start.4 = (f32[3,48,256]{2,1,0:T(8,128)S(1)}, f32[3,48,256]{2,1,0:T(8,128)S(1)}, u32[]{:S(2)}, u32[]{:S(2)}) collective-permute-start(f32[3,48,256]{2,1,0:T(8,128)S(1)} %get-tuple-element.96.after), channel_id=1, source_target_pairs={{0,1},{1,2},{2,3},{3,4},{4,5},{5,6},{6,7},{8,9},{9,10},{10,11},{11... | collective-permute-start | bytes 442376 | tf_op jit(solution)/shard_map/ppermute | solution.py:594
  58.1 0.2 matrices.1
  58.3 1.7 circuit.4
  60.1 1.3 collective-permute-start.5
  61.4 0.0 collective-permute-done.4.front
  61.4 25.3 %all_to_all.61 = f32[128,2,128]{2,1,0:T(2,128)S(1)} all-to-all(f32[128,2,128]{2,1,0:T(2,128)S(1)} %bitcast.34), channel_id=1, replica_groups=mesh['gz'=16,'gy'=8] {'gz','gy'}, dimensions={0} | all-to-all | bytes 262144 | tf_op jit(solution)/shard_map/all_to_all | solution.py:598
  86.7 0.0 collective-permute-done.5.back
  86.7 3.1 %field.6 = (f32[2,42,16,256]{3,2,1,0:T(8,128)S(1)}, f32[42,16,256]{2,1,0:T(8,128)S(1)}, f32[3,42,16,256]{3,2,1,0:T(8,128)S(1)}, f32[2,48,256]{2,1,0:T(8,128)S(1)}) custom-call(f32[3,48,256]{2,1,0:T(8,128)S(1)} %collective-permute-done.4.front, f32[3,48,256]{2,1,0:T(8,128)S(1)} %collective-permute-done.5.back, f32[3,48,256]{2,1,0:T(8,128)S(1)} %base.4.near, ...), custom_call_target="tpu_custom_call" | custom-call | tf_op jit(solution)/shard_map/field/pallas_call | solution.py:418
  89.9 2.1 %ports.5 = (f32[42,16,256]{2,1,0:T(8,128)S(1)}, f32[3,48,256]{2,1,0:T(8,128)S(1)}) custom-call(s32[193]{0:T(256)S(1)} %pad_add_fusion.found.table, f32[256,128]{1,0:T(8,128)S(1)} %bitcast.23, f32[96,8]{1,0:T(8,128)S(1)} %get-tuple-element.79.columns, f32[96,1]{1,0:T(8,128)S(1)} %get-tuple-element.101.sample, f32[96,1]{1,0:T(8,128)S(1)} %get-tuple-element.88.coef, ...), custom_call_target="tpu_custom_call" | custom-call | tf_op jit(solution)/shard_map/ports/pallas_call | solution.py:490
  92.0 2.5 %collective-permute-start.6 = (f32[3,48,256]{2,1,0:T(8,128)S(1)}, f32[3,48,256]{2,1,0:T(8,128)S(1)}, u32[]{:S(2)}, u32[]{:S(2)}) collective-permute-start(f32[3,48,256]{2,1,0:T(8,128)S(1)} %get-tuple-element.109.after), channel_id=1, source_target_pairs={{0,1},{1,2},{2,3},{3,4},{4,5},{5,6},{6,7},{8,9},{9,10},{10,11},{11... | collective-permute-start | bytes 442376 | tf_op jit(solution)/shard_map/ppermute | solution.py:594
  94.5 1.7 circuit.5
  96.2 1.3 collective-permute-start.7
  97.5 0.0 collective-permute-done.6.front
  97.5 19.0 %all_to_all.62 = f32[128,2,128]{2,1,0:T(2,128)S(1)} all-to-all(f32[128,2,128]{2,1,0:T(2,128)S(1)} %bitcast.31), channel_id=1, replica_groups=mesh['gz'=16,'gy'=8] {'gz','gy'}, dimensions={0} | all-to-all | bytes 262144 | tf_op jit(solution)/shard_map/all_to_all | solution.py:598
  116.5 0.0 collective-permute-done.7.back
  116.5 3.0 %field.7 = (f32[2,42,16,256]{3,2,1,0:T(8,128)S(1)}, f32[42,16,256]{2,1,0:T(8,128)S(1)}, f32[3,42,16,256]{3,2,1,0:T(8,128)S(1)}, f32[2,48,256]{2,1,0:T(8,128)S(1)}) custom-call(f32[3,48,256]{2,1,0:T(8,128)S(1)} %collective-permute-done.6.front, f32[3,48,256]{2,1,0:T(8,128)S(1)} %collective-permute-done.7.back, f32[3,48,256]{2,1,0:T(8,128)S(1)} %base.5.near, ...), custom_call_target="tpu_custom_call" | custom-call | tf_op jit(solution)/shard_map/field/pallas_call | solution.py:418
  119.5 2.1 %ports.6 = (f32[42,16,256]{2,1,0:T(8,128)S(1)}, f32[3,48,256]{2,1,0:T(8,128)S(1)}) custom-call(s32[193]{0:T(256)S(1)} %pad_add_fusion.found.table, f32[256,128]{1,0:T(8,128)S(1)} %bitcast.25, f32[96,8]{1,0:T(8,128)S(1)} %get-tuple-element.79.columns, f32[96,1]{1,0:T(8,128)S(1)} %get-tuple-element.114.sample, f32[96,1]{1,0:T(8,128)S(1)} %get-tuple-element.88.coef, ...), custom_call_target="tpu_custom_call" | custom-call | tf_op jit(solution)/shard_map/ports/pallas_call | solution.py:490
  121.7 2.5 %collective-permute-start.8 = (f32[3,48,256]{2,1,0:T(8,128)S(1)}, f32[3,48,256]{2,1,0:T(8,128)S(1)}, u32[]{:S(2)}, u32[]{:S(2)}) collective-permute-start(f32[3,48,256]{2,1,0:T(8,128)S(1)} %get-tuple-element.122.after), channel_id=1, source_target_pairs={{0,1},{1,2},{2,3},{3,4},{4,5},{5,6},{6,7},{8,9},{9,10},{10,11},{11... | collective-permute-start | bytes 442376 | tf_op jit(solution)/shard_map/ppermute | solution.py:594
  124.1 1.7 circuit.6
  125.9 1.3 collective-permute-start.9
  127.2 0.0 collective-permute-done.8.front
  127.2 19.0 %all_to_all.63 = f32[128,2,128]{2,1,0:T(2,128)S(1)} all-to-all(f32[128,2,128]{2,1,0:T(2,128)S(1)} %bitcast.32), channel_id=1, replica_groups=mesh['gz'=16,'gy'=8] {'gz','gy'}, dimensions={0} | all-to-all | bytes 262144 | tf_op jit(solution)/shard_map/all_to_all | solution.py:598
  146.2 0.0 collective-permute-done.9.back
  146.2 2.8 %field.8 = (f32[2,42,16,256]{3,2,1,0:T(8,128)S(1)}, f32[42,16,256]{2,1,0:T(8,128)S(1)}, f32[3,42,16,256]{3,2,1,0:T(8,128)S(1)}, f32[2,48,256]{2,1,0:T(8,128)S(1)}) custom-call(f32[3,48,256]{2,1,0:T(8,128)S(1)} %collective-permute-done.8.front, f32[3,48,256]{2,1,0:T(8,128)S(1)} %collective-permute-done.9.back, f32[3,48,256]{2,1,0:T(8,128)S(1)} %base.6.near, ...), custom_call_target="tpu_custom_call" | custom-call | tf_op jit(solution)/shard_map/field/pallas_call | solution.py:418
  149.0 2.1 %ports.7 = (f32[42,16,256]{2,1,0:T(8,128)S(1)}, f32[3,48,256]{2,1,0:T(8,128)S(1)}) custom-call(s32[193]{0:T(256)S(1)} %pad_add_fusion.found.table, f32[256,128]{1,0:T(8,128)S(1)} %bitcast.27, f32[96,8]{1,0:T(8,128)S(1)} %get-tuple-element.79.columns, f32[96,1]{1,0:T(8,128)S(1)} %get-tuple-element.127.sample, f32[96,1]{1,0:T(8,128)S(1)} %get-tuple-element.88.coef, ...), custom_call_target="tpu_custom_call" | custom-call | tf_op jit(solution)/shard_map/ports/pallas_call | solution.py:490
  151.1 2.5 %collective-permute-start.10 = (f32[3,48,256]{2,1,0:T(8,128)S(1)}, f32[3,48,256]{2,1,0:T(8,128)S(1)}, u32[]{:S(2)}, u32[]{:S(2)}) collective-permute-start(f32[3,48,256]{2,1,0:T(8,128)S(1)} %get-tuple-element.135.after), channel_id=1, source_target_pairs={{0,1},{1,2},{2,3},{3,4},{4,5},{5,6},{6,7},{8,9},{9,10},{10,11},{11... | collective-permute-start | bytes 442376 | tf_op jit(solution)/shard_map/ppermute | solution.py:594
  153.6 1.7 circuit.7
  155.4 1.3 collective-permute-start.11
  156.7 19.0 %all_to_all.64 = f32[128,2,128]{2,1,0:T(2,128)S(1)} all-to-all(f32[128,2,128]{2,1,0:T(2,128)S(1)} %bitcast.33), channel_id=1, replica_groups=mesh['gz'=16,'gy'=8] {'gz','gy'}, dimensions={0} | all-to-all | bytes 262144 | tf_op jit(solution)/shard_map/all_to_all | solution.py:598
  175.7 0.0 collective-permute-done.11.back
  175.7 3.3 %field.9 = (f32[2,42,16,256]{3,2,1,0:T(8,128)S(1)}, f32[42,16,256]{2,1,0:T(8,128)S(1)}, f32[3,42,16,256]{3,2,1,0:T(8,128)S(1)}, f32[2,48,256]{2,1,0:T(8,128)}) custom-call(f32[3,48,256]{2,1,0:T(8,128)S(1)} %collective-permute-done.10.front, f32[3,48,256]{2,1,0:T(8,128)S(1)} %collective-permute-done.11.back, f32[3,48,256]{2,1,0:T(8,128)S(1)} %base.7.near, ...), custom_call_target="tpu_custom_call" | custom-call | tf_op jit(solution)/shard_map/field/pallas_call | solution.py:418
  178.9 3.5 %finish.1 = (f32[3,32,16,256]{3,2,1,0:T(8,128)}, f32[3,32,16,256]{3,2,1,0:T(8,128)}, f32[1,128]{1,0:T(1,128)}) custom-call(s32[193]{0:T(256)S(1)} %pad_add_fusion.found.table, s32[2,4]{1,0:T(2,128)S(1)} %copy-done.5, f32[256,128]{1,0:T(8,128)S(1)} %bitcast.30, f32[96,8]{1,0:T(8,128)S(1)} %get-tuple-element.79.columns, ...), custom_call_target="tpu_custom_call" | custom-call | tf_op jit(solution)/shard_map/finish/pallas_call | solution.py:568
  (15 shorter events, 0.2 us)
Async XLA Ops:
  0.6 0.7 copy-start.6
  2.5 7.8 %copy-start.1 = (s32[4096]{0:T(1024)S(1)}, s32[4096]{0:T(1024)}, u32[]{:S(2)}) copy-start(s32[4096]{0:T(1024)} %nodes.1) | copy-start | bytes 49156
  2.5 7.8 %copy-start.2 = (f32[4096]{0:T(1024)S(1)}, f32[4096]{0:T(1024)}, u32[]{:S(2)}) copy-start(f32[4096]{0:T(1024)} %gains.1) | copy-start | bytes 49156
  2.6 7.8 %copy-start.8 = (s32[32]{0:T(128)S(1)}, s32[32]{0:T(128)}, u32[]{:S(2)}) copy-start(s32[32]{0:T(128)} %cells.1) | copy-start | bytes 388
  3.8 30.9 %collective-permute-start.1 = (f32[40,16,256]{2,1,0:T(8,128)S(1)}, f32[40,16,256]{2,1,0:T(8,128)S(1)}, u32[]{:S(2)}, u32[]{:S(2)}) collective-permute-start(f32[40,16,256]{2,1,0:T(8,128)S(1)} %slab.3.after), channel_id=1, source_target_pairs={{8,0},{16,8},{24,16},{32,24},{40,32},{48,40},{56,48},{64,56},{72,6... | collective-permute-start | bytes 1966088 | tf_op jit(solution)/shard_map/ppermute | solution.py:594
  7.2 27.6 %collective-permute-start = (f32[40,16,256]{2,1,0:T(8,128)S(1)}, f32[40,16,256]{2,1,0:T(8,128)S(1)}, u32[]{:S(2)}, u32[]{:S(2)}) collective-permute-start(f32[40,16,256]{2,1,0:T(8,128)S(1)} %slab.2.after), channel_id=1, source_target_pairs={{0,8},{8,16},{16,24},{24,32},{32,40},{40,48},{48,56},{56,64},{64,7... | collective-permute-start | bytes 1966088 | tf_op jit(solution)/shard_map/ppermute | solution.py:594
  34.7 0.8 copy-start.9
  34.8 1.0 copy-start.10
  38.9 8.5 %collective-permute-start.3 = (f32[2,48,256]{2,1,0:T(8,128)S(1)}, f32[2,48,256]{2,1,0:T(8,128)S(1)}, u32[]{:S(2)}, u32[]{:S(2)}) collective-permute-start(f32[2,48,256]{2,1,0:T(8,128)S(1)} %get-tuple-element.90.near), channel_id=1, source_target_pairs={{1,0},{2,1},{3,2},{4,3},{5,4},{6,5},{7,6},{9,8},{10,9},{11,10},{12... | collective-permute-start | bytes 294920 | tf_op jit(solution)/shard_map/ppermute | solution.py:594
  40.2 8.3 %collective-permute-start.2 = (f32[5,48,256]{2,1,0:T(8,128)S(1)}, f32[5,48,256]{2,1,0:T(8,128)S(1)}, u32[]{:S(2)}, u32[]{:S(2)}) collective-permute-start(f32[5,48,256]{2,1,0:T(8,128)S(1)} %get-tuple-element.89), channel_id=1, source_target_pairs={{0,1},{1,2},{2,3},{3,4},{4,5},{5,6},{6,7},{8,9},{9,10},{10,11},{11... | collective-permute-start | bytes 737288 | tf_op jit(solution)/shard_map/ppermute | solution.py:594
  51.8 6.3 %copy-start = (f32[2,4,64,64]{3,2,1,0:T(8,128)S(1)}, f32[2,4,64,64]{3,2,1,0:T(8,128)}, u32[]{:S(2)}) copy-start(f32[2,4,64,64]{3,2,1,0:T(8,128)} %off.1) | copy-start | bytes 393220
  51.8 6.3 %copy-start.3 = (f32[2,64,64]{2,1,0:T(8,128)S(1)}, f32[2,64,64]{2,1,0:T(8,128)}, u32[]{:S(2)}) copy-start(f32[2,64,64]{2,1,0:T(8,128)} %diag.1) | copy-start | bytes 98308
  51.9 6.3 %copy-start.4 = (f32[2,64,64]{2,1,0:T(8,128)S(1)}, f32[2,64,64]{2,1,0:T(8,128)}, u32[]{:S(2)}) copy-start(f32[2,64,64]{2,1,0:T(8,128)} %inv.1) | copy-start | bytes 98308
  51.9 6.5 %copy-start.5 = (s32[2,4]{1,0:T(2,128)S(1)}, s32[2,4]{1,0:T(2,128)}, u32[]{:S(2)}) copy-start(s32[2,4]{1,0:T(2,128)} %off_cols.9) | copy-start | bytes 100
  51.9 6.5 %copy-start.7 = (f32[128]{0:T(128)S(1)}, f32[128]{0:T(128)}, u32[]{:S(2)}) copy-start(f32[128]{0:T(128)} %param.23) | copy-start | bytes 1540
  54.0 7.4 %collective-permute-start.4 = (f32[3,48,256]{2,1,0:T(8,128)S(1)}, f32[3,48,256]{2,1,0:T(8,128)S(1)}, u32[]{:S(2)}, u32[]{:S(2)}) collective-permute-start(f32[3,48,256]{2,1,0:T(8,128)S(1)} %get-tuple-element.96.after), channel_id=1, source_target_pairs={{0,1},{1,2},{2,3},{3,4},{4,5},{5,6},{6,7},{8,9},{9,10},{10,11},{11... | collective-permute-start | bytes 442376 | tf_op jit(solution)/shard_map/ppermute | solution.py:594
  60.1 26.6 %collective-permute-start.5 = (f32[3,48,256]{2,1,0:T(8,128)S(1)}, f32[3,48,256]{2,1,0:T(8,128)S(1)}, u32[]{:S(2)}, u32[]{:S(2)}) collective-permute-start(f32[3,48,256]{2,1,0:T(8,128)S(1)} %base.4.near), channel_id=1, source_target_pairs={{1,0},{2,1},{3,2},{4,3},{5,4},{6,5},{7,6},{9,8},{10,9},{11,10},{12... | collective-permute-start | bytes 442376 | tf_op jit(solution)/shard_map/ppermute | solution.py:594
  92.0 5.5 %collective-permute-start.6 = (f32[3,48,256]{2,1,0:T(8,128)S(1)}, f32[3,48,256]{2,1,0:T(8,128)S(1)}, u32[]{:S(2)}, u32[]{:S(2)}) collective-permute-start(f32[3,48,256]{2,1,0:T(8,128)S(1)} %get-tuple-element.109.after), channel_id=1, source_target_pairs={{0,1},{1,2},{2,3},{3,4},{4,5},{5,6},{6,7},{8,9},{9,10},{10,11},{11... | collective-permute-start | bytes 442376 | tf_op jit(solution)/shard_map/ppermute | solution.py:594
  96.2 20.3 %collective-permute-start.7 = (f32[3,48,256]{2,1,0:T(8,128)S(1)}, f32[3,48,256]{2,1,0:T(8,128)S(1)}, u32[]{:S(2)}, u32[]{:S(2)}) collective-permute-start(f32[3,48,256]{2,1,0:T(8,128)S(1)} %base.5.near), channel_id=1, source_target_pairs={{1,0},{2,1},{3,2},{4,3},{5,4},{6,5},{7,6},{9,8},{10,9},{11,10},{12... | collective-permute-start | bytes 442376 | tf_op jit(solution)/shard_map/ppermute | solution.py:594
  121.7 5.5 %collective-permute-start.8 = (f32[3,48,256]{2,1,0:T(8,128)S(1)}, f32[3,48,256]{2,1,0:T(8,128)S(1)}, u32[]{:S(2)}, u32[]{:S(2)}) collective-permute-start(f32[3,48,256]{2,1,0:T(8,128)S(1)} %get-tuple-element.122.after), channel_id=1, source_target_pairs={{0,1},{1,2},{2,3},{3,4},{4,5},{5,6},{6,7},{8,9},{9,10},{10,11},{11... | collective-permute-start | bytes 442376 | tf_op jit(solution)/shard_map/ppermute | solution.py:594
  125.9 20.3 %collective-permute-start.9 = (f32[3,48,256]{2,1,0:T(8,128)S(1)}, f32[3,48,256]{2,1,0:T(8,128)S(1)}, u32[]{:S(2)}, u32[]{:S(2)}) collective-permute-start(f32[3,48,256]{2,1,0:T(8,128)S(1)} %base.6.near), channel_id=1, source_target_pairs={{1,0},{2,1},{3,2},{4,3},{5,4},{6,5},{7,6},{9,8},{10,9},{11,10},{12... | collective-permute-start | bytes 442376 | tf_op jit(solution)/shard_map/ppermute | solution.py:594
  151.1 5.5 %collective-permute-start.10 = (f32[3,48,256]{2,1,0:T(8,128)S(1)}, f32[3,48,256]{2,1,0:T(8,128)S(1)}, u32[]{:S(2)}, u32[]{:S(2)}) collective-permute-start(f32[3,48,256]{2,1,0:T(8,128)S(1)} %get-tuple-element.135.after), channel_id=1, source_target_pairs={{0,1},{1,2},{2,3},{3,4},{4,5},{5,6},{6,7},{8,9},{9,10},{10,11},{11... | collective-permute-start | bytes 442376 | tf_op jit(solution)/shard_map/ppermute | solution.py:594
  155.4 20.3 %collective-permute-start.11 = (f32[3,48,256]{2,1,0:T(8,128)S(1)}, f32[3,48,256]{2,1,0:T(8,128)S(1)}, u32[]{:S(2)}, u32[]{:S(2)}) collective-permute-start(f32[3,48,256]{2,1,0:T(8,128)S(1)} %base.7.near), channel_id=1, source_target_pairs={{1,0},{2,1},{3,2},{4,3},{5,4},{6,5},{7,6},{9,8},{10,9},{11,10},{12... | collective-permute-start | bytes 442376 | tf_op jit(solution)/shard_map/ppermute | solution.py:594

commit v10 on v9

--- a/solution.py
+++ b/solution.py
@@ -22,7 +22,6 @@
 PAD = 0
 TALL = CY
 STACK = 48
-SPARE = 3
 PARTS = 8
 SIDES = ((0, 0), (-1, 0), (1, 0))
 REACH = len(SIDES) * PORT_DEV
@@ -101,10 +100,12 @@
     return [e_in.at[k] for k in range(3)] + [h_in.at[k] for k in range(3)] + [coef_in, loss_in]
 
 
-def write_rows(stack, sources, row):
+def write_rows(stack, sources, swap):
+    even = lax.axis_index("gy") % 2 == 0
+    row = jnp.where(even, CY - 1, 0) if swap == 0 else jnp.where(even, 0, CY - 1)
     for slot, source in enumerate(sources):
         for layer in range(LAYERS):
-            stack[slot, layer : layer + 1, :] = source[layer, row : row + 1, :]
+            stack[slot, layer : layer + 1, :] = source[layer, pl.ds(row, 1), :]
         stack[slot, LAYERS:STACK, :] = jnp.zeros((STACK - LAYERS, NX), f32)
 
 
@@ -263,7 +264,7 @@
 
 
 def halo_kernel(
-    lower, upper, e_in, h_in, coef_in, loss_in, e_xy, e_z, h, media, up, down, sems,
+    lower, upper, e_in, h_in, coef_in, loss_in, e_xy, e_z, h, media, first, second, sems,
 ):
     copies, copy = copier(sems)
     targets = [
@@ -276,8 +277,8 @@
         copy(upper.at[given], targets[part].at[pl.ds(DEPTH + CZ, DEPTH)])
     for job in copies:
         job.wait()
-    write_rows(up, targets[:4] + [targets[5]], CY - 1)
-    write_rows(down, (targets[0], targets[2]), 0)
+    for swap, stack in enumerate((first, second)):
+        write_rows(stack, targets[:4] + [targets[5]], swap)
 
     @pl.loop(0, LAYERS)
     def _(layer):
@@ -310,7 +311,7 @@
             onchip((3,) + CUBE),
             onchip((2,) + CUBE),
             stack_of(5),
-            stack_of(2),
+            stack_of(5),
         ),
         in_specs=[HBM] * 6,
         out_specs=(VM,) * 6,
@@ -332,8 +333,11 @@
 
 
 def field_kernel(
-    step, base, front, back, near, edge_in, media, e_xy, e_z, h, to_xy, to_z, to_h, edge
+    step, base, *refs
 ):
+    first, second, sent_first, sent_second = refs[:4]
+    edge_in, media, e_xy, e_z, h, to_xy, to_z, to_h, edge, beyond_rows = refs[4:]
+    even = lax.axis_index("gy") % 2 == 0
     low_z = jnp.where(lax.axis_index("gz") > 0, time_step, 0.0)
     low_y = jnp.where(lax.axis_index("gy") > 0, time_step, 0.0)
     lane = lanes_of(TALL, NX)
@@ -354,12 +358,23 @@
         return jnp.where(first_row, beyond, pltpu.roll(value, 1, 0))
 
     span = pl.ds(0, LAYERS)
-    out_x, out_y, out_z = front[0, span, :], front[1, span, :], front[2, span, :]
-    out_y_above = front[1, pl.ds(1, LAYERS), :]
+
+    def behind(slot, part=span):
+        return jnp.where(even, second[slot, part, :], first[slot, part, :])
+
+    for slot, kind in enumerate((0, 2)):
+        beyond_rows[slot, span, :] = jnp.where(even, first[kind, span, :], second[kind, span, :])
+    near_x, near_z = (
+        jnp.where(even, sent_second[kind, span, :], sent_first[kind, span, :]) for kind in (0, 2)
+    )
+    out_x, out_y, out_z = behind(0), behind(1), behind(2)
+    out_y_above = behind(1, pl.ds(1, LAYERS))
     tall_lane = lanes_of(LAYERS, NX)
     out_y_next = jnp.where(tall_lane == NX - 1, 0.0, pltpu.roll(out_y, NX - 1, 1))
-    near_x, near_z = near[0, span, :], near[1, span, :]
-    edge_x, edge_z = edge_in[base, span, :], edge_in[base + 1, span, :]
+    if base:
+        edge_x, edge_z = behind(base), behind(base + 1)
+    else:
+        edge_x, edge_z = edge_in[0, span, :], edge_in[1, span, :]
     edge[0, span, :] = edge_x - low_y * ((near_z - out_z) - (out_y_above - out_y))
     edge[1, span, :] = edge_z - low_y * ((out_y_next - out_y) - (near_x - out_x))
 
@@ -367,9 +382,9 @@
         e_x, e_y, e_zz = e_xy[0, layer], e_xy[1, layer], e_z[layer]
         rate = jnp.where(layer < DEPTH, low_z, time_step)
         beyond = pl.ds(layer, 1)
-        curl_x = (next_y(e_zz, back[1, beyond, :]) - e_zz) - (e_xy[1, layer + 1] - e_y)
+        curl_x = (next_y(e_zz, beyond_rows[1, beyond, :]) - e_zz) - (e_xy[1, layer + 1] - e_y)
         curl_y = (e_xy[0, layer + 1] - e_x) - (next_x(e_zz) - e_zz)
-        curl_z = (next_x(e_y) - e_y) - (next_y(e_x, back[0, beyond, :]) - e_x)
+        curl_z = (next_x(e_y) - e_y) - (next_y(e_x, beyond_rows[0, beyond, :]) - e_x)
         return (h[0, layer] - rate * curl_x, h[1, layer] - rate * curl_y, h[2, layer] - rate * curl_z)
 
     def electric(layer):
@@ -413,17 +428,18 @@
     put_e(last, electric(last))
 
 
-def field(step, front, back, near, edge, media, e_xy, e_z, h):
+def field(step, came, sent, edge, media, e_xy, e_z, h):
     first = edge is None
     return pl.pallas_call(
         functools.partial(field_kernel, step, 3 if first else 0),
         name="field",
         out_shape=(onchip((2,) + CUBE), onchip(CUBE), onchip((3,) + CUBE), onchip((2, STACK, NX))),
-        in_specs=[VM] * 8,
+        in_specs=[VM] * 9,
         out_specs=(VM,) * 4,
+        scratch_shapes=[pltpu.VMEM((2, STACK, NX), f32)],
         compiler_params=params(),
     )(
-        front, back, near, front if first else keep(edge),
+        *came, *sent, came[0] if first else keep(edge),
         keep(media), keep(e_xy), keep(e_z), keep(h),
     )
 
@@ -479,11 +495,11 @@
 
 
 def ports_kernel(
-    stride, table, arrived, columns, sample, coef, e_xy, e_in, e_z, up, near_rows, deltas,
+    stride, table, arrived, columns, sample, coef, e_xy, e_in, e_z, first, near_rows, deltas,
 ):
     e_z[...] = e_in[...]
     apply_ports(stride, table, arrived, columns, sample, coef, e_z, near_rows, deltas)
-    write_rows(up, (e_xy.at[0], e_xy.at[1], e_z), CY - 1)
+    write_rows(first, (e_xy.at[0], e_xy.at[1], e_z), 0)
 
 
 def ports(table, arrived, columns, sample, coef, e_xy, e_z):
@@ -498,17 +514,15 @@
     )(table, arrived, columns, keep(sample), keep(coef), keep(e_xy), keep(e_z))
 
 
-def base_kernel(e_xy, e_z, after, down):
-    write_rows(down, (e_xy.at[0], e_z), 0)
-    for slot in range(2, SPARE):
-        down[slot] = jnp.zeros((STACK, NX), f32)
-
-
-def base_rows(e_xy, e_z, after):
-    return pl.pallas_call(
-        base_kernel,
-        name="base",
-        out_shape=stack_of(SPARE),
+def second_kernel(e_xy, e_z, after, second):
+    write_rows(second, (e_xy.at[0], e_xy.at[1], e_z), 1)
+
+
+def second_rows(e_xy, e_z, after):
+    return pl.pallas_call(
+        second_kernel,
+        name="second",
+        out_shape=stack_of(3),
         in_specs=[VM, VM, ANY],
         out_specs=VM,
         compiler_params=params(),
@@ -592,6 +606,12 @@
     count = lax.axis_size(axis)
     first, last = (max(0, -steps), min(count, count - steps))
     return lax.ppermute(value, axis, [(source, source + steps) for source in range(first, last)])
+
+
+def swapped(value, axis, start):
+    count = lax.axis_size(axis)
+    pairs = [(low, low + 1) for low in range(start, count - 1, 2)]
+    return lax.ppermute(value, axis, pairs + [(high, low) for low, high in pairs])
 
 
 def exchange(value):
@@ -623,24 +643,25 @@
     arrived = exchange(out)
     lower, upper, arrived = lax.optimization_barrier((lower, upper, arrived))
     mats = matrices(diag_blocks, inv_blocks, off_blocks)
-    e_xy, e_z, h, media, up, down = halo(lower, upper, *grids)
+    e_xy, e_z, h, media, first, second = halo(lower, upper, *grids)
     found, columns = plan(n_gz, n_gy, arrived, port_node, port_gain)
     table = jnp.concatenate([found[0], found[1], found[7, 0:1]])
     sample, coef = samples(table, columns, e_z, media)
     edge = None
     for step in range(1, STEPS + 1):
-        front = shifted(up, "gy", 1)
+        came_first = swapped(first, "gy", 0)
         if step > 1:
-            out, volts, sample = circuit(table, off_cols, arrived, columns, volts, mats, e_z, up)
-            down = base_rows(e_xy, e_z, out)
-        back = shifted(down, "gy", -1)
+            out, volts, sample = circuit(table, off_cols, arrived, columns, volts, mats, e_z, first)
+            second = second_rows(e_xy, e_z, out)
+        came_second = swapped(second, "gy", 1)
         if step > 1:
-            out, front = lax.optimization_barrier((out, front))
+            out, came_first = lax.optimization_barrier((out, came_first))
             arrived = exchange(out)
             arrived, e_z = lax.optimization_barrier((arrived, e_z))
-        e_xy, e_z, h, edge = field(step, front, back, down, edge, media, e_xy, e_z, h)
+        came, sent = (came_first, came_second), (first, second)
+        e_xy, e_z, h, edge = field(step, came, sent, edge, media, e_xy, e_z, h)
         if step < STEPS:
-            e_z, up = ports(table, arrived, columns, sample, coef, e_xy, e_z)
+            e_z, first = ports(table, arrived, columns, sample, coef, e_xy, e_z)
         else:
             e_end, h_end, volts = finish(
                 table, off_cols, arrived, columns, sample, coef, volts, mats, e_xy, e_z, h

time: 183 us -> 164 us (0.90)
  starting transfers between devices: 28.4 us -> 15.5 us
  blocking collectives: 104 us -> 91.6 us
  waiting for transfers between devices: 1.18 us -> 7.78 us
    ppermute x12 -> x2, starting transfers between devices: 28.4 us -> 6.52 us  [shifted(): lax.ppermute(value, axis, [(source, source + steps) for source in range(f...]
    all_to_all x5, blocking collectives: 104 us -> 91.6 us  [exchange(): return lax.all_to_all(value, ('gz', 'gy'), 0, 0, tiled=True)]
    ppermute x0 -> x10, starting transfers between devices: none -> 8.98 us  [swapped(): lax.ppermute(value, axis, pairs + [(high, low) for low, high in pairs])]
    ppermute x0 -> x10, waiting for transfers between devices: none -> 7.77 us  [swapped(): lax.ppermute(value, axis, pairs + [(high, low) for low, high in pairs])]
  transfers between devices with their start and end apart: 12 -> 12, of which waited for: 1 -> 4; matrix products, arithmetic and copies ran while one was open for 1% -> 1% of each run, Pallas kernels for 6% -> 7%
where the time goes in v10:
time: 164 us
  blocking collectives  91.6 us (56%)
  Pallas kernels  45 us (27%)
  starting transfers between devices  15.5 us (9%)
  waiting for transfers between devices  7.78 us (5%)
  local copies, waits for them, and re-layouts  2.29 us (1%)
    all_to_all x5, blocking collectives, exchange(): return lax.all_to_all(value, ('gz', 'gy'), 0, 0, tiled=True)  91.6 us
    pallas_call x5, Pallas kernels, field(): pl.pallas_call(functools.partial(field_kernel, step, 3 if first else 0),...  15.5 us
    ppermute x10, starting transfers between devices, swapped(): lax.ppermute(value, axis, pairs + [(high, low) for low, high in pairs])  8.98 us
    pallas_call x4, Pallas kernels, ports(): pl.pallas_call(functools.partial(ports_kernel, arrived.shape[0] // ND), n...  8.47 us
    ppermute x10, waiting for transfers between devices, swapped(): lax.ppermute(value, axis, pairs + [(high, low) for low, high in pairs])  7.77 us
    pallas_call x4, Pallas kernels, circuit(): pl.pallas_call(functools.partial(circuit_kernel, arrived.shape[0] // ND),...  6.79 us
    ppermute x2, starting transfers between devices, shifted(): lax.ppermute(value, axis, [(source, source + steps) for source in range(f...  6.52 us
    pallas_call x1, Pallas kernels, finish(): pl.pallas_call(functools.partial(finish_kernel, arrived.shape[0] // ND),...  3.46 us
  transfers between devices with their start and end apart: 12, of which 4 were waited for; matrix products, arithmetic and copies ran while one was open for 1% of the time, Pallas kernels for 7%

profile of v10, /device:TPU:1, one launch (start us, length us, event | category | flops | bytes accessed | tf_op | source)
XLA Modules:
  0.0 163.8 jit_solution(12678371873088667745)
XLA Ops:
  0.6 0.0 copy-start.6
  0.6 0.6 copy-done.6
  1.3 1.2 slab.2.after
  2.5 0.0 copy-start.1
  2.5 0.0 copy-start.2
  2.6 0.0 copy-start.8
  2.6 1.2 slab.3.after
  3.8 3.3 %collective-permute-start.1 = (f32[40,16,256]{2,1,0:T(8,128)S(1)}, f32[40,16,256]{2,1,0:T(8,128)S(1)}, u32[]{:S(2)}, u32[]{:S(2)}) collective-permute-start(f32[40,16,256]{2,1,0:T(8,128)S(1)} %slab.3.after), channel_id=1, source_target_pairs={{8,0},{16,8},{24,16},{32,24},{40,32},{48,40},{56,48},{64,56},{72,6... | collective-permute-start | bytes 1966088 | tf_op jit(solution)/shard_map/ppermute | solution.py:608
  7.2 3.2 %collective-permute-start = (f32[40,16,256]{2,1,0:T(8,128)S(1)}, f32[40,16,256]{2,1,0:T(8,128)S(1)}, u32[]{:S(2)}, u32[]{:S(2)}) collective-permute-start(f32[40,16,256]{2,1,0:T(8,128)S(1)} %slab.2.after), channel_id=1, source_target_pairs={{0,8},{8,16},{16,24},{24,32},{32,40},{40,48},{48,56},{56,64},{64,7... | collective-permute-start | bytes 1966088 | tf_op jit(solution)/shard_map/ppermute | solution.py:608
  10.4 2.7 %begin.1 = f32[512,128]{1,0:T(8,128)S(1)} custom-call(s32[32]{0:T(128)S(1)} %copy-done.8, s32[4096]{0:T(1024)S(1)} %copy-done.1, f32[4096]{0:T(1024)S(1)} %copy-done.2, f32[3,32,16,256]{3,2,1,0:T(8,128)} %e_in.7, s32[1,32]{1,0:T(1,128)S(1)} %bitcast.40, f32[1,128]{1,0:T(1,128)S(1)} %bitcast.38, f32[40,16,256]{2,1,0:T(8,128)S(1)} %slab.3.after), custom_call_target="tpu_custom_call" | custom-call | tf_op jit(solution)/shard_map/begin/pallas_call | solution.py:163
  13.1 21.7 %all_to_all.60 = f32[128,4,128]{2,1,0:T(4,128)S(1)} all-to-all(f32[128,4,128]{2,1,0:T(4,128)S(1)} %bitcast.29), channel_id=1, replica_groups=mesh['gz'=16,'gy'=8] {'gz','gy'}, dimensions={0} | all-to-all | bytes 524288 | tf_op jit(solution)/shard_map/all_to_all | solution.py:618
  34.7 0.0 collective-permute-done.1.upper
  34.7 0.0 collective-permute-done.lower
  34.8 0.0 copy-start.10
  34.8 0.8 copy-done.9
  35.6 0.2 copy-done.10
  35.8 3.2 %halo.1 = (f32[2,42,16,256]{3,2,1,0:T(8,128)S(1)}, f32[42,16,256]{2,1,0:T(8,128)S(1)}, f32[3,42,16,256]{3,2,1,0:T(8,128)S(1)}, f32[2,42,16,256]{3,2,1,0:T(8,128)...) custom-call(f32[40,16,256]{2,1,0:T(8,128)} %copy-done.10, f32[40,16,256]{2,1,0:T(8,128)} %copy-done.9, ...), custom_call_target="tpu_custom_call" | custom-call | tf_op jit(solution)/shard_map/halo/pallas_call | solution.py:305
  39.0 0.6 collective-permute-start.2
  39.6 0.7 collective-permute-start.3
  40.3 0.4 plan.1
  40.7 0.5 slice.11
  41.3 0.7 pad_add_fusion.found.table
  42.0 1.4 samples.1
  43.4 2.5 %collective-permute-done.2.refs_0_.refs_4_ = f32[5,48,256]{2,1,0:T(8,128)S(1)} collective-permute-done((f32[5,48,256]{2,1,0:T(8,128)S(1)}, f32[5,48,256]{2,1,0:T(8,128)S(1)}, u32[]{:S(2)}, u32[]{:S(2)}) %collective-permute-start.2) | collective-permute-done | bytes 245792 | tf_op jit(solution)/shard_map/ppermute | solution.py:614
  45.9 3.3 %field.5 = (f32[2,42,16,256]{3,2,1,0:T(8,128)S(1)}, f32[42,16,256]{2,1,0:T(8,128)S(1)}, f32[3,42,16,256]{3,2,1,0:T(8,128)S(1)}, f32[2,48,256]{2,1,0:T(8,128)S(1)}) custom-call(f32[5,48,256]{2,1,0:T(8,128)S(1)} %collective-permute-done.2.refs_0_.refs_4_, f32[5,48,256]{2,1,0:T(8,128)S(1)} %collective-permute-done.3.refs_1_, ...), custom_call_target="tpu_custom_call" | custom-call | tf_op jit(solution)/shard_map/field/pallas_call | solution.py:433
  49.2 0.0 copy-start
  49.2 0.0 copy-start.3
  49.2 0.0 copy-start.4
  49.3 0.0 copy-start.5
  49.3 0.0 copy-start.7
  49.3 2.1 %ports.4 = (f32[42,16,256]{2,1,0:T(8,128)S(1)}, f32[3,48,256]{2,1,0:T(8,128)S(1)}) custom-call(s32[193]{0:T(256)S(1)} %pad_add_fusion.found.table, f32[512,128]{1,0:T(8,128)S(1)} %bitcast.21, f32[96,8]{1,0:T(8,128)S(1)} %get-tuple-element.79.columns, f32[96,1]{1,0:T(8,128)S(1)} %get-tuple-element.87.sample, f32[96,1]{1,0:T(8,128)S(1)} %get-tuple-element.88.coef, ...), custom_call_target="tpu_custom_call" | custom-call | tf_op jit(solution)/shard_map/ports/pallas_call | solution.py:506
  51.4 3.1 %collective-permute-start.4 = (f32[3,48,256]{2,1,0:T(8,128)S(1)}, f32[3,48,256]{2,1,0:T(8,128)S(1)}, u32[]{:S(2)}, u32[]{:S(2)}) collective-permute-start(f32[3,48,256]{2,1,0:T(8,128)S(1)} %get-tuple-element.96.after.refs_2_), channel_id=1, source_target_pairs={{0,1},{2,3},{4,5},{6,7},{1,0},{3,2},{5,4},{7,6},{8,9},{10,11},{12,... | collective-permute-start | bytes 442376 | tf_op jit(solution)/shard_map/ppermute | solution.py:614
  54.5 0.2 matrices.1
  54.7 1.7 %circuit.4 = (f32[256,128]{1,0:T(8,128)S(1)}, f32[1,128]{1,0:T(1,128)S(1)}, f32[96,1]{1,0:T(8,128)S(1)}) custom-call(s32[193]{0:T(256)S(1)} %pad_add_fusion.found.table, s32[2,4]{1,0:T(2,128)S(1)} %copy-done.5, f32[512,128]{1,0:T(8,128)S(1)} %bitcast.22, f32[96,8]{1,0:T(8,128)S(1)} %get-tuple-element.79.columns, f32[1,128]{1,0:T(1,128)S(1)} %bitcast.39, ...), custom_call_target="tpu_custom_call" | custom-call | tf_op jit(solution)/shard_map/circuit/pallas_call | solution.py:552
  56.4 0.1 second.4.refs_3_
  56.5 0.7 collective-permute-start.5
  57.2 0.0 collective-permute-done.4.refs_0_
  57.2 22.0 %all_to_all.61 = f32[128,2,128]{2,1,0:T(2,128)S(1)} all-to-all(f32[128,2,128]{2,1,0:T(2,128)S(1)} %bitcast.34), channel_id=1, replica_groups=mesh['gz'=16,'gy'=8] {'gz','gy'}, dimensions={0} | all-to-all | bytes 262144 | tf_op jit(solution)/shard_map/all_to_all | solution.py:618
  79.2 3.1 %field.6 = (f32[2,42,16,256]{3,2,1,0:T(8,128)S(1)}, f32[42,16,256]{2,1,0:T(8,128)S(1)}, f32[3,42,16,256]{3,2,1,0:T(8,128)S(1)}, f32[2,48,256]{2,1,0:T(8,128)S(1)}) custom-call(f32[3,48,256]{2,1,0:T(8,128)S(1)} %collective-permute-done.4.refs_0_, f32[3,48,256]{2,1,0:T(8,128)S(1)} %collective-permute-done.5.refs_1_, ...), custom_call_target="tpu_custom_call" | custom-call | tf_op jit(solution)/shard_map/field/pallas_call | solution.py:433
  82.4 2.1 %ports.5 = (f32[42,16,256]{2,1,0:T(8,128)S(1)}, f32[3,48,256]{2,1,0:T(8,128)S(1)}) custom-call(s32[193]{0:T(256)S(1)} %pad_add_fusion.found.table, f32[256,128]{1,0:T(8,128)S(1)} %bitcast.23, f32[96,8]{1,0:T(8,128)S(1)} %get-tuple-element.79.columns, f32[96,1]{1,0:T(8,128)S(1)} %get-tuple-element.101.sample, f32[96,1]{1,0:T(8,128)S(1)} %get-tuple-element.88.coef, ...), custom_call_target="tpu_custom_call" | custom-call | tf_op jit(solution)/shard_map/ports/pallas_call | solution.py:506
  84.5 0.6 collective-permute-start.6
  85.1 1.7 %circuit.5 = (f32[256,128]{1,0:T(8,128)S(1)}, f32[1,128]{1,0:T(1,128)S(1)}, f32[96,1]{1,0:T(8,128)S(1)}) custom-call(s32[193]{0:T(256)S(1)} %pad_add_fusion.found.table, s32[2,4]{1,0:T(2,128)S(1)} %copy-done.5, f32[256,128]{1,0:T(8,128)S(1)} %bitcast.24, f32[96,8]{1,0:T(8,128)S(1)} %get-tuple-element.79.columns, f32[1,128]{1,0:T(1,128)S(1)} %get-tuple-element.100.volts, ...), custom_call_target="tpu_custom_call" | custom-call | tf_op jit(solution)/shard_map/circuit/pallas_call | solution.py:552
  86.8 0.1 second.5.refs_3_
  86.9 0.7 collective-permute-start.7
  87.6 1.8 %collective-permute-done.6.refs_0_ = f32[3,48,256]{2,1,0:T(8,128)S(1)} collective-permute-done((f32[3,48,256]{2,1,0:T(8,128)S(1)}, f32[3,48,256]{2,1,0:T(8,128)S(1)}, u32[]{:S(2)}, u32[]{:S(2)}) %collective-permute-start.6) | collective-permute-done | bytes 147488 | tf_op jit(solution)/shard_map/ppermute | solution.py:614
  89.4 16.0 %all_to_all.62 = f32[128,2,128]{2,1,0:T(2,128)S(1)} all-to-all(f32[128,2,128]{2,1,0:T(2,128)S(1)} %bitcast.31), channel_id=1, replica_groups=mesh['gz'=16,'gy'=8] {'gz','gy'}, dimensions={0} | all-to-all | bytes 262144 | tf_op jit(solution)/shard_map/all_to_all | solution.py:618
  105.3 3.0 %field.7 = (f32[2,42,16,256]{3,2,1,0:T(8,128)S(1)}, f32[42,16,256]{2,1,0:T(8,128)S(1)}, f32[3,42,16,256]{3,2,1,0:T(8,128)S(1)}, f32[2,48,256]{2,1,0:T(8,128)S(1)}) custom-call(f32[3,48,256]{2,1,0:T(8,128)S(1)} %collective-permute-done.6.refs_0_, f32[3,48,256]{2,1,0:T(8,128)S(1)} %collective-permute-done.7.refs_1_, ...), custom_call_target="tpu_custom_call" | custom-call | tf_op jit(solution)/shard_map/field/pallas_call | solution.py:433
  108.3 2.1 %ports.6 = (f32[42,16,256]{2,1,0:T(8,128)S(1)}, f32[3,48,256]{2,1,0:T(8,128)S(1)}) custom-call(s32[193]{0:T(256)S(1)} %pad_add_fusion.found.table, f32[256,128]{1,0:T(8,128)S(1)} %bitcast.25, f32[96,8]{1,0:T(8,128)S(1)} %get-tuple-element.79.columns, f32[96,1]{1,0:T(8,128)S(1)} %get-tuple-element.114.sample, f32[96,1]{1,0:T(8,128)S(1)} %get-tuple-element.88.coef, ...), custom_call_target="tpu_custom_call" | custom-call | tf_op jit(solution)/shard_map/ports/pallas_call | solution.py:506
  110.5 0.6 collective-permute-start.8
  111.1 1.7 %circuit.6 = (f32[256,128]{1,0:T(8,128)S(1)}, f32[1,128]{1,0:T(1,128)S(1)}, f32[96,1]{1,0:T(8,128)S(1)}) custom-call(s32[193]{0:T(256)S(1)} %pad_add_fusion.found.table, s32[2,4]{1,0:T(2,128)S(1)} %copy-done.5, f32[256,128]{1,0:T(8,128)S(1)} %bitcast.26, f32[96,8]{1,0:T(8,128)S(1)} %get-tuple-element.79.columns, f32[1,128]{1,0:T(1,128)S(1)} %get-tuple-element.113.volts, ...), custom_call_target="tpu_custom_call" | custom-call | tf_op jit(solution)/shard_map/circuit/pallas_call | solution.py:552
  112.8 0.1 second.6.refs_3_
  112.9 0.7 collective-permute-start.9
  113.6 1.8 %collective-permute-done.8.refs_0_ = f32[3,48,256]{2,1,0:T(8,128)S(1)} collective-permute-done((f32[3,48,256]{2,1,0:T(8,128)S(1)}, f32[3,48,256]{2,1,0:T(8,128)S(1)}, u32[]{:S(2)}, u32[]{:S(2)}) %collective-permute-start.8) | collective-permute-done | bytes 147488 | tf_op jit(solution)/shard_map/ppermute | solution.py:614
  115.3 16.0 %all_to_all.63 = f32[128,2,128]{2,1,0:T(2,128)S(1)} all-to-all(f32[128,2,128]{2,1,0:T(2,128)S(1)} %bitcast.32), channel_id=1, replica_groups=mesh['gz'=16,'gy'=8] {'gz','gy'}, dimensions={0} | all-to-all | bytes 262144 | tf_op jit(solution)/shard_map/all_to_all | solution.py:618
  131.3 2.8 %field.8 = (f32[2,42,16,256]{3,2,1,0:T(8,128)S(1)}, f32[42,16,256]{2,1,0:T(8,128)S(1)}, f32[3,42,16,256]{3,2,1,0:T(8,128)S(1)}, f32[2,48,256]{2,1,0:T(8,128)S(1)}) custom-call(f32[3,48,256]{2,1,0:T(8,128)S(1)} %collective-permute-done.8.refs_0_, f32[3,48,256]{2,1,0:T(8,128)S(1)} %collective-permute-done.9.refs_1_, ...), custom_call_target="tpu_custom_call" | custom-call | tf_op jit(solution)/shard_map/field/pallas_call | solution.py:433
  134.2 2.1 %ports.7 = (f32[42,16,256]{2,1,0:T(8,128)S(1)}, f32[3,48,256]{2,1,0:T(8,128)S(1)}) custom-call(s32[193]{0:T(256)S(1)} %pad_add_fusion.found.table, f32[256,128]{1,0:T(8,128)S(1)} %bitcast.27, f32[96,8]{1,0:T(8,128)S(1)} %get-tuple-element.79.columns, f32[96,1]{1,0:T(8,128)S(1)} %get-tuple-element.127.sample, f32[96,1]{1,0:T(8,128)S(1)} %get-tuple-element.88.coef, ...), custom_call_target="tpu_custom_call" | custom-call | tf_op jit(solution)/shard_map/ports/pallas_call | solution.py:506
  136.3 0.6 collective-permute-start.10
  136.9 1.7 %circuit.7 = (f32[256,128]{1,0:T(8,128)S(1)}, f32[1,128]{1,0:T(1,128)S(1)}, f32[96,1]{1,0:T(8,128)S(1)}) custom-call(s32[193]{0:T(256)S(1)} %pad_add_fusion.found.table, s32[2,4]{1,0:T(2,128)S(1)} %copy-done.5, f32[256,128]{1,0:T(8,128)S(1)} %bitcast.28, f32[96,8]{1,0:T(8,128)S(1)} %get-tuple-element.79.columns, f32[1,128]{1,0:T(1,128)S(1)} %get-tuple-element.126.volts, ...), custom_call_target="tpu_custom_call" | custom-call | tf_op jit(solution)/shard_map/circuit/pallas_call | solution.py:552
  138.6 0.1 second.7.refs_3_
  138.7 0.7 collective-permute-start.11
  139.4 1.8 %collective-permute-done.10.refs_0_ = f32[3,48,256]{2,1,0:T(8,128)S(1)} collective-permute-done((f32[3,48,256]{2,1,0:T(8,128)S(1)}, f32[3,48,256]{2,1,0:T(8,128)S(1)}, u32[]{:S(2)}, u32[]{:S(2)}) %collective-permute-start.10) | collective-permute-done | bytes 147488 | tf_op jit(solution)/shard_map/ppermute | solution.py:614
  141.1 16.0 %all_to_all.64 = f32[128,2,128]{2,1,0:T(2,128)S(1)} all-to-all(f32[128,2,128]{2,1,0:T(2,128)S(1)} %bitcast.33), channel_id=1, replica_groups=mesh['gz'=16,'gy'=8] {'gz','gy'}, dimensions={0} | all-to-all | bytes 262144 | tf_op jit(solution)/shard_map/all_to_all | solution.py:618
  157.1 3.3 %field.9 = (f32[2,42,16,256]{3,2,1,0:T(8,128)S(1)}, f32[42,16,256]{2,1,0:T(8,128)S(1)}, f32[3,42,16,256]{3,2,1,0:T(8,128)S(1)}, f32[2,48,256]{2,1,0:T(8,128)}) custom-call(f32[3,48,256]{2,1,0:T(8,128)S(1)} %collective-permute-done.10.refs_0_, f32[3,48,256]{2,1,0:T(8,128)S(1)} %collective-permute-done.11.refs_1_, ...), custom_call_target="tpu_custom_call" | custom-call | tf_op jit(solution)/shard_map/field/pallas_call | solution.py:433
  160.4 3.5 %finish.1 = (f32[3,32,16,256]{3,2,1,0:T(8,128)}, f32[3,32,16,256]{3,2,1,0:T(8,128)}, f32[1,128]{1,0:T(1,128)}) custom-call(s32[193]{0:T(256)S(1)} %pad_add_fusion.found.table, s32[2,4]{1,0:T(2,128)S(1)} %copy-done.5, f32[256,128]{1,0:T(8,128)S(1)} %bitcast.30, f32[96,8]{1,0:T(8,128)S(1)} %get-tuple-element.79.columns, ...), custom_call_target="tpu_custom_call" | custom-call | tf_op jit(solution)/shard_map/finish/pallas_call | solution.py:582
  (15 shorter events, 0.0 us)
Async XLA Ops:
  0.6 0.7 copy-start.6
  2.5 7.8 %copy-start.1 = (s32[4096]{0:T(1024)S(1)}, s32[4096]{0:T(1024)}, u32[]{:S(2)}) copy-start(s32[4096]{0:T(1024)} %nodes.1) | copy-start | bytes 49156
  2.5 7.8 %copy-start.2 = (f32[4096]{0:T(1024)S(1)}, f32[4096]{0:T(1024)}, u32[]{:S(2)}) copy-start(f32[4096]{0:T(1024)} %gains.1) | copy-start | bytes 49156
  2.6 7.8 %copy-start.8 = (s32[32]{0:T(128)S(1)}, s32[32]{0:T(128)}, u32[]{:S(2)}) copy-start(s32[32]{0:T(128)} %cells.1) | copy-start | bytes 388
  3.8 30.9 %collective-permute-start.1 = (f32[40,16,256]{2,1,0:T(8,128)S(1)}, f32[40,16,256]{2,1,0:T(8,128)S(1)}, u32[]{:S(2)}, u32[]{:S(2)}) collective-permute-start(f32[40,16,256]{2,1,0:T(8,128)S(1)} %slab.3.after), channel_id=1, source_target_pairs={{8,0},{16,8},{24,16},{32,24},{40,32},{48,40},{56,48},{64,56},{72,6... | collective-permute-start | bytes 1966088 | tf_op jit(solution)/shard_map/ppermute | solution.py:608
  7.2 27.6 %collective-permute-start = (f32[40,16,256]{2,1,0:T(8,128)S(1)}, f32[40,16,256]{2,1,0:T(8,128)S(1)}, u32[]{:S(2)}, u32[]{:S(2)}) collective-permute-start(f32[40,16,256]{2,1,0:T(8,128)S(1)} %slab.2.after), channel_id=1, source_target_pairs={{0,8},{8,16},{16,24},{24,32},{32,40},{40,48},{48,56},{56,64},{64,7... | collective-permute-start | bytes 1966088 | tf_op jit(solution)/shard_map/ppermute | solution.py:608
  34.7 0.8 copy-start.9
  34.8 1.0 copy-start.10
  39.0 6.9 %collective-permute-start.2 = (f32[5,48,256]{2,1,0:T(8,128)S(1)}, f32[5,48,256]{2,1,0:T(8,128)S(1)}, u32[]{:S(2)}, u32[]{:S(2)}) collective-permute-start(f32[5,48,256]{2,1,0:T(8,128)S(1)} %get-tuple-element.89.refs_2_), channel_id=1, source_target_pairs={{0,1},{2,3},{4,5},{6,7},{1,0},{3,2},{5,4},{7,6},{8,9},{10,11},{12,... | collective-permute-start | bytes 737288 | tf_op jit(solution)/shard_map/ppermute | solution.py:614
  39.6 6.3 %collective-permute-start.3 = (f32[5,48,256]{2,1,0:T(8,128)S(1)}, f32[5,48,256]{2,1,0:T(8,128)S(1)}, u32[]{:S(2)}, u32[]{:S(2)}) collective-permute-start(f32[5,48,256]{2,1,0:T(8,128)S(1)} %get-tuple-element.90.refs_3_), channel_id=1, source_target_pairs={{1,2},{3,4},{5,6},{2,1},{4,3},{6,5},{9,10},{11,12},{13,14},{10,9},... | collective-permute-start | bytes 737288 | tf_op jit(solution)/shard_map/ppermute | solution.py:614
  49.2 5.3 %copy-start = (f32[2,4,64,64]{3,2,1,0:T(8,128)S(1)}, f32[2,4,64,64]{3,2,1,0:T(8,128)}, u32[]{:S(2)}) copy-start(f32[2,4,64,64]{3,2,1,0:T(8,128)} %off.1) | copy-start | bytes 393220
  49.2 5.3 %copy-start.3 = (f32[2,64,64]{2,1,0:T(8,128)S(1)}, f32[2,64,64]{2,1,0:T(8,128)}, u32[]{:S(2)}) copy-start(f32[2,64,64]{2,1,0:T(8,128)} %diag.1) | copy-start | bytes 98308
  49.2 5.3 %copy-start.4 = (f32[2,64,64]{2,1,0:T(8,128)S(1)}, f32[2,64,64]{2,1,0:T(8,128)}, u32[]{:S(2)}) copy-start(f32[2,64,64]{2,1,0:T(8,128)} %inv.1) | copy-start | bytes 98308
  49.3 5.4 %copy-start.5 = (s32[2,4]{1,0:T(2,128)S(1)}, s32[2,4]{1,0:T(2,128)}, u32[]{:S(2)}) copy-start(s32[2,4]{1,0:T(2,128)} %off_cols.9) | copy-start | bytes 100
  49.3 5.4 %copy-start.7 = (f32[128]{0:T(128)S(1)}, f32[128]{0:T(128)}, u32[]{:S(2)}) copy-start(f32[128]{0:T(128)} %param.23) | copy-start | bytes 1540
  51.4 5.8 %collective-permute-start.4 = (f32[3,48,256]{2,1,0:T(8,128)S(1)}, f32[3,48,256]{2,1,0:T(8,128)S(1)}, u32[]{:S(2)}, u32[]{:S(2)}) collective-permute-start(f32[3,48,256]{2,1,0:T(8,128)S(1)} %get-tuple-element.96.after.refs_2_), channel_id=1, source_target_pairs={{0,1},{2,3},{4,5},{6,7},{1,0},{3,2},{5,4},{7,6},{8,9},{10,11},{12,... | collective-permute-start | bytes 442376 | tf_op jit(solution)/shard_map/ppermute | solution.py:614
  56.5 22.7 %collective-permute-start.5 = (f32[3,48,256]{2,1,0:T(8,128)S(1)}, f32[3,48,256]{2,1,0:T(8,128)S(1)}, u32[]{:S(2)}, u32[]{:S(2)}) collective-permute-start(f32[3,48,256]{2,1,0:T(8,128)S(1)} %second.4.refs_3_), channel_id=1, source_target_pairs={{1,2},{3,4},{5,6},{2,1},{4,3},{6,5},{9,10},{11,12},{13,14},{10,9},... | collective-permute-start | bytes 442376 | tf_op jit(solution)/shard_map/ppermute | solution.py:614
  84.5 4.9 %collective-permute-start.6 = (f32[3,48,256]{2,1,0:T(8,128)S(1)}, f32[3,48,256]{2,1,0:T(8,128)S(1)}, u32[]{:S(2)}, u32[]{:S(2)}) collective-permute-start(f32[3,48,256]{2,1,0:T(8,128)S(1)} %get-tuple-element.109.after.refs_2_), channel_id=1, source_target_pairs={{0,1},{2,3},{4,5},{6,7},{1,0},{3,2},{5,4},{7,6},{8,9},{10,11},{12,... | collective-permute-start | bytes 442376 | tf_op jit(solution)/shard_map/ppermute | solution.py:614
  86.9 18.4 %collective-permute-start.7 = (f32[3,48,256]{2,1,0:T(8,128)S(1)}, f32[3,48,256]{2,1,0:T(8,128)S(1)}, u32[]{:S(2)}, u32[]{:S(2)}) collective-permute-start(f32[3,48,256]{2,1,0:T(8,128)S(1)} %second.5.refs_3_), channel_id=1, source_target_pairs={{1,2},{3,4},{5,6},{2,1},{4,3},{6,5},{9,10},{11,12},{13,14},{10,9},... | collective-permute-start | bytes 442376 | tf_op jit(solution)/shard_map/ppermute | solution.py:614
  110.5 4.9 %collective-permute-start.8 = (f32[3,48,256]{2,1,0:T(8,128)S(1)}, f32[3,48,256]{2,1,0:T(8,128)S(1)}, u32[]{:S(2)}, u32[]{:S(2)}) collective-permute-start(f32[3,48,256]{2,1,0:T(8,128)S(1)} %get-tuple-element.122.after.refs_2_), channel_id=1, source_target_pairs={{0,1},{2,3},{4,5},{6,7},{1,0},{3,2},{5,4},{7,6},{8,9},{10,11},{12,... | collective-permute-start | bytes 442376 | tf_op jit(solution)/shard_map/ppermute | solution.py:614
  112.9 18.4 %collective-permute-start.9 = (f32[3,48,256]{2,1,0:T(8,128)S(1)}, f32[3,48,256]{2,1,0:T(8,128)S(1)}, u32[]{:S(2)}, u32[]{:S(2)}) collective-permute-start(f32[3,48,256]{2,1,0:T(8,128)S(1)} %second.6.refs_3_), channel_id=1, source_target_pairs={{1,2},{3,4},{5,6},{2,1},{4,3},{6,5},{9,10},{11,12},{13,14},{10,9},... | collective-permute-start | bytes 442376 | tf_op jit(solution)/shard_map/ppermute | solution.py:614
  136.3 4.9 %collective-permute-start.10 = (f32[3,48,256]{2,1,0:T(8,128)S(1)}, f32[3,48,256]{2,1,0:T(8,128)S(1)}, u32[]{:S(2)}, u32[]{:S(2)}) collective-permute-start(f32[3,48,256]{2,1,0:T(8,128)S(1)} %get-tuple-element.135.after.refs_2_), channel_id=1, source_target_pairs={{0,1},{2,3},{4,5},{6,7},{1,0},{3,2},{5,4},{7,6},{8,9},{10,11},{12,... | collective-permute-start | bytes 442376 | tf_op jit(solution)/shard_map/ppermute | solution.py:614
  138.7 18.4 %collective-permute-start.11 = (f32[3,48,256]{2,1,0:T(8,128)S(1)}, f32[3,48,256]{2,1,0:T(8,128)S(1)}, u32[]{:S(2)}, u32[]{:S(2)}) collective-permute-start(f32[3,48,256]{2,1,0:T(8,128)S(1)} %second.7.refs_3_), channel_id=1, source_target_pairs={{1,2},{3,4},{5,6},{2,1},{4,3},{6,5},{9,10},{11,12},{13,14},{10,9},... | collective-permute-start | bytes 442376 | tf_op jit(solution)/shard_map/ppermute | solution.py:614

commit v11 on v10

--- a/solution.py
+++ b/solution.py
@@ -113,18 +113,21 @@
     return jax.ShapeDtypeStruct((count, STACK, NX), f32)
 
 
-def slab_kernel(top, e_in, h_in, coef_in, loss_in, after, slab, sems):
+def slab_kernel(swap, e_in, h_in, coef_in, loss_in, after, slab, sems):
     copies, copy = copier(sems)
-    layers = pl.ds(CZ - DEPTH if top else 0, DEPTH)
+    even = lax.axis_index("gz") % 2 == 0
+    top, bottom = CZ - DEPTH, 0
+    start = jnp.where(even, top, bottom) if swap == 0 else jnp.where(even, bottom, top)
+    layers = pl.ds(start, DEPTH)
     for part, source in enumerate(sources_of(e_in, h_in, coef_in, loss_in)):
         copy(source.at[layers], slab.at[pl.ds(part * DEPTH, DEPTH)])
     for job in copies:
         job.wait()
 
 
-def slab_of(top, grids, after):
-    return pl.pallas_call(
-        functools.partial(slab_kernel, top),
+def slab_of(swap, grids, after):
+    return pl.pallas_call(
+        functools.partial(slab_kernel, swap),
         name="slab",
         out_shape=jax.ShapeDtypeStruct((PARTS * DEPTH, CY, NX), f32),
         in_specs=[HBM] * 4 + [ANY],
@@ -264,17 +267,19 @@
 
 
 def halo_kernel(
-    lower, upper, e_in, h_in, coef_in, loss_in, e_xy, e_z, h, media, first, second, sems,
+    came_first, came_second, e_in, h_in, coef_in, loss_in,
+    e_xy, e_z, h, media, first, second, sems,
 ):
     copies, copy = copier(sems)
+    even, high = lax.axis_index("gz") % 2 == 0, DEPTH + CZ
     targets = [
         e_xy.at[0], e_xy.at[1], e_z, h.at[0], h.at[1], h.at[2], media.at[0], media.at[1],
     ]
     for part, source in enumerate(sources_of(e_in, h_in, coef_in, loss_in)):
         given = pl.ds(part * DEPTH, DEPTH)
         copy(source, targets[part].at[pl.ds(DEPTH, CZ)])
-        copy(lower.at[given], targets[part].at[pl.ds(0, DEPTH)])
-        copy(upper.at[given], targets[part].at[pl.ds(DEPTH + CZ, DEPTH)])
+        copy(came_first.at[given], targets[part].at[pl.ds(jnp.where(even, high, 0), DEPTH)])
+        copy(came_second.at[given], targets[part].at[pl.ds(jnp.where(even, 0, high), DEPTH)])
     for job in copies:
         job.wait()
     for swap, stack in enumerate((first, second)):
@@ -602,12 +607,6 @@
     )
 
 
-def shifted(value, axis, steps):
-    count = lax.axis_size(axis)
-    first, last = (max(0, -steps), min(count, count - steps))
-    return lax.ppermute(value, axis, [(source, source + steps) for source in range(first, last)])
-
-
 def swapped(value, axis, start):
     count = lax.axis_size(axis)
     pairs = [(low, low + 1) for low in range(start, count - 1, 2)]
@@ -635,15 +634,15 @@
     n_gz, n_gy = lax.axis_size("gz"), lax.axis_size("gy")
     grids = (e_field, h_field, e_coef, e_loss)
     volts = volts_init.reshape(1, NODE_DEV)
-    up = slab_of(True, grids, volts)
-    lower = shifted(up, "gz", 1)
-    down = slab_of(False, grids, up)
-    upper = shifted(down, "gz", -1)
-    out = begin(n_gy, port_cell, port_node, port_gain, e_field, volts, down)
+    slab_first = slab_of(0, grids, volts)
+    slab_came = swapped(slab_first, "gz", 0)
+    slab_second = slab_of(1, grids, slab_first)
+    slab_next = swapped(slab_second, "gz", 1)
+    out = begin(n_gy, port_cell, port_node, port_gain, e_field, volts, slab_second)
     arrived = exchange(out)
-    lower, upper, arrived = lax.optimization_barrier((lower, upper, arrived))
+    slab_came, slab_next, arrived = lax.optimization_barrier((slab_came, slab_next, arrived))
     mats = matrices(diag_blocks, inv_blocks, off_blocks)
-    e_xy, e_z, h, media, first, second = halo(lower, upper, *grids)
+    e_xy, e_z, h, media, first, second = halo(slab_came, slab_next, *grids)
     found, columns = plan(n_gz, n_gy, arrived, port_node, port_gain)
     table = jnp.concatenate([found[0], found[1], found[7, 0:1]])
     sample, coef = samples(table, columns, e_z, media)

time: 164 us -> 163 us (level)
  starting transfers between devices: 15.5 us -> 13.6 us
    ppermute x2 -> x0, starting transfers between devices: 6.52 us -> none  [shifted(): lax.ppermute(value, axis, [(source, source + steps) for source in range(f...]
    ppermute x10 -> x12, starting transfers between devices: 8.98 us -> 13.6 us  [swapped(): lax.ppermute(value, axis, pairs + [(high, low) for low, high in pairs])]
    ppermute x10 -> x12, waiting for transfers between devices: 7.77 us -> 7.79 us  [swapped(): lax.ppermute(value, axis, pairs + [(high, low) for low, high in pairs])]
where the time goes in v11:
time: 163 us
  blocking collectives  92.4 us (57%)
  Pallas kernels  45 us (28%)
  starting transfers between devices  13.6 us (8%)
  waiting for transfers between devices  7.79 us (5%)
  local copies, waits for them, and re-layouts  2.29 us (1%)
    all_to_all x5, blocking collectives, exchange(): return lax.all_to_all(value, ('gz', 'gy'), 0, 0, tiled=True)  92.4 us
    pallas_call x5, Pallas kernels, field(): pl.pallas_call(functools.partial(field_kernel, step, 3 if first else 0),...  15.5 us
    ppermute x12, starting transfers between devices, swapped(): lax.ppermute(value, axis, pairs + [(high, low) for low, high in pairs])  13.6 us
    pallas_call x4, Pallas kernels, ports(): pl.pallas_call(functools.partial(ports_kernel, arrived.shape[0] // ND), n...  8.47 us
    ppermute x12, waiting for transfers between devices, swapped(): lax.ppermute(value, axis, pairs + [(high, low) for low, high in pairs])  7.79 us
    pallas_call x4, Pallas kernels, circuit(): pl.pallas_call(functools.partial(circuit_kernel, arrived.shape[0] // ND),...  6.79 us
    pallas_call x1, Pallas kernels, finish(): pl.pallas_call(functools.partial(finish_kernel, arrived.shape[0] // ND),...  3.46 us
  transfers between devices with their start and end apart: 12, of which 4 were waited for; matrix products, arithmetic and copies ran while one was open for 1% of the time, Pallas kernels for 7%

profile of v11, /device:TPU:1, one launch (start us, length us, event | category | flops | bytes accessed | tf_op | source)
XLA Modules:
  0.0 162.8 jit_solution(11574946409218605597)
XLA Ops:
  0.6 0.0 copy-start.6
  0.6 0.6 copy-done.6
  1.3 1.2 slab.2.after
  2.5 0.0 copy-start.1
  2.5 0.0 copy-start.2
  2.6 0.0 copy-start.8
  2.6 1.3 slab.3.after
  3.8 4.6 %collective-permute-start.1 = (f32[40,16,256]{2,1,0:T(8,128)S(1)}, f32[40,16,256]{2,1,0:T(8,128)S(1)}, u32[]{:S(2)}, u32[]{:S(2)}) collective-permute-start(f32[40,16,256]{2,1,0:T(8,128)S(1)} %slab.3.after), channel_id=1, source_target_pairs={{8,16},{24,32},{40,48},{56,64},{72,80},{88,96},{104,112},{16,8},{3... | collective-permute-start | bytes 1966088 | tf_op jit(solution)/shard_map/ppermute | solution.py:613
  8.4 0.1 collective-permute-start
  8.6 2.7 %begin.1 = f32[512,128]{1,0:T(8,128)S(1)} custom-call(s32[32]{0:T(128)S(1)} %copy-done.8, s32[4096]{0:T(1024)S(1)} %copy-done.1, f32[4096]{0:T(1024)S(1)} %copy-done.2, f32[3,32,16,256]{3,2,1,0:T(8,128)} %e_in.7, s32[1,32]{1,0:T(1,128)S(1)} %bitcast.40, f32[1,128]{1,0:T(1,128)S(1)} %bitcast.38, f32[40,16,256]{2,1,0:T(8,128)S(1)} %slab.3.after), custom_call_target="tpu_custom_call" | custom-call | tf_op jit(solution)/shard_map/begin/pallas_call | solution.py:166
  11.2 21.2 %all_to_all.60 = f32[128,4,128]{2,1,0:T(4,128)S(1)} all-to-all(f32[128,4,128]{2,1,0:T(4,128)S(1)} %bitcast.29), channel_id=1, replica_groups=mesh['gz'=16,'gy'=8] {'gz','gy'}, dimensions={0} | all-to-all | bytes 524288 | tf_op jit(solution)/shard_map/all_to_all | solution.py:617
  32.4 0.0 collective-permute-done.1.came_second
  32.4 0.0 collective-permute-done.came_first
  32.4 0.0 copy-start.10
  32.4 0.8 copy-done.9
  33.2 0.2 copy-done.10
  33.4 3.2 %halo.1 = (f32[2,42,16,256]{3,2,1,0:T(8,128)S(1)}, f32[42,16,256]{2,1,0:T(8,128)S(1)}, f32[3,42,16,256]{3,2,1,0:T(8,128)S(1)}, f32[2,42,16,256]{3,2,1,0:T(8,128)...) custom-call(f32[40,16,256]{2,1,0:T(8,128)} %copy-done.10, f32[40,16,256]{2,1,0:T(8,128)} %copy-done.9, ...), custom_call_target="tpu_custom_call" | custom-call | tf_op jit(solution)/shard_map/halo/pallas_call | solution.py:310
  36.6 0.6 collective-permute-start.2
  37.2 0.7 collective-permute-start.3
  37.9 0.4 plan.1
  38.4 0.5 slice.11
  38.9 0.7 pad_add_fusion.found.table
  39.6 1.4 samples.1
  41.1 2.5 %collective-permute-done.2.refs_0_.refs_4_ = f32[5,48,256]{2,1,0:T(8,128)S(1)} collective-permute-done((f32[5,48,256]{2,1,0:T(8,128)S(1)}, f32[5,48,256]{2,1,0:T(8,128)S(1)}, u32[]{:S(2)}, u32[]{:S(2)}) %collective-permute-start.2) | collective-permute-done | bytes 245792 | tf_op jit(solution)/shard_map/ppermute | solution.py:613
  43.6 3.3 %field.5 = (f32[2,42,16,256]{3,2,1,0:T(8,128)S(1)}, f32[42,16,256]{2,1,0:T(8,128)S(1)}, f32[3,42,16,256]{3,2,1,0:T(8,128)S(1)}, f32[2,48,256]{2,1,0:T(8,128)S(1)}) custom-call(f32[5,48,256]{2,1,0:T(8,128)S(1)} %collective-permute-done.2.refs_0_.refs_4_, f32[5,48,256]{2,1,0:T(8,128)S(1)} %collective-permute-done.3.refs_1_, ...), custom_call_target="tpu_custom_call" | custom-call | tf_op jit(solution)/shard_map/field/pallas_call | solution.py:438
  46.9 0.0 copy-start
  46.9 0.0 copy-start.3
  46.9 0.0 copy-start.4
  46.9 0.0 copy-start.5
  46.9 0.0 copy-start.7
  46.9 2.1 %ports.4 = (f32[42,16,256]{2,1,0:T(8,128)S(1)}, f32[3,48,256]{2,1,0:T(8,128)S(1)}) custom-call(s32[193]{0:T(256)S(1)} %pad_add_fusion.found.table, f32[512,128]{1,0:T(8,128)S(1)} %bitcast.21, f32[96,8]{1,0:T(8,128)S(1)} %get-tuple-element.79.columns, f32[96,1]{1,0:T(8,128)S(1)} %get-tuple-element.87.sample, f32[96,1]{1,0:T(8,128)S(1)} %get-tuple-element.88.coef, ...), custom_call_target="tpu_custom_call" | custom-call | tf_op jit(solution)/shard_map/ports/pallas_call | solution.py:511
  49.0 3.1 %collective-permute-start.4 = (f32[3,48,256]{2,1,0:T(8,128)S(1)}, f32[3,48,256]{2,1,0:T(8,128)S(1)}, u32[]{:S(2)}, u32[]{:S(2)}) collective-permute-start(f32[3,48,256]{2,1,0:T(8,128)S(1)} %get-tuple-element.96.after.refs_2_), channel_id=1, source_target_pairs={{0,1},{2,3},{4,5},{6,7},{1,0},{3,2},{5,4},{7,6},{8,9},{10,11},{12,... | collective-permute-start | bytes 442376 | tf_op jit(solution)/shard_map/ppermute | solution.py:613
  52.2 0.2 matrices.1
  52.3 1.7 %circuit.4 = (f32[256,128]{1,0:T(8,128)S(1)}, f32[1,128]{1,0:T(1,128)S(1)}, f32[96,1]{1,0:T(8,128)S(1)}) custom-call(s32[193]{0:T(256)S(1)} %pad_add_fusion.found.table, s32[2,4]{1,0:T(2,128)S(1)} %copy-done.5, f32[512,128]{1,0:T(8,128)S(1)} %bitcast.22, f32[96,8]{1,0:T(8,128)S(1)} %get-tuple-element.79.columns, f32[1,128]{1,0:T(1,128)S(1)} %bitcast.39, ...), custom_call_target="tpu_custom_call" | custom-call | tf_op jit(solution)/shard_map/circuit/pallas_call | solution.py:557
  54.1 0.1 second.4.refs_3_
  54.1 0.7 collective-permute-start.5
  54.8 23.3 %all_to_all.61 = f32[128,2,128]{2,1,0:T(2,128)S(1)} all-to-all(f32[128,2,128]{2,1,0:T(2,128)S(1)} %bitcast.34), channel_id=1, replica_groups=mesh['gz'=16,'gy'=8] {'gz','gy'}, dimensions={0} | all-to-all | bytes 262144 | tf_op jit(solution)/shard_map/all_to_all | solution.py:617
  78.2 0.0 collective-permute-done.5.refs_1_
  78.2 3.1 %field.6 = (f32[2,42,16,256]{3,2,1,0:T(8,128)S(1)}, f32[42,16,256]{2,1,0:T(8,128)S(1)}, f32[3,42,16,256]{3,2,1,0:T(8,128)S(1)}, f32[2,48,256]{2,1,0:T(8,128)S(1)}) custom-call(f32[3,48,256]{2,1,0:T(8,128)S(1)} %collective-permute-done.4.refs_0_, f32[3,48,256]{2,1,0:T(8,128)S(1)} %collective-permute-done.5.refs_1_, ...), custom_call_target="tpu_custom_call" | custom-call | tf_op jit(solution)/shard_map/field/pallas_call | solution.py:438
  81.3 2.1 %ports.5 = (f32[42,16,256]{2,1,0:T(8,128)S(1)}, f32[3,48,256]{2,1,0:T(8,128)S(1)}) custom-call(s32[193]{0:T(256)S(1)} %pad_add_fusion.found.table, f32[256,128]{1,0:T(8,128)S(1)} %bitcast.23, f32[96,8]{1,0:T(8,128)S(1)} %get-tuple-element.79.columns, f32[96,1]{1,0:T(8,128)S(1)} %get-tuple-element.101.sample, f32[96,1]{1,0:T(8,128)S(1)} %get-tuple-element.88.coef, ...), custom_call_target="tpu_custom_call" | custom-call | tf_op jit(solution)/shard_map/ports/pallas_call | solution.py:511
  83.5 0.6 collective-permute-start.6
  84.1 1.7 %circuit.5 = (f32[256,128]{1,0:T(8,128)S(1)}, f32[1,128]{1,0:T(1,128)S(1)}, f32[96,1]{1,0:T(8,128)S(1)}) custom-call(s32[193]{0:T(256)S(1)} %pad_add_fusion.found.table, s32[2,4]{1,0:T(2,128)S(1)} %copy-done.5, f32[256,128]{1,0:T(8,128)S(1)} %bitcast.24, f32[96,8]{1,0:T(8,128)S(1)} %get-tuple-element.79.columns, f32[1,128]{1,0:T(1,128)S(1)} %get-tuple-element.100.volts, ...), custom_call_target="tpu_custom_call" | custom-call | tf_op jit(solution)/shard_map/circuit/pallas_call | solution.py:557
  85.8 0.1 second.5.refs_3_
  85.9 0.7 collective-permute-start.7
  86.6 1.8 %collective-permute-done.6.refs_0_ = f32[3,48,256]{2,1,0:T(8,128)S(1)} collective-permute-done((f32[3,48,256]{2,1,0:T(8,128)S(1)}, f32[3,48,256]{2,1,0:T(8,128)S(1)}, u32[]{:S(2)}, u32[]{:S(2)}) %collective-permute-start.6) | collective-permute-done | bytes 147488 | tf_op jit(solution)/shard_map/ppermute | solution.py:613
  88.3 16.0 %all_to_all.62 = f32[128,2,128]{2,1,0:T(2,128)S(1)} all-to-all(f32[128,2,128]{2,1,0:T(2,128)S(1)} %bitcast.31), channel_id=1, replica_groups=mesh['gz'=16,'gy'=8] {'gz','gy'}, dimensions={0} | all-to-all | bytes 262144 | tf_op jit(solution)/shard_map/all_to_all | solution.py:617
  104.3 3.0 %field.7 = (f32[2,42,16,256]{3,2,1,0:T(8,128)S(1)}, f32[42,16,256]{2,1,0:T(8,128)S(1)}, f32[3,42,16,256]{3,2,1,0:T(8,128)S(1)}, f32[2,48,256]{2,1,0:T(8,128)S(1)}) custom-call(f32[3,48,256]{2,1,0:T(8,128)S(1)} %collective-permute-done.6.refs_0_, f32[3,48,256]{2,1,0:T(8,128)S(1)} %collective-permute-done.7.refs_1_, ...), custom_call_target="tpu_custom_call" | custom-call | tf_op jit(solution)/shard_map/field/pallas_call | solution.py:438
  107.3 2.1 %ports.6 = (f32[42,16,256]{2,1,0:T(8,128)S(1)}, f32[3,48,256]{2,1,0:T(8,128)S(1)}) custom-call(s32[193]{0:T(256)S(1)} %pad_add_fusion.found.table, f32[256,128]{1,0:T(8,128)S(1)} %bitcast.25, f32[96,8]{1,0:T(8,128)S(1)} %get-tuple-element.79.columns, f32[96,1]{1,0:T(8,128)S(1)} %get-tuple-element.114.sample, f32[96,1]{1,0:T(8,128)S(1)} %get-tuple-element.88.coef, ...), custom_call_target="tpu_custom_call" | custom-call | tf_op jit(solution)/shard_map/ports/pallas_call | solution.py:511
  109.4 0.6 collective-permute-start.8
  110.1 1.7 %circuit.6 = (f32[256,128]{1,0:T(8,128)S(1)}, f32[1,128]{1,0:T(1,128)S(1)}, f32[96,1]{1,0:T(8,128)S(1)}) custom-call(s32[193]{0:T(256)S(1)} %pad_add_fusion.found.table, s32[2,4]{1,0:T(2,128)S(1)} %copy-done.5, f32[256,128]{1,0:T(8,128)S(1)} %bitcast.26, f32[96,8]{1,0:T(8,128)S(1)} %get-tuple-element.79.columns, f32[1,128]{1,0:T(1,128)S(1)} %get-tuple-element.113.volts, ...), custom_call_target="tpu_custom_call" | custom-call | tf_op jit(solution)/shard_map/circuit/pallas_call | solution.py:557
  111.7 0.1 second.6.refs_3_
  111.8 0.7 collective-permute-start.9
  112.5 1.8 %collective-permute-done.8.refs_0_ = f32[3,48,256]{2,1,0:T(8,128)S(1)} collective-permute-done((f32[3,48,256]{2,1,0:T(8,128)S(1)}, f32[3,48,256]{2,1,0:T(8,128)S(1)}, u32[]{:S(2)}, u32[]{:S(2)}) %collective-permute-start.8) | collective-permute-done | bytes 147488 | tf_op jit(solution)/shard_map/ppermute | solution.py:613
  114.3 16.0 %all_to_all.63 = f32[128,2,128]{2,1,0:T(2,128)S(1)} all-to-all(f32[128,2,128]{2,1,0:T(2,128)S(1)} %bitcast.32), channel_id=1, replica_groups=mesh['gz'=16,'gy'=8] {'gz','gy'}, dimensions={0} | all-to-all | bytes 262144 | tf_op jit(solution)/shard_map/all_to_all | solution.py:617
  130.3 2.8 %field.8 = (f32[2,42,16,256]{3,2,1,0:T(8,128)S(1)}, f32[42,16,256]{2,1,0:T(8,128)S(1)}, f32[3,42,16,256]{3,2,1,0:T(8,128)S(1)}, f32[2,48,256]{2,1,0:T(8,128)S(1)}) custom-call(f32[3,48,256]{2,1,0:T(8,128)S(1)} %collective-permute-done.8.refs_0_, f32[3,48,256]{2,1,0:T(8,128)S(1)} %collective-permute-done.9.refs_1_, ...), custom_call_target="tpu_custom_call" | custom-call | tf_op jit(solution)/shard_map/field/pallas_call | solution.py:438
  133.1 2.1 %ports.7 = (f32[42,16,256]{2,1,0:T(8,128)S(1)}, f32[3,48,256]{2,1,0:T(8,128)S(1)}) custom-call(s32[193]{0:T(256)S(1)} %pad_add_fusion.found.table, f32[256,128]{1,0:T(8,128)S(1)} %bitcast.27, f32[96,8]{1,0:T(8,128)S(1)} %get-tuple-element.79.columns, f32[96,1]{1,0:T(8,128)S(1)} %get-tuple-element.127.sample, f32[96,1]{1,0:T(8,128)S(1)} %get-tuple-element.88.coef, ...), custom_call_target="tpu_custom_call" | custom-call | tf_op jit(solution)/shard_map/ports/pallas_call | solution.py:511
  135.2 0.6 collective-permute-start.10
  135.9 1.7 %circuit.7 = (f32[256,128]{1,0:T(8,128)S(1)}, f32[1,128]{1,0:T(1,128)S(1)}, f32[96,1]{1,0:T(8,128)S(1)}) custom-call(s32[193]{0:T(256)S(1)} %pad_add_fusion.found.table, s32[2,4]{1,0:T(2,128)S(1)} %copy-done.5, f32[256,128]{1,0:T(8,128)S(1)} %bitcast.28, f32[96,8]{1,0:T(8,128)S(1)} %get-tuple-element.79.columns, f32[1,128]{1,0:T(1,128)S(1)} %get-tuple-element.126.volts, ...), custom_call_target="tpu_custom_call" | custom-call | tf_op jit(solution)/shard_map/circuit/pallas_call | solution.py:557
  137.5 0.1 second.7.refs_3_
  137.6 0.7 collective-permute-start.11
  138.3 1.8 %collective-permute-done.10.refs_0_ = f32[3,48,256]{2,1,0:T(8,128)S(1)} collective-permute-done((f32[3,48,256]{2,1,0:T(8,128)S(1)}, f32[3,48,256]{2,1,0:T(8,128)S(1)}, u32[]{:S(2)}, u32[]{:S(2)}) %collective-permute-start.10) | collective-permute-done | bytes 147488 | tf_op jit(solution)/shard_map/ppermute | solution.py:613
  140.1 16.0 %all_to_all.64 = f32[128,2,128]{2,1,0:T(2,128)S(1)} all-to-all(f32[128,2,128]{2,1,0:T(2,128)S(1)} %bitcast.33), channel_id=1, replica_groups=mesh['gz'=16,'gy'=8] {'gz','gy'}, dimensions={0} | all-to-all | bytes 262144 | tf_op jit(solution)/shard_map/all_to_all | solution.py:617
  156.1 3.3 %field.9 = (f32[2,42,16,256]{3,2,1,0:T(8,128)S(1)}, f32[42,16,256]{2,1,0:T(8,128)S(1)}, f32[3,42,16,256]{3,2,1,0:T(8,128)S(1)}, f32[2,48,256]{2,1,0:T(8,128)}) custom-call(f32[3,48,256]{2,1,0:T(8,128)S(1)} %collective-permute-done.10.refs_0_, f32[3,48,256]{2,1,0:T(8,128)S(1)} %collective-permute-done.11.refs_1_, ...), custom_call_target="tpu_custom_call" | custom-call | tf_op jit(solution)/shard_map/field/pallas_call | solution.py:438
  159.3 3.5 %finish.1 = (f32[3,32,16,256]{3,2,1,0:T(8,128)}, f32[3,32,16,256]{3,2,1,0:T(8,128)}, f32[1,128]{1,0:T(1,128)}) custom-call(s32[193]{0:T(256)S(1)} %pad_add_fusion.found.table, s32[2,4]{1,0:T(2,128)S(1)} %copy-done.5, f32[256,128]{1,0:T(8,128)S(1)} %bitcast.30, f32[96,8]{1,0:T(8,128)S(1)} %get-tuple-element.79.columns, ...), custom_call_target="tpu_custom_call" | custom-call | tf_op jit(solution)/shard_map/finish/pallas_call | solution.py:587
  (15 shorter events, 0.0 us)
Async XLA Ops:
  0.6 0.7 copy-start.6
  2.5 6.0 %copy-start.1 = (s32[4096]{0:T(1024)S(1)}, s32[4096]{0:T(1024)}, u32[]{:S(2)}) copy-start(s32[4096]{0:T(1024)} %nodes.1) | copy-start | bytes 49156
  2.5 6.0 %copy-start.2 = (f32[4096]{0:T(1024)S(1)}, f32[4096]{0:T(1024)}, u32[]{:S(2)}) copy-start(f32[4096]{0:T(1024)} %gains.1) | copy-start | bytes 49156
  2.6 6.0 %copy-start.8 = (s32[32]{0:T(128)S(1)}, s32[32]{0:T(128)}, u32[]{:S(2)}) copy-start(s32[32]{0:T(128)} %cells.1) | copy-start | bytes 388
  3.8 28.6 %collective-permute-start.1 = (f32[40,16,256]{2,1,0:T(8,128)S(1)}, f32[40,16,256]{2,1,0:T(8,128)S(1)}, u32[]{:S(2)}, u32[]{:S(2)}) collective-permute-start(f32[40,16,256]{2,1,0:T(8,128)S(1)} %slab.3.after), channel_id=1, source_target_pairs={{8,16},{24,32},{40,48},{56,64},{72,80},{88,96},{104,112},{16,8},{3... | collective-permute-start | bytes 1966088 | tf_op jit(solution)/shard_map/ppermute | solution.py:613
  8.4 24.0 %collective-permute-start = (f32[40,16,256]{2,1,0:T(8,128)S(1)}, f32[40,16,256]{2,1,0:T(8,128)S(1)}, u32[]{:S(2)}, u32[]{:S(2)}) collective-permute-start(f32[40,16,256]{2,1,0:T(8,128)S(1)} %slab.2.after), channel_id=1, source_target_pairs={{0,8},{16,24},{32,40},{48,56},{64,72},{80,88},{96,104},{112,120},{... | collective-permute-start | bytes 1966088 | tf_op jit(solution)/shard_map/ppermute | solution.py:613
  32.4 0.8 copy-start.9
  32.4 1.0 copy-start.10
  36.6 6.9 %collective-permute-start.2 = (f32[5,48,256]{2,1,0:T(8,128)S(1)}, f32[5,48,256]{2,1,0:T(8,128)S(1)}, u32[]{:S(2)}, u32[]{:S(2)}) collective-permute-start(f32[5,48,256]{2,1,0:T(8,128)S(1)} %get-tuple-element.89.refs_2_), channel_id=1, source_target_pairs={{0,1},{2,3},{4,5},{6,7},{1,0},{3,2},{5,4},{7,6},{8,9},{10,11},{12,... | collective-permute-start | bytes 737288 | tf_op jit(solution)/shard_map/ppermute | solution.py:613
  37.2 6.3 %collective-permute-start.3 = (f32[5,48,256]{2,1,0:T(8,128)S(1)}, f32[5,48,256]{2,1,0:T(8,128)S(1)}, u32[]{:S(2)}, u32[]{:S(2)}) collective-permute-start(f32[5,48,256]{2,1,0:T(8,128)S(1)} %get-tuple-element.90.refs_3_), channel_id=1, source_target_pairs={{1,2},{3,4},{5,6},{2,1},{4,3},{6,5},{9,10},{11,12},{13,14},{10,9},... | collective-permute-start | bytes 737288 | tf_op jit(solution)/shard_map/ppermute | solution.py:613
  46.9 5.3 %copy-start = (f32[2,4,64,64]{3,2,1,0:T(8,128)S(1)}, f32[2,4,64,64]{3,2,1,0:T(8,128)}, u32[]{:S(2)}) copy-start(f32[2,4,64,64]{3,2,1,0:T(8,128)} %off.1) | copy-start | bytes 393220
  46.9 5.3 %copy-start.3 = (f32[2,64,64]{2,1,0:T(8,128)S(1)}, f32[2,64,64]{2,1,0:T(8,128)}, u32[]{:S(2)}) copy-start(f32[2,64,64]{2,1,0:T(8,128)} %diag.1) | copy-start | bytes 98308
  46.9 5.3 %copy-start.4 = (f32[2,64,64]{2,1,0:T(8,128)S(1)}, f32[2,64,64]{2,1,0:T(8,128)}, u32[]{:S(2)}) copy-start(f32[2,64,64]{2,1,0:T(8,128)} %inv.1) | copy-start | bytes 98308
  46.9 5.4 %copy-start.5 = (s32[2,4]{1,0:T(2,128)S(1)}, s32[2,4]{1,0:T(2,128)}, u32[]{:S(2)}) copy-start(s32[2,4]{1,0:T(2,128)} %off_cols.9) | copy-start | bytes 100
  46.9 5.4 %copy-start.7 = (f32[128]{0:T(128)S(1)}, f32[128]{0:T(128)}, u32[]{:S(2)}) copy-start(f32[128]{0:T(128)} %param.23) | copy-start | bytes 1540
  49.0 5.8 %collective-permute-start.4 = (f32[3,48,256]{2,1,0:T(8,128)S(1)}, f32[3,48,256]{2,1,0:T(8,128)S(1)}, u32[]{:S(2)}, u32[]{:S(2)}) collective-permute-start(f32[3,48,256]{2,1,0:T(8,128)S(1)} %get-tuple-element.96.after.refs_2_), channel_id=1, source_target_pairs={{0,1},{2,3},{4,5},{6,7},{1,0},{3,2},{5,4},{7,6},{8,9},{10,11},{12,... | collective-permute-start | bytes 442376 | tf_op jit(solution)/shard_map/ppermute | solution.py:613
  54.1 24.0 %collective-permute-start.5 = (f32[3,48,256]{2,1,0:T(8,128)S(1)}, f32[3,48,256]{2,1,0:T(8,128)S(1)}, u32[]{:S(2)}, u32[]{:S(2)}) collective-permute-start(f32[3,48,256]{2,1,0:T(8,128)S(1)} %second.4.refs_3_), channel_id=1, source_target_pairs={{1,2},{3,4},{5,6},{2,1},{4,3},{6,5},{9,10},{11,12},{13,14},{10,9},... | collective-permute-start | bytes 442376 | tf_op jit(solution)/shard_map/ppermute | solution.py:613
  83.5 4.9 %collective-permute-start.6 = (f32[3,48,256]{2,1,0:T(8,128)S(1)}, f32[3,48,256]{2,1,0:T(8,128)S(1)}, u32[]{:S(2)}, u32[]{:S(2)}) collective-permute-start(f32[3,48,256]{2,1,0:T(8,128)S(1)} %get-tuple-element.109.after.refs_2_), channel_id=1, source_target_pairs={{0,1},{2,3},{4,5},{6,7},{1,0},{3,2},{5,4},{7,6},{8,9},{10,11},{12,... | collective-permute-start | bytes 442376 | tf_op jit(solution)/shard_map/ppermute | solution.py:613
  85.9 18.4 %collective-permute-start.7 = (f32[3,48,256]{2,1,0:T(8,128)S(1)}, f32[3,48,256]{2,1,0:T(8,128)S(1)}, u32[]{:S(2)}, u32[]{:S(2)}) collective-permute-start(f32[3,48,256]{2,1,0:T(8,128)S(1)} %second.5.refs_3_), channel_id=1, source_target_pairs={{1,2},{3,4},{5,6},{2,1},{4,3},{6,5},{9,10},{11,12},{13,14},{10,9},... | collective-permute-start | bytes 442376 | tf_op jit(solution)/shard_map/ppermute | solution.py:613
  109.4 4.9 %collective-permute-start.8 = (f32[3,48,256]{2,1,0:T(8,128)S(1)}, f32[3,48,256]{2,1,0:T(8,128)S(1)}, u32[]{:S(2)}, u32[]{:S(2)}) collective-permute-start(f32[3,48,256]{2,1,0:T(8,128)S(1)} %get-tuple-element.122.after.refs_2_), channel_id=1, source_target_pairs={{0,1},{2,3},{4,5},{6,7},{1,0},{3,2},{5,4},{7,6},{8,9},{10,11},{12,... | collective-permute-start | bytes 442376 | tf_op jit(solution)/shard_map/ppermute | solution.py:613
  111.8 18.4 %collective-permute-start.9 = (f32[3,48,256]{2,1,0:T(8,128)S(1)}, f32[3,48,256]{2,1,0:T(8,128)S(1)}, u32[]{:S(2)}, u32[]{:S(2)}) collective-permute-start(f32[3,48,256]{2,1,0:T(8,128)S(1)} %second.6.refs_3_), channel_id=1, source_target_pairs={{1,2},{3,4},{5,6},{2,1},{4,3},{6,5},{9,10},{11,12},{13,14},{10,9},... | collective-permute-start | bytes 442376 | tf_op jit(solution)/shard_map/ppermute | solution.py:613
  135.2 4.9 %collective-permute-start.10 = (f32[3,48,256]{2,1,0:T(8,128)S(1)}, f32[3,48,256]{2,1,0:T(8,128)S(1)}, u32[]{:S(2)}, u32[]{:S(2)}) collective-permute-start(f32[3,48,256]{2,1,0:T(8,128)S(1)} %get-tuple-element.135.after.refs_2_), channel_id=1, source_target_pairs={{0,1},{2,3},{4,5},{6,7},{1,0},{3,2},{5,4},{7,6},{8,9},{10,11},{12,... | collective-permute-start | bytes 442376 | tf_op jit(solution)/shard_map/ppermute | solution.py:613
  137.6 18.4 %collective-permute-start.11 = (f32[3,48,256]{2,1,0:T(8,128)S(1)}, f32[3,48,256]{2,1,0:T(8,128)S(1)}, u32[]{:S(2)}, u32[]{:S(2)}) collective-permute-start(f32[3,48,256]{2,1,0:T(8,128)S(1)} %second.7.refs_3_), channel_id=1, source_target_pairs={{1,2},{3,4},{5,6},{2,1},{4,3},{6,5},{9,10},{11,12},{13,14},{10,9},... | collective-permute-start | bytes 442376 | tf_op jit(solution)/shard_map/ppermute | solution.py:613
